TPU v7x, 32 devices: a whole 2x2x4 slice. The times are simulated.
32 devices in a mesh: dp: 16 (over z, y, x), tensor: 2 (over core).
Axes of the slice: x: 2, y: 2, z: 4, core: 2. Of those that a mesh axis runs over, the one named last changes fastest.
Arguments:
- tokens: bfloat16 [16, 512, 384], P('dp'), may hold values from -6 to 6
- lengths: int32 [16], replicated, may hold values from 1 to 512, 5120 in all
- dealing: int32 [16], replicated, may hold values from 0 to 15, each once
- bucket_table: int32 [1023], replicated, may hold values from 0 to 511, as said below
- relative: bfloat16 [512, 384], replicated, may hold values from -6 to 6
- w_query: bfloat16 [384, 384], P(None, 'tensor'), may hold values from -0.3125 to 0.3125
- b_query: bfloat16 [384], P('tensor'), may hold values from -3 to 3
- w_key: bfloat16 [384, 384], P(None, 'tensor'), may hold values from -0.3125 to 0.3125
- b_key: bfloat16 [384], P('tensor'), may hold values from -3 to 3
- w_value: bfloat16 [384, 384], P(None, 'tensor'), may hold values from -0.3125 to 0.3125
- b_value: bfloat16 [384], P('tensor'), may hold values from -3 to 3
- w_out: bfloat16 [384, 384], P('tensor'), may hold values from -3 to 3
- b_out: bfloat16 [384], replicated, may hold values from -3 to 3
- attn_gain: bfloat16 [384], replicated, may hold values from 0.25 to 1.75
- attn_shift: bfloat16 [384], replicated, may hold values from -3 to 3
- w_up: bfloat16 [384, 1536], P(None, 'tensor'), may hold values from -0.3125 to 0.3125
- b_up: bfloat16 [1536], P('tensor'), may hold values from -3 to 3
- w_down: bfloat16 [1536, 384], P('tensor'), may hold values from -0.21875 to 0.21875
- b_down: bfloat16 [384], replicated, may hold values from -3 to 3
- ffn_gain: bfloat16 [384], replicated, may hold values from 0.25 to 1.75
- ffn_shift: bfloat16 [384], replicated, may hold values from -3 to 3
- cotangent: bfloat16 [16, 512, 384], P('dp'), may hold values from -6 to 6
Outputs:
- y_out: bfloat16 [16, 512, 384], P('dp')
- grad_tokens: bfloat16 [16, 512, 384], P('dp')
- grad_relative_embedding: float32 [512, 384], replicated
- grad_w_query: float32 [384, 384], P(None, 'tensor')
- grad_b_query: float32 [384], P('tensor')
- grad_w_key: float32 [384, 384], P(None, 'tensor')
- grad_b_key: float32 [384], P('tensor')
- grad_w_value: float32 [384, 384], P(None, 'tensor')
- grad_b_value: float32 [384], P('tensor')
- grad_w_out: float32 [384, 384], P('tensor')
- grad_b_out: float32 [384], replicated
- grad_attn_gain: float32 [384], replicated
- grad_attn_shift: float32 [384], replicated
- grad_w_up: float32 [384, 1536], P(None, 'tensor')
- grad_b_up: float32 [1536], P('tensor')
- grad_w_down: float32 [1536, 384], P('tensor')
- grad_b_down: float32 [384], replicated
- grad_ffn_gain: float32 [384], replicated
- grad_ffn_shift: float32 [384], replicated
Inputs may be any that keep to these rules, and one draw needn't show every extreme that they name: Each of 0 to 15 appears once; slot k of the dealt order holds initial sequence dealing[k], and dp index g holds slots g * 1 to (g + 1) - 1. `bucket_table`: nondecreasing along its entries; entry a - b + 511 is the bucket of position a relative to position b.
All inputs are finite; a program needn't handle non-finite values.
Results may differ from a plain program's by a relative error of at most 0.024.
Values may be sent and summed in bfloat16 or wider, within the bound.
No kernel may reach another device: no remote copies, remote signals or barrier semaphores. Data moves between devices by JAX's collectives and lax.ppermute only.
A program may use at most 128 MiB of HBM per device.

v0:
```python
from functools import partial
import math

import jax
import jax.numpy as jnp
from jax import lax
from jax.sharding import PartitionSpec as P

HEAD_DIM = 64


EPSILON = 1e-07
PRECISION_FULL = lax.Precision.HIGHEST
ROOT_HALF = 0.7071067811865476
INV_ROOT_TAU = 0.3989422804014327


def norm_forward(values, norm_gain, norm_shift):
    center = values - jnp.mean(values, axis=-1, keepdims=True)
    inverse = lax.rsqrt(jnp.mean(center * center, axis=-1, keepdims=True) + EPSILON)
    normed = center * inverse
    return (normed * norm_gain + norm_shift, normed, inverse)


def norm_backward(upstream, normed, inverse, norm_gain):
    scaled = upstream * norm_gain
    mean_one = jnp.mean(scaled, axis=-1, keepdims=True)
    mean_two = jnp.mean(scaled * normed, axis=-1, keepdims=True)
    return inverse * (scaled - mean_one - normed * mean_two)


def contract_rows(left, right):
    return lax.dot_general(
        left, right, (((0,), (0,)), ((), ())), preferred_element_type=jnp.float32
    )


def contract_cols(left, right):
    return lax.dot_general(
        left, right, (((1,), (1,)), ((), ())), preferred_element_type=jnp.float32
    )


def exact_rows(left, right):
    return lax.dot_general(
        left,
        right,
        (((0,), (0,)), ((), ())),
        precision=PRECISION_FULL,
        preferred_element_type=jnp.float32,
    )


def exact_cols(left, right):
    return lax.dot_general(
        left,
        right,
        (((1,), (1,)), ((), ())),
        precision=PRECISION_FULL,
        preferred_element_type=jnp.float32,
    )


def skew_rows(values, out_cols):
    heads_now, row_count, width_now = values.shape
    padded = jnp.pad(values, ((0, 0), (0, 0), (0, 1)))
    flat = padded.reshape(heads_now, row_count * (width_now + 1))
    flat = jnp.pad(flat, ((0, 0), (0, row_count)))
    return flat.reshape(heads_now, row_count, width_now + 2)[:, :, :out_cols]


def place_near(values, out_cols):
    return jnp.flip(skew_rows(values, out_cols), 2)


def place_far(values, out_cols):
    return jnp.transpose(jnp.flip(skew_rows(values, out_cols), 2), (0, 2, 1))


def block_scores(query_tile_block, key_rows, pk_slice, pq_slice, key_valid, score_scale):
    block_rows = query_tile_block.shape[0]
    seq_rows = key_rows.shape[0]
    content = jnp.einsum(
        "ihd,jhd->hij", query_tile_block, key_rows, preferred_element_type=jnp.float32
    )
    near_terms = jnp.einsum(
        "ihd,thd->hit", query_tile_block, pk_slice, preferred_element_type=jnp.float32
    )
    far_terms = jnp.einsum("jhd,thd->hjt", key_rows, pq_slice, preferred_element_type=jnp.float32)
    to_pos, pull_near = jax.vjp(lambda values: place_near(values, seq_rows), near_terms)
    from_pos, pull_far = jax.vjp(lambda values: place_far(values, block_rows), far_terms)
    scores = (content + to_pos + from_pos) * score_scale
    return (jnp.where(key_valid[None, None, :], scores, -1e30), pull_near, pull_far)


def offset_slices(pk_offsets, pq_offsets, bucket_table):
    return (pk_offsets, pq_offsets, bucket_table, bucket_table)


def sequence_forward(seq_item, pk_offsets, pq_offsets, bucket_table, block_rows, score_scale):
    queries, key_rows, value_rows, length_now = seq_item
    seq_rows = queries.shape[0]
    key_valid = jnp.arange(seq_rows, dtype=jnp.int32) < length_now

    def one_block(first_row):
        pk_slice, pq_slice, near_ids, far_ids = offset_slices(pk_offsets, pq_offsets, bucket_table)
        scores, pull_near, pull_far = block_scores(
            queries, key_rows, pk_slice, pq_slice, key_valid, score_scale
        )
        row_max = jnp.max(scores, axis=2, keepdims=True)
        log_total = row_max + jnp.log(jnp.sum(jnp.exp(scores - row_max), axis=2, keepdims=True))
        row_valid = first_row + jnp.arange(block_rows, dtype=jnp.int32) < length_now
        weights = jnp.where(row_valid[None, :, None], jnp.exp(scores - log_total), 0.0)
        context = jnp.einsum(
            "hij,jhd->ihd",
            weights.astype(jnp.bfloat16),
            value_rows,
            preferred_element_type=jnp.float32,
        )
        return (context.astype(jnp.bfloat16), log_total[:, :, 0])

    first_rows = jnp.arange(0, seq_rows, block_rows, dtype=jnp.int32)
    contexts, log_totals = lax.map(one_block, first_rows)
    return (contexts.reshape(queries.shape), log_totals)


def sequence_backward(
    seq_carry,
    seq_item,
    pos_query,
    position_key,
    pk_offsets,
    pq_offsets,
    bucket_table,
    block_rows,
    score_scale,
):
    pos_key_sum, pos_query_sum = seq_carry
    queries, key_rows, value_rows, length_now, log_totals, grad_context = seq_item
    seq_rows, heads_here, head_dim = queries.shape
    buckets = pos_query.shape[0]
    key_valid = jnp.arange(seq_rows, dtype=jnp.int32) < length_now

    def one_block(block_state, block_item):
        grad_keys, grad_values, grad_table, grad_pos_key = block_state
        first_row, log_total = block_item
        pk_slice, pq_slice, near_ids, far_ids = offset_slices(pk_offsets, pq_offsets, bucket_table)
        scores, pull_near, pull_far = block_scores(
            queries, key_rows, pk_slice, pq_slice, key_valid, score_scale
        )
        row_valid = first_row + jnp.arange(block_rows, dtype=jnp.int32) < length_now
        weights = jnp.where(row_valid[None, :, None], jnp.exp(scores - log_total[:, :, None]), 0.0)
        grad_weights = jnp.einsum(
            "ihd,jhd->hij", grad_context, value_rows, preferred_element_type=jnp.float32
        )
        row_dot = jnp.sum(weights * grad_weights, axis=2, keepdims=True)
        grad_scores = (weights * (grad_weights - row_dot)).astype(jnp.bfloat16)
        grad_values = grad_values + jnp.einsum(
            "hij,ihd->jhd",
            weights.astype(jnp.bfloat16),
            grad_context,
            preferred_element_type=jnp.float32,
        )
        grad_keys = grad_keys + score_scale * jnp.einsum(
            "hij,ihd->jhd", grad_scores, queries, preferred_element_type=jnp.float32
        )
        scaled_scores = score_scale * grad_scores.astype(jnp.float32)
        grad_near = pull_near(scaled_scores)[0]
        near_sums = jax.ops.segment_sum(
            jnp.transpose(grad_near, (2, 0, 1)), near_ids, num_segments=buckets
        )
        grad_query_lookup = jnp.transpose(near_sums, (1, 2, 0)).astype(jnp.bfloat16)
        grad_far = pull_far(scaled_scores)[0]
        far_sums = jax.ops.segment_sum(
            jnp.transpose(grad_far, (2, 0, 1)), far_ids, num_segments=buckets
        )
        grad_table = grad_table + jnp.transpose(far_sums, (1, 2, 0))
        grad_query = score_scale * jnp.einsum(
            "hij,jhd->ihd", grad_scores, key_rows, preferred_element_type=jnp.float32
        )
        grad_query = grad_query + jnp.einsum(
            "yuo,oya->uya", grad_query_lookup, position_key, preferred_element_type=jnp.float32
        )
        grad_pos_key = grad_pos_key + jnp.einsum(
            "tsa,stu->atu", grad_query_lookup, queries, preferred_element_type=jnp.float32
        )
        return ((grad_keys, grad_values, grad_table, grad_pos_key), grad_query.astype(jnp.bfloat16))

    first_rows = jnp.arange(0, seq_rows, block_rows, dtype=jnp.int32)
    start_state = (
        jnp.zeros((seq_rows, heads_here, head_dim), jnp.float32),
        jnp.zeros((seq_rows, heads_here, head_dim), jnp.float32),
        jnp.zeros((heads_here, seq_rows, buckets), jnp.float32),
        pos_key_sum,
    )
    end_state, grad_queries = lax.scan(one_block, start_state, (first_rows, log_totals))
    grad_keys, grad_values, grad_table, pos_key_sum = end_state
    table_low = grad_table.astype(jnp.bfloat16)
    grad_keys = grad_keys + jnp.einsum(
        "hjb,bhd->jhd", table_low, pos_query, preferred_element_type=jnp.float32
    )
    pos_query_sum = pos_query_sum + jnp.einsum(
        "hjb,jhd->bhd", table_low, key_rows, preferred_element_type=jnp.float32
    )
    outputs = (
        grad_queries.reshape(queries.shape),
        grad_keys.astype(jnp.bfloat16),
        grad_values.astype(jnp.bfloat16),
    )
    return ((pos_key_sum, pos_query_sum), outputs)


def on_device(
    tokens,
    lengths,
    dealing,
    bucket_table,
    relative,
    w_query,
    b_query,
    w_key,
    b_key,
    w_value,
    b_value,
    w_out,
    b_out,
    attn_gain,
    attn_shift,
    w_up,
    b_up,
    w_down,
    b_down,
    ffn_gain,
    ffn_shift,
    cotangent,
):
    seq_here, seq_rows, model_width = tokens.shape
    rows_here = seq_here * seq_rows
    total_seqs = dealing.shape[0]
    part_cols = w_query.shape[1]
    heads_here = part_cols // HEAD_DIM
    buckets = relative.shape[0]
    block_rows = min(512, seq_rows)
    score_scale = 1.0 / math.sqrt(3.0 * HEAD_DIM)
    row_pieces = lax.all_to_all(tokens, "dp", split_axis=1, concat_axis=0, tiled=True)
    dealt_pieces = jnp.take(row_pieces, dealing, axis=0)
    dealt = lax.all_to_all(dealt_pieces, "dp", split_axis=0, concat_axis=1, tiled=True)
    group_index = lax.axis_index("dp")
    my_slots = lax.dynamic_slice_in_dim(dealing, group_index * seq_here, seq_here)
    seq_ids = jnp.arange(total_seqs, dtype=jnp.int32)
    my_lengths = jnp.sum(
        jnp.where(my_slots[:, None] == seq_ids[None, :], lengths[None, :], 0), axis=1
    )
    row_mask = (jnp.arange(seq_rows, dtype=jnp.int32)[None, :] < my_lengths[:, None]).astype(
        jnp.float32
    )
    flat_rows = dealt.reshape(rows_here, model_width)
    w_qkv = jnp.concatenate([w_query, w_key, w_value], axis=1)
    b_qkv = jnp.concatenate([b_query, b_key, b_value]).astype(jnp.float32)
    projected = (jnp.dot(flat_rows, w_qkv, preferred_element_type=jnp.float32) + b_qkv).astype(
        jnp.bfloat16
    )
    seq_shape = (seq_here, seq_rows, heads_here, HEAD_DIM)
    queries = projected[:, :part_cols].reshape(seq_shape)
    key_rows = projected[:, part_cols : 2 * part_cols].reshape(seq_shape)
    value_rows = projected[:, 2 * part_cols :].reshape(seq_shape)
    pos_query = (
        (
            jnp.dot(relative, w_query, preferred_element_type=jnp.float32)
            + b_query.astype(jnp.float32)
        )
        .astype(jnp.bfloat16)
        .reshape(buckets, heads_here, HEAD_DIM)
    )
    position_key = (
        (jnp.dot(relative, w_key, preferred_element_type=jnp.float32) + b_key.astype(jnp.float32))
        .astype(jnp.bfloat16)
        .reshape(buckets, heads_here, HEAD_DIM)
    )
    pk_offsets = jnp.take(position_key, bucket_table, axis=0)
    pq_offsets = jnp.take(pos_query, bucket_table, axis=0)
    forward_fn = partial(
        sequence_forward,
        pk_offsets=pk_offsets,
        pq_offsets=pq_offsets,
        bucket_table=bucket_table,
        block_rows=block_rows,
        score_scale=score_scale,
    )
    contexts, log_totals = lax.map(forward_fn, (queries, key_rows, value_rows, my_lengths))
    context_flat = contexts.reshape(rows_here, part_cols)
    attn_part = jnp.dot(context_flat, w_out, preferred_element_type=jnp.float32)
    attn = lax.psum(attn_part, "tensor") + b_out.astype(jnp.float32)
    attn_gain32 = attn_gain.astype(jnp.float32)
    hidden, mid_normed, mid_inverse = norm_forward(
        flat_rows.astype(jnp.float32) + attn, attn_gain32, attn_shift.astype(jnp.float32)
    )
    hidden_low = hidden.astype(jnp.bfloat16)
    up_sum = jnp.dot(hidden_low, w_up, preferred_element_type=jnp.float32) + b_up.astype(
        jnp.float32
    )
    activated = jax.nn.gelu(up_sum, approximate=False).astype(jnp.bfloat16)
    down_part = jnp.dot(activated, w_down, preferred_element_type=jnp.float32)
    tensor_half = lax.axis_index("tensor")
    half_rows = seq_rows // lax.axis_size("tensor")

    def take_half(array):
        return lax.dynamic_slice_in_dim(
            array.reshape(seq_here, seq_rows, model_width), tensor_half * half_rows, half_rows, 1
        )

    grad_out = cotangent.reshape(rows_here, model_width).astype(jnp.float32) * row_mask.reshape(
        rows_here, 1
    )
    ffn_gain32 = ffn_gain.astype(jnp.float32)
    ffn_shift32 = ffn_shift.astype(jnp.float32)
    b_down32 = b_down.astype(jnp.float32)
    down_sum = lax.psum(down_part, "tensor") + b_down32
    out_rows, out_normed, out_inverse = norm_forward(hidden + down_sum, ffn_gain32, ffn_shift32)
    grad_pre = norm_backward(grad_out, out_normed, out_inverse, ffn_gain32)
    half_grad_out = take_half(grad_out)
    half_normed = take_half(out_normed)
    half_pre = take_half(grad_pre)
    y_out = out_rows.astype(jnp.bfloat16).reshape(seq_here, seq_rows, model_width)
    grad_pre_low = grad_pre.astype(jnp.bfloat16)
    grad_ffn_gain = jnp.sum(half_grad_out * half_normed, axis=(0, 1))
    grad_ffn_shift = jnp.sum(half_grad_out, axis=(0, 1))
    grad_b_down = jnp.sum(half_pre.astype(jnp.bfloat16), axis=(0, 1), dtype=jnp.float32)
    grad_w_down = contract_rows(activated, grad_pre_low)
    grad_act = contract_cols(grad_pre_low, w_down)
    up_cdf = 0.5 * (1.0 + lax.erf(up_sum * ROOT_HALF))
    upward_density = jnp.exp(-0.5 * up_sum * up_sum) * INV_ROOT_TAU
    grad_up_low = (grad_act * (up_cdf + up_sum * upward_density)).astype(jnp.bfloat16)
    grad_w_up = contract_rows(hidden_low, grad_up_low)
    grad_b_up = jnp.sum(grad_up_low, axis=0, dtype=jnp.float32)
    ffn_grads = (grad_w_up, grad_b_up, grad_w_down)
    hidden_part = contract_cols(grad_up_low, w_up)
    grad_hidden = lax.psum(hidden_part, "tensor") + grad_pre
    grad_mid = norm_backward(grad_hidden, mid_normed, mid_inverse, attn_gain32)
    grad_mid_low = grad_mid.astype(jnp.bfloat16)
    half_hidden_grad = take_half(grad_hidden)
    grad_attn_gain = jnp.sum(half_hidden_grad * take_half(mid_normed), axis=(0, 1))
    grad_attn_shift = jnp.sum(half_hidden_grad, axis=(0, 1))
    grad_b_out = jnp.sum(take_half(grad_mid).astype(jnp.bfloat16), axis=(0, 1), dtype=jnp.float32)
    grad_w_out = contract_rows(context_flat, grad_mid_low)
    grad_context = contract_cols(grad_mid_low, w_out).astype(jnp.bfloat16).reshape(seq_shape)
    backward_fn = partial(
        sequence_backward,
        pos_query=pos_query,
        position_key=position_key,
        pk_offsets=pk_offsets,
        pq_offsets=pq_offsets,
        bucket_table=bucket_table,
        block_rows=block_rows,
        score_scale=score_scale,
    )
    pos_zeros = jnp.zeros((buckets, heads_here, HEAD_DIM), jnp.float32)
    pos_sums, seq_grads = lax.scan(
        backward_fn,
        (pos_zeros, pos_zeros),
        (queries, key_rows, value_rows, my_lengths, log_totals, grad_context),
    )
    grad_pos_key = pos_sums[0].reshape(buckets, part_cols)
    grad_pos_query = pos_sums[1].reshape(buckets, part_cols)
    grad_qkv = jnp.concatenate(
        [
            seq_grads[0].reshape(rows_here, part_cols),
            seq_grads[1].reshape(rows_here, part_cols),
            seq_grads[2].reshape(rows_here, part_cols),
        ],
        axis=1,
    )
    grad_w_qkv = contract_rows(flat_rows, grad_qkv)
    grad_b_qkv = jnp.sum(grad_qkv, axis=0, dtype=jnp.float32)
    relative32 = relative.astype(jnp.float32)
    grad_w_query = grad_w_qkv[:, :part_cols] + exact_rows(relative32, grad_pos_query)
    grad_b_query = grad_b_qkv[:part_cols] + jnp.sum(grad_pos_query, axis=0)
    grad_w_key = grad_w_qkv[:, part_cols : 2 * part_cols] + exact_rows(relative32, grad_pos_key)
    grad_b_key = grad_b_qkv[part_cols : 2 * part_cols] + jnp.sum(grad_pos_key, axis=0)
    grad_w_value = grad_w_qkv[:, 2 * part_cols :]
    grad_b_value = grad_b_qkv[2 * part_cols :]
    relative_part = exact_cols(grad_pos_query, w_query.astype(jnp.float32)) + exact_cols(
        grad_pos_key, w_key.astype(jnp.float32)
    )
    input_part = contract_cols(grad_qkv, w_qkv)
    summed = lax.psum(
        (
            input_part,
            relative_part,
            grad_attn_gain,
            grad_attn_shift,
            grad_b_out,
            grad_ffn_gain,
            grad_ffn_shift,
            grad_b_down,
        ),
        "tensor",
    )
    grad_input = (
        (grad_mid + summed[0]).astype(jnp.bfloat16).reshape(seq_here, seq_rows, model_width)
    )
    back_rows = lax.all_to_all(grad_input, "dp", split_axis=1, concat_axis=0, tiled=True)
    inverse = jnp.zeros((total_seqs,), jnp.int32).at[dealing].set(seq_ids)
    ordered = jnp.take(back_rows, inverse, axis=0)
    grad_tokens = lax.all_to_all(ordered, "dp", split_axis=0, concat_axis=1, tiled=True)
    rest = (
        summed[1],
        grad_w_query,
        grad_b_query,
        grad_w_key,
        grad_b_key,
        grad_w_value,
        grad_b_value,
        grad_w_out,
        summed[4],
        summed[2],
        summed[3],
        summed[7],
        summed[5],
        summed[6],
    )
    all_grads = tuple(lax.psum(ffn_grads + rest, "dp"))
    ffn_grads = all_grads[:3]
    rest = all_grads[3:]
    return (
        y_out,
        grad_tokens,
        rest[0],
        rest[1],
        rest[2],
        rest[3],
        rest[4],
        rest[5],
        rest[6],
        rest[7],
        rest[8],
        rest[9],
        rest[10],
        ffn_grads[0],
        ffn_grads[1],
        ffn_grads[2],
        rest[11],
        rest[12],
        rest[13],
    )


def solution(mesh):
    return jax.shard_map(
        on_device,
        mesh=mesh,
        in_specs=(
            P("dp", None, None),
            P(),
            P(),
            P(),
            P(),
            P(None, "tensor"),
            P("tensor"),
            P(None, "tensor"),
            P("tensor"),
            P(None, "tensor"),
            P("tensor"),
            P("tensor", None),
            P(),
            P(),
            P(),
            P(None, "tensor"),
            P("tensor"),
            P("tensor", None),
            P(),
            P(),
            P(),
            P("dp", None, None),
        ),
        out_specs=(
            P("dp", None, None),
            P("dp", None, None),
            P(),
            P(None, "tensor"),
            P("tensor"),
            P(None, "tensor"),
            P("tensor"),
            P(None, "tensor"),
            P("tensor"),
            P("tensor", None),
            P(),
            P(),
            P(),
            P(None, "tensor"),
            P("tensor"),
            P("tensor", None),
            P(),
            P(),
            P(),
        ),
        check_vma=False,
    )
```

profile of v0, /device:TPU:0, one launch (start us, length us, event | category | flops | bytes accessed | tf_op | source)
XLA Modules:
  0.0 936.3 jit_solution(8524536991930268715)
XLA Ops:
  7.2 1.7 copy.124
  9.4 3.0 reduce.16
  13.3 8.3 all-to-all-start
  25.0 3.9 gather_fusion.1
  28.9 7.6 gather_fusion.2
  39.4 6.9 all-to-all-start.1
  47.2 1.6 constant_dynamic-update-slice_fusion
  48.8 4.7 broadcast_select_fusion.1
  53.5 4.8 all-to-all-done.1
  61.8 7.6 copy.109
  69.3 9.2 pad.71
  78.6 14.7 %reshape.309 = f32[3,512,1025]{2,1,0:T(8,128)} reshape(f32[3,524800]{1,0:T(4,128)} %pad.71) | data formatting | bytes 12595200 | tf_op jit(solution)/shard_map/while/body/eval_jaxpr/while/body/eval_jaxpr/jvp()/reshape | solution.py:69
  93.3 3.8 slice.69
  97.1 3.5 copy.107
  100.7 25.2 %rev.28 = f32[3,512,512]{1,2,0:T(8,128)} reverse(f32[3,512,512]{1,2,0:T(8,128)} %copy.107), dimensions={2} | reverse | bytes 6291456 | tf_op jit(solution)/shard_map/while/body/eval_jaxpr/while/body/eval_jaxpr/jvp(jit(_flip))/rev | solution.py:73
  127.7 7.6 copy.110
  135.3 9.2 pad.73
  144.5 14.7 %reshape.312 = f32[3,512,1025]{2,1,0:T(8,128)} reshape(f32[3,524800]{1,0:T(4,128)} %pad.73) | data formatting | bytes 12595200 | tf_op jit(solution)/shard_map/while/body/eval_jaxpr/while/body/eval_jaxpr/jvp()/reshape | solution.py:69
  159.2 3.8 slice.70
  163.0 26.0 %rev.29 = f32[3,512,512]{2,1,0:T(8,128)} reverse(f32[3,512,512]{2,1,0:T(8,128)} %slice.70), dimensions={2} | reverse | bytes 6291456 | tf_op jit(solution)/shard_map/while/body/eval_jaxpr/while/body/eval_jaxpr/jvp(jit(_flip))/rev | solution.py:77
  189.0 3.8 fusion.56
  196.8 17.0 %all-reduce.16.cloned.1.call-done = f32[512,384]{1,0:T(8,128)} async-done(((f32[512,384]{1,0:T(8,128)}), f32[512,384]{1,0:T(8,128)}) %all-reduce.16.cloned.1.call-update) | async-done | bytes 786448 | tf_op jit(solution)/shard_map/psum | solution.py:293
  216.2 4.9 fusion.5
  223.4 19.6 %all-reduce.18.cloned.1.call-done = f32[512,384]{1,0:T(8,128)} async-done(((f32[512,384]{1,0:T(8,128)}), f32[512,384]{1,0:T(8,128)}) %all-reduce.18.cloned.1.call-update) | async-done | bytes 786448 | tf_op jit(solution)/shard_map/psum | solution.py:318
  250.4 20.3 %all-reduce.20.cloned.1.call-done = f32[512,384]{1,0:T(8,128)} async-done(((f32[512,384]{1,0:T(8,128)}), f32[512,384]{1,0:T(8,128)}) %all-reduce.20.cloned.1.call-update) | async-done | bytes 786448 | tf_op jit(solution)/shard_map/psum | solution.py:338
  272.2 1.8 subtract_multiply_fusion
  276.1 3.0 multiply_bitcast_fusion
  279.1 23.3 %reverse.3 = f32[3,512,512]{1,2,0:T(8,128)} reverse(bf16[3,512,512]{1,2,0:T(8,128)(2,1)} %get-tuple-element.241), dimensions={2} | reverse | bytes 4718592 | tf_op jit(solution)/shard_map/reverse
  302.5 2.8 convolution_multiply_fusion.1
  309.0 2.8 copy.108
  311.8 5.3 pad.74.clone
  317.1 14.0 %reshape.315 = f32[3,524800]{1,0:T(4,128)} reshape(f32[3,512,1025]{2,1,0:T(8,128)} %pad.74.clone) | data formatting | bytes 12595200 | tf_op jit(solution)/shard_map/while/body/eval_jaxpr/while/body/eval_jaxpr/transpose(jvp())/reshape | solution.py:69
  331.1 3.4 slice-done
  334.4 3.8 copy.122
  338.3 3.8 slice_bitcast_fusion.1
  342.1 9.5 %copy.92 = f32[1023,3,512]{2,1,0:T(4,128)} copy(f32[1023,3,512]{0,2,1:T(8,128)} %slice_bitcast_fusion.1) | data formatting | bytes 12570624 | tf_op jit(solution)/shard_map/while/body/eval_jaxpr/while/body/eval_jaxpr/transpose | solution.py:170
  351.5 2.6 broadcast.177.clone.1
  354.1 131.6 %scatter_fusion = f32[512,3,512]{2,1,0:T(4,128)} fusion(f32[512,3,512]{2,1,0:T(4,128)} %broadcast.177.clone.1, s32[1023]{0:T(1024)S(1)} %copy-done.70, f32[1023,3,512]{2,1,0:T(4,128)} %copy.92), kind=kCustom, calls=%fused_computation.4 | custom fusion | flops 1571328 | bytes 18860028 | tf_op jit(solution)/shard_map/while/body/eval_jaxpr/while/body/eval_jaxpr/scatter-add | solution.py:169
  485.7 4.2 convert_bitcast_fusion.1
  489.9 2.9 copy.93
  495.3 22.3 %rev.31 = f32[3,512,512]{2,1,0:T(8,128)S(1)} reverse(f32[3,512,512]{2,1,0:T(8,128)} %get-tuple-element.240), dimensions={2} | reverse | bytes 6291456 | tf_op jit(solution)/shard_map/while/body/eval_jaxpr/while/body/eval_jaxpr/transpose(jvp(jit(_flip)))/rev | solution.py:77
  517.6 3.4 pad.77
  521.1 14.0 %reshape.318 = f32[3,524800]{1,0:T(4,128)} reshape(f32[3,512,1025]{2,1,0:T(8,128)} %pad.77) | data formatting | bytes 12595200 | tf_op jit(solution)/shard_map/while/body/eval_jaxpr/while/body/eval_jaxpr/transpose(jvp())/reshape | solution.py:69
  535.0 3.4 slice-done.1
  538.4 3.9 copy.121
  542.3 3.8 slice_bitcast_fusion
  546.1 9.5 %copy.95 = f32[1023,3,512]{2,1,0:T(4,128)} copy(f32[1023,3,512]{0,2,1:T(8,128)} %slice_bitcast_fusion) | data formatting | bytes 12570624 | tf_op jit(solution)/shard_map/while/body/eval_jaxpr/while/body/eval_jaxpr/transpose | solution.py:175
  555.6 2.6 broadcast.177.clone
  558.1 131.6 %scatter_fusion.1 = f32[512,3,512]{2,1,0:T(4,128)} fusion(f32[512,3,512]{2,1,0:T(4,128)} %broadcast.177.clone, s32[1023]{0:T(1024)S(1)} %copy-done.70, f32[1023,3,512]{2,1,0:T(4,128)} %copy.95), kind=kCustom, calls=%fused_computation.5 | custom fusion | flops 1571328 | bytes 18860028 | tf_op jit(solution)/shard_map/while/body/eval_jaxpr/while/body/eval_jaxpr/scatter-add | solution.py:174
  689.7 4.3 convert_bitcast_fusion
  694.0 2.9 copy.96
  699.6 1.6 convolution_add_fusion.2
  702.8 1.6 fusion.39
  704.5 1.5 fusion.42
  710.6 13.9 %all-reduce.24.cloned.1.call-done = (f32[512,384]{1,0:T(8,128)}, f32[512,384]{1,0:T(8,128)}) async-done(((f32[512,384]{1,0:T(8,128)}, f32[512,384]{1,0:T(8,128)}), (f32[512,384]{1,0:T(8,128)}, f32[512,384]{1,0:T(8,128)})) %all-reduce.24.cloned.1.call-update) | async-done | bytes 1572880 | tf_op jit(solution)/shard_map/psum | solution.py:386
  726.4 3.0 reduce.17
  730.2 6.8 all-to-all-start.2
  737.9 19.3 %all-to-all-done.2 = bf16[16,2,6144]{2,1,0:T(2,128)(2,1)S(1)} async-done(((bf16[16,2,6144]{2,1,0:T(2,128)(2,1)}), bf16[16,2,6144]{2,1,0:T(2,128)(2,1)S(1)}, u32[]{:S(2)}, u32[]{:S(2)}) %all-to-all-start.2) | async-done | bytes 393248 | tf_op jit(solution)/shard_map/all_to_all | solution.py:402
  758.3 1.7 gather_fusion.3
  760.9 8.3 all-to-all-start.3
  771.7 3.3 all-reduce.8
  775.3 77.8 %all-reduce.6 = (f32[192]{0:T(256)}, f32[192]{0:T(256)}, f32[192]{0:T(256)}, f32[384]{0:T(512)}, f32[384]{0:T(512)}, /*index=5*/f32[384]{0:T(512)}, f32[768]{0:T(1024)}, f32[384]{0:T(512)}, f32[384]{0:T(512)}, f32[384]{0:T(512)}) all-reduce(f32[192]{0:T(256)S(1)} %get-tuple-element.254, ...), channel_id=1, replica_groups=mesh['dp'=16,'tensor'=2] {'dp'}, use_global_device_ids=true, to_apply=%region_24.27 | all-reduce | flops 3648 | bytes 29184 | tf_op jit(solution)/shard_map/psum | solution.py:422
  853.1 68.5 %all-reduce.22.cloned.1.call-done = (f32[512,384]{1,0:T(8,128)}, f32[384,192]{0,1:T(8,128)}, f32[384,192]{0,1:T(8,128)}, f32[384,192]{0,1:T(8,128)}, f32[192,384...) async-done(((f32[512,384]{1,0:T(8,128)}, f32[384,192]{0,1:T(8,128)}, f32[384,192]{0,1:T(8,128)}, f32[384,192]{0,1:T(8,128)}, f32[192,384]{1,0:T(8,128)}, ...) | async-done | bytes 4325392 | tf_op jit(solution)/shard_map/psum | solution.py:422
  922.3 2.2 copy.147
  (304 shorter events, 61.7 us)
Async XLA Ops:
  7.2 209.0 %copy-start = (bf16[384,768]{1,0:T(8,128)(2,1)S(1)}, bf16[384,768]{1,0:T(8,128)(2,1)}, u32[]{:S(2)}) copy-start(bf16[384,768]{1,0:T(8,128)(2,1)} %param.41) | copy-start | bytes 1769476
  8.9 12.8 %copy-start.91 = (bf16[192]{0:T(256)(128)(2,1)S(1)}, bf16[192]{0:T(256)(128)(2,1)}, u32[]{:S(2)}) copy-start(bf16[192]{0:T(256)(128)(2,1)} %param.34) | copy-start | bytes 1156
  8.9 12.8 %copy-start.13 = (bf16[512,384]{1,0:T(8,128)(2,1)S(1)}, bf16[512,384]{1,0:T(8,128)(2,1)}, u32[]{:S(2)}) copy-start(bf16[512,384]{1,0:T(8,128)(2,1)} %param.30) | copy-start | bytes 1179652
  8.9 12.8 %copy-start.44 = (bf16[384,192]{0,1:T(8,128)(2,1)S(1)}, bf16[384,192]{0,1:T(8,128)(2,1)}, u32[]{:S(2)}) copy-start(bf16[384,192]{0,1:T(8,128)(2,1)} %param.33) | copy-start | bytes 442372
  12.4 9.9 %copy-start.70 = (s32[1023]{0:T(1024)S(1)}, s32[1023]{0:T(1024)}, u32[]{:S(2)}) copy-start(s32[1023]{0:T(1024)} %param.29) | copy-start | bytes 12280
  12.5 9.9 %copy-start.92 = (bf16[192]{0:T(256)(128)(2,1)S(1)}, bf16[192]{0:T(256)(128)(2,1)}, u32[]{:S(2)}) copy-start(bf16[192]{0:T(256)(128)(2,1)} %param.32) | copy-start | bytes 1156
  12.5 9.9 %copy-start.47 = (bf16[384,192]{0,1:T(8,128)(2,1)S(1)}, bf16[384,192]{0,1:T(8,128)(2,1)}, u32[]{:S(2)}) copy-start(bf16[384,192]{0,1:T(8,128)(2,1)} %param.31) | copy-start | bytes 442372
  13.3 24.1 %all-to-all-start = ((bf16[16,2,6144]{2,1,0:T(2,128)(2,1)}), bf16[16,2,6144]{2,1,0:T(2,128)(2,1)S(1)}, u32[]{:S(2)}, u32[]{:S(2)}) async-start(bf16[16,2,6144]{2,1,0:T(2,128)(2,1)} %reshape.399), calls=%async_computation | async-start | bytes 786432 | tf_op jit(solution)/shard_map/all_to_all | solution.py:245
  21.7 2.0 copy-start.88
  22.7 2.2 copy-start.31
  24.9 11.5 %copy-start.81 = (s32[16]{0:T(128)}, s32[16]{0:T(128)S(1)}, u32[]{:S(2)}) copy-start(s32[16]{0:T(128)S(1)} %get-tuple-element.269) | copy-start | bytes 196
  28.8 7.6 copy-start.90
  28.9 7.7 copy-start.48
  28.9 7.7 copy-start.45
  37.8 11.0 %copy-start.23 = (bf16[1023,3,64]{2,1,0:T(4,128)(2,1)S(1)}, bf16[1023,3,64]{2,1,0:T(4,128)(2,1)}, u32[]{:S(2)}) copy-start(bf16[1023,3,64]{2,1,0:T(4,128)(2,1)} %gather_fusion.2) | copy-start | bytes 1178500
  39.4 18.9 %all-to-all-start.1 = ((bf16[16,32,384]{2,1,0:T(8,128)(2,1)}), bf16[16,32,384]{2,1,0:T(8,128)(2,1)S(1)}, u32[]{:S(2)}, u32[]{:S(2)}) async-start(bf16[16,32,384]{2,1,0:T(8,128)(2,1)} %broadcast_select_fusion.3), calls=%async_computation.1 | async-start | bytes 786432 | tf_op jit(solution)/shard_map/all_to_all | solution.py:247
  46.3 167.5 %all-reduce.16.cloned.1.call-start = ((), (), s32[]{:S(2)}) async-start(), calls=%async_computation.4 | async-start | bytes 1572864 | tf_op jit(solution)/shard_map/psum | solution.py:293
  47.2 146.1 %copy-start.76 = (pred[512]{0:T(512)(128)(4,1)}, pred[512]{0:T(512)(128)(4,1)S(1)}, u32[]{:S(2)}) copy-start(pred[512]{0:T(512)(128)(4,1)S(1)} %iota_compare_fusion) | copy-start | bytes 1540
  53.5 6.4 copy-start.26
  59.9 129.1 %copy-start.18 = (bf16[512,192]{0,1:T(8,128)(2,1)}, bf16[512,192]{0,1:T(8,128)(2,1)S(1)}, u32[]{:S(2)}) copy-start(bf16[512,192]{0,1:T(8,128)(2,1)S(1)} %get-tuple-element.249) | copy-start | bytes 589828
  59.9 129.1 %copy-start.20 = (bf16[512,192]{0,1:T(8,128)(2,1)}, bf16[512,192]{0,1:T(8,128)(2,1)S(1)}, u32[]{:S(2)}) copy-start(bf16[512,192]{0,1:T(8,128)(2,1)S(1)} %get-tuple-element.248) | copy-start | bytes 589828
  59.9 133.4 %copy-start.37 = (bf16[512,192]{0,1:T(8,128)(2,1)}, bf16[512,192]{0,1:T(8,128)(2,1)S(1)}, u32[]{:S(2)}) copy-start(bf16[512,192]{0,1:T(8,128)(2,1)S(1)} %get-tuple-element.250) | copy-start | bytes 589828
  100.7 25.2 %copy-start.25 = (bf16[1023,3,64]{2,1,0:T(4,128)(2,1)S(1)}, bf16[1023,3,64]{2,1,0:T(4,128)(2,1)}, u32[]{:S(2)}) copy-start(bf16[1023,3,64]{2,1,0:T(4,128)(2,1)} %get-tuple-element.256) | copy-start | bytes 1178500
  195.1 20.3 %copy-start.35 = (bf16[3,64,512]{2,1,0:T(8,128)(2,1)}, bf16[3,64,512]{2,1,0:T(8,128)(2,1)S(1)}, u32[]{:S(2)}) copy-start(bf16[3,64,512]{2,1,0:T(8,128)(2,1)S(1)} %convolution_convert_fusion.2) | copy-start | bytes 589828
  196.6 46.3 %all-reduce.18.cloned.1.call-start = ((), (), s32[]{:S(2)}) async-start(), calls=%async_computation.5 | async-start | bytes 1572864 | tf_op jit(solution)/shard_map/psum | solution.py:318
  196.7 46.2 %copy-start.74 = (f32[384]{0:T(512)}, f32[384]{0:T(512)S(1)}, u32[]{:S(2)}) copy-start(f32[384]{0:T(512)S(1)} %convert_element_type.199) | copy-start | bytes 4612
  216.2 54.5 %copy-start.5 = (f32[512,384]{1,0:T(8,128)}, f32[512,384]{1,0:T(8,128)S(1)}, u32[]{:S(2)}) copy-start(f32[512,384]{1,0:T(8,128)S(1)} %subtract_multiply_fusion.3) | copy-start | bytes 2359300
  216.2 4.9 copy-start.64
  221.1 23.2 %copy-start.27 = (bf16[512,768]{1,0:T(8,128)(2,1)}, bf16[512,768]{1,0:T(8,128)(2,1)S(1)}, u32[]{:S(2)}) copy-start(bf16[512,768]{1,0:T(8,128)(2,1)S(1)} %get-tuple-element.259) | copy-start | bytes 2359300
  222.6 48.1 %all-reduce.20.cloned.1.call-start = ((), (), s32[]{:S(2)}) async-start(), calls=%async_computation.6 | async-start | bytes 1572864 | tf_op jit(solution)/shard_map/psum | solution.py:338
  245.1 2.3 copy-start.93
  246.4 24.3 %copy-start.10 = (f32[512,384]{1,0:T(8,128)}, f32[512,384]{1,0:T(8,128)S(1)}, u32[]{:S(2)}) copy-start(f32[512,384]{1,0:T(8,128)S(1)} %get-tuple-element.246) | copy-start | bytes 2359300
  248.9 23.2 %copy-start.29 = (bf16[512,768]{1,0:T(8,128)(2,1)}, bf16[512,768]{1,0:T(8,128)(2,1)S(1)}, u32[]{:S(2)}) copy-start(bf16[512,768]{1,0:T(8,128)(2,1)S(1)} %get-tuple-element.268) | copy-start | bytes 2359300
  250.4 474.2 %all-reduce.24.cloned.1.call-start = ((), (), s32[]{:S(2)}) async-start(), calls=%async_computation.8 | async-start | bytes 3145728 | tf_op jit(solution)/shard_map/psum | solution.py:386
  272.1 3.1 copy-start.17
  272.1 2.7 copy-start.63
  272.2 3.0 copy-start.3
  272.2 3.0 copy-start.38
  272.2 3.0 copy-start.77
  302.5 2.8 copy-start.4
  302.5 2.8 copy-start.21
  331.1 3.4 slice-start
  489.9 2.9 copy-start.22
  535.0 3.4 slice-start.1
  694.0 2.9 copy-start.19
  698.6 2.6 copy-start.55
  698.9 2.3 copy-start.52
  698.9 2.3 copy-start.59
  698.9 2.3 copy-start.72
  702.8 218.8 %all-reduce.22.cloned.1.call-start = ((), (), s32[]{:S(2)}) async-start(), calls=%async_computation.7 | async-start | bytes 8650752 | tf_op jit(solution)/shard_map/psum | solution.py:422
  706.0 2.2 copy-start.14
  730.2 26.9 %all-to-all-start.2 = ((bf16[16,2,6144]{2,1,0:T(2,128)(2,1)}), bf16[16,2,6144]{2,1,0:T(2,128)(2,1)S(1)}, u32[]{:S(2)}, u32[]{:S(2)}) async-start(bf16[16,2,6144]{2,1,0:T(2,128)(2,1)} %reshape.401), calls=%async_computation.2 | async-start | bytes 786432 | tf_op jit(solution)/shard_map/all_to_all | solution.py:402
  758.3 10.9 %copy-start.16 = (f32[512,384]{1,0:T(8,128)S(1)}, f32[512,384]{1,0:T(8,128)}, u32[]{:S(2)}) copy-start(f32[512,384]{1,0:T(8,128)} %copy-done.15) | copy-start | bytes 2359300
  760.9 14.4 %copy-start.79 = (f32[768]{0:T(1024)S(1)}, f32[768]{0:T(1024)}, u32[]{:S(2)}) copy-start(f32[768]{0:T(1024)} %get-tuple-element.267) | copy-start | bytes 9220
  760.9 92.2 %all-to-all-start.3 = ((bf16[16,32,384]{2,1,0:T(8,128)(2,1)}), bf16[16,32,384]{2,1,0:T(8,128)(2,1)S(1)}, u32[]{:S(2)}, u32[]{:S(2)}) async-start(bf16[16,32,384]{2,1,0:T(8,128)(2,1)} %broadcast_select_fusion.2), calls=%async_computation.3 | async-start | bytes 786432 | tf_op jit(solution)/shard_map/all_to_all | solution.py:405
  769.2 5.8 copy-start.54
  769.2 5.8 copy-start.57
  769.2 5.8 copy-start.61
  921.6 2.9 copy-start.69
  921.6 3.6 copy-start.68
  921.6 4.4 copy-start.67
  922.3 4.3 copy-start.66
  922.3 5.0 copy-start.51
  927.4 2.0 copy-start.1
  (41 other events, 56.2 us)
Sparse Core Ops, SparseCore 0:
  196.7 16.9 all-reduce.15
  222.7 20.1 all-reduce.17
  250.5 20.1 all-reduce.19
  702.9 21.6 all-reduce.23
  732.0 189.5 all-reduce.21
where the time goes:
time: 953 us; the launch traced here: 936 us
  local copies, waits for them, and re-layouts  304 us (32%)
  other arithmetic  302 us (32%)
  waiting for transfers between devices  163 us (17%)
  blocking collectives  81.1 us (9%)
  matrix products  39.8 us (4%)
  starting transfers between devices  30.7 us (3%)
  between operations  15.5 us (2%)
    scatter-add x1, other arithmetic, one_block(): jax.ops.segment_sum(jnp.transpose(grad_near, (2, 0, 1)), near_ids, num_se...  132 us
    scatter-add x1, other arithmetic, one_block(): jax.ops.segment_sum(jnp.transpose(grad_far, (2, 0, 1)), far_ids, num_segm...  132 us
    psum x1, blocking collectives, on_device(): all_grads = tuple(lax.psum(ffn_grads + rest, 'dp'))  77.8 us
    psum x1, waiting for transfers between devices, on_device(): all_grads = tuple(lax.psum(ffn_grads + rest, 'dp'))  68.5 us
    reshape x4, local copies, waits for them, and re-layouts, skew_rows(): return flat.reshape(heads_now, row_count, width_now + 2)[:, :, :out_cols]  57.4 us
    unnamed x214, local copies, waits for them, and re-layouts  51.8 us
    rev x2, local copies, waits for them, and re-layouts, place_far(): return jnp.transpose(jnp.flip(skew_rows(values, out_cols), 2), (0, 2, 1))  48.3 us
    another operation x3, local copies, waits for them, and re-layouts  28.5 us
  transfers between devices with their start and end apart: 9, of which 7 were waited for; matrix products, arithmetic and copies ran while one was open for 4% of the time, Pallas kernels for 0%

commit v1 on v0

v1 whole, which is shorter than its diff:
```python
import math

import jax
import jax.numpy as jnp
from jax import lax
from jax.experimental import pallas as pl
from jax.experimental.pallas import tpu as pltpu
from jax.sharding import PartitionSpec as P

HEAD_DIM = 64
EPSILON = 1e-07
ROOT_HALF = 0.7071067811865476
INV_ROOT_TAU = 0.3989422804014327
BLOCK = 128
LOW = jnp.bfloat16
WIDE = jnp.float32

NN = (((1,), (0,)), ((), ()))
NT = (((1,), (1,)), ((), ()))
TN = (((0,), (0,)), ((), ()))
TT = (((0,), (1,)), ((), ()))


def mm(left, right, dims=NN):
    return lax.dot_general(left, right, dims, preferred_element_type=WIDE)


def pieces(first, count, chunk):
    out = []
    done = 0
    while done < count:
        place, offset = divmod(first + done, chunk)
        take = min(chunk - offset, count - done)
        out.append((place, offset, done, take))
        done += take
    return out


def chunk_rows(rows, parts, unit):
    return -(-(-(-rows // parts)) // unit) * unit


def call(body, out_shapes, args, scratch=(), smem=0, flops=10**9, moved=4 * 10**6, aliases=None):
    specs = [
        pl.BlockSpec(memory_space=pltpu.SMEM if i < smem else pltpu.VMEM) for i in range(len(args))
    ]
    return pl.pallas_call(
        body,
        out_shape=[jax.ShapeDtypeStruct(shape, kind) for shape, kind in out_shapes],
        in_specs=specs,
        out_specs=[pl.BlockSpec(memory_space=pltpu.VMEM) for _ in out_shapes],
        scratch_shapes=list(scratch),
        input_output_aliases=aliases or {},
        compiler_params=pltpu.CompilerParams(vmem_limit_bytes=40 * 1024 * 1024),
        cost_estimate=pl.CostEstimate(flops=flops, bytes_accessed=moved, transcendentals=0),
    )(*args)


def permute_body(scatter, dealing, source, target):
    total, rows, _ = source.shape

    def step(k, carry):
        if scatter:
            target[dealing[k]] = source[k]
        else:
            target[k] = source[dealing[k]]
        return carry

    lax.fori_loop(0, total, step, 0, unroll=True)


def attention_forward(
    lengths, x, relative, table, wq, bq, wk, bk, wv, bv, wout,
    q_out, k_out, v_out, tab_out, prob_out, ctx_out, attn_out, far_scratch,
):
    length = lengths[lax.axis_index("dp")]
    heads, rows, _ = q_out.shape
    span = tab_out.shape[3]
    buckets = relative.shape[0]
    window = rows + BLOCK
    scale = 1.0 / math.sqrt(3.0 * HEAD_DIM)
    xv = x[...]
    for weight, bias, out in ((wq, bq, q_out), (wk, bk, k_out), (wv, bv, v_out)):
        full = (mm(xv, weight[...]) + bias[...].astype(WIDE)).astype(LOW)
        for h in range(heads):
            out[h] = full[:, h * HEAD_DIM : (h + 1) * HEAD_DIM]
    rel = relative[...]
    hot = jnp.where(
        lax.broadcasted_iota(jnp.int32, (buckets, span), 0) == table[...], 1.0, 0.0
    ).astype(LOW)
    for slot, (weight, bias) in enumerate(((wq, bq), (wk, bk))):
        low = (mm(rel, weight[...]) + bias[...].astype(WIDE)).astype(LOW)
        spread = mm(low, hot, TN).astype(LOW)
        for h in range(heads):
            tab_out[slot, h] = spread[h * HEAD_DIM : (h + 1) * HEAD_DIM]
    key_ok = lax.broadcasted_iota(jnp.int32, (1, rows), 1) < length
    attn_out_acc = attn_out

    def head(h, carry):
        keys = k_out[h]
        values = v_out[h]
        for b in range(rows // BLOCK):
            j0 = b * BLOCK
            w0 = rows - BLOCK - j0
            far = mm(k_out[h, j0 : j0 + BLOCK, :], tab_out[0, h, :, w0 : w0 + window])
            far = pltpu.roll(far, window - BLOCK + 1, 1, stride=1, stride_axis=0)[:, :rows]
            far_scratch[:, j0 : j0 + BLOCK] = far.T
        for a in range(rows // BLOCK):
            i0 = a * BLOCK
            w0 = rows - BLOCK - i0
            block_q = q_out[h, i0 : i0 + BLOCK, :]
            near = mm(block_q, tab_out[1, h, :, w0 : w0 + window])
            near = pltpu.roll(near, window - BLOCK + 1, 1, stride=1, stride_axis=0)[:, :rows]
            score = (mm(block_q, keys, NT) + near + far_scratch[i0 : i0 + BLOCK, :]) * scale
            score = jnp.where(key_ok, score, -1e30)
            top = jnp.max(score, axis=1, keepdims=True)
            weights = jnp.exp(score - top)
            row_ok = i0 + lax.broadcasted_iota(jnp.int32, (BLOCK, 1), 0) < length
            norm = jnp.where(row_ok, 1.0 / jnp.sum(weights, axis=1, keepdims=True), 0.0)
            prob = (weights * norm).astype(LOW)
            prob_out[h, i0 : i0 + BLOCK, :] = prob
            ctx_out[h, i0 : i0 + BLOCK, :] = mm(prob, values).astype(LOW)
        return carry

    lax.fori_loop(0, heads, head, 0)
    total = mm(ctx_out[0], wout[0:HEAD_DIM, :])
    for h in range(1, heads):
        total += mm(ctx_out[h], wout[h * HEAD_DIM : (h + 1) * HEAD_DIM, :])
    attn_out_acc[...] = total.astype(LOW)


def row_norm(values):
    center = values - jnp.mean(values, axis=-1, keepdims=True)
    inverse = lax.rsqrt(jnp.mean(center * center, axis=-1, keepdims=True) + EPSILON)
    return center * inverse, inverse


def norm_back(scaled, normed, inverse):
    one = jnp.mean(scaled, axis=-1, keepdims=True)
    two = jnp.mean(scaled * normed, axis=-1, keepdims=True)
    return inverse * (scaled - one - normed * two)


def ffn_forward(
    x, mine, theirs, bout, gain, shift, wup, bup, wdown,
    normed_out, inverse_out, hidden_out, act_out, slope_out, down_out,
):
    rows = x.shape[0]

    def block(i, carry):
        here = pl.ds(pl.multiple_of(i * BLOCK, BLOCK), BLOCK)
        attn = mine[here, :].astype(WIDE) + theirs[here, :].astype(WIDE) + bout[...].astype(WIDE)
        normed, inverse = row_norm(x[here, :].astype(WIDE) + attn)
        normed_out[here, :] = normed
        inverse_out[here, :] = inverse
        low = (normed * gain[...].astype(WIDE) + shift[...].astype(WIDE)).astype(LOW)
        hidden_out[here, :] = low
        u = mm(low, wup[...]) + bup[...].astype(WIDE)
        cdf = 0.5 * (1.0 + lax.erf(u * ROOT_HALF))
        density = jnp.exp(-0.5 * u * u) * INV_ROOT_TAU
        act = (u * cdf).astype(LOW)
        act_out[here, :] = act
        slope_out[here, :] = (cdf + u * density).astype(LOW)
        down_out[here, :] = mm(act, wdown[...]).astype(LOW)
        return carry

    lax.fori_loop(0, rows // BLOCK, block, 0)


def ffn_backward(
    chunk, piece, lengths,
    mine, theirs, bdown, normed, gain, shift, fgain, fshift, cot_mine, cot_theirs,
    hidden, act, slope, wup, wdown,
    buffer_out, part_out, gf_out, small_out, low_scratch, gu_scratch,
):
    length = lengths[lax.axis_index("dp")]
    side = lax.axis_index("tensor")
    rows, width = normed.shape
    half = rows // 2
    total = buffer_out.shape[0]
    units = act.shape[1]
    sums = [jnp.zeros((1, width), WIDE) for _ in range(3)]
    for i in range(rows // BLOCK):
        here = slice(i * BLOCK, (i + 1) * BLOCK)
        source = (i * BLOCK) // half
        local = slice(i * BLOCK - source * half, (i + 1) * BLOCK - source * half)
        cot = jnp.where(side == source, cot_mine[local, :], cot_theirs[local, :]).astype(WIDE)
        f = mine[here, :].astype(WIDE) + theirs[here, :].astype(WIDE) + bdown[...].astype(WIDE)
        h = normed[here, :] * gain[...].astype(WIDE) + shift[...].astype(WIDE)
        n2, r2 = row_norm(h + f)
        y = (n2 * fgain[...].astype(WIDE) + fshift[...].astype(WIDE)).astype(LOW)

        @pl.when(side == source)
        def _():
            for p in range(BLOCK // piece):
                place = local.start // piece + p
                buffer_out[place, chunk : chunk + piece, :] = y[p * piece : (p + 1) * piece]

        row_ok = i * BLOCK + lax.broadcasted_iota(jnp.int32, (BLOCK, 1), 0) < length
        gy = jnp.where(row_ok, cot, 0.0)
        gf = norm_back(gy * fgain[...].astype(WIDE), n2, r2)
        gf_out[here, :] = gf
        low = gf.astype(LOW)
        low_scratch[here, :] = low
        sums[0] += jnp.sum(low.astype(WIDE), axis=0, keepdims=True)
        sums[1] += jnp.sum(gy * n2, axis=0, keepdims=True)
        sums[2] += jnp.sum(gy, axis=0, keepdims=True)
    gu_sum = jnp.zeros((1, units), WIDE)
    for i in range(rows // BLOCK):
        here = slice(i * BLOCK, (i + 1) * BLOCK)
        gu = (mm(low_scratch[here, :], wdown[...], NT) * slope[here, :].astype(WIDE)).astype(LOW)
        gu_scratch[here, :] = gu
        gu_sum += jnp.sum(gu.astype(WIDE), axis=0, keepdims=True)
        part_out[here, :] = mm(gu, wup[...], NT).astype(LOW)
    small_out[...] = jnp.zeros_like(small_out)
    for k in range(units // width):
        small_out[k : k + 1, :] = gu_sum[:, k * width : (k + 1) * width]
    for k in range(3):
        small_out[units // width + k : units // width + k + 1, :] = sums[k]

    def put(first, value):
        for place, offset, start, take in pieces(first, value.shape[0], chunk):
            buffer_out[place, offset : offset + take, :] = value[start : start + take]

    put(units, mm(act[...], low_scratch[...], TN).astype(LOW))
    for k in range(units // width):
        columns = slice(k * width, (k + 1) * width)
        put(k * width, mm(hidden[...], gu_scratch[:, columns], TN).astype(LOW))
    for place in range(-(-2 * units // chunk), total):
        buffer_out[place, :chunk, :] = jnp.zeros((chunk, width), LOW)
    for place in range(half // piece, total):
        buffer_out[place, chunk:, :] = jnp.zeros((piece, width), LOW)


def attention_backward(
    x, relative, table, wq, wk, wv, wout,
    mine, theirs, gf, normed, inverse, gain,
    q, k, v, tab, prob, ctx,
    send_out, keep_out, gp_out, weights_out, small_out,
    gpb_scratch, gs_scratch, gpk_scratch, gpq_scratch, g_scratch, rel_scratch, gctx_scratch,
):
    side = lax.axis_index("tensor")
    heads, rows, _ = q.shape
    width = x.shape[1]
    half = rows // 2
    span = tab.shape[3]
    buckets = relative.shape[0]
    window = rows + BLOCK
    scale = 1.0 / math.sqrt(3.0 * HEAD_DIM)
    blocks = rows // BLOCK
    part = heads * HEAD_DIM
    sums = [jnp.zeros((1, width), WIDE) for _ in range(3)]
    for i in range(blocks):
        here = slice(i * BLOCK, (i + 1) * BLOCK)
        gh = gf[here, :] + (mine[here, :].astype(WIDE) + theirs[here, :].astype(WIDE))
        n1 = normed[here, :]
        gp = norm_back(gh * gain[...].astype(WIDE), n1, inverse[here, :])
        gp_out[here, :] = gp
        low = gp.astype(LOW)
        gpb_scratch[here, :] = low
        sums[0] += jnp.sum(low.astype(WIDE), axis=0, keepdims=True)
        sums[1] += jnp.sum(gh * n1, axis=0, keepdims=True)
        sums[2] += jnp.sum(gh, axis=0, keepdims=True)
        grad = mm(low, wout[...], NT).astype(LOW)
        for h in range(heads):
            gctx_scratch[h, here, :] = grad[:, h * HEAD_DIM : (h + 1) * HEAD_DIM]
    small_out[...] = jnp.zeros_like(small_out)
    for n in range(3):
        small_out[2 + n : 3 + n, :] = sums[n]
    for h in range(heads):
        weights_out[width + part + h * HEAD_DIM : width + part + (h + 1) * HEAD_DIM, :] = mm(
            ctx[h], gpb_scratch[...], TN
        ).astype(LOW)
    anti = jnp.where(
        lax.broadcasted_iota(jnp.int32, (BLOCK, BLOCK), 0)
        + lax.broadcasted_iota(jnp.int32, (BLOCK, BLOCK), 1)
        == BLOCK - 1,
        1.0,
        0.0,
    ).astype(LOW)
    pad = jnp.zeros((BLOCK, BLOCK), WIDE)

    def head(h, carry):
        keys = k[h]
        queries = q[h]
        gpk_scratch[h] = jnp.zeros((HEAD_DIM, span), WIDE)
        gpq_scratch[h] = jnp.zeros((HEAD_DIM, span), WIDE)
        for i in range(blocks):
            i0 = i * BLOCK
            w0 = rows - BLOCK - i0
            weights = prob[h, i0 : i0 + BLOCK, :].astype(WIDE)
            gprob = mm(gctx_scratch[h, i0 : i0 + BLOCK, :], v[h], NT)
            dots = jnp.sum(weights * gprob, axis=1, keepdims=True)
            gs = (weights * (gprob - dots)).astype(LOW)
            gs_scratch[i0 : i0 + BLOCK, :] = gs
            turned = mm(anti, gs)
            moved = pltpu.roll(
                jnp.concatenate([turned, pad], axis=1), 0, 1, stride=1, stride_axis=0
            ).astype(LOW)
            table_here = tab[1, h, :, w0 : w0 + window]
            gq = (mm(turned.astype(LOW), keys) + mm(moved, table_here, NT)) * scale
            g_scratch[0, h, i0 : i0 + BLOCK, :] = mm(anti, gq.astype(LOW)).astype(LOW)
            turned_q = mm(anti, q[h, i0 : i0 + BLOCK, :]).astype(LOW)
            gpk_scratch[h, :, w0 : w0 + window] += mm(turned_q, moved, TN)
        for b in range(blocks):
            j0 = b * BLOCK
            w0 = rows - BLOCK - j0
            turned = mm(anti, gs_scratch[:, j0 : j0 + BLOCK], NT)
            moved = pltpu.roll(
                jnp.concatenate([turned, pad], axis=1), 0, 1, stride=1, stride_axis=0
            ).astype(LOW)
            table_here = tab[0, h, :, w0 : w0 + window]
            gk = (mm(turned.astype(LOW), queries) + mm(moved, table_here, NT)) * scale
            g_scratch[1, h, j0 : j0 + BLOCK, :] = mm(anti, gk.astype(LOW)).astype(LOW)
            turned_k = mm(anti, k[h, j0 : j0 + BLOCK, :]).astype(LOW)
            gpq_scratch[h, :, w0 : w0 + window] += mm(turned_k, moved, TN)
        g_scratch[2, h] = mm(prob[h], gctx_scratch[h], TN).astype(LOW)
        return carry

    lax.fori_loop(0, heads, head, 0)
    hot = jnp.where(
        lax.broadcasted_iota(jnp.int32, (buckets, span), 0) == table[...], 1.0, 0.0
    ).astype(LOW)
    gpq = jnp.concatenate(
        [mm(hot, gpq_scratch[h].astype(LOW), NT) * scale for h in range(heads)], axis=1
    )
    gpk = jnp.concatenate(
        [mm(hot, gpk_scratch[h].astype(LOW), NT) * scale for h in range(heads)], axis=1
    )
    gpq_low, gpk_low = gpq.astype(LOW), gpk.astype(LOW)
    rel_scratch[...] = mm(gpq_low, wq[...], NT) + mm(gpk_low, wk[...], NT)
    send_out[rows : rows + half, :] = rel_scratch[
        pl.ds(pl.multiple_of((1 - side) * half, half), half), :
    ].astype(LOW)
    keep_out[...] = rel_scratch[pl.ds(pl.multiple_of(side * half, half), half), :].astype(LOW)
    gq = jnp.concatenate([g_scratch[0, h] for h in range(heads)], axis=1)
    gk = jnp.concatenate([g_scratch[1, h] for h in range(heads)], axis=1)
    gv = jnp.concatenate([g_scratch[2, h] for h in range(heads)], axis=1)
    send_out[:rows, :] = (
        mm(gq, wq[...], NT) + mm(gk, wk[...], NT) + mm(gv, wv[...], NT)
    ).astype(LOW)
    xv = x[...]
    rel = relative[...]
    weights_out[:width, 0:part] = (mm(xv, gq, TN) + mm(rel, gpq_low, TN)).astype(LOW)
    weights_out[:width, part : 2 * part] = (mm(xv, gk, TN) + mm(rel, gpk_low, TN)).astype(LOW)
    grad_v = mm(xv, gv, TN).astype(LOW)
    weights_out[width : width + part, 0:part] = grad_v[:part]
    weights_out[width : width + part, part : 2 * part] = grad_v[part:]
    small_out[0:1, 0:part] = jnp.sum(gq.astype(WIDE), axis=0, keepdims=True) + jnp.sum(
        gpq, axis=0, keepdims=True
    )
    small_out[0:1, part : 2 * part] = jnp.sum(gk.astype(WIDE), axis=0, keepdims=True) + jnp.sum(
        gpk, axis=0, keepdims=True
    )
    small_out[1:2, 0:part] = jnp.sum(gv.astype(WIDE), axis=0, keepdims=True)


def tail_pack(
    chunk, send, got, keep, gp, weights, small_ffn, small_attn, y_moved, buffer_out, grad_out
):
    total, piece, width = y_moved.shape
    rows = gp.shape[0]

    def put(first, value):
        for place, offset, start, take in pieces(first, value.shape[0], chunk):
            buffer_out[place, offset : offset + take, :] = value[start : start + take]

    count = weights.shape[0]
    put(0, weights)
    put(count, (keep[...].astype(WIDE) + got[rows:, :].astype(WIDE)).astype(LOW))
    count += keep.shape[0]
    small = jnp.concatenate([small_ffn[...], small_attn[...]], axis=0).astype(LOW)
    put(count, small)
    count += small.shape[0]
    place, offset = divmod(count, chunk)
    if offset:
        buffer_out[place, offset:chunk, :] = jnp.zeros((chunk - offset, width), LOW)
        place += 1
    for rest in range(place, total):
        buffer_out[rest, :chunk, :] = jnp.zeros((chunk, width), LOW)
    buffer_out[:, chunk:, :] = y_moved[...]
    for i in range(rows // BLOCK):
        here = slice(i * BLOCK, (i + 1) * BLOCK)
        both = send[here, :].astype(WIDE) + got[here, :].astype(WIDE)
        grad_out[here, :] = (gp[here, :] + both).astype(LOW)


def reduce_first(chunk, dealing, got, sum_out, y_out):
    total = got.shape[0]
    acc = got[0, :chunk, :].astype(WIDE)
    for k in range(1, total):
        acc += got[k, :chunk, :].astype(WIDE)
    sum_out[...] = acc.astype(LOW)
    for k in range(total):
        y_out[k] = got[dealing[k], chunk:, :]


def reduce_second(chunk, got, first, spread_out, y_out):
    total = got.shape[0]
    piece = got.shape[1] - chunk
    acc = got[0, :chunk, :].astype(WIDE)
    for k in range(1, total):
        acc += got[k, :chunk, :].astype(WIDE)
    low = acc.astype(LOW)
    ahead = first.shape[0]
    for k in range(spread_out.shape[0]):
        spread_out[k, :ahead, :] = first[...]
        spread_out[k, ahead:, :] = low
    for k in range(y_out.shape[0] // piece):
        y_out[k * piece : (k + 1) * piece, :] = got[k, chunk:, :]


def unpack(
    chunk_one, chunk_two, gathered,
    wup_out, wdown_out, bup_out, wq_out, wk_out, wv_out, wout_out, rel_out,
    bq_out, bk_out, bv_out, bout_out, again_out, ashift_out, bdown_out, fgain_out, fshift_out,
):
    inner = gathered.shape[0]
    width = gathered.shape[3]
    units = wup_out.shape[1]
    part = wq_out.shape[1]

    def rows(first, count, chunk, base):
        for place, offset, start, take in pieces(first, count, chunk):
            yield start, take, gathered[
                place % inner, place // inner, base + offset : base + offset + take, :
            ].astype(WIDE)

    for k in range(units // width):
        for start, take, value in rows(k * width, width, chunk_one, 0):
            wup_out[start : start + take, k * width : (k + 1) * width] = value
    for start, take, value in rows(units, units, chunk_one, 0):
        wdown_out[start : start + take, :] = value
    for start, take, value in rows(0, width, chunk_two, chunk_one):
        wq_out[start : start + take, :] = value[:, :part]
        wk_out[start : start + take, :] = value[:, part:]
    for start, take, value in rows(width, part, chunk_two, chunk_one):
        wv_out[start : start + take, :] = value[:, :part]
        wv_out[part + start : part + start + take, :] = value[:, part:]
    for start, take, value in rows(width + part, part, chunk_two, chunk_one):
        wout_out[start : start + take, :] = value
    first = width + 2 * part
    for start, take, value in rows(first, rel_out.shape[0], chunk_two, chunk_one):
        rel_out[start : start + take, :] = value.astype(LOW)
    first += rel_out.shape[0]
    small = jnp.concatenate([value for _, _, value in rows(first, 16, chunk_two, chunk_one)], axis=0)
    ups = units // width
    for k in range(ups):
        bup_out[:, k * width : (k + 1) * width] = small[k : k + 1]
    bdown_out[...] = small[ups : ups + 1]
    fgain_out[...] = small[ups + 1 : ups + 2]
    fshift_out[...] = small[ups + 2 : ups + 3]
    bq_out[...] = small[8:9, :part]
    bk_out[...] = small[8:9, part:]
    bv_out[...] = small[9:10, :part]
    bout_out[...] = small[10:11]
    again_out[...] = small[11:12]
    ashift_out[...] = small[12:13]


def with_statics(body, *statics):
    def wrapped(*refs):
        body(*statics, *refs)

    wrapped.__name__ = body.__name__
    return wrapped


def swap(array):
    return lax.ppermute(array, "tensor", [(0, 1), (1, 0)])


def exchange(array, groups=None):
    return lax.all_to_all(
        array, "dp", split_axis=0, concat_axis=0, tiled=True, axis_index_groups=groups
    )


def on_device(
    tokens, lengths, dealing, bucket_table, relative,
    w_query, b_query, w_key, b_key, w_value, b_value, w_out, b_out,
    attn_gain, attn_shift, w_up, b_up, w_down, b_down, ffn_gain, ffn_shift, cotangent,
):
    _, rows, width = tokens.shape
    total = dealing.shape[0]
    part = w_query.shape[1]
    heads = part // HEAD_DIM
    units = w_up.shape[1]
    half = rows // 2
    span = 2 * rows
    piece = max(16, half // total)
    spots = half // piece
    side = lax.axis_index("tensor")
    chunk_one = chunk_rows(2 * units, total, 8)
    chunk_two = chunk_rows(width + 2 * part + half + 16, total, 8)

    def row(vector):
        return vector.reshape(1, -1)

    def padded(array):
        if spots == total:
            return array
        return jnp.pad(array, ((0, total - spots), (0, 0), (0, 0)))

    cot_half = lax.dynamic_slice_in_dim(cotangent[0], side * half, half, 0)
    cot_got = exchange(padded(cot_half.reshape(spots, piece, width)))
    (cot_turned,) = call(
        with_statics(permute_body, True), [(cot_got.shape, LOW)], (dealing, cot_got), smem=1
    )
    cot_back = exchange(cot_turned)
    cot_mine = cot_back[:spots].reshape(half, width)
    cot_theirs = swap(cot_mine)

    x = tokens[0]
    table = jnp.pad(jnp.flip(bucket_table), (0, span - bucket_table.shape[0]), constant_values=-1)
    table = table.reshape(1, span)
    q, k, v, tab, prob, ctx, attn_part = call(
        attention_forward,
        [((heads, rows, HEAD_DIM), LOW)] * 3
        + [((2, heads, HEAD_DIM, span), LOW), ((heads, rows, rows), LOW)]
        + [((heads, rows, HEAD_DIM), LOW), ((rows, width), LOW)],
        (lengths, x, relative, table, w_query, row(b_query), w_key, row(b_key), w_value,
         row(b_value), w_out),
        scratch=[pltpu.VMEM((rows, rows), WIDE)],
        smem=1,
        flops=10**10,
    )
    attn_got = swap(attn_part)
    normed, inverse, hidden, act, slope, down_part = call(
        ffn_forward,
        [((rows, width), WIDE), ((rows, 1), WIDE), ((rows, width), LOW), ((rows, units), LOW),
         ((rows, units), LOW), ((rows, width), LOW)],
        (x, attn_part, attn_got, row(b_out), row(attn_gain), row(attn_shift), w_up, row(b_up),
         w_down),
        flops=4 * 10**9,
    )
    down_got = swap(down_part)
    buffer_one, hidden_part, gf, small_ffn = call(
        with_statics(ffn_backward, chunk_one, piece),
        [((total, chunk_one + piece, width), LOW), ((rows, width), LOW), ((rows, width), WIDE),
         ((8, width), WIDE)],
        (lengths, down_part, down_got, row(b_down), normed, row(attn_gain), row(attn_shift),
         row(ffn_gain), row(ffn_shift), cot_mine, cot_theirs, hidden, act, slope, w_up, w_down),
        scratch=[pltpu.VMEM((rows, width), LOW), pltpu.VMEM((rows, units), LOW)],
        smem=1,
        flops=4 * 10**9,
    )
    hidden_got = swap(hidden_part)
    got_one = exchange(buffer_one)
    send, keep, gp, weights, small_attn = call(
        attention_backward,
        [((rows + half, width), LOW), ((half, width), LOW), ((rows, width), WIDE),
         ((width + 2 * part, width), LOW), ((8, width), WIDE)],
        (x, relative, table, w_query, w_key, w_value, w_out, hidden_part, hidden_got, gf, normed,
         inverse, row(attn_gain), q, k, v, tab, prob, ctx),
        scratch=[
            pltpu.VMEM((rows, width), LOW),
            pltpu.VMEM((rows, rows), LOW),
            pltpu.VMEM((heads, HEAD_DIM, span), WIDE),
            pltpu.VMEM((heads, HEAD_DIM, span), WIDE),
            pltpu.VMEM((3, heads, rows, HEAD_DIM), LOW),
            pltpu.VMEM((rows, width), WIDE),
            pltpu.VMEM((heads, rows, HEAD_DIM), LOW),
        ],
        flops=2 * 10**10,
    )
    sent = swap(send)
    sum_one, y_moved = call(
        with_statics(reduce_first, chunk_one),
        [((chunk_one, width), LOW), ((total, piece, width), LOW)],
        (dealing, got_one),
        smem=1,
    )
    buffer_two, grad_tokens = call(
        with_statics(tail_pack, chunk_two),
        [((total, chunk_two + piece, width), LOW), ((rows, width), LOW)],
        (send, sent, keep, gp, weights, small_ffn, small_attn, y_moved),
    )
    got_two = exchange(buffer_two)
    inner = 1 << ((total.bit_length()) // 2)
    outer = total // inner
    ring_far = [[o * inner + i for o in range(outer)] for i in range(inner)]
    ring_near = [[o * inner + i for i in range(inner)] for o in range(outer)]
    chunk = chunk_one + chunk_two
    spread, y_half = call(
        with_statics(reduce_second, chunk_two),
        [((outer, chunk, width), LOW), ((half, width), LOW)],
        (got_two, sum_one),
    )
    lines = exchange(spread, ring_far)
    y_other = swap(y_half)
    wide = jnp.broadcast_to(lines[None], (inner, outer, chunk, width)).reshape(
        inner * outer, chunk, width
    )
    gathered = exchange(wide, ring_near).reshape(inner, outer, chunk, width)
    out = call(
        with_statics(unpack, chunk_one, chunk_two),
        [((width, units), WIDE), ((units, width), WIDE), ((1, units), WIDE)]
        + [((width, part), WIDE)] * 3
        + [((part, width), WIDE), ((half, width), LOW)]
        + [((1, part), WIDE)] * 3
        + [((1, width), WIDE)] * 6,
        (gathered,),
    )
    (g_up, g_down, g_bup, g_wq, g_wk, g_wv, g_wout, rel_half, g_bq, g_bk, g_bv, g_bout, g_again,
     g_ashift, g_bdown, g_fgain, g_fshift) = out
    rel_other = swap(rel_half)

    def join(own, other):
        first = jnp.where(side == 0, own, other)
        second = jnp.where(side == 0, other, own)
        return jnp.concatenate([first, second], axis=0)

    y = join(y_half, y_other)[None]
    g_rel = join(rel_half, rel_other).astype(WIDE)
    return (
        y, grad_tokens[None], g_rel, g_wq, g_bq[0], g_wk, g_bk[0], g_wv, g_bv[0], g_wout,
        g_bout[0], g_again[0], g_ashift[0], g_up, g_bup[0], g_down, g_bdown[0], g_fgain[0],
        g_fshift[0],
    )


def solution(mesh):
    return jax.shard_map(
        on_device,
        mesh=mesh,
        in_specs=(
            P("dp", None, None), P(), P(), P(), P(),
            P(None, "tensor"), P("tensor"), P(None, "tensor"), P("tensor"),
            P(None, "tensor"), P("tensor"), P("tensor", None), P(), P(), P(),
            P(None, "tensor"), P("tensor"), P("tensor", None), P(), P(), P(),
            P("dp", None, None),
        ),
        out_specs=(
            P("dp", None, None), P("dp", None, None), P(),
            P(None, "tensor"), P("tensor"), P(None, "tensor"), P("tensor"),
            P(None, "tensor"), P("tensor"), P("tensor", None), P(), P(), P(),
            P(None, "tensor"), P("tensor"), P("tensor", None), P(), P(), P(),
        ),
        check_vma=False,
    )
```

time: 953 us -> 207 us (0.22); the launches traced: 936 us -> 205 us
  other arithmetic: 302 us -> 7.88 us
  local copies, waits for them, and re-layouts: 304 us -> 40.9 us
  waiting for transfers between devices: 163 us -> 26.4 us
  Pallas kernels: 0 us -> 51 us
  matrix products: 39.8 us -> 0 us
  blocking collectives: 81.1 us -> 51.4 us
  between operations: 15.5 us -> 1.13 us
    scatter-add x2 -> x0, other arithmetic: 263 us -> none  [the longest x1 132 us: one_block(): jax.ops.segment_sum(jnp.transpose(grad_near, (2, 0, 1)), near_ids, num_se...]
    psum x5 -> x0, waiting for transfers between devices: 139 us -> none  [the longest x1 68.5 us: on_device(): all_grads = tuple(lax.psum(ffn_grads + rest, 'dp'))]
    psum x2 -> x0, blocking collectives: 81.1 us -> none  [the longest x1 77.8 us: on_device(): all_grads = tuple(lax.psum(ffn_grads + rest, 'dp'))]
    rev x3 -> x0, local copies, waits for them, and re-layouts: 73.5 us -> none  [the longest x2 48.3 us: place_far(): return jnp.transpose(jnp.flip(skew_rows(values, out_cols), 2), (0, 2, 1))]
    reshape x7 -> x10, local copies, waits for them, and re-layouts: 58.6 us -> 2.01 us  [row(): return vector.reshape(1, -1)]
    all_to_all x0 -> x2, blocking collectives: none -> 51.4 us  [exchange(): lax.all_to_all(array, 'dp', split_axis=0, concat_axis=0, tiled=True, axis...]
    pallas_call x0 -> x9, Pallas kernels: none -> 51 us  [call(): pl.pallas_call(body, out_shape=[jax.ShapeDtypeStruct(shape, kind) for sha...]
    dot_general x30 -> x0, matrix products: 39.8 us -> none  [the longest x1 4.86 us: on_device(): jnp.dot(hidden_low, w_up, preferred_element_type=jnp.float32)]
  transfers between devices with their start and end apart: 9 -> 11, of which waited for: 7 -> 4; matrix products, arithmetic and copies ran while one was open for 4% -> 7% of each run, Pallas kernels for 0% -> 22%
where the time goes in v1:
time: 207 us; the launch traced here: 205 us
  blocking collectives  51.4 us (25%)
  Pallas kernels  51 us (25%)
  local copies, waits for them, and re-layouts  40.9 us (20%)
  starting transfers between devices  26.6 us (13%)
  waiting for transfers between devices  26.4 us (13%)
  other arithmetic  7.88 us (4%)
    all_to_all x2, blocking collectives, exchange(): lax.all_to_all(array, 'dp', split_axis=0, concat_axis=0, tiled=True, axis...  51.4 us
    pallas_call x9, Pallas kernels, call(): pl.pallas_call(body, out_shape=[jax.ShapeDtypeStruct(shape, kind) for sha...  51 us
    unnamed x112, local copies, waits for them, and re-layouts  36.7 us
    all_to_all x4, starting transfers between devices, exchange(): lax.all_to_all(array, 'dp', split_axis=0, concat_axis=0, tiled=True, axis...  25.7 us
    all_to_all x4, waiting for transfers between devices, exchange(): lax.all_to_all(array, 'dp', split_axis=0, concat_axis=0, tiled=True, axis...  23.5 us
    pallas_call x7, other arithmetic, call(): pl.pallas_call(body, out_shape=[jax.ShapeDtypeStruct(shape, kind) for sha...  4.18 us
  transfers between devices with their start and end apart: 11, of which 4 were waited for; matrix products, arithmetic and copies ran while one was open for 7% of the time, Pallas kernels for 22%

profile of v1, /device:TPU:0, one launch (start us, length us, event | category | flops | bytes accessed | tf_op | source)
XLA Modules:
  0.0 205.3 jit_solution(5345566939042826546)
XLA Ops:
  0.7 0.9 copy-done
  1.7 0.7 constant_dynamic-slice_fusion
  2.4 8.3 %all-to-all-start = ((bf16[16,16,384]{2,1,0:T(8,128)(2,1)}), bf16[16,16,384]{2,1,0:T(8,128)(2,1)S(1)}, u32[]{:S(2)}, u32[]{:S(2)}) async-start(bf16[16,16,384]{2,1,0:T(8,128)(2,1)} %bitcast.2), calls=%async_computation | async-start | bytes 393216 | tf_op jit(solution)/shard_map/all_to_all | solution.py:474
  10.7 0.7 reshape.90.bq
  11.4 0.7 reshape.91.bk
  12.7 0.8 reverse
  13.5 1.0 copy.44.wq
  14.6 1.0 copy.45.wk
  15.9 10.6 %shard_map.357 = (bf16[3,512,64]{2,1,0:T(8,128)(2,1)S(1)}, bf16[3,512,64]{2,1,0:T(8,128)(2,1)S(1)}, bf16[3,512,64]{2,1,0:T(8,128)(2,1)S(1)}, bf16[2,3,64,1024]{3...) custom-call(s32[16]{0:T(128)S(1)} %copy-done.11, ...), custom_call_target="tpu_custom_call" | custom-call | flops 10000000000 | bytes 4000000 | tf_op jit(solution)/shard_map/pallas_call | solution.py:47
  26.5 1.2 copy-done.32
  27.7 0.9 copy-done.34
  28.6 0.8 copy-done.36
  29.3 0.7 copy-done.38
  30.1 0.8 copy-done.40
  30.8 0.8 copy-done.42
  31.7 1.2 shard_map.359
  33.0 6.9 %all-to-all-start.1 = ((bf16[16,16,384]{2,1,0:T(8,128)(2,1)}), bf16[16,16,384]{2,1,0:T(8,128)(2,1)S(1)}, u32[]{:S(2)}, u32[]{:S(2)}) async-start(bf16[16,16,384]{2,1,0:T(8,128)(2,1)} %shard_map.359), calls=%async_computation.1 | async-start | bytes 393216 | tf_op jit(solution)/shard_map/all_to_all | solution.py:474
  40.0 4.7 %shard_map.358 = (f32[512,384]{1,0:T(8,128)S(1)}, f32[512,1]{1,0:T(8,128)S(1)}, bf16[512,384]{1,0:T(8,128)(2,1)S(1)}, bf16[512,768]{1,0:T(8,128)(2,1)S(1)}, bf16...) custom-call(bf16[512,384]{1,0:T(8,128)(2,1)S(1)} %bitcast.19, bf16[512,384]{1,0:T(8,128)(2,1)S(1)} %get-tuple-element.64.mine, ...), custom_call_target="tpu_custom_call" | custom-call | flops 4000000000 | bytes 4000000 | tf_op jit(solution)/shard_map/pallas_call | solution.py:47
  44.7 0.9 copy-done.19
  45.6 0.9 copy-done.24
  46.4 0.9 copy-done.26
  47.3 0.7 copy-done.28
  48.1 0.7 copy-done.30
  49.3 1.4 collective-permute-done.1.refs_2_
  51.0 1.1 copy-done.20
  52.1 1.1 copy-done.25
  53.2 1.1 copy-done.27
  54.4 1.0 copy-done.29
  55.4 5.4 %shard_map.360 = (bf16[16,112,384]{2,1,0:T(8,128)(2,1)}, bf16[512,384]{1,0:T(8,128)(2,1)}, f32[512,384]{1,0:T(8,128)S(1)}, f32[8,384]{1,0:T(8,128)S(1)}) custom-call(s32[16]{0:T(128)S(1)} %copy-done.11, bf16[512,384]{1,0:T(8,128)(2,1)} %get-tuple-element.65.refs_1_, bf16[512,384]{1,0:T(8,128)(2,1)S(1)} %collective-permute-done.1.refs_2_, ...), custom_call_target="tpu_custom_call" | custom-call | flops 4000000000 | bytes 4000000 | tf_op jit(solution)/shard_map/pallas_call | solution.py:47
  60.8 0.9 copy-done.22
  61.9 6.8 %all-to-all-start.2 = ((bf16[16,112,384]{2,1,0:T(8,128)(2,1)}), bf16[16,112,384]{2,1,0:T(8,128)(2,1)S(1)}, u32[]{:S(2)}, u32[]{:S(2)}) async-start(bf16[16,112,384]{2,1,0:T(8,128)(2,1)} %get-tuple-element.85), calls=%async_computation.2 | async-start | bytes 2752512 | tf_op jit(solution)/shard_map/all_to_all | solution.py:474
  68.8 0.7 copy-done.8
  69.5 1.0 copy-done.7
  70.5 1.0 copy-done.9
  71.5 1.1 copy-done.21
  72.7 1.1 copy-done.23
  73.8 0.9 copy-done.31
  74.7 1.4 copy-done.33
  76.1 1.1 copy-done.35
  77.3 1.0 copy-done.37
  78.3 1.0 copy-done.39
  79.3 1.0 copy-done.41
  80.3 1.0 copy-done.43
  81.3 25.4 %shard_map.361 = (bf16[768,384]{1,0:T(8,128)(2,1)S(1)}, bf16[256,384]{1,0:T(8,128)(2,1)S(1)}, f32[512,384]{1,0:T(8,128)S(1)}, bf16[768,384]{1,0:T(8,128)(2,1)S(1)}, f32[8,384]{1,0:T(8,128)S(1)}) custom-call(bf16[512,384]{1,0:T(8,128)(2,1)S(1)} %bitcast.20, bf16[512,384]{1,0:T(8,128)(2,1)S(1)} %copy-done.7, s32[1,1024]{1,0:T(1,128)S(1)} %bitcast.17, ...), custom_call_target="tpu_custom_call" | custom-call | flops 20000000000 | bytes 4000000 | tf_op jit(solution)/shard_map/pallas_call | solution.py:47
  106.7 0.9 copy-done.13
  107.6 0.8 copy-done.15
  108.4 0.7 copy-done.17
  109.2 0.7 shard_map.362
  109.9 1.2 collective-permute-done.4.refs_1_
  111.1 1.0 shard_map.363
  112.1 35.0 %all_to_all.30.refs_0_ = bf16[16,88,384]{2,1,0:T(8,128)(2,1)S(1)} all-to-all(bf16[16,88,384]{2,1,0:T(8,128)(2,1)S(1)} %get-tuple-element.87), channel_id=1, replica_groups=mesh['dp'=16,'tensor'=2] {'dp'}, dimensions={0} | all-to-all | bytes 2162688 | tf_op jit(solution)/shard_map/all_to_all | solution.py:474
  147.2 16.4 %all_to_all.31 = bf16[4,168,384]{2,1,0:T(8,128)(2,1)S(1)} all-to-all(bf16[4,168,384]{2,1,0:T(8,128)(2,1)S(1)} %get-tuple-element.91), channel_id=1, replica_groups={{0,8,16,24},{2,10,18,26},{4,12,20,28},{6,14,22,30},{1,9,17,25},{3,11,19..., dimensions={0} | all-to-all | bytes 1032192 | tf_op jit(solution)/shard_map/all_to_all | solution.py:474
  163.6 1.5 broadcast_in_dim.14
  165.1 3.6 %all-to-all-start.5 = ((bf16[16,168,384]{2,1,0:T(8,128)(2,1)}), bf16[16,168,384]{2,1,0:T(8,128)(2,1)S(1)}, u32[]{:S(2)}, u32[]{:S(2)}) async-start(bf16[16,168,384]{2,1,0:T(8,128)(2,1)} %bitcast.21), calls=%async_computation.5 | async-start | bytes 4128768 | tf_op jit(solution)/shard_map/all_to_all | solution.py:474
  168.8 23.5 %all-to-all-done.5 = bf16[16,168,384]{2,1,0:T(8,128)(2,1)S(1)} async-done(((bf16[16,168,384]{2,1,0:T(8,128)(2,1)}), bf16[16,168,384]{2,1,0:T(8,128)(2,1)S(1)}, u32[]{:S(2)}, u32[]{:S(2)}) %all-to-all-start.5) | async-done | bytes 2064416 | tf_op jit(solution)/shard_map/all_to_all | solution.py:474
  192.3 1.7 shard_map.365
  194.0 0.7 copy-done.1
  194.8 1.0 broadcast_select_fusion.3
  195.8 0.8 maximum_bitcast_fusion
  196.6 0.9 copy.47
  201.6 0.9 copy.48
  202.5 0.9 copy.49
  203.4 1.0 broadcast_select_fusion.1
  204.3 0.9 maximum_convert_fusion
  (105 shorter events, 6.6 us)
Async XLA Ops:
  0.7 1.0 copy-start
  0.7 14.9 %copy-start.44 = (bf16[384,192]{0,1:T(8,128)(2,1)S(1)}, bf16[384,192]{0,1:T(8,128)(2,1)}, u32[]{:S(2)}) copy-start(bf16[384,192]{0,1:T(8,128)(2,1)} %param.31) | copy-start | bytes 442372
  0.7 15.1 %copy-start.10 = (bf16[192,384]{1,0:T(8,128)(2,1)S(1)}, bf16[192,384]{1,0:T(8,128)(2,1)}, u32[]{:S(2)}) copy-start(bf16[192,384]{1,0:T(8,128)(2,1)} %wout.3) | copy-start | bytes 442372
  0.7 15.1 %copy-start.6 = (bf16[512,384]{1,0:T(8,128)(2,1)S(1)}, bf16[512,384]{1,0:T(8,128)(2,1)}, u32[]{:S(2)}) copy-start(bf16[512,384]{1,0:T(8,128)(2,1)} %relative.3) | copy-start | bytes 1179652
  0.7 15.1 %copy-start.11 = (s32[16]{0:T(128)S(1)}, s32[16]{0:T(128)}, u32[]{:S(2)}) copy-start(s32[16]{0:T(128)} %refs_0_.4) | copy-start | bytes 196
  0.7 15.1 %copy-start.5 = (bf16[1,512,384]{2,1,0:T(8,128)(2,1)S(1)}, bf16[1,512,384]{2,1,0:T(8,128)(2,1)}, u32[]{:S(2)}) copy-start(bf16[1,512,384]{2,1,0:T(8,128)(2,1)} %param.22) | copy-start | bytes 1179652
  2.4 29.4 %all-to-all-start = ((bf16[16,16,384]{2,1,0:T(8,128)(2,1)}), bf16[16,16,384]{2,1,0:T(8,128)(2,1)S(1)}, u32[]{:S(2)}, u32[]{:S(2)}) async-start(bf16[16,16,384]{2,1,0:T(8,128)(2,1)} %bitcast.2), calls=%async_computation | async-start | bytes 393216 | tf_op jit(solution)/shard_map/all_to_all | solution.py:474
  15.8 15.8 %copy-start.46 = (bf16[384]{0:T(512)(128)(2,1)S(1)}, bf16[384]{0:T(512)(128)(2,1)}, u32[]{:S(2)}) copy-start(bf16[384]{0:T(512)(128)(2,1)} %param.35) | copy-start | bytes 2308
  15.8 15.8 %copy-start.47 = (bf16[384]{0:T(512)(128)(2,1)S(1)}, bf16[384]{0:T(512)(128)(2,1)}, u32[]{:S(2)}) copy-start(bf16[384]{0:T(512)(128)(2,1)} %param.36) | copy-start | bytes 2308
  15.8 15.8 %copy-start.48 = (bf16[384]{0:T(512)(128)(2,1)S(1)}, bf16[384]{0:T(512)(128)(2,1)}, u32[]{:S(2)}) copy-start(bf16[384]{0:T(512)(128)(2,1)} %param.34) | copy-start | bytes 2308
  15.9 15.8 %copy-start.45 = (bf16[768]{0:T(1024)(128)(2,1)S(1)}, bf16[768]{0:T(1024)(128)(2,1)}, u32[]{:S(2)}) copy-start(bf16[768]{0:T(1024)(128)(2,1)} %param.38) | copy-start | bytes 4612
  15.9 15.9 %copy-start.12 = (s32[16]{0:T(128)S(1)}, s32[16]{0:T(128)}, u32[]{:S(2)}) copy-start(s32[16]{0:T(128)} %refs_0_.5) | copy-start | bytes 196
  26.5 1.2 copy-start.32
  27.7 0.9 copy-start.34
  28.6 0.8 copy-start.36
  29.3 0.7 copy-start.38
  30.1 0.8 copy-start.40
  30.8 0.8 copy-start.42
  31.6 8.3 %collective-permute-start = (bf16[512,384]{1,0:T(8,128)(2,1)S(1)}, bf16[512,384]{1,0:T(8,128)(2,1)}, u32[]{:S(2)}, u32[]{:S(2)}) collective-permute-start(bf16[512,384]{1,0:T(8,128)(2,1)S(1)} %get-tuple-element.64.mine), channel_id=1, source_target_pairs={{0,1},{1,0},{2,3},{3,2},{4,5},{5,4},{6,7},{7,6},{8,9},{9,8},{10,11... | collective-permute-start | bytes 1179656 | tf_op jit(solution)/shard_map/ppermute | solution.py:470
  31.7 8.2 %copy-start.3 = (bf16[384,768]{1,0:T(8,128)(2,1)S(1)}, bf16[384,768]{1,0:T(8,128)(2,1)}, u32[]{:S(2)}) copy-start(bf16[384,768]{1,0:T(8,128)(2,1)} %refs_14_.1) | copy-start | bytes 1769476
  31.7 8.2 %copy-start.4 = (bf16[768,384]{1,0:T(8,128)(2,1)S(1)}, bf16[768,384]{1,0:T(8,128)(2,1)}, u32[]{:S(2)}) copy-start(bf16[768,384]{1,0:T(8,128)(2,1)} %refs_15_.1) | copy-start | bytes 1769476
  33.0 16.0 %all-to-all-start.1 = ((bf16[16,16,384]{2,1,0:T(8,128)(2,1)}), bf16[16,16,384]{2,1,0:T(8,128)(2,1)S(1)}, u32[]{:S(2)}, u32[]{:S(2)}) async-start(bf16[16,16,384]{2,1,0:T(8,128)(2,1)} %shard_map.359), calls=%async_computation.1 | async-start | bytes 393216 | tf_op jit(solution)/shard_map/all_to_all | solution.py:474
  39.9 9.4 %copy-start.49 = (bf16[384]{0:T(512)(128)(2,1)S(1)}, bf16[384]{0:T(512)(128)(2,1)}, u32[]{:S(2)}) copy-start(bf16[384]{0:T(512)(128)(2,1)} %param.40) | copy-start | bytes 2308
  39.9 9.4 %copy-start.50 = (bf16[384]{0:T(512)(128)(2,1)S(1)}, bf16[384]{0:T(512)(128)(2,1)}, u32[]{:S(2)}) copy-start(bf16[384]{0:T(512)(128)(2,1)} %param.41) | copy-start | bytes 2308
  39.9 9.4 %copy-start.51 = (bf16[384]{0:T(512)(128)(2,1)S(1)}, bf16[384]{0:T(512)(128)(2,1)}, u32[]{:S(2)}) copy-start(bf16[384]{0:T(512)(128)(2,1)} %param.42) | copy-start | bytes 2308
  44.7 0.9 copy-start.19
  45.6 0.9 copy-start.24
  46.4 0.9 copy-start.26
  47.3 0.7 copy-start.28
  48.1 0.7 copy-start.30
  48.8 1.9 collective-permute-start.1
  49.0 2.0 collective-permute-start.2
  51.0 1.1 copy-start.20
  52.1 1.1 copy-start.25
  53.2 1.1 copy-start.27
  54.4 1.0 copy-start.29
  60.8 0.9 copy-start.22
  61.7 7.1 %collective-permute-start.3 = (bf16[512,384]{1,0:T(8,128)(2,1)}, bf16[512,384]{1,0:T(8,128)(2,1)S(1)}, u32[]{:S(2)}, u32[]{:S(2)}) collective-permute-start(bf16[512,384]{1,0:T(8,128)(2,1)} %get-tuple-element.70.mine), channel_id=1, source_target_pairs={{0,1},{1,0},{2,3},{3,2},{4,5},{5,4},{6,7},{7,6},{8,9},{9,8},{10,11... | collective-permute-start | bytes 1179656 | tf_op jit(solution)/shard_map/ppermute | solution.py:470
  61.9 47.2 %all-to-all-start.2 = ((bf16[16,112,384]{2,1,0:T(8,128)(2,1)}), bf16[16,112,384]{2,1,0:T(8,128)(2,1)S(1)}, u32[]{:S(2)}, u32[]{:S(2)}) async-start(bf16[16,112,384]{2,1,0:T(8,128)(2,1)} %get-tuple-element.85), calls=%async_computation.2 | async-start | bytes 2752512 | tf_op jit(solution)/shard_map/all_to_all | solution.py:474
  68.8 0.7 copy-start.8
  69.5 1.0 copy-start.7
  70.5 1.0 copy-start.9
  71.5 1.1 copy-start.21
  72.7 1.1 copy-start.23
  73.8 0.9 copy-start.31
  74.7 1.4 copy-start.33
  76.1 1.1 copy-start.35
  77.3 1.0 copy-start.37
  78.3 1.0 copy-start.39
  79.3 1.0 copy-start.41
  80.3 1.0 copy-start.43
  106.7 0.9 copy-start.13
  107.6 0.8 copy-start.15
  108.4 0.7 copy-start.17
  109.1 2.0 copy-start.18
  109.1 2.0 collective-permute-start.4
  109.2 1.9 copy-start.14
  109.2 1.9 copy-start.16
  165.1 27.2 %all-to-all-start.5 = ((bf16[16,168,384]{2,1,0:T(8,128)(2,1)}), bf16[16,168,384]{2,1,0:T(8,128)(2,1)S(1)}, u32[]{:S(2)}, u32[]{:S(2)}) async-start(bf16[16,168,384]{2,1,0:T(8,128)(2,1)} %bitcast.21), calls=%async_computation.5 | async-start | bytes 4128768 | tf_op jit(solution)/shard_map/all_to_all | solution.py:474
  168.7 26.0 %collective-permute-start.5 = (bf16[256,384]{1,0:T(8,128)(2,1)S(1)}, bf16[256,384]{1,0:T(8,128)(2,1)}, u32[]{:S(2)}, u32[]{:S(2)}) collective-permute-start(bf16[256,384]{1,0:T(8,128)(2,1)S(1)} %get-tuple-element.89), channel_id=1, source_target_pairs={{0,1},{1,0},{2,3},{3,2},{4,5},{5,4},{6,7},{7,6},{8,9},{9,8},{10,11... | collective-permute-start | bytes 589832 | tf_op jit(solution)/shard_map/ppermute | solution.py:470
  194.0 0.7 copy-start.1
  194.8 1.8 copy-start.2
  194.8 8.6 %collective-permute-start.6 = (bf16[256,384]{1,0:T(8,128)(2,1)}, bf16[256,384]{1,0:T(8,128)(2,1)S(1)}, u32[]{:S(2)}, u32[]{:S(2)}) collective-permute-start(bf16[256,384]{1,0:T(8,128)(2,1)} %get-tuple-element.92), channel_id=1, source_target_pairs={{0,1},{1,0},{2,3},{3,2},{4,5},{5,4},{6,7},{7,6},{8,9},{9,8},{10,11... | collective-permute-start | bytes 589832 | tf_op jit(solution)/shard_map/ppermute | solution.py:470

commit v2 on v1

v2 whole, which is shorter than its diff:
```python
import math

import jax
import jax.numpy as jnp
from jax import lax
from jax.experimental import pallas as pl
from jax.experimental.pallas import tpu as pltpu
from jax.sharding import PartitionSpec as P

HEAD_DIM = 64
EPSILON = 1e-07
ROOT_HALF = 0.7071067811865476
INV_ROOT_TAU = 0.3989422804014327
BLOCK = 128
LOW = jnp.bfloat16
WIDE = jnp.float32

NN = (((1,), (0,)), ((), ()))
NT = (((1,), (1,)), ((), ()))
TN = (((0,), (0,)), ((), ()))
TT = (((0,), (1,)), ((), ()))


def mm(left, right, dims=NN):
    return lax.dot_general(left, right, dims, preferred_element_type=WIDE)


def pieces(first, count, chunk):
    out = []
    done = 0
    while done < count:
        place, offset = divmod(first + done, chunk)
        take = min(chunk - offset, count - done)
        out.append((place, offset, done, take))
        done += take
    return out


def chunk_rows(rows, parts, unit):
    return -(-(-(-rows // parts)) // unit) * unit


def call(body, out_shapes, args, scratch=(), smem=0, flops=10**9, moved=4 * 10**6, aliases=None):
    specs = [
        pl.BlockSpec(memory_space=pltpu.SMEM if i < smem else pltpu.VMEM) for i in range(len(args))
    ]
    return pl.pallas_call(
        body,
        out_shape=[jax.ShapeDtypeStruct(shape, kind) for shape, kind in out_shapes],
        in_specs=specs,
        out_specs=[pl.BlockSpec(memory_space=pltpu.VMEM) for _ in out_shapes],
        scratch_shapes=list(scratch),
        input_output_aliases=aliases or {},
        compiler_params=pltpu.CompilerParams(vmem_limit_bytes=16 * 1024 * 1024),
        cost_estimate=pl.CostEstimate(flops=flops, bytes_accessed=moved, transcendentals=0),
    )(*args)


def permute_body(piece, dealing, source, target):
    for k in range(source.shape[0]):
        there = dealing[k]
        target[there, :piece, :] = source[k, :piece, :]
        target[k, piece:, :] = source[there, piece:, :]


def assemble(mine, theirs, spots, first, piece, target):
    side = lax.axis_index("tensor")
    half = spots * piece
    for source, base in ((mine, side * half), (theirs, (1 - side) * half)):
        for p in range(spots):
            target[pl.ds(pl.multiple_of(base + p * piece, piece), piece), :] = source[
                p, first : first + piece, :
            ]


def project(x, weights, biases, outs):
    for weight, bias, out in zip(weights, biases, outs):
        full = (mm(x, weight[...], NT) + bias[...].astype(WIDE)[None, :]).astype(LOW)
        for h in range(out.shape[0]):
            out[h] = full[:, h * HEAD_DIM : (h + 1) * HEAD_DIM]


def anti_diagonal():
    return jnp.where(
        lax.broadcasted_iota(jnp.int32, (BLOCK, BLOCK), 0)
        + lax.broadcasted_iota(jnp.int32, (BLOCK, BLOCK), 1)
        == BLOCK - 1,
        1.0,
        0.0,
    ).astype(LOW)


def one_hot(table, buckets):
    anti = anti_diagonal()
    entries = table[...]
    high = entries // 256
    turned = mm(high.astype(WIDE).astype(LOW), anti) * 256.0 + mm(
        (entries - high * 256).astype(WIDE).astype(LOW), anti
    )
    turned = turned.astype(jnp.int32)
    count = table.shape[0]
    rows = lax.broadcasted_iota(jnp.int32, (buckets, BLOCK), 0)
    return jnp.concatenate(
        [
            jnp.where(rows == turned[count - 1 - b : count - b, :], 1.0, 0.0).astype(LOW)
            for b in range(count)
        ],
        axis=1,
    )


def attend(length, q, k, v, tab, wout, ctx, attn_out, far_scratch, prob_out):
    heads, rows, _ = q.shape
    window = rows + BLOCK
    scale = 1.0 / math.sqrt(3.0 * HEAD_DIM)
    key_ok = lax.broadcasted_iota(jnp.int32, (1, rows), 1) < length

    def head(h, carry):
        keys = k[h]
        values = v[h]
        for b in range(rows // BLOCK):
            j0 = b * BLOCK
            w0 = rows - BLOCK - j0
            far = mm(k[h, j0 : j0 + BLOCK, :], tab[0, h, :, w0 : w0 + window])
            far = pltpu.roll(far, window - BLOCK, 1, stride=1, stride_axis=0)[:, :rows]
            far_scratch[:, j0 : j0 + BLOCK] = far.T
        for a in range(rows // BLOCK):
            i0 = a * BLOCK
            w0 = rows - BLOCK - i0
            block_q = q[h, i0 : i0 + BLOCK, :]
            near = mm(block_q, tab[1, h, :, w0 : w0 + window])
            near = pltpu.roll(near, window - BLOCK, 1, stride=1, stride_axis=0)[:, :rows]
            score = (mm(block_q, keys, NT) + near + far_scratch[i0 : i0 + BLOCK, :]) * scale
            score = jnp.where(key_ok, score, -1e30)
            top = jnp.max(score, axis=1, keepdims=True)
            weights = jnp.exp(score - top)
            row_ok = i0 + lax.broadcasted_iota(jnp.int32, (BLOCK, 1), 0) < length
            norm = jnp.where(row_ok, 1.0 / jnp.sum(weights, axis=1, keepdims=True), 0.0)
            prob = (weights * norm).astype(LOW)
            if prob_out is not None:
                prob_out[h, i0 : i0 + BLOCK, :] = prob
            ctx[h, i0 : i0 + BLOCK, :] = mm(prob, values).astype(LOW)
        return carry

    lax.fori_loop(0, heads, head, 0)
    total = mm(ctx[0], wout[0:HEAD_DIM, :])
    for h in range(1, heads):
        total += mm(ctx[h], wout[h * HEAD_DIM : (h + 1) * HEAD_DIM, :])
    attn_out[...] = total.astype(LOW)


def attention_forward(
    lengths, x, relative, table, wq, bq, wk, bk, wv, bv, wout,
    q_out, k_out, v_out, tab_out, prob_out, ctx_out, attn_out, far_scratch,
):
    length = lengths[lax.axis_index("dp")]
    project(x[...], (wq, wk, wv), (bq, bk, bv), (q_out, k_out, v_out))
    rel = relative[...]
    hot = one_hot(table, relative.shape[0])
    for slot, (weight, bias) in enumerate(((wq, bq), (wk, bk))):
        low = (mm(rel, weight[...], NT) + bias[...].astype(WIDE)[None, :]).astype(LOW)
        spread = mm(low, hot, TN).astype(LOW)
        for h in range(q_out.shape[0]):
            tab_out[slot, h] = spread[h * HEAD_DIM : (h + 1) * HEAD_DIM]
    attend(length, q_out, k_out, v_out, tab_out, wout, ctx_out, attn_out, far_scratch, prob_out)


def attention_dealt(
    spots, piece, lengths, dealing, mine, theirs, tab, wq, bq, wk, bk, wv, bv, wout,
    x_out, attn_out, q, k, v, ctx, far_scratch,
):
    length = lengths[dealing[lax.axis_index("dp")]]
    assemble(mine, theirs, spots, piece, piece, x_out)
    project(x_out[...], (wq, wk, wv), (bq, bk, bv), (q, k, v))
    attend(length, q, k, v, tab, wout, ctx, attn_out, far_scratch, None)


def row_norm(values):
    center = values - jnp.mean(values, axis=-1, keepdims=True)
    inverse = lax.rsqrt(jnp.mean(center * center, axis=-1, keepdims=True) + EPSILON)
    return center * inverse, inverse


def norm_back(scaled, normed, inverse):
    one = jnp.mean(scaled, axis=-1, keepdims=True)
    two = jnp.mean(scaled * normed, axis=-1, keepdims=True)
    return inverse * (scaled - one - normed * two)


def ffn_forward(
    keep, x, mine, theirs, bout, gain, shift, wup, bup, wdown, normed_out, down_out,
    inverse_out=None, hidden_out=None, act_out=None, slope_out=None,
):
    rows = x.shape[0]

    def block(i, carry):
        here = pl.ds(pl.multiple_of(i * BLOCK, BLOCK), BLOCK)
        attn = mine[here, :].astype(WIDE) + theirs[here, :].astype(WIDE) + wide_row(bout)
        normed, inverse = row_norm(x[here, :].astype(WIDE) + attn)
        normed_out[here, :] = normed
        low = (normed * wide_row(gain) + wide_row(shift)).astype(LOW)
        u = mm(low, wup[...]) + wide_row(bup)
        cdf = 0.5 * (1.0 + lax.erf(u * ROOT_HALF))
        act = (u * cdf).astype(LOW)
        if keep:
            inverse_out[here, :] = inverse
            hidden_out[here, :] = low
            act_out[here, :] = act
            density = jnp.exp(-0.5 * u * u) * INV_ROOT_TAU
            slope_out[here, :] = (cdf + u * density).astype(LOW)
        down_out[here, :] = mm(act, wdown[...]).astype(LOW)
        return carry

    lax.fori_loop(0, rows // BLOCK, block, 0)


def wide_row(vector):
    return vector[...].astype(WIDE)[None, :]


def second_norm(here, mine, theirs, bdown, normed, gain, shift):
    f = mine[here, :].astype(WIDE) + theirs[here, :].astype(WIDE) + wide_row(bdown)
    return row_norm(normed[here, :] * wide_row(gain) + wide_row(shift) + f)


def finish_dealt(mine, theirs, bdown, normed, gain, shift, fgain, fshift, y_out):
    for i in range(normed.shape[0] // BLOCK):
        here = slice(i * BLOCK, (i + 1) * BLOCK)
        n2, _ = second_norm(here, mine, theirs, bdown, normed, gain, shift)
        y_out[here, :] = (n2 * wide_row(fgain) + wide_row(fshift)).astype(LOW)


def put(buffer, chunk, base, first, value):
    inner = buffer.shape[0]
    for place, offset, start, take in pieces(first, value.shape[0], chunk):
        buffer[place % inner, place // inner, base + offset : base + offset + take, :] = value[
            start : start + take
        ]


def put_zeros(buffer, chunk, first):
    inner, outer, _, width = buffer.shape
    left = inner * outer * chunk - first
    if left > 0:
        put(buffer, chunk, 0, first, jnp.zeros((left, width), buffer.dtype))


def ffn_backward(
    chunk, spots, piece, lengths,
    mine, theirs, bdown, normed, gain, shift, fgain, cot_mine, cot_theirs,
    hidden, act, slope, wup, wdown,
    buffer_out, part_out, gf_out, small_out, low_scratch, gu_scratch, cot_scratch,
):
    length = lengths[lax.axis_index("dp")]
    rows, width = normed.shape
    units = act.shape[1]
    assemble(cot_mine, cot_theirs, spots, 0, piece, cot_scratch)
    sums = [jnp.zeros((1, width), WIDE) for _ in range(3)]
    for i in range(rows // BLOCK):
        here = slice(i * BLOCK, (i + 1) * BLOCK)
        n2, r2 = second_norm(here, mine, theirs, bdown, normed, gain, shift)
        row_ok = i * BLOCK + lax.broadcasted_iota(jnp.int32, (BLOCK, 1), 0) < length
        gy = jnp.where(row_ok, cot_scratch[here, :].astype(WIDE), 0.0)
        gf = norm_back(gy * wide_row(fgain), n2, r2)
        gf_out[here, :] = gf
        low = gf.astype(LOW)
        low_scratch[here, :] = low
        sums[0] += jnp.sum(low.astype(WIDE), axis=0, keepdims=True)
        sums[1] += jnp.sum(gy * n2, axis=0, keepdims=True)
        sums[2] += jnp.sum(gy, axis=0, keepdims=True)
    gu_sum = jnp.zeros((1, units), WIDE)
    for i in range(rows // BLOCK):
        here = slice(i * BLOCK, (i + 1) * BLOCK)
        gu = (mm(low_scratch[here, :], wdown[...], NT) * slope[here, :].astype(WIDE)).astype(LOW)
        gu_scratch[here, :] = gu
        gu_sum += jnp.sum(gu.astype(WIDE), axis=0, keepdims=True)
        part_out[here, :] = mm(gu, wup[...], NT).astype(LOW)
    small_out[...] = jnp.zeros_like(small_out)
    for k in range(units // width):
        small_out[k : k + 1, :] = gu_sum[:, k * width : (k + 1) * width]
    for k in range(3):
        small_out[units // width + k : units // width + k + 1, :] = sums[k]
    put(buffer_out, chunk, 0, units, mm(act[...], low_scratch[...], TN).astype(LOW))
    for k in range(units // width):
        columns = slice(k * width, (k + 1) * width)
        put(
            buffer_out, chunk, 0, k * width,
            mm(hidden[...], gu_scratch[:, columns], TN).astype(LOW),
        )
    put_zeros(buffer_out, chunk, 2 * units)


def attention_backward(
    x, relative, table, wq, wk, wv, wout,
    mine, theirs, gf, normed, inverse, gain,
    q, k, v, tab, prob, ctx,
    send_out, keep_out, gp_out, weights_out, small_out,
    gpb_scratch, gs_scratch, gpk_scratch, gpq_scratch, g_scratch, rel_scratch, gctx_scratch,
):
    side = lax.axis_index("tensor")
    heads, rows, _ = q.shape
    width = x.shape[1]
    half = rows // 2
    span = tab.shape[3]
    buckets = relative.shape[0]
    window = rows + BLOCK
    scale = 1.0 / math.sqrt(3.0 * HEAD_DIM)
    blocks = rows // BLOCK
    part = heads * HEAD_DIM
    sums = [jnp.zeros((1, width), WIDE) for _ in range(3)]
    for i in range(blocks):
        here = slice(i * BLOCK, (i + 1) * BLOCK)
        gh = gf[here, :] + (mine[here, :].astype(WIDE) + theirs[here, :].astype(WIDE))
        n1 = normed[here, :]
        gp = norm_back(gh * wide_row(gain), n1, inverse[here, :])
        gp_out[here, :] = gp
        low = gp.astype(LOW)
        gpb_scratch[here, :] = low
        sums[0] += jnp.sum(low.astype(WIDE), axis=0, keepdims=True)
        sums[1] += jnp.sum(gh * n1, axis=0, keepdims=True)
        sums[2] += jnp.sum(gh, axis=0, keepdims=True)
        grad = mm(low, wout[...], NT).astype(LOW)
        for h in range(heads):
            gctx_scratch[h, here, :] = grad[:, h * HEAD_DIM : (h + 1) * HEAD_DIM]
    small_out[...] = jnp.zeros_like(small_out)
    for n in range(3):
        small_out[2 + n : 3 + n, :] = sums[n]
    for h in range(heads):
        first = 3 * part + h * HEAD_DIM
        weights_out[first : first + HEAD_DIM, :] = mm(ctx[h], gpb_scratch[...], TN).astype(LOW)
    anti = anti_diagonal()
    pad = jnp.zeros((BLOCK, BLOCK), WIDE)

    def head(h, carry):
        keys = k[h]
        queries = q[h]
        gpk_scratch[h] = jnp.zeros((HEAD_DIM, span), WIDE)
        gpq_scratch[h] = jnp.zeros((HEAD_DIM, span), WIDE)
        for i in range(blocks):
            i0 = i * BLOCK
            w0 = rows - BLOCK - i0
            weights = prob[h, i0 : i0 + BLOCK, :].astype(WIDE)
            gprob = mm(gctx_scratch[h, i0 : i0 + BLOCK, :], v[h], NT)
            dots = jnp.sum(weights * gprob, axis=1, keepdims=True)
            gs = (weights * (gprob - dots)).astype(LOW)
            gs_scratch[i0 : i0 + BLOCK, :] = gs
            turned = mm(anti, gs)
            moved = pltpu.roll(
                jnp.concatenate([turned, pad], axis=1), 1, 1, stride=1, stride_axis=0
            ).astype(LOW)
            table_here = tab[1, h, :, w0 : w0 + window]
            gq = (mm(turned.astype(LOW), keys) + mm(moved, table_here, NT)) * scale
            g_scratch[0, h, i0 : i0 + BLOCK, :] = mm(anti, gq.astype(LOW)).astype(LOW)
            turned_q = mm(anti, q[h, i0 : i0 + BLOCK, :]).astype(LOW)
            gpk_scratch[h, :, w0 : w0 + window] += mm(turned_q, moved, TN)
        for b in range(blocks):
            j0 = b * BLOCK
            w0 = rows - BLOCK - j0
            turned = mm(anti, gs_scratch[:, j0 : j0 + BLOCK], NT)
            moved = pltpu.roll(
                jnp.concatenate([turned, pad], axis=1), 1, 1, stride=1, stride_axis=0
            ).astype(LOW)
            table_here = tab[0, h, :, w0 : w0 + window]
            gk = (mm(turned.astype(LOW), queries) + mm(moved, table_here, NT)) * scale
            g_scratch[1, h, j0 : j0 + BLOCK, :] = mm(anti, gk.astype(LOW)).astype(LOW)
            turned_k = mm(anti, k[h, j0 : j0 + BLOCK, :]).astype(LOW)
            gpq_scratch[h, :, w0 : w0 + window] += mm(turned_k, moved, TN)
        g_scratch[2, h] = mm(prob[h], gctx_scratch[h], TN).astype(LOW)
        return carry

    lax.fori_loop(0, heads, head, 0)
    hot = one_hot(table, buckets)
    gpq = jnp.concatenate(
        [mm(hot, gpq_scratch[h].astype(LOW), NT) * scale for h in range(heads)], axis=1
    )
    gpk = jnp.concatenate(
        [mm(hot, gpk_scratch[h].astype(LOW), NT) * scale for h in range(heads)], axis=1
    )
    gpq_low, gpk_low = gpq.astype(LOW), gpk.astype(LOW)
    rel_scratch[...] = mm(gpq_low, wq[...]) + mm(gpk_low, wk[...])
    send_out[rows : rows + half, :] = rel_scratch[
        pl.ds(pl.multiple_of((1 - side) * half, half), half), :
    ].astype(LOW)
    keep_out[...] = rel_scratch[pl.ds(pl.multiple_of(side * half, half), half), :].astype(LOW)
    gq = jnp.concatenate([g_scratch[0, h] for h in range(heads)], axis=1)
    gk = jnp.concatenate([g_scratch[1, h] for h in range(heads)], axis=1)
    gv = jnp.concatenate([g_scratch[2, h] for h in range(heads)], axis=1)
    send_out[:rows, :] = (
        mm(gq, wq[...]) + mm(gk, wk[...]) + mm(gv, wv[...])
    ).astype(LOW)
    xv = x[...]
    rel = relative[...]
    weights_out[:part, :] = (mm(gq, xv, TN) + mm(gpq_low, rel, TN)).astype(LOW)
    weights_out[part : 2 * part, :] = (mm(gk, xv, TN) + mm(gpk_low, rel, TN)).astype(LOW)
    weights_out[2 * part : 3 * part, :] = mm(gv, xv, TN).astype(LOW)
    small_out[0:1, 0:part] = jnp.sum(gq.astype(WIDE), axis=0, keepdims=True) + jnp.sum(
        gpq, axis=0, keepdims=True
    )
    small_out[0:1, part : 2 * part] = jnp.sum(gk.astype(WIDE), axis=0, keepdims=True) + jnp.sum(
        gpk, axis=0, keepdims=True
    )
    small_out[1:2, 0:part] = jnp.sum(gv.astype(WIDE), axis=0, keepdims=True)


def tail_pack(
    chunk, send, got, keep, gp, weights, small_ffn, small_attn, buffer_out, grad_out
):
    rows = gp.shape[0]
    count = weights.shape[0]
    put(buffer_out, chunk, 0, 0, weights)
    both = (keep[...].astype(WIDE) + got[rows:, :].astype(WIDE)).astype(LOW)
    put(buffer_out, chunk, 0, count, both)
    count += keep.shape[0]
    small = jnp.concatenate([small_ffn[...], small_attn[...]], axis=0).astype(LOW)
    put(buffer_out, chunk, 0, count, small)
    put_zeros(buffer_out, chunk, count + small.shape[0])
    for i in range(rows // BLOCK):
        here = slice(i * BLOCK, (i + 1) * BLOCK)
        both = send[here, :].astype(WIDE) + got[here, :].astype(WIDE)
        grad_out[here, :] = (gp[here, :] + both).astype(LOW)


def add_up(got):
    acc = got[0].astype(WIDE)
    for k in range(1, got.shape[0]):
        acc += got[k].astype(WIDE)
    return acc.astype(LOW)


def reduce_near(got, sum_out):
    sum_out[...] = add_up(got)


def reduce_near_both(first, got, sum_out):
    ahead = first.shape[1]
    sum_out[:, :ahead, :] = first[...]
    sum_out[:, ahead:, :] = add_up(got)


def reduce_far(got, spread_out):
    low = add_up(got)
    for k in range(spread_out.shape[0]):
        spread_out[k] = low


def spread_near(lines, spread_out):
    for k in range(spread_out.shape[0]):
        spread_out[k] = lines[...]


def unpack(
    chunk_one, chunk_two, gathered,
    wup_out, wdown_out, bup_out, wq_out, wk_out, wv_out, wout_out, rel_out,
    bq_out, bk_out, bv_out, bout_out, again_out, ashift_out, bdown_out, fgain_out, fshift_out,
):
    inner = gathered.shape[0]
    width = gathered.shape[3]
    units = wup_out.shape[1]
    part = wq_out.shape[0]

    def rows(first, count, chunk, base):
        for place, offset, start, take in pieces(first, count, chunk):
            yield start, take, gathered[
                place % inner, place // inner, base + offset : base + offset + take, :
            ].astype(WIDE)

    for k in range(units // width):
        for start, take, value in rows(k * width, width, chunk_one, 0):
            wup_out[start : start + take, k * width : (k + 1) * width] = value
    for start, take, value in rows(units, units, chunk_one, 0):
        wdown_out[start : start + take, :] = value
    for k, out in enumerate((wq_out, wk_out, wv_out, wout_out)):
        for start, take, value in rows(k * part, part, chunk_two, chunk_one):
            out[start : start + take, :] = value
    first = 4 * part
    for start, take, value in rows(first, rel_out.shape[0], chunk_two, chunk_one):
        rel_out[start : start + take, :] = value.astype(LOW)
    first += rel_out.shape[0]
    small = jnp.concatenate([value for _, _, value in rows(first, 16, chunk_two, chunk_one)], axis=0)
    ups = units // width
    for k in range(ups):
        bup_out[k * width : (k + 1) * width] = small[k]
    bdown_out[...] = small[ups]
    fgain_out[...] = small[ups + 1]
    fshift_out[...] = small[ups + 2]
    bq_out[...] = small[8, :part]
    bk_out[...] = small[8, part:]
    bv_out[...] = small[9, :part]
    bout_out[...] = small[10]
    again_out[...] = small[11]
    ashift_out[...] = small[12]


def join_relative(mine, theirs, out):
    side = lax.axis_index("tensor")
    half = mine.shape[0]
    out[pl.ds(pl.multiple_of(side * half, half), half), :] = mine[...].astype(WIDE)
    out[pl.ds(pl.multiple_of((1 - side) * half, half), half), :] = theirs[...].astype(WIDE)


def with_statics(body, *statics):
    def wrapped(*refs):
        body(*statics, *refs)

    wrapped.__name__ = body.__name__
    return wrapped


def swap(array):
    return lax.ppermute(array, "tensor", [(0, 1), (1, 0)])


def exchange(array, groups=None):
    return lax.all_to_all(
        array, "dp", split_axis=0, concat_axis=0, tiled=True, axis_index_groups=groups
    )


def on_device(
    tokens, lengths, dealing, bucket_table, relative,
    w_query, b_query, w_key, b_key, w_value, b_value, w_out, b_out,
    attn_gain, attn_shift, w_up, b_up, w_down, b_down, ffn_gain, ffn_shift, cotangent,
):
    _, rows, width = tokens.shape
    total = dealing.shape[0]
    part = w_query.shape[1]
    heads = part // HEAD_DIM
    units = w_up.shape[1]
    half = rows // 2
    span = 2 * rows
    piece = max(16, half // total)
    spots = half // piece
    side = lax.axis_index("tensor")
    inner = 1 << ((total.bit_length()) // 2)
    outer = total // inner
    far_groups = [[o * inner + i for o in range(outer)] for i in range(inner)]
    near_groups = [[o * inner + i for i in range(inner)] for o in range(outer)]
    chunk_one = chunk_rows(2 * units, total, 8)
    chunk_two = chunk_rows(4 * part + half + 16, total, 8)
    chunk = chunk_one + chunk_two

    def cut(array):
        mine = lax.dynamic_slice_in_dim(array[0], side * half, half, 0)
        return mine.reshape(spots, piece, width)

    moving = jnp.concatenate([cut(cotangent), cut(tokens)], axis=1)
    if spots < total:
        moving = jnp.pad(moving, ((0, total - spots), (0, 0), (0, 0)))
    arrived = exchange(moving)
    (turned,) = call(
        with_statics(permute_body, piece), [(arrived.shape, LOW)], (dealing, arrived), smem=1
    )
    dealt_mine = exchange(turned)
    dealt_theirs = swap(dealt_mine)

    x = tokens[0]
    table = jnp.pad(bucket_table, (0, span - bucket_table.shape[0]), constant_values=-1)
    table = table.reshape(span // BLOCK, BLOCK)
    projections = (w_query.T, b_query, w_key.T, b_key, w_value.T, b_value, w_out)
    head_shape = (heads, rows, HEAD_DIM)
    q, k, v, tab, prob, ctx, attn_part = call(
        attention_forward,
        [(head_shape, LOW)] * 3
        + [((2, heads, HEAD_DIM, span), LOW), ((heads, rows, rows), LOW)]
        + [(head_shape, LOW), ((rows, width), LOW)],
        (lengths, x, relative, table) + projections,
        scratch=[pltpu.VMEM((rows, rows), WIDE)],
        smem=1,
        flops=10**10,
    )
    attn_got = swap(attn_part)
    ffn_weights = (b_out, attn_gain, attn_shift, w_up, b_up, w_down)
    normed, down_part, inverse, hidden, act, slope = call(
        with_statics(ffn_forward, True),
        [((rows, width), WIDE), ((rows, width), LOW), ((rows, 1), WIDE), ((rows, width), LOW),
         ((rows, units), LOW), ((rows, units), LOW)],
        (x, attn_part, attn_got) + ffn_weights,
        flops=4 * 10**9,
    )
    down_got = swap(down_part)
    buffer_one, hidden_part, gf, small_ffn = call(
        with_statics(ffn_backward, chunk_one, spots, piece),
        [((inner, outer, chunk_one, width), LOW), ((rows, width), LOW), ((rows, width), WIDE),
         ((8, width), WIDE)],
        (lengths, down_part, down_got, b_down, normed, attn_gain, attn_shift,
         ffn_gain, dealt_mine, dealt_theirs, hidden, act, slope, w_up, w_down),
        scratch=[
            pltpu.VMEM((rows, width), LOW),
            pltpu.VMEM((rows, units), LOW),
            pltpu.VMEM((rows, width), LOW),
        ],
        smem=1,
        flops=4 * 10**9,
    )
    hidden_got = swap(hidden_part)
    near_one = exchange(buffer_one, near_groups)
    send, keep, gp, weights, small_attn = call(
        attention_backward,
        [((rows + half, width), LOW), ((half, width), LOW), ((rows, width), WIDE),
         ((4 * part, width), LOW), ((8, width), WIDE)],
        (x, relative, table, w_query.T, w_key.T, w_value.T, w_out, hidden_part, hidden_got, gf,
         normed, inverse, attn_gain, q, k, v, tab, prob, ctx),
        scratch=[
            pltpu.VMEM((rows, width), LOW),
            pltpu.VMEM((rows, rows), LOW),
            pltpu.VMEM((heads, HEAD_DIM, span), WIDE),
            pltpu.VMEM((heads, HEAD_DIM, span), WIDE),
            pltpu.VMEM((3, heads, rows, HEAD_DIM), LOW),
            pltpu.VMEM((rows, width), WIDE),
            pltpu.VMEM((heads, rows, HEAD_DIM), LOW),
        ],
        flops=2 * 10**10,
    )
    sent = swap(send)
    buffer_two, grad_tokens = call(
        with_statics(tail_pack, chunk_two),
        [((inner, outer, chunk_two, width), LOW), ((rows, width), LOW)],
        (send, sent, keep, gp, weights, small_ffn, small_attn),
    )
    near_two = exchange(buffer_two, near_groups)
    (sum_one,) = call(reduce_near, [((outer, chunk_one, width), LOW)], (near_one,))
    (sums,) = call(reduce_near_both, [((outer, chunk, width), LOW)], (sum_one, near_two))
    (spread,) = call(reduce_far, [((outer, chunk, width), LOW)], (exchange(sums, far_groups),))
    lines = exchange(spread, far_groups)
    (wide,) = call(spread_near, [((inner, outer, chunk, width), LOW)], (lines,))
    gathered = exchange(wide, near_groups)

    dealt_mine, dealt_theirs, tab, _ = lax.optimization_barrier(
        (dealt_mine, dealt_theirs, tab, buffer_two)
    )
    x_dealt, attn_dealt = call(
        with_statics(attention_dealt, spots, piece),
        [((rows, width), LOW), ((rows, width), LOW)],
        (lengths, dealing, dealt_mine, dealt_theirs, tab) + projections,
        scratch=[pltpu.VMEM(head_shape, LOW) for _ in range(4)] + [pltpu.VMEM((rows, rows), WIDE)],
        smem=2,
        flops=10**10,
    )
    normed_dealt, down_dealt = call(
        with_statics(ffn_forward, False),
        [((rows, width), WIDE), ((rows, width), LOW)],
        (x_dealt, attn_dealt, swap(attn_dealt)) + ffn_weights,
        flops=4 * 10**9,
    )
    (y,) = call(
        finish_dealt,
        [((rows, width), LOW)],
        (down_dealt, swap(down_dealt), b_down, normed_dealt, attn_gain, attn_shift, ffn_gain,
         ffn_shift),
    )
    out = call(
        with_statics(unpack, chunk_one, chunk_two),
        [((width, units), WIDE), ((units, width), WIDE), ((units,), WIDE)]
        + [((part, width), WIDE)] * 4
        + [((half, width), LOW)]
        + [((part,), WIDE)] * 3
        + [((width,), WIDE)] * 6,
        (gathered,),
    )
    (g_up, g_down, g_bup, g_wq, g_wk, g_wv, g_wout, rel_half, g_bq, g_bk, g_bv, g_bout, g_again,
     g_ashift, g_bdown, g_fgain, g_fshift) = out
    (g_rel,) = call(join_relative, [((rows, width), WIDE)], (rel_half, swap(rel_half)))
    return (
        y[None], grad_tokens[None], g_rel, g_wq.T, g_bq, g_wk.T, g_bk, g_wv.T, g_bv, g_wout,
        g_bout, g_again, g_ashift, g_up, g_bup, g_down, g_bdown, g_fgain, g_fshift,
    )


def solution(mesh):
    return jax.shard_map(
        on_device,
        mesh=mesh,
        in_specs=(
            P("dp", None, None), P(), P(), P(), P(),
            P(None, "tensor"), P("tensor"), P(None, "tensor"), P("tensor"),
            P(None, "tensor"), P("tensor"), P("tensor", None), P(), P(), P(),
            P(None, "tensor"), P("tensor"), P("tensor", None), P(), P(), P(),
            P("dp", None, None),
        ),
        out_specs=(
            P("dp", None, None), P("dp", None, None), P(),
            P(None, "tensor"), P("tensor"), P(None, "tensor"), P("tensor"),
            P(None, "tensor"), P("tensor"), P("tensor", None), P(), P(), P(),
            P(None, "tensor"), P("tensor"), P("tensor", None), P(), P(), P(),
        ),
        check_vma=False,
    )
```

time: 207 us -> 194 us (0.937)
  blocking collectives: 51.4 us -> 16.2 us
  Pallas kernels: 51 us -> 65.6 us
  waiting for transfers between devices: 26.4 us -> 38 us
  other arithmetic: 7.88 us -> 0.79 us
  starting transfers between devices: 26.6 us -> 31.3 us
    all_to_all x2 -> x1, blocking collectives: 51.4 us -> 16.2 us  [exchange(): lax.all_to_all(array, 'dp', split_axis=0, concat_axis=0, tiled=True, axis...]
    pallas_call x9 -> x15, Pallas kernels: 51 us -> 65.6 us  [call(): pl.pallas_call(body, out_shape=[jax.ShapeDtypeStruct(shape, kind) for sha...]
    all_to_all x4 -> x6, waiting for transfers between devices: 23.5 us -> 32.7 us  [exchange(): lax.all_to_all(array, 'dp', split_axis=0, concat_axis=0, tiled=True, axis...]
    all_to_all x4 -> x6, starting transfers between devices: 25.7 us -> 30.2 us  [exchange(): lax.all_to_all(array, 'dp', split_axis=0, concat_axis=0, tiled=True, axis...]
    pallas_call x7 -> x0, other arithmetic: 4.18 us -> none  [call(): pl.pallas_call(body, out_shape=[jax.ShapeDtypeStruct(shape, kind) for sha...]
    ppermute x7 -> x8, waiting for transfers between devices: 2.86 us -> 5.29 us  [swap(): return lax.ppermute(array, 'tensor', [(0, 1), (1, 0)])]
    unnamed x112 -> x128, local copies, waits for them, and re-layouts: 36.7 us -> 38.6 us
  transfers between devices with their start and end apart: 11 -> 14, of which waited for: 4 -> 8; matrix products, arithmetic and copies ran while one was open for 7% -> 0% of each run, Pallas kernels for 22% -> 30%
where the time goes in v2:
time: 194 us; the launch traced here: 193 us
  Pallas kernels  65.6 us (34%)
  local copies, waits for them, and re-layouts  39.7 us (20%)
  waiting for transfers between devices  38 us (20%)
  starting transfers between devices  31.3 us (16%)
  blocking collectives  16.2 us (8%)
    pallas_call x15, Pallas kernels, call(): pl.pallas_call(body, out_shape=[jax.ShapeDtypeStruct(shape, kind) for sha...  65.6 us
    unnamed x128, local copies, waits for them, and re-layouts  38.6 us
    all_to_all x6, waiting for transfers between devices, exchange(): lax.all_to_all(array, 'dp', split_axis=0, concat_axis=0, tiled=True, axis...  32.7 us
    all_to_all x6, starting transfers between devices, exchange(): lax.all_to_all(array, 'dp', split_axis=0, concat_axis=0, tiled=True, axis...  30.2 us
    all_to_all x1, blocking collectives, exchange(): lax.all_to_all(array, 'dp', split_axis=0, concat_axis=0, tiled=True, axis...  16.2 us
    ppermute x8, waiting for transfers between devices, swap(): return lax.ppermute(array, 'tensor', [(0, 1), (1, 0)])  5.29 us
  transfers between devices with their start and end apart: 14, of which 8 were waited for; matrix products, arithmetic and copies ran while one was open for 0% of the time, Pallas kernels for 30%

profile of v2, /device:TPU:0, one launch (start us, length us, event | category | flops | bytes accessed | tf_op | source)
XLA Modules:
  0.0 192.8 jit_solution(8570799726612415376)
XLA Ops:
  0.7 1.0 copy-done
  1.8 1.0 constant_dynamic-slice_fusion
  2.8 0.8 pad_maximum_fusion
  3.6 8.3 %all-to-all-start = ((bf16[16,32,384]{2,1,0:T(8,128)(2,1)}), bf16[16,32,384]{2,1,0:T(8,128)(2,1)S(1)}, u32[]{:S(2)}, u32[]{:S(2)}) async-start(bf16[16,32,384]{2,1,0:T(8,128)(2,1)} %pad_maximum_fusion), calls=%async_computation | async-start | bytes 786432 | tf_op jit(solution)/shard_map/all_to_all | solution.py:514
  12.1 11.4 %shard_map.358 = (bf16[3,512,64]{2,1,0:T(8,128)(2,1)S(1)}, bf16[3,512,64]{2,1,0:T(8,128)(2,1)S(1)}, bf16[3,512,64]{2,1,0:T(8,128)(2,1)S(1)}, bf16[2,3,64,1024]{3...) custom-call(s32[16]{0:T(128)S(1)} %copy-done.28, ...), custom_call_target="tpu_custom_call" | custom-call | flops 10000000000 | bytes 4000000 | tf_op jit(solution)/shard_map/pallas_call | solution.py:47
  23.5 1.1 copy-done.50
  24.6 0.9 copy-done.52
  26.2 0.7 copy-done.57
  27.0 0.7 copy-done.59
  28.6 1.3 shard_map.357
  29.9 6.9 %all-to-all-start.1 = ((bf16[16,32,384]{2,1,0:T(8,128)(2,1)}), bf16[16,32,384]{2,1,0:T(8,128)(2,1)S(1)}, u32[]{:S(2)}, u32[]{:S(2)}) async-start(bf16[16,32,384]{2,1,0:T(8,128)(2,1)} %shard_map.357), calls=%async_computation.1 | async-start | bytes 786432 | tf_op jit(solution)/shard_map/all_to_all | solution.py:514
  36.9 4.0 %shard_map.359 = (f32[512,384]{1,0:T(8,128)S(1)}, bf16[512,384]{1,0:T(8,128)(2,1)S(1)}, f32[512,1]{1,0:T(8,128)S(1)}, bf16[512,384]{1,0:T(8,128)(2,1)S(1)}, bf16...) custom-call(bf16[512,384]{1,0:T(8,128)(2,1)S(1)} %bitcast.14, bf16[512,384]{1,0:T(8,128)(2,1)} %get-tuple-element.68.refs_1_, ...), custom_call_target="tpu_custom_call" | custom-call | flops 4000000000 | bytes 4000000 | tf_op jit(solution)/shard_map/pallas_call | solution.py:47
  41.0 0.9 copy-done.37
  41.9 0.9 copy-done.42
  42.7 0.9 copy-done.44
  43.6 0.7 copy-done.46
  45.3 4.8 %all-to-all-done.1.refs_8_.refs_2_ = bf16[16,32,384]{2,1,0:T(8,128)(2,1)S(1)} async-done(((bf16[16,32,384]{2,1,0:T(8,128)(2,1)}), bf16[16,32,384]{2,1,0:T(8,128)(2,1)S(1)}, u32[]{:S(2)}, u32[]{:S(2)}) %all-to-all-start.1) | async-done | bytes 393248 | tf_op jit(solution)/shard_map/all_to_all | solution.py:514
  50.1 1.7 collective-permute-done.refs_9_.refs_3_
  51.8 1.3 copy-done.38
  53.1 1.1 copy-done.43
  54.2 1.1 copy-done.45
  55.3 1.0 copy-done.47
  56.3 4.8 %shard_map.360 = (bf16[4,4,96,384]{3,2,1,0:T(8,128)(2,1)}, bf16[512,384]{1,0:T(8,128)(2,1)}, f32[512,384]{1,0:T(8,128)S(1)}, f32[8,384]{1,0:T(8,128)S(1)}) custom-call(s32[16]{0:T(128)S(1)} %copy-done.28, bf16[512,384]{1,0:T(8,128)(2,1)S(1)} %get-tuple-element.69.refs_1_, bf16[512,384]{1,0:T(8,128)(2,1)} %collective-permute-done.2.refs_2_, ...), custom_call_target="tpu_custom_call" | custom-call | flops 4000000000 | bytes 4000000 | tf_op jit(solution)/shard_map/pallas_call | solution.py:47
  61.1 0.9 copy-done.40
  62.2 3.7 %all-to-all-start.2 = ((bf16[4,4,96,384]{3,2,1,0:T(8,128)(2,1)}), bf16[4,4,96,384]{3,2,1,0:T(8,128)(2,1)S(1)}, u32[]{:S(2)}, u32[]{:S(2)}) async-start(bf16[4,4,96,384]{3,2,1,0:T(8,128)(2,1)} %get-tuple-element.97), calls=%async_computation.2 | async-start | bytes 2359296 | tf_op jit(solution)/shard_map/all_to_all | solution.py:514
  65.9 0.9 copy-done.10
  66.8 0.9 copy-done.13
  67.7 0.9 copy-done.16
  68.7 0.9 copy-done.19
  69.6 1.1 copy-done.39
  70.7 1.1 copy-done.41
  71.8 0.9 copy-done.49
  72.8 1.4 copy-done.51
  74.2 1.1 copy-done.53
  75.3 1.0 copy-done.56
  76.3 1.0 copy-done.58
  77.3 1.0 copy-done.60
  78.3 1.0 copy-done.62
  79.3 25.5 %shard_map.361 = (bf16[768,384]{1,0:T(8,128)(2,1)S(1)}, bf16[256,384]{1,0:T(8,128)(2,1)S(1)}, f32[512,384]{1,0:T(8,128)S(1)}, bf16[768,384]{1,0:T(8,128)(2,1)S(1)}, f32[8,384]{1,0:T(8,128)S(1)}) custom-call(bf16[512,384]{1,0:T(8,128)(2,1)S(1)} %bitcast.15, bf16[512,384]{1,0:T(8,128)(2,1)S(1)} %copy-done.6, s32[8,128]{1,0:T(8,128)S(1)} %pad_bitcast_fusion.table, ...), custom_call_target="tpu_custom_call" | custom-call | flops 20000000000 | bytes 4000000 | tf_op jit(solution)/shard_map/pallas_call | solution.py:47
  105.2 1.6 collective-permute-done.4.refs_1_
  106.8 1.2 shard_map.362
  108.0 4.0 %all-to-all-start.3 = ((bf16[4,4,72,384]{3,2,1,0:T(8,128)(2,1)}), bf16[4,4,72,384]{3,2,1,0:T(8,128)(2,1)S(1)}, u32[]{:S(2)}, u32[]{:S(2)}) async-start(bf16[4,4,72,384]{3,2,1,0:T(8,128)(2,1)} %get-tuple-element.88), calls=%async_computation.3 | async-start | bytes 1769472 | tf_op jit(solution)/shard_map/all_to_all | solution.py:514
  112.9 11.3 %all-to-all-done.3.got = bf16[4,4,72,384]{3,2,1,0:T(8,128)(2,1)S(1)} async-done(((bf16[4,4,72,384]{3,2,1,0:T(8,128)(2,1)}), bf16[4,4,72,384]{3,2,1,0:T(8,128)(2,1)S(1)}, u32[]{:S(2)}, u32[]{:S(2)}) %all-to-all-start.3) | async-done | bytes 884768 | tf_op jit(solution)/shard_map/all_to_all | solution.py:514
  124.2 1.0 copy-done.36
  125.3 16.2 %all_to_all.35.got = bf16[4,168,384]{2,1,0:T(8,128)(2,1)S(1)} all-to-all(bf16[4,168,384]{2,1,0:T(8,128)(2,1)S(1)} %shard_map.367), channel_id=1, replica_groups={{0,8,16,24},{2,10,18,26},{4,12,20,28},{6,14,22,30},{1,9,17,25},{3,11,19..., dimensions={0} | all-to-all | bytes 1032192 | tf_op jit(solution)/shard_map/all_to_all | solution.py:514
  141.5 0.9 shard_map.368
  142.4 3.5 %all-to-all-start.5 = ((bf16[4,168,384]{2,1,0:T(8,128)(2,1)}), bf16[4,168,384]{2,1,0:T(8,128)(2,1)S(1)}, u32[]{:S(2)}, u32[]{:S(2)}) async-start(bf16[4,168,384]{2,1,0:T(8,128)(2,1)} %shard_map.368), calls=%async_computation.5 | async-start | bytes 1032192 | tf_op jit(solution)/shard_map/all_to_all | solution.py:514
  145.9 13.4 %all-to-all-done.5.lines = bf16[4,168,384]{2,1,0:T(8,128)(2,1)S(1)} async-done(((bf16[4,168,384]{2,1,0:T(8,128)(2,1)}), bf16[4,168,384]{2,1,0:T(8,128)(2,1)S(1)}, u32[]{:S(2)}, u32[]{:S(2)}) %all-to-all-start.5) | async-done | bytes 516128 | tf_op jit(solution)/shard_map/all_to_all | solution.py:514
  159.4 1.3 copy-done.1
  160.7 3.8 %all-to-all-start.6 = ((bf16[4,4,168,384]{3,2,1,0:T(8,128)(2,1)}), bf16[4,4,168,384]{3,2,1,0:T(8,128)(2,1)S(1)}, u32[]{:S(2)}, u32[]{:S(2)}) async-start(bf16[4,4,168,384]{3,2,1,0:T(8,128)(2,1)} %copy-done.1), calls=%async_computation.6 | async-start | bytes 4128768 | tf_op jit(solution)/shard_map/all_to_all | solution.py:514
  164.5 1.0 copy-done.8
  165.5 0.9 copy-done.11
  166.4 0.9 copy-done.14
  167.4 0.9 copy-done.17
  168.3 0.9 copy-done.20
  169.2 1.1 copy-done.54
  170.3 9.4 %shard_map.363 = (bf16[512,384]{1,0:T(8,128)(2,1)S(1)}, bf16[512,384]{1,0:T(8,128)(2,1)S(1)}) custom-call(s32[16]{0:T(128)S(1)} %copy-done.28, s32[16]{0:T(128)S(1)} %copy-done.29, bf16[16,32,384]{2,1,0:T(8,128)(2,1)S(1)} %all-to-all-done.1.refs_8_.refs_2_, bf16[16,32,384]{2,1,0:T(8,128)(2,1)S(1)} %copy-done.8, bf16[2,3,64,1024]{3,2,1,0:T(8,128)(2,1)S(1)} %copy-done.54, ...), custom_call_target="tpu_custom_call" | custom-call | flops 10000000000 | bytes 4000000 | tf_op jit(solution)/shard_map/pallas_call | solution.py:47
  179.8 1.7 collective-permute-done.5.refs_2_
  181.5 2.7 %shard_map.364 = (f32[512,384]{1,0:T(8,128)S(1)}, bf16[512,384]{1,0:T(8,128)(2,1)S(1)}) custom-call(bf16[512,384]{1,0:T(8,128)(2,1)S(1)} %get-tuple-element.92.refs_0_, bf16[512,384]{1,0:T(8,128)(2,1)S(1)} %get-tuple-element.93.refs_1_, bf16[512,384]{1,0:T(8,128)(2,1)S(1)} %collective-permute-done.5.refs_2_, bf16[384]{0:T(512)(128)(2,1)S(1)} %copy-done.22, ...), custom_call_target="tpu_custom_call" | custom-call | flops 4000000000 | bytes 4000000 | tf_op jit(solution)/shard_map/pallas_call | solution.py:47
  184.2 0.9 copy-done.33
  185.2 3.2 %all-to-all-done.6.refs_0_ = bf16[4,4,168,384]{3,2,1,0:T(8,128)(2,1)S(1)} async-done(((bf16[4,4,168,384]{3,2,1,0:T(8,128)(2,1)}), bf16[4,4,168,384]{3,2,1,0:T(8,128)(2,1)S(1)}, u32[]{:S(2)}, u32[]{:S(2)}) %all-to-all-start.6) | async-done | bytes 2064416 | tf_op jit(solution)/shard_map/all_to_all | solution.py:514
  188.4 2.0 %shard_map.370 = (f32[384,768]{1,0:T(8,128)}, f32[768,384]{1,0:T(8,128)}, f32[768]{0:T(1024)}, f32[192,384]{1,0:T(8,128)}, f32[192,384]{1,0:T(8,128)}, /*index=5...) custom-call(bf16[4,4,168,384]{3,2,1,0:T(8,128)(2,1)S(1)} %all-to-all, ...), custom_call_target="tpu_custom_call" | custom-call | flops 1000000000 | bytes 4000000 | tf_op jit(solution)/shard_map/pallas_call | solution.py:47
  190.5 1.2 shard_map.365
  191.9 0.9 shard_map.371
  (112 shorter events, 4.9 us)
Async XLA Ops:
  0.7 1.0 copy-start
  1.7 10.3 %copy-start.63 = (s32[1023]{0:T(1024)S(1)}, s32[1023]{0:T(1024)}, u32[]{:S(2)}) copy-start(s32[1023]{0:T(1024)} %param.25) | copy-start | bytes 12280
  1.7 10.3 %copy-start.2 = (bf16[1,512,384]{2,1,0:T(8,128)(2,1)S(1)}, bf16[1,512,384]{2,1,0:T(8,128)(2,1)}, u32[]{:S(2)}) copy-start(bf16[1,512,384]{2,1,0:T(8,128)(2,1)} %param.22) | copy-start | bytes 1179652
  1.7 10.3 %copy-start.6 = (bf16[512,384]{1,0:T(8,128)(2,1)S(1)}, bf16[512,384]{1,0:T(8,128)(2,1)}, u32[]{:S(2)}) copy-start(bf16[512,384]{1,0:T(8,128)(2,1)} %relative.3) | copy-start | bytes 1179652
  1.7 10.3 %copy-start.9 = (bf16[384,192]{0,1:T(8,128)(2,1)S(1)}, bf16[384,192]{0,1:T(8,128)(2,1)}, u32[]{:S(2)}) copy-start(bf16[384,192]{0,1:T(8,128)(2,1)} %param.27) | copy-start | bytes 442372
  1.7 10.3 %copy-start.12 = (bf16[384,192]{0,1:T(8,128)(2,1)S(1)}, bf16[384,192]{0,1:T(8,128)(2,1)}, u32[]{:S(2)}) copy-start(bf16[384,192]{0,1:T(8,128)(2,1)} %param.29) | copy-start | bytes 442372
  1.7 10.3 %copy-start.15 = (bf16[384,192]{0,1:T(8,128)(2,1)S(1)}, bf16[384,192]{0,1:T(8,128)(2,1)}, u32[]{:S(2)}) copy-start(bf16[384,192]{0,1:T(8,128)(2,1)} %param.31) | copy-start | bytes 442372
  1.7 10.3 %copy-start.18 = (bf16[192,384]{1,0:T(8,128)(2,1)S(1)}, bf16[192,384]{1,0:T(8,128)(2,1)}, u32[]{:S(2)}) copy-start(bf16[192,384]{1,0:T(8,128)(2,1)} %refs_11_.1) | copy-start | bytes 442372
  1.7 10.3 %copy-start.28 = (s32[16]{0:T(128)S(1)}, s32[16]{0:T(128)}, u32[]{:S(2)}) copy-start(s32[16]{0:T(128)} %refs_0_.5) | copy-start | bytes 196
  1.7 10.3 %copy-start.30 = (bf16[192]{0:T(256)(128)(2,1)S(1)}, bf16[192]{0:T(256)(128)(2,1)}, u32[]{:S(2)}) copy-start(bf16[192]{0:T(256)(128)(2,1)} %refs_6_.6) | copy-start | bytes 1156
  1.7 10.3 %copy-start.31 = (bf16[192]{0:T(256)(128)(2,1)S(1)}, bf16[192]{0:T(256)(128)(2,1)}, u32[]{:S(2)}) copy-start(bf16[192]{0:T(256)(128)(2,1)} %refs_8_.4) | copy-start | bytes 1156
  1.7 10.3 %copy-start.32 = (bf16[192]{0:T(256)(128)(2,1)S(1)}, bf16[192]{0:T(256)(128)(2,1)}, u32[]{:S(2)}) copy-start(bf16[192]{0:T(256)(128)(2,1)} %refs_10_.1) | copy-start | bytes 1156
  3.6 25.0 %all-to-all-start = ((bf16[16,32,384]{2,1,0:T(8,128)(2,1)}), bf16[16,32,384]{2,1,0:T(8,128)(2,1)S(1)}, u32[]{:S(2)}, u32[]{:S(2)}) async-start(bf16[16,32,384]{2,1,0:T(8,128)(2,1)} %pad_maximum_fusion), calls=%async_computation | async-start | bytes 786432 | tf_op jit(solution)/shard_map/all_to_all | solution.py:514
  12.1 16.5 %copy-start.29 = (s32[16]{0:T(128)S(1)}, s32[16]{0:T(128)}, u32[]{:S(2)}) copy-start(s32[16]{0:T(128)} %refs_1_.1) | copy-start | bytes 196
  23.5 1.1 copy-start.50
  28.5 8.4 %copy-start.3 = (bf16[384,768]{1,0:T(8,128)(2,1)S(1)}, bf16[384,768]{1,0:T(8,128)(2,1)}, u32[]{:S(2)}) copy-start(bf16[384,768]{1,0:T(8,128)(2,1)} %refs_6_.7) | copy-start | bytes 1769476
  28.5 8.4 %copy-start.4 = (bf16[768,384]{1,0:T(8,128)(2,1)S(1)}, bf16[768,384]{1,0:T(8,128)(2,1)}, u32[]{:S(2)}) copy-start(bf16[768,384]{1,0:T(8,128)(2,1)} %refs_8_.5) | copy-start | bytes 1769476
  28.5 8.4 %copy-start.21 = (bf16[768]{0:T(1024)(128)(2,1)S(1)}, bf16[768]{0:T(1024)(128)(2,1)}, u32[]{:S(2)}) copy-start(bf16[768]{0:T(1024)(128)(2,1)} %refs_7_.5) | copy-start | bytes 4612
  28.5 8.4 %copy-start.22 = (bf16[384]{0:T(512)(128)(2,1)S(1)}, bf16[384]{0:T(512)(128)(2,1)}, u32[]{:S(2)}) copy-start(bf16[384]{0:T(512)(128)(2,1)} %refs_3_.5) | copy-start | bytes 2308
  28.5 8.4 %copy-start.23 = (bf16[384]{0:T(512)(128)(2,1)S(1)}, bf16[384]{0:T(512)(128)(2,1)}, u32[]{:S(2)}) copy-start(bf16[384]{0:T(512)(128)(2,1)} %gain.3) | copy-start | bytes 2308
  28.5 8.4 %copy-start.24 = (bf16[384]{0:T(512)(128)(2,1)S(1)}, bf16[384]{0:T(512)(128)(2,1)}, u32[]{:S(2)}) copy-start(bf16[384]{0:T(512)(128)(2,1)} %shift.1) | copy-start | bytes 2308
  28.5 8.4 %collective-permute-start.1 = (bf16[512,384]{1,0:T(8,128)(2,1)}, bf16[512,384]{1,0:T(8,128)(2,1)}, u32[]{:S(2)}, u32[]{:S(2)}) collective-permute-start(bf16[512,384]{1,0:T(8,128)(2,1)} %get-tuple-element.68.refs_1_), channel_id=1, source_target_pairs={{0,1},{1,0},{2,3},{3,2},{4,5},{5,4},{6,7},{7,6},{8,9},{9,8},{10,11... | collective-permute-start | bytes 1179656 | tf_op jit(solution)/shard_map/ppermute | solution.py:510
  29.9 20.1 %all-to-all-start.1 = ((bf16[16,32,384]{2,1,0:T(8,128)(2,1)}), bf16[16,32,384]{2,1,0:T(8,128)(2,1)S(1)}, u32[]{:S(2)}, u32[]{:S(2)}) async-start(bf16[16,32,384]{2,1,0:T(8,128)(2,1)} %shard_map.357), calls=%async_computation.1 | async-start | bytes 786432 | tf_op jit(solution)/shard_map/all_to_all | solution.py:514
  36.8 14.9 %copy-start.25 = (bf16[384]{0:T(512)(128)(2,1)S(1)}, bf16[384]{0:T(512)(128)(2,1)}, u32[]{:S(2)}) copy-start(bf16[384]{0:T(512)(128)(2,1)} %bdown.1) | copy-start | bytes 2308
  36.9 14.9 %copy-start.26 = (bf16[384]{0:T(512)(128)(2,1)S(1)}, bf16[384]{0:T(512)(128)(2,1)}, u32[]{:S(2)}) copy-start(bf16[384]{0:T(512)(128)(2,1)} %fgain.1) | copy-start | bytes 2308
  45.1 5.0 %collective-permute-start.2 = (bf16[512,384]{1,0:T(8,128)(2,1)S(1)}, bf16[512,384]{1,0:T(8,128)(2,1)}, u32[]{:S(2)}, u32[]{:S(2)}) collective-permute-start(bf16[512,384]{1,0:T(8,128)(2,1)S(1)} %get-tuple-element.69.refs_1_), channel_id=1, source_target_pairs={{0,1},{1,0},{2,3},{3,2},{4,5},{5,4},{6,7},{7,6},{8,9},{9,8},{10,11... | collective-permute-start | bytes 1179656 | tf_op jit(solution)/shard_map/ppermute | solution.py:510
  50.1 1.7 collective-permute-start
  51.8 9.4 %copy-start.7 = (bf16[16,32,384]{2,1,0:T(8,128)(2,1)}, bf16[16,32,384]{2,1,0:T(8,128)(2,1)S(1)}, u32[]{:S(2)}) copy-start(bf16[16,32,384]{2,1,0:T(8,128)(2,1)S(1)} %collective-permute-done.refs_9_.refs_3_) | copy-start | bytes 1179652
  51.8 1.3 copy-start.38
  53.1 1.1 copy-start.43
  54.2 1.1 copy-start.45
  55.3 1.0 copy-start.47
  62.0 3.9 %collective-permute-start.3 = (bf16[512,384]{1,0:T(8,128)(2,1)}, bf16[512,384]{1,0:T(8,128)(2,1)}, u32[]{:S(2)}, u32[]{:S(2)}) collective-permute-start(bf16[512,384]{1,0:T(8,128)(2,1)} %get-tuple-element.74.mine), channel_id=1, source_target_pairs={{0,1},{1,0},{2,3},{3,2},{4,5},{5,4},{6,7},{7,6},{8,9},{9,8},{10,11... | collective-permute-start | bytes 1179656 | tf_op jit(solution)/shard_map/ppermute | solution.py:510
  62.2 45.8 %all-to-all-start.2 = ((bf16[4,4,96,384]{3,2,1,0:T(8,128)(2,1)}), bf16[4,4,96,384]{3,2,1,0:T(8,128)(2,1)S(1)}, u32[]{:S(2)}, u32[]{:S(2)}) async-start(bf16[4,4,96,384]{3,2,1,0:T(8,128)(2,1)} %get-tuple-element.97), calls=%async_computation.2 | async-start | bytes 2359296 | tf_op jit(solution)/shard_map/all_to_all | solution.py:514
  65.9 0.9 copy-start.10
  66.8 0.9 copy-start.13
  67.7 0.9 copy-start.16
  68.6 0.9 copy-start.19
  69.6 1.1 copy-start.39
  70.7 1.1 copy-start.41
  71.8 0.9 copy-start.49
  72.8 1.4 copy-start.51
  74.2 1.1 copy-start.53
  75.3 1.0 copy-start.56
  76.3 1.0 copy-start.58
  77.3 1.0 copy-start.60
  78.3 1.0 copy-start.62
  104.8 2.1 %collective-permute-start.4 = (bf16[768,384]{1,0:T(8,128)(2,1)S(1)}, bf16[768,384]{1,0:T(8,128)(2,1)S(1)}, u32[]{:S(2)}, u32[]{:S(2)}) collective-permute-start(bf16[768,384]{1,0:T(8,128)(2,1)S(1)} %get-tuple-element.82.refs_0_), channel_id=1, source_target_pairs={{0,1},{1,0},{2,3},{3,2},{4,5},{5,4},{6,7},{7,6},{8,9},{9,8},{10,11... | collective-permute-start | bytes 1769480 | tf_op jit(solution)/shard_map/ppermute | solution.py:510
  108.0 16.2 %all-to-all-start.3 = ((bf16[4,4,72,384]{3,2,1,0:T(8,128)(2,1)}), bf16[4,4,72,384]{3,2,1,0:T(8,128)(2,1)S(1)}, u32[]{:S(2)}, u32[]{:S(2)}) async-start(bf16[4,4,72,384]{3,2,1,0:T(8,128)(2,1)} %get-tuple-element.88), calls=%async_computation.3 | async-start | bytes 1769472 | tf_op jit(solution)/shard_map/all_to_all | solution.py:514
  124.2 1.0 copy-start.36
  142.4 16.8 %all-to-all-start.5 = ((bf16[4,168,384]{2,1,0:T(8,128)(2,1)}), bf16[4,168,384]{2,1,0:T(8,128)(2,1)S(1)}, u32[]{:S(2)}, u32[]{:S(2)}) async-start(bf16[4,168,384]{2,1,0:T(8,128)(2,1)} %shard_map.368), calls=%async_computation.5 | async-start | bytes 1032192 | tf_op jit(solution)/shard_map/all_to_all | solution.py:514
  159.4 1.3 copy-start.1
  160.7 27.7 %all-to-all-start.6 = ((bf16[4,4,168,384]{3,2,1,0:T(8,128)(2,1)}), bf16[4,4,168,384]{3,2,1,0:T(8,128)(2,1)S(1)}, u32[]{:S(2)}, u32[]{:S(2)}) async-start(bf16[4,4,168,384]{3,2,1,0:T(8,128)(2,1)} %copy-done.1), calls=%async_computation.6 | async-start | bytes 4128768 | tf_op jit(solution)/shard_map/all_to_all | solution.py:514
  164.5 1.0 copy-start.8
  165.5 0.9 copy-start.11
  166.4 0.9 copy-start.14
  167.4 0.9 copy-start.17
  169.2 1.1 copy-start.54
  170.3 11.2 %copy-start.5 = (bf16[768,384]{1,0:T(8,128)(2,1)S(1)}, bf16[768,384]{1,0:T(8,128)(2,1)}, u32[]{:S(2)}) copy-start(bf16[768,384]{1,0:T(8,128)(2,1)} %refs_8_.5) | copy-start | bytes 1769476
  179.7 1.8 collective-permute-start.5
  185.0 5.4 %copy-start.27 = (bf16[384]{0:T(512)(128)(2,1)S(1)}, bf16[384]{0:T(512)(128)(2,1)}, u32[]{:S(2)}) copy-start(bf16[384]{0:T(512)(128)(2,1)} %fshift.1) | copy-start | bytes 2308
  185.0 5.4 %collective-permute-start.6 = (bf16[512,384]{1,0:T(8,128)(2,1)S(1)}, bf16[512,384]{1,0:T(8,128)(2,1)S(1)}, u32[]{:S(2)}, u32[]{:S(2)}) collective-permute-start(bf16[512,384]{1,0:T(8,128)(2,1)S(1)} %get-tuple-element.94.mine), channel_id=1, source_target_pairs={{0,1},{1,0},{2,3},{3,2},{4,5},{5,4},{6,7},{7,6},{8,9},{9,8},{10,11... | collective-permute-start | bytes 1179656 | tf_op jit(solution)/shard_map/ppermute | solution.py:510
  188.4 2.1 %copy-start.34 = (f32[512,384]{1,0:T(8,128)S(1)}, f32[512,384]{1,0:T(8,128)}, u32[]{:S(2)}) copy-start(f32[512,384]{1,0:T(8,128)} %copy-done.33) | copy-start | bytes 2359300
  190.4 1.5 collective-permute-start.7
  (14 other events, 11.4 us)

commit v3 on v2

v3 whole, which is shorter than its diff:
```python
import math

import jax
import jax.numpy as jnp
from jax import lax
from jax.experimental import pallas as pl
from jax.experimental.pallas import tpu as pltpu
from jax.sharding import PartitionSpec as P

HEAD_DIM = 64
EPSILON = 1e-07
ROOT_HALF = 0.7071067811865476
INV_ROOT_TAU = 0.3989422804014327
BLOCK = 128
LOW = jnp.bfloat16
WIDE = jnp.float32

NN = (((1,), (0,)), ((), ()))
NT = (((1,), (1,)), ((), ()))
TN = (((0,), (0,)), ((), ()))
TT = (((0,), (1,)), ((), ()))


def mm(left, right, dims=NN):
    return lax.dot_general(left, right, dims, preferred_element_type=WIDE)


def pieces(first, count, chunk):
    out = []
    done = 0
    while done < count:
        place, offset = divmod(first + done, chunk)
        take = min(chunk - offset, count - done)
        out.append((place, offset, done, take))
        done += take
    return out


def chunk_rows(rows, parts, unit):
    return -(-(-(-rows // parts)) // unit) * unit


class Part:
    def __init__(self, array, axis, start, count):
        self.array, self.axis, self.start, self.count = array, axis, start, count


class Stack:
    def __init__(self, arrays):
        self.arrays = tuple(arrays)


class Here:
    def __init__(self, *what):
        self.what = what


class Pieces:
    def __init__(self, count, shape, kind):
        self.count, self.shape, self.kind = count, shape, kind


class Fetched:
    def __init__(self, buffer, copies):
        self.buffer, self.copies = buffer, copies
        self.shape, self.dtype = buffer.shape, buffer.dtype
        for copy in copies:
            copy.start()

    def ready(self):
        for copy in self.copies:
            copy.wait()
        self.copies = ()

    def __getitem__(self, index):
        self.ready()
        return self.buffer[index]


class Shipped:
    def __init__(self, buffer, copies):
        self.buffer, self.copies, self.sent = buffer, copies, False
        self.shape, self.dtype = buffer.shape, buffer.dtype

    def send(self):
        if not self.sent:
            for copy in self.copies:
                copy.start()
        self.sent = True

    def wait(self):
        for copy in self.copies:
            copy.wait()

    def __getitem__(self, index):
        return self.buffer[index]

    def __setitem__(self, index, value):
        self.buffer[index] = value


def ready(*refs):
    for ref in refs:
        ref.ready()


def send(*refs):
    for ref in refs:
        ref.send()


def position(inner):
    index = lax.axis_index("dp")
    return index % inner


def call(body, outs, args, scratch=(), smem=0, flops=1):
    arrays, buffers, copies_in, here_in, here_out, loose = [], [], 0, set(), set(), set()
    for arg in args[smem:]:
        if isinstance(arg, Part):
            shape = list(arg.array.shape)
            shape[arg.axis] = arg.count
            arrays.append(arg.array)
            buffers.append(pltpu.VMEM(tuple(shape), arg.array.dtype))
            copies_in += 1
        elif isinstance(arg, Here):
            arrays.append(arg.what[0])
            here_in.add(len(arrays) - 1)
        elif isinstance(arg, Stack):
            first = arg.arrays[0]
            here_in.update(range(len(arrays), len(arrays) + len(arg.arrays)))
            loose.update(range(len(arrays), len(arrays) + len(arg.arrays)))
            arrays.extend(arg.arrays)
            buffers.append(pltpu.VMEM((len(arg.arrays),) + first.shape, first.dtype))
            copies_in += len(arg.arrays)
        else:
            arrays.append(arg)
            buffers.append(pltpu.VMEM(arg.shape, arg.dtype))
            copies_in += 1
    results, out_buffers, copies_out = [], [], 0
    for out in outs:
        if isinstance(out, Pieces):
            results += [pltpu.HBM(out.shape, out.kind)] * out.count
            out_buffers.append(pltpu.VMEM((out.count,) + out.shape, out.kind))
            copies_out += out.count
        elif isinstance(out, Here):
            here_out.add(len(results))
            results.append(jax.ShapeDtypeStruct(*out.what))
        else:
            results.append(pltpu.HBM(*out))
            out_buffers.append(pltpu.VMEM(*out))
            copies_out += 1

    def kernel(*refs):
        refs = list(refs)
        scalars = [refs.pop(0) for _ in range(smem)]
        sources = [refs.pop(0) for _ in arrays]
        targets = [refs.pop(0) for _ in results]
        in_sems, out_sems = refs.pop(0), refs.pop(0)
        fetched, shipped = [], []
        count = 0
        for arg in args[smem:]:
            if isinstance(arg, Here):
                fetched.append(Fetched(sources.pop(0), ()))
                continue
            buffer = refs.pop(0)
            if isinstance(arg, Stack):
                copies = []
                near = position(len(arg.arrays))
                for k in range(len(arg.arrays)):
                    copies.append(
                        pltpu.make_async_copy(
                            sources.pop(0), buffer.at[k ^ near], in_sems.at[count]
                        )
                    )
                    count += 1
            else:
                source = sources.pop(0)
                if isinstance(arg, Part):
                    window = (slice(None),) * arg.axis + (pl.ds(arg.start, arg.count),)
                    source = source.at[window]
                copies = [pltpu.make_async_copy(source, buffer, in_sems.at[count])]
                count += 1
            fetched.append(Fetched(buffer, copies))
        count = 0
        for out in outs:
            if isinstance(out, Here):
                shipped.append(Shipped(targets.pop(0), ()))
                continue
            buffer = refs.pop(0)
            if isinstance(out, Pieces):
                ends = [(buffer.at[k], targets.pop(0)) for k in range(out.count)]
            else:
                ends = [(buffer, targets.pop(0))]
            copies = []
            for source, target in ends:
                copies.append(pltpu.make_async_copy(source, target, out_sems.at[count]))
                count += 1
            shipped.append(Shipped(buffer, copies))
        body(*scalars, *fetched, *shipped, *refs)
        ready(*fetched)
        send(*shipped)
        for ship in shipped:
            ship.wait()

    kernel.__name__ = body.__name__
    space = pltpu.MemorySpace.HBM
    got = pl.pallas_call(
        kernel,
        out_shape=results,
        in_specs=[pl.BlockSpec(memory_space=pltpu.SMEM) for _ in range(smem)]
        + [
            pl.BlockSpec(memory_space=pltpu.VMEM if i in here_in - loose else pl.ANY if i in loose else space)
            for i in range(len(arrays))
        ],
        out_specs=[
            pl.BlockSpec(memory_space=pltpu.VMEM if i in here_out else space)
            for i in range(len(results))
        ],
        scratch_shapes=[
            pltpu.SemaphoreType.DMA((max(copies_in, 1),)),
            pltpu.SemaphoreType.DMA((max(copies_out, 1),)),
        ]
        + buffers
        + out_buffers
        + list(scratch),
        compiler_params=pltpu.CompilerParams(vmem_limit_bytes=40 * 1024 * 1024),
        cost_estimate=pl.CostEstimate(flops=flops, bytes_accessed=1, transcendentals=0),
    )(
        *args[:smem],
        *(
            array if i in here_in else pltpu.with_memory_space_constraint(array, space)
            for i, array in enumerate(arrays)
        ),
    )
    final = []
    for out in outs:
        if isinstance(out, Pieces):
            final.append(list(got[: out.count]))
            got = got[out.count :]
        else:
            final.append(got[0])
            got = got[1:]
    return final


def call_here(body, outs, args, smem=0):
    return pl.pallas_call(
        body,
        out_shape=[jax.ShapeDtypeStruct(shape, kind) for shape, kind in outs],
        in_specs=[
            pl.BlockSpec(memory_space=pltpu.SMEM if i < smem else pltpu.VMEM) for i in range(len(args))
        ],
        out_specs=[pl.BlockSpec(memory_space=pltpu.VMEM) for _ in outs],
    )(*args)


def permute_body(piece, dealing, source, target):
    for k in range(source.shape[0]):
        there = dealing[k]
        target[there, :piece, :] = source[k, :piece, :]
        target[k, piece:, :] = source[there, piece:, :]


def assemble(mine, theirs, spots, first, piece, target):
    side = lax.axis_index("tensor")
    half = spots * piece
    for source, base in ((mine, side * half), (theirs, (1 - side) * half)):
        for p in range(spots):
            target[pl.ds(pl.multiple_of(base + p * piece, piece), piece), :] = source[
                p, first : first + piece, :
            ]


def project(x, weights, biases, outs):
    for weight, bias, out in zip(weights, biases, outs):
        full = (mm(x, weight[...], NT) + bias[...].astype(WIDE)[None, :]).astype(LOW)
        for h in range(out.shape[0]):
            out[h] = full[:, h * HEAD_DIM : (h + 1) * HEAD_DIM]


def anti_diagonal():
    return jnp.where(
        lax.broadcasted_iota(jnp.int32, (BLOCK, BLOCK), 0)
        + lax.broadcasted_iota(jnp.int32, (BLOCK, BLOCK), 1)
        == BLOCK - 1,
        1.0,
        0.0,
    ).astype(LOW)


def one_hot(table, buckets):
    anti = anti_diagonal()
    entries = table[...]
    high = entries // 256
    turned = mm(high.astype(WIDE).astype(LOW), anti) * 256.0 + mm(
        (entries - high * 256).astype(WIDE).astype(LOW), anti
    )
    turned = turned.astype(jnp.int32)
    count = table.shape[0]
    rows = lax.broadcasted_iota(jnp.int32, (buckets, BLOCK), 0)
    return jnp.concatenate(
        [
            jnp.where(rows == turned[count - 1 - b : count - b, :], 1.0, 0.0).astype(LOW)
            for b in range(count)
        ],
        axis=1,
    )


def attend(length, q, k, v, tab, wout, ctx, attn_out, far_scratch, prob_out):
    heads, rows, _ = q.shape
    window = rows + BLOCK
    scale = 1.0 / math.sqrt(3.0 * HEAD_DIM)
    key_ok = lax.broadcasted_iota(jnp.int32, (1, rows), 1) < length

    def head(h, carry):
        keys = k[h]
        values = v[h]
        for b in range(rows // BLOCK):
            j0 = b * BLOCK
            w0 = rows - BLOCK - j0
            far = mm(k[h, j0 : j0 + BLOCK, :], tab[0, h, :, w0 : w0 + window])
            far = pltpu.roll(far, window - BLOCK, 1, stride=1, stride_axis=0)[:, :rows]
            far_scratch[:, j0 : j0 + BLOCK] = far.T
        for a in range(rows // BLOCK):
            i0 = a * BLOCK
            w0 = rows - BLOCK - i0
            block_q = q[h, i0 : i0 + BLOCK, :]
            near = mm(block_q, tab[1, h, :, w0 : w0 + window])
            near = pltpu.roll(near, window - BLOCK, 1, stride=1, stride_axis=0)[:, :rows]
            score = (mm(block_q, keys, NT) + near + far_scratch[i0 : i0 + BLOCK, :]) * scale
            score = jnp.where(key_ok, score, -1e30)
            top = jnp.max(score, axis=1, keepdims=True)
            weights = jnp.exp(score - top)
            row_ok = i0 + lax.broadcasted_iota(jnp.int32, (BLOCK, 1), 0) < length
            norm = jnp.where(row_ok, 1.0 / jnp.sum(weights, axis=1, keepdims=True), 0.0)
            prob = (weights * norm).astype(LOW)
            if prob_out is not None:
                prob_out[h, i0 : i0 + BLOCK, :] = prob
            ctx[h, i0 : i0 + BLOCK, :] = mm(prob, values).astype(LOW)
        return carry

    lax.fori_loop(0, heads, head, 0)
    total = mm(ctx[0], wout[0:HEAD_DIM, :])
    for h in range(1, heads):
        total += mm(ctx[h], wout[h * HEAD_DIM : (h + 1) * HEAD_DIM, :])
    attn_out[...] = total.astype(LOW)


def attention_forward(
    lengths, x, relative, table, wq, bq, wk, bk, wv, bv, wout,
    q_out, k_out, v_out, tab_out, prob_out, ctx_out, attn_out, far_scratch,
):
    length = lengths[lax.axis_index("dp")]
    project(x[...], (wq, wk, wv), (bq, bk, bv), (q_out, k_out, v_out))
    send(q_out, k_out, v_out)
    rel = relative[...]
    hot = one_hot(table, relative.shape[0])
    for slot, (weight, bias) in enumerate(((wq, bq), (wk, bk))):
        low = (mm(rel, weight[...], NT) + bias[...].astype(WIDE)[None, :]).astype(LOW)
        spread = mm(low, hot, TN).astype(LOW)
        for h in range(q_out.shape[0]):
            tab_out[slot, h] = spread[h * HEAD_DIM : (h + 1) * HEAD_DIM]
    send(tab_out)
    attend(length, q_out, k_out, v_out, tab_out, wout, ctx_out, attn_out, far_scratch, prob_out)


def attention_dealt(
    spots, piece, lengths, dealing, mine, theirs, tab, wq, bq, wk, bk, wv, bv, wout,
    x_out, attn_out, q, k, v, ctx, far_scratch,
):
    length = lengths[dealing[lax.axis_index("dp")]]
    assemble(mine, theirs, spots, piece, piece, x_out)
    send(x_out)
    project(x_out[...], (wq, wk, wv), (bq, bk, bv), (q, k, v))
    ready(tab)
    attend(length, q, k, v, tab, wout, ctx, attn_out, far_scratch, None)


def row_norm(values):
    center = values - jnp.mean(values, axis=-1, keepdims=True)
    inverse = lax.rsqrt(jnp.mean(center * center, axis=-1, keepdims=True) + EPSILON)
    return center * inverse, inverse


def norm_back(scaled, normed, inverse):
    one = jnp.mean(scaled, axis=-1, keepdims=True)
    two = jnp.mean(scaled * normed, axis=-1, keepdims=True)
    return inverse * (scaled - one - normed * two)


def ffn_forward(
    keep, x, mine, theirs, bout, gain, shift, wup, bup, wdown, normed_out, down_out,
    inverse_out=None, hidden_out=None, act_out=None, slope_out=None,
):
    rows = x.shape[0]
    ready(x, mine, theirs, bout, gain, shift, wup, bup, wdown)

    def block(i, carry):
        here = pl.ds(pl.multiple_of(i * BLOCK, BLOCK), BLOCK)
        attn = mine[here, :].astype(WIDE) + theirs[here, :].astype(WIDE) + wide_row(bout)
        normed, inverse = row_norm(x[here, :].astype(WIDE) + attn)
        normed_out[here, :] = normed
        low = (normed * wide_row(gain) + wide_row(shift)).astype(LOW)
        u = mm(low, wup[...]) + wide_row(bup)
        cdf = 0.5 * (1.0 + lax.erf(u * ROOT_HALF))
        act = (u * cdf).astype(LOW)
        if keep:
            inverse_out[here, :] = inverse
            hidden_out[here, :] = low
            act_out[here, :] = act
            density = jnp.exp(-0.5 * u * u) * INV_ROOT_TAU
            slope_out[here, :] = (cdf + u * density).astype(LOW)
        down_out[here, :] = mm(act, wdown[...]).astype(LOW)
        return carry

    lax.fori_loop(0, rows // BLOCK, block, 0)


def wide_row(vector):
    return vector[...].astype(WIDE)[None, :]


def second_norm(here, mine, theirs, bdown, normed, gain, shift):
    f = mine[here, :].astype(WIDE) + theirs[here, :].astype(WIDE) + wide_row(bdown)
    return row_norm(normed[here, :] * wide_row(gain) + wide_row(shift) + f)


def finish_dealt(mine, theirs, bdown, normed, gain, shift, fgain, fshift, y_out):
    for i in range(normed.shape[0] // BLOCK):
        here = slice(i * BLOCK, (i + 1) * BLOCK)
        n2, _ = second_norm(here, mine, theirs, bdown, normed, gain, shift)
        y_out[here, :] = (n2 * wide_row(fgain) + wide_row(fshift)).astype(LOW)


def put(buffer, chunk, first, value):
    near = position(buffer.shape[0])
    for place, offset, start, take in pieces(first, value.shape[0], chunk):
        buffer[place ^ near, offset : offset + take, :] = value[start : start + take]


def put_zeros(buffer, chunk, first):
    inner, _, width = buffer.shape
    left = inner * chunk - first
    if left > 0:
        put(buffer, chunk, first, jnp.zeros((left, width), buffer.dtype))


def ffn_backward(
    chunk, spots, piece, lengths,
    mine, theirs, bdown, normed, gain, shift, fgain, cot_mine, cot_theirs,
    hidden, act, slope, wup, wdown,
    part_out, gf_out, small_out, buffer_out, low_scratch, gu_scratch, cot_scratch,
):
    length = lengths[lax.axis_index("dp")]
    rows, width = normed.shape
    units = act.shape[1]
    assemble(cot_mine, cot_theirs, spots, 0, piece, cot_scratch)
    sums = [jnp.zeros((1, width), WIDE) for _ in range(3)]
    for i in range(rows // BLOCK):
        here = slice(i * BLOCK, (i + 1) * BLOCK)
        n2, r2 = second_norm(here, mine, theirs, bdown, normed, gain, shift)
        row_ok = i * BLOCK + lax.broadcasted_iota(jnp.int32, (BLOCK, 1), 0) < length
        gy = jnp.where(row_ok, cot_scratch[here, :].astype(WIDE), 0.0)
        gf = norm_back(gy * wide_row(fgain), n2, r2)
        gf_out[here, :] = gf
        low = gf.astype(LOW)
        low_scratch[here, :] = low
        sums[0] += jnp.sum(low.astype(WIDE), axis=0, keepdims=True)
        sums[1] += jnp.sum(gy * n2, axis=0, keepdims=True)
        sums[2] += jnp.sum(gy, axis=0, keepdims=True)
    send(gf_out)
    gu_sum = jnp.zeros((1, units), WIDE)
    for i in range(rows // BLOCK):
        here = slice(i * BLOCK, (i + 1) * BLOCK)
        gu = (mm(low_scratch[here, :], wdown[...], NT) * slope[here, :].astype(WIDE)).astype(LOW)
        gu_scratch[here, :] = gu
        gu_sum += jnp.sum(gu.astype(WIDE), axis=0, keepdims=True)
        part_out[here, :] = mm(gu, wup[...], NT).astype(LOW)
    send(part_out)
    small_out[...] = jnp.zeros(small_out.shape, WIDE)
    for k in range(units // width):
        small_out[k : k + 1, :] = gu_sum[:, k * width : (k + 1) * width]
    for k in range(3):
        small_out[units // width + k : units // width + k + 1, :] = sums[k]
    put(buffer_out, chunk, units, mm(act[...], low_scratch[...], TN).astype(LOW))
    for k in range(units // width):
        columns = slice(k * width, (k + 1) * width)
        put(
            buffer_out, chunk, k * width,
            mm(hidden[...], gu_scratch[:, columns], TN).astype(LOW),
        )
    put_zeros(buffer_out, chunk, 2 * units)


def head_backward(h, q, k, v, tab, prob, gctx, anti, g_out, gpq_out, gpk_out, gs_scratch, gp_scratch):
    rows = q.shape[1]
    span = tab.shape[3]
    window = rows + BLOCK
    scale = 1.0 / math.sqrt(3.0 * HEAD_DIM)
    blocks = rows // BLOCK
    pad = jnp.zeros((BLOCK, BLOCK), WIDE)
    keys = k[h]
    queries = q[h]
    gp_scratch[...] = jnp.zeros((2, HEAD_DIM, span), WIDE)
    for i in range(blocks):
        i0 = i * BLOCK
        w0 = rows - BLOCK - i0
        weights = prob[h, i0 : i0 + BLOCK, :].astype(WIDE)
        gprob = mm(gctx[h, i0 : i0 + BLOCK, :], v[h], NT)
        dots = jnp.sum(weights * gprob, axis=1, keepdims=True)
        gs = (weights * (gprob - dots)).astype(LOW)
        gs_scratch[i0 : i0 + BLOCK, :] = gs
        turned = mm(anti, gs)
        moved = pltpu.roll(
            jnp.concatenate([turned, pad], axis=1), 1, 1, stride=1, stride_axis=0
        ).astype(LOW)
        table_here = tab[1, h, :, w0 : w0 + window]
        gq = (mm(turned.astype(LOW), keys) + mm(moved, table_here, NT)) * scale
        g_out[0, h, i0 : i0 + BLOCK, :] = mm(anti, gq.astype(LOW)).astype(LOW)
        turned_q = mm(anti, q[h, i0 : i0 + BLOCK, :]).astype(LOW)
        gp_scratch[1, :, w0 : w0 + window] += mm(turned_q, moved, TN)
    for b in range(blocks):
        j0 = b * BLOCK
        w0 = rows - BLOCK - j0
        turned = mm(anti, gs_scratch[:, j0 : j0 + BLOCK], NT)
        moved = pltpu.roll(
            jnp.concatenate([turned, pad], axis=1), 1, 1, stride=1, stride_axis=0
        ).astype(LOW)
        table_here = tab[0, h, :, w0 : w0 + window]
        gk = (mm(turned.astype(LOW), queries) + mm(moved, table_here, NT)) * scale
        g_out[1, h, j0 : j0 + BLOCK, :] = mm(anti, gk.astype(LOW)).astype(LOW)
        turned_k = mm(anti, k[h, j0 : j0 + BLOCK, :]).astype(LOW)
        gp_scratch[0, :, w0 : w0 + window] += mm(turned_k, moved, TN)
    g_out[2, h] = mm(prob[h], gctx[h], TN).astype(LOW)
    gpq_out[h] = gp_scratch[0].astype(LOW)
    gpk_out[h] = gp_scratch[1].astype(LOW)


def attention_backward(
    wout, mine, theirs, gf, normed, inverse, gain, ctx, q, k, v, tab, prob,
    gp_out, wout_out, small_out, gctx_out, g_out, gpq_out, gpk_out,
    gpb_scratch, gs_scratch, gp_scratch, gctx_scratch,
):
    heads, rows, _ = ctx.shape
    width = gp_out.shape[1]
    first = q.shape[0]
    blocks = rows // BLOCK
    sums = [jnp.zeros((1, width), WIDE) for _ in range(3)]
    for i in range(blocks):
        here = slice(i * BLOCK, (i + 1) * BLOCK)
        gh = gf[here, :] + (mine[here, :].astype(WIDE) + theirs[here, :].astype(WIDE))
        n1 = normed[here, :]
        gp = norm_back(gh * wide_row(gain), n1, inverse[here, :])
        gp_out[here, :] = gp
        low = gp.astype(LOW)
        gpb_scratch[here, :] = low
        sums[0] += jnp.sum(low.astype(WIDE), axis=0, keepdims=True)
        sums[1] += jnp.sum(gh * n1, axis=0, keepdims=True)
        sums[2] += jnp.sum(gh, axis=0, keepdims=True)
        grad = mm(low, wout[...], NT).astype(LOW)
        for h in range(heads):
            part = grad[:, h * HEAD_DIM : (h + 1) * HEAD_DIM]
            if h < first:
                gctx_scratch[h, here, :] = part
            else:
                gctx_out[h - first, here, :] = part
    small_out[...] = jnp.zeros(small_out.shape, WIDE)
    for n in range(3):
        small_out[2 + n : 3 + n, :] = sums[n]
    for h in range(heads):
        wout_out[h * HEAD_DIM : (h + 1) * HEAD_DIM, :] = mm(ctx[h], gpb_scratch[...], TN).astype(LOW)
    send(gp_out, small_out, wout_out, gctx_out)
    anti = anti_diagonal()
    ready(q, k, v, tab, prob)

    def head(h, carry):
        head_backward(
            h, q, k, v, tab, prob, gctx_scratch, anti, g_out, gpq_out, gpk_out, gs_scratch, gp_scratch
        )
        return carry

    lax.fori_loop(0, first, head, 0)


def attention_backward_last(
    table, wq, wk, wv, gctx, q, k, v, tab, prob, before, gpq_before, gpk_before,
    g_out, gpq_out, gpk_out, send_out, keep_out,
    gs_scratch, gp_scratch, gpq_scratch, gpk_scratch, rel_scratch,
):
    side = lax.axis_index("tensor")
    buckets = rel_scratch.shape[0]
    half = buckets // 2
    scale = 1.0 / math.sqrt(3.0 * HEAD_DIM)
    anti = anti_diagonal()
    head_backward(
        0, q, k, v, tab, prob, gctx, anti, g_out, gpq_scratch, gpk_scratch, gs_scratch, gp_scratch
    )
    send(g_out)
    hot = one_hot(table, buckets)
    for first, here, out in (
        (gpq_before, gpq_scratch, gpq_out), (gpk_before, gpk_scratch, gpk_out)
    ):
        parts = [first[h] for h in range(first.shape[0])] + [here[0]]
        out[...] = mm(hot, jnp.concatenate(parts, axis=0), NT) * scale
    rel_scratch[...] = mm(gpq_out[...].astype(LOW), wq[...]) + mm(gpk_out[...].astype(LOW), wk[...])
    send(gpq_out, gpk_out)
    rows = buckets
    send_out[rows:, :] = rel_scratch[
        pl.ds(pl.multiple_of((1 - side) * half, half), half), :
    ].astype(LOW)
    keep_out[...] = rel_scratch[pl.ds(pl.multiple_of(side * half, half), half), :].astype(LOW)
    send_out[:rows, :] = (
        mm(together(0, before, g_out), wq[...])
        + mm(together(1, before, g_out), wk[...])
        + mm(together(2, before, g_out), wv[...])
    ).astype(LOW)


def together(slot, before, last):
    parts = [before[slot, h] for h in range(before.shape[1])] + [last[slot, 0]]
    return jnp.concatenate(parts, axis=1)


def weight_gradients(
    chunk, x, relative, before, last, gpq, gpk, wout_grad, small_ffn, small_attn, keep, got,
    buffer_out,
):
    part = gpq.shape[1]
    xv = x[...]
    rel = relative[...]
    gq, gk, gv = (together(slot, before, last) for slot in range(3))
    put(
        buffer_out, chunk, 0,
        (mm(gq, xv, TN) + mm(gpq[...].astype(LOW), rel, TN)).astype(LOW),
    )
    put(
        buffer_out, chunk, part,
        (mm(gk, xv, TN) + mm(gpk[...].astype(LOW), rel, TN)).astype(LOW),
    )
    put(buffer_out, chunk, 2 * part, mm(gv, xv, TN).astype(LOW))
    put(buffer_out, chunk, 3 * part, wout_grad[...])
    half = keep.shape[0]
    both = (keep[...].astype(WIDE) + got[got.shape[0] - half :, :].astype(WIDE)).astype(LOW)
    put(buffer_out, chunk, 4 * part, both)
    count = 4 * part + keep.shape[0]
    bias = [
        jnp.sum(gq.astype(WIDE), axis=0, keepdims=True) + jnp.sum(gpq[...], axis=0, keepdims=True),
        jnp.sum(gk.astype(WIDE), axis=0, keepdims=True) + jnp.sum(gpk[...], axis=0, keepdims=True),
        jnp.sum(gv.astype(WIDE), axis=0, keepdims=True),
    ]
    second = jnp.concatenate([bias[2], jnp.zeros_like(bias[2])], axis=1)
    small = jnp.concatenate(
        [small_ffn[...], jnp.concatenate(bias[:2], axis=1), second, small_attn[2:, :]], axis=0
    ).astype(LOW)
    put(buffer_out, chunk, count, small)
    put_zeros(buffer_out, chunk, count + small.shape[0])


def finish_tokens(gp, mine, theirs, grad_out):
    for i in range(gp.shape[0] // BLOCK):
        here = slice(i * BLOCK, (i + 1) * BLOCK)
        both = mine[here, :].astype(WIDE) + theirs[here, :].astype(WIDE)
        grad_out[here, :] = (gp[here, :] + both).astype(LOW)


def add_up(*refs):
    parts, sum_out = refs[:-1], refs[-1]
    acc = parts[0][...].astype(WIDE)
    for other in parts[1:]:
        acc += other[...].astype(WIDE)
    sum_out[...] = acc.astype(LOW)


def chunks(gathered, first, count):
    for place, offset, start, take in pieces(first, count, gathered.shape[1]):
        yield start, take, gathered[place, offset : offset + take, :].astype(WIDE)


def unpack_ffn(gathered, wup_out, wdown_out):
    width, units = wup_out.shape
    for start, take, value in chunks(gathered, units, units):
        wdown_out[start : start + take, :] = value
    send(wdown_out)
    for k in range(units // width):
        for start, take, value in chunks(gathered, k * width, width):
            wup_out[start : start + take, k * width : (k + 1) * width] = value


def unpack_relative(first, gathered, rel_out):
    for start, take, value in chunks(gathered, first, rel_out.shape[0]):
        rel_out[start : start + take, :] = value.astype(LOW)


def unpack_attention(
    first, gathered, wq_out, wk_out, wv_out, wout_out, bup_out,
    bq_out, bk_out, bv_out, bout_out, again_out, ashift_out, bdown_out, fgain_out, fshift_out,
):
    part, width = wq_out.shape
    units = bup_out.shape[0]
    for k, out in enumerate((wq_out, wk_out, wv_out, wout_out)):
        for start, take, value in chunks(gathered, k * part, part):
            out[start : start + take, :] = value
        send(out)
    small = jnp.concatenate([value for _, _, value in chunks(gathered, first, 16)], axis=0)
    ups = units // width
    for k in range(ups):
        bup_out[k * width : (k + 1) * width] = small[k]
    bdown_out[...] = small[ups]
    fgain_out[...] = small[ups + 1]
    fshift_out[...] = small[ups + 2]
    bq_out[...] = small[8, :part]
    bk_out[...] = small[8, part:]
    bv_out[...] = small[9, :part]
    bout_out[...] = small[10]
    again_out[...] = small[11]
    ashift_out[...] = small[12]


def join_relative(mine, theirs, out):
    side = lax.axis_index("tensor")
    half = mine.shape[0]
    out[pl.ds(pl.multiple_of(side * half, half), half), :] = mine[...].astype(WIDE)
    out[pl.ds(pl.multiple_of((1 - side) * half, half), half), :] = theirs[...].astype(WIDE)


def with_statics(body, *statics):
    def wrapped(*refs):
        body(*statics, *refs)

    wrapped.__name__ = body.__name__
    return wrapped


def swap(array):
    return lax.ppermute(array, "tensor", [(0, 1), (1, 0)])


def exchange(array):
    return lax.all_to_all(array, "dp", split_axis=0, concat_axis=0, tiled=True)


def trade(arrays, groups):
    got = []
    for k, array in enumerate(arrays, 1):
        pairs = [(group[p], group[p ^ k]) for group in groups for p in range(len(group))]
        got.append(lax.ppermute(array, "dp", pairs))
    return got


def after(value, *others):
    return lax.optimization_barrier((value,) + others)[0]


class Sequence:
    def __init__(self):
        self.last = None

    def run(self, body, outs, args, scratch=(), smem=0, flops=1):
        args = list(args)
        if self.last is not None:
            free = [i for i in range(smem, len(args)) if not isinstance(args[i], (Here, Stack))]
            if free:
                arg = args[free[0]]
                if isinstance(arg, Part):
                    args[free[0]] = Part(after(arg.array, self.last), arg.axis, arg.start, arg.count)
                else:
                    args[free[0]] = after(arg, self.last)
            elif isinstance(args[smem], Stack):
                first = args[smem].arrays
                args[smem] = Stack((after(first[0], self.last),) + first[1:])
            else:
                args[smem] = Here(after(args[smem].what[0], self.last))
        got = call(body, outs, args, scratch, smem, flops)
        self.last = got[0][0] if isinstance(got[0], list) else got[0]
        return got


def on_device(
    tokens, lengths, dealing, bucket_table, relative,
    w_query, b_query, w_key, b_key, w_value, b_value, w_out, b_out,
    attn_gain, attn_shift, w_up, b_up, w_down, b_down, ffn_gain, ffn_shift, cotangent,
):
    _, rows, width = tokens.shape
    total = dealing.shape[0]
    part = w_query.shape[1]
    heads = part // HEAD_DIM
    units = w_up.shape[1]
    half = rows // 2
    span = 2 * rows
    piece = max(16, half // total)
    spots = half // piece
    side = lax.axis_index("tensor")
    inner = 1 << ((total.bit_length()) // 2)
    outer = total // inner
    near_groups = [[o * inner + i for i in range(inner)] for o in range(outer)]
    chunk_one = chunk_rows(2 * units, inner, 16)
    chunk_two = chunk_rows(4 * part + half + 16, inner, 16)

    sequence = Sequence()
    run = sequence.run

    def cut(array):
        mine = lax.dynamic_slice_in_dim(array[0], side * half, half, 0)
        return mine.reshape(spots, piece, width)

    moving = jnp.concatenate([cut(cotangent), cut(tokens)], axis=1)
    if spots < total:
        moving = jnp.pad(moving, ((0, total - spots), (0, 0), (0, 0)))
    arrived = exchange(moving)
    x = tokens[0]
    table = jnp.pad(bucket_table, (0, span - bucket_table.shape[0]), constant_values=-1)
    table = table.reshape(span // BLOCK, BLOCK)
    projections = (w_query.T, b_query, w_key.T, b_key, w_value.T, b_value, w_out)
    head_shape = (heads, rows, HEAD_DIM)
    q, k, v, tab, prob, ctx, attn_part = run(
        attention_forward,
        [(head_shape, LOW)] * 3
        + [((2, heads, HEAD_DIM, span), LOW), ((heads, rows, rows), LOW)]
        + [(head_shape, LOW), Here((rows, width), LOW)],
        (lengths, x, relative, table) + projections,
        scratch=[pltpu.VMEM((rows, rows), WIDE)],
        smem=1,
    )
    arrived = after(arrived, sequence.last)
    (turned,) = call_here(
        with_statics(permute_body, piece), [(arrived.shape, LOW)], (dealing, arrived), smem=1
    )
    sequence.last = turned
    dealt_mine = exchange(turned)
    dealt_theirs = swap(dealt_mine)
    attn_got = swap(attn_part)
    ffn_weights = (b_out, attn_gain, attn_shift, w_up, b_up, w_down)
    normed, down_part, inverse, hidden, act, slope = run(
        with_statics(ffn_forward, True),
        [((rows, width), WIDE), Here((rows, width), LOW), ((rows, 1), WIDE), ((rows, width), LOW),
         ((rows, units), LOW), ((rows, units), LOW)],
        (x, Here(attn_part), Here(attn_got)) + ffn_weights,
    )
    down_got = swap(down_part)
    hidden_part, gf, small_ffn, near_one = run(
        with_statics(ffn_backward, chunk_one, spots, piece),
        [Here((rows, width), LOW), ((rows, width), WIDE), ((8, width), WIDE),
         Pieces(inner, (chunk_one, width), LOW)],
        (lengths, Here(down_part), Here(down_got), b_down, normed, attn_gain, attn_shift,
         ffn_gain, Here(dealt_mine), Here(dealt_theirs), hidden, act, slope, w_up, w_down),
        scratch=[
            pltpu.VMEM((rows, width), LOW),
            pltpu.VMEM((rows, units), LOW),
            pltpu.VMEM((rows, width), LOW),
        ],
        smem=1,
    )
    hidden_got = swap(hidden_part)
    near_one[1:] = trade(near_one[1:], near_groups)

    def total_of(own, got):
        (out,) = run(add_up, [(own.shape, LOW)], (own,) + tuple(Here(array) for array in got))
        return out

    def far_step(array, step):
        reach = inner << step
        return lax.ppermute(array, "dp", [(p, p ^ reach) for p in range(total)])

    steps = outer.bit_length() - 1

    def gather_near(line):
        return Stack([line] + trade([line] * (inner - 1), near_groups))

    before = heads - 1
    gp, wout_grad, small_attn, gctx, g_before, gpq_before, gpk_before = run(
        attention_backward,
        [((rows, width), WIDE), ((part, width), LOW), ((8, width), WIDE),
         ((1, rows, HEAD_DIM), LOW), ((3, before, rows, HEAD_DIM), LOW),
         ((before, HEAD_DIM, span), LOW), ((before, HEAD_DIM, span), LOW)],
        (w_out, Here(hidden_part), Here(hidden_got), gf, normed, inverse, attn_gain, ctx)
        + tuple(Part(array, 0, 0, before) for array in (q, k, v))
        + (Part(tab, 1, 0, before), Part(prob, 0, 0, before)),
        scratch=[
            pltpu.VMEM((rows, width), LOW),
            pltpu.VMEM((rows, rows), LOW),
            pltpu.VMEM((2, HEAD_DIM, span), WIDE),
            pltpu.VMEM((before, rows, HEAD_DIM), LOW),
        ],
    )
    line_one = total_of(near_one[0], near_one[1:])
    got_one = far_step(line_one, 0)
    g_last, gpq, gpk, send_part, rel_keep = run(
        attention_backward_last,
        [((3, 1, rows, HEAD_DIM), LOW), ((rows, part), WIDE), ((rows, part), WIDE),
         ((rows + half, width), LOW), ((half, width), LOW)],
        (table, w_query.T, w_key.T, w_value.T, gctx)
        + tuple(Part(array, 0, before, 1) for array in (q, k, v))
        + (Part(tab, 1, before, 1), Part(prob, 0, before, 1), g_before, gpq_before, gpk_before),
        scratch=[
            pltpu.VMEM((rows, rows), LOW),
            pltpu.VMEM((2, HEAD_DIM, span), WIDE),
            pltpu.VMEM((1, HEAD_DIM, span), LOW),
            pltpu.VMEM((1, HEAD_DIM, span), LOW),
            pltpu.VMEM((rows, width), WIDE),
        ],
    )
    for step in range(1, steps):
        line_one = total_of(line_one, [got_one])
        got_one = far_step(line_one, step)
    send_got = swap(after(send_part, line_one))
    (near_two,) = run(
        with_statics(weight_gradients, chunk_two),
        [Pieces(inner, (chunk_two, width), LOW)],
        (x, relative, g_before, g_last, gpq, gpk, wout_grad, small_ffn, small_attn, rel_keep,
         Here(send_got)),
    )
    near_two[1:] = trade(near_two[1:], near_groups)

    x_dealt, attn_dealt = run(
        with_statics(attention_dealt, spots, piece),
        [((rows, width), LOW), Here((rows, width), LOW)],
        (lengths, dealing, dealt_mine, dealt_theirs, tab) + projections,
        scratch=[pltpu.VMEM(head_shape, LOW) for _ in range(4)] + [pltpu.VMEM((rows, rows), WIDE)],
        smem=2,
    )
    line_two = total_of(near_two[0], near_two[1:])
    got_two = far_step(line_two, 0)
    line_one = total_of(line_one, [got_one])
    all_one = gather_near(line_one)
    attn_dealt_got = swap(after(attn_dealt, line_one))
    normed_dealt, down_dealt = run(
        with_statics(ffn_forward, False),
        [((rows, width), WIDE), Here((rows, width), LOW)],
        (x_dealt, Here(attn_dealt), Here(attn_dealt_got)) + ffn_weights,
    )
    for step in range(1, steps):
        line_two = total_of(line_two, [got_two])
        got_two = far_step(line_two, step)
    g_up, g_down = run(
        unpack_ffn, [((width, units), WIDE), ((units, width), WIDE)], (all_one,),
        flops=10**11,
    )
    down_dealt_got = swap(after(down_dealt, line_two))
    (grad_tokens,) = run(
        finish_tokens,
        [((rows, width), LOW)],
        (gp, Part(send_part, 0, 0, rows), Part(send_got, 0, 0, rows)),
    )
    (y,) = run(
        finish_dealt,
        [((rows, width), LOW)],
        (Here(down_dealt), Here(down_dealt_got), b_down, normed_dealt, attn_gain, attn_shift,
         ffn_gain, ffn_shift),
    )
    line_two = total_of(line_two, [got_two])
    all_two = gather_near(line_two)
    first = 4 * part
    (rel_half,) = run(with_statics(unpack_relative, first), [Here((half, width), LOW)], (all_two,))
    rel_other = swap(rel_half)
    g_wq, g_wk, g_wv, g_wout, g_bup, g_bq, g_bk, g_bv, g_bout, g_again, g_ashift, g_bdown, g_fgain, g_fshift = run(
        with_statics(unpack_attention, first + half),
        [((part, width), WIDE)] * 4
        + [((units,), WIDE)]
        + [((part,), WIDE)] * 3
        + [((width,), WIDE)] * 6,
        (all_two,),
    )
    (g_rel,) = run(join_relative, [((rows, width), WIDE)], (Here(rel_half), Here(rel_other)))
    return (
        y[None], grad_tokens[None], g_rel, g_wq.T, g_bq, g_wk.T, g_bk, g_wv.T, g_bv, g_wout,
        g_bout, g_again, g_ashift, g_up, g_bup, g_down, g_bdown, g_fgain, g_fshift,
    )


def solution(mesh):
    return jax.shard_map(
        on_device,
        mesh=mesh,
        in_specs=(
            P("dp", None, None), P(), P(), P(), P(),
            P(None, "tensor"), P("tensor"), P(None, "tensor"), P("tensor"),
            P(None, "tensor"), P("tensor"), P("tensor", None), P(), P(), P(),
            P(None, "tensor"), P("tensor"), P("tensor", None), P(), P(), P(),
            P("dp", None, None),
        ),
        out_specs=(
            P("dp", None, None), P("dp", None, None), P(),
            P(None, "tensor"), P("tensor"), P(None, "tensor"), P("tensor"),
            P(None, "tensor"), P("tensor"), P("tensor", None), P(), P(), P(),
            P(None, "tensor"), P("tensor"), P("tensor", None), P(), P(), P(),
        ),
        check_vma=False,
    )
```

time: 194 us -> 165 us (0.85)
  local copies, waits for them, and re-layouts: 39.7 us -> 4.26 us
  Pallas kernels: 65.6 us -> 101 us
  blocking collectives: 16.2 us -> 0 us
  waiting for transfers between devices: 38 us -> 22.5 us
  starting transfers between devices: 31.3 us -> 34.7 us
    unnamed x128 -> x20, local copies, waits for them, and re-layouts: 38.6 us -> 2.69 us
    pallas_call x15 -> x21, Pallas kernels: 65.6 us -> 101 us  [the longest x20 98.9 us: call(): pl.pallas_call(kernel, out_shape=results, in_specs=[pl.BlockSpec(memory_s...]
    all_to_all x6 -> x2, waiting for transfers between devices: 32.7 us -> 4.44 us  [exchange(): return lax.all_to_all(array, 'dp', split_axis=0, concat_axis=0, tiled=True)]
    ppermute x0 -> x16, starting transfers between devices: none -> 18.8 us  [the longest x12 14.1 us: trade(): got.append(lax.ppermute(array, 'dp', pairs))]
    all_to_all x1 -> x0, blocking collectives: 16.2 us -> none  [exchange(): lax.all_to_all(array, 'dp', split_axis=0, concat_axis=0, tiled=True, axis...]
    all_to_all x6 -> x2, starting transfers between devices: 30.2 us -> 15.3 us  [exchange(): return lax.all_to_all(array, 'dp', split_axis=0, concat_axis=0, tiled=True)]
    ppermute x0 -> x16, waiting for transfers between devices: none -> 13.7 us  [the longest x12 12 us: trade(): got.append(lax.ppermute(array, 'dp', pairs))]
  transfers between devices with their start and end apart: 14 -> 26, of which waited for: 8 -> 9; matrix products, arithmetic and copies ran while one was open for 0% -> 0% of each run, Pallas kernels for 30% -> 50%
where the time goes in v3:
time: 165 us; the launch traced here: 164 us
  Pallas kernels  101 us (61%)
  starting transfers between devices  34.7 us (21%)
  waiting for transfers between devices  22.5 us (14%)
  local copies, waits for them, and re-layouts  4.26 us (3%)
    pallas_call x20, Pallas kernels, call(): pl.pallas_call(kernel, out_shape=results, in_specs=[pl.BlockSpec(memory_s...  98.9 us
    all_to_all x2, starting transfers between devices, exchange(): return lax.all_to_all(array, 'dp', split_axis=0, concat_axis=0, tiled=True)  15.3 us
    ppermute x12, starting transfers between devices, trade(): got.append(lax.ppermute(array, 'dp', pairs))  14.1 us
    ppermute x12, waiting for transfers between devices, trade(): got.append(lax.ppermute(array, 'dp', pairs))  12 us
    ppermute x4, starting transfers between devices, far_step(): return lax.ppermute(array, 'dp', [(p, p ^ reach) for p in range(total)])  4.61 us
    all_to_all x2, waiting for transfers between devices, exchange(): return lax.all_to_all(array, 'dp', split_axis=0, concat_axis=0, tiled=True)  4.44 us
    ppermute x8, waiting for transfers between devices, swap(): return lax.ppermute(array, 'tensor', [(0, 1), (1, 0)])  4.38 us
  transfers between devices with their start and end apart: 26, of which 9 were waited for; matrix products, arithmetic and copies ran while one was open for 0% of the time, Pallas kernels for 50%

profile of v3, /device:TPU:0, one launch (start us, length us, event | category | flops | bytes accessed | tf_op | source)
XLA Modules:
  0.0 164.2 jit_solution(3779727048175972126)
XLA Ops:
  0.7 0.0 copy-start
  0.7 1.0 copy-done
  1.7 1.0 constant_dynamic-slice_fusion
  2.6 0.8 pad_maximum_fusion
  3.4 8.3 %all-to-all-start = ((bf16[16,32,384]{2,1,0:T(8,128)(2,1)}), bf16[16,32,384]{2,1,0:T(8,128)(2,1)S(1)}, u32[]{:S(2)}, u32[]{:S(2)}) async-start(bf16[16,32,384]{2,1,0:T(8,128)(2,1)} %pad_maximum_fusion), calls=%async_computation | async-start | bytes 786432 | tf_op jit(solution)/shard_map/all_to_all | solution.py:741
  11.8 0.6 pad_bitcast_fusion.refs_3_.refs_0_
  12.4 14.0 %shard_map.357 = (bf16[3,512,64]{2,1,0:T(8,128)(2,1)}, bf16[3,512,64]{2,1,0:T(8,128)(2,1)}, bf16[3,512,64]{2,1,0:T(8,128)(2,1)}, bf16[2,3,64,1024]{3,2,1,0:T(8,1...) custom-call(s32[16]{0:T(128)S(1)} %copy-done.6, ...), custom_call_target="tpu_custom_call" | custom-call | flops 1 | bytes 1 | tf_op jit(solution)/shard_map/pallas_call | solution.py:208
  26.4 0.0 copy-start.8
  26.4 0.7 copy-done.8
  27.2 1.8 %shard_map.358 = bf16[16,32,384]{2,1,0:T(8,128)(2,1)} custom-call(s32[16]{0:T(128)} %refs_1_.3, bf16[16,32,384]{2,1,0:T(8,128)(2,1)} %copy-done.8), custom_call_target="tpu_custom_call" | custom-call | tf_op jit(solution)/shard_map/pallas_call | solution.py:248
  29.0 6.9 %all-to-all-start.1 = ((bf16[16,32,384]{2,1,0:T(8,128)(2,1)}), bf16[16,32,384]{2,1,0:T(8,128)(2,1)S(1)}, u32[]{:S(2)}, u32[]{:S(2)}) async-start(bf16[16,32,384]{2,1,0:T(8,128)(2,1)} %shard_map.358), calls=%async_computation.1 | async-start | bytes 786432 | tf_op jit(solution)/shard_map/all_to_all | solution.py:741
  35.9 0.1 collective-permute-start
  36.0 1.7 %collective-permute-done.refs_2_ = bf16[512,384]{1,0:T(8,128)(2,1)S(1)} collective-permute-done((bf16[512,384]{1,0:T(8,128)(2,1)S(1)}, bf16[512,384]{1,0:T(8,128)(2,1)S(1)}, u32[]{:S(2)}, u32[]{:S(2)}) %collective-permute-start) | collective-permute-done | bytes 393248 | tf_op jit(solution)/shard_map/ppermute | solution.py:737
  37.7 5.6 %shard_map.359 = (f32[512,384]{1,0:T(8,128)}, bf16[512,384]{1,0:T(8,128)(2,1)S(1)}, f32[512,1]{1,0:T(8,128)}, bf16[512,384]{1,0:T(8,128)(2,1)}, bf16[512,768]{1,0:T(8,128)(2,1)}, /*index=5*/bf16[512,768]{1,0:T(8,128)(2,1)}) custom-call(bf16[512,384]{1,0:T(8,128)(2,1)} %bitcast.14, bf16[512,384]{1,0:T(8,128)(2,1)S(1)} %get-tuple-element.101.refs_1_, ...), custom_call_target="tpu_custom_call" | custom-call | flops 1 | bytes 1 | tf_op jit(solution)/shard_map/pallas_call | solution.py:208
  43.3 0.2 collective-permute-start.1
  43.5 4.4 %all-to-all-done.1.refs_8_.refs_2_ = bf16[16,32,384]{2,1,0:T(8,128)(2,1)S(1)} async-done(((bf16[16,32,384]{2,1,0:T(8,128)(2,1)}), bf16[16,32,384]{2,1,0:T(8,128)(2,1)S(1)}, u32[]{:S(2)}, u32[]{:S(2)}) %all-to-all-start.1) | async-done | bytes 393248 | tf_op jit(solution)/shard_map/all_to_all | solution.py:741
  47.9 0.0 collective-permute-start.2
  47.9 1.7 %collective-permute-done.2.refs_9_.refs_3_ = bf16[16,32,384]{2,1,0:T(8,128)(2,1)S(1)} collective-permute-done((bf16[16,32,384]{2,1,0:T(8,128)(2,1)S(1)}, bf16[16,32,384]{2,1,0:T(8,128)(2,1)S(1)}, u32[]{:S(2)}, u32[]{:S(2)}) %collective-permute-start.2) | collective-permute-done | bytes 393248 | tf_op jit(solution)/shard_map/ppermute | solution.py:737
  49.6 6.8 %shard_map.360 = (bf16[512,384]{1,0:T(8,128)(2,1)S(1)}, f32[512,384]{1,0:T(8,128)}, f32[8,384]{1,0:T(8,128)}, bf16[384,384]{1,0:T(8,128)(2,1)}, bf16[384,384]{1,...) custom-call(s32[16]{0:T(128)S(1)} %copy-done.6, bf16[512,384]{1,0:T(8,128)(2,1)S(1)} %get-tuple-element.102.refs_1_, ...), custom_call_target="tpu_custom_call" | custom-call | flops 1 | bytes 1 | tf_op jit(solution)/shard_map/pallas_call | solution.py:208
  56.5 0.2 collective-permute-start.3
  56.7 0.6 collective-permute-start.4
  57.2 0.9 collective-permute-start.5
  58.1 2.1 %collective-permute-start.6 = (bf16[384,384]{1,0:T(8,128)(2,1)}, bf16[384,384]{1,0:T(8,128)(2,1)S(1)}, u32[]{:S(2)}, u32[]{:S(2)}) collective-permute-start(bf16[384,384]{1,0:T(8,128)(2,1)} %get-tuple-element.122), channel_id=1, source_target_pairs={{0,6},{2,4},{4,2},{6,0},{8,14},{10,12},{12,10},{14,8},{16,22},{18,... | collective-permute-start | bytes 884744 | tf_op jit(solution)/shard_map/ppermute | solution.py:748
  60.2 17.5 %shard_map.361 = (f32[512,384]{1,0:T(8,128)}, bf16[192,384]{1,0:T(8,128)(2,1)}, f32[8,384]{1,0:T(8,128)}, bf16[1,512,64]{2,1,0:T(8,128)(2,1)}, bf16[3,2,512,64]{...) custom-call(bf16[192,384]{1,0:T(8,128)(2,1)} %refs_11_.1, ...), custom_call_target="tpu_custom_call" | custom-call | flops 1 | bytes 1 | tf_op jit(solution)/shard_map/pallas_call | solution.py:208
  77.7 1.9 %shard_map.362.refs_0_ = bf16[384,384]{1,0:T(8,128)(2,1)} custom-call(bf16[384,384]{1,0:T(8,128)(2,1)} %get-tuple-element.119.refs_0_, bf16[384,384]{1,0:T(8,128)(2,1)S(1)} %collective-permute-done.4.refs_1_, bf16[384,384]{1,0:T(8,128)(2,1)S(1)} %collective-permute-done.5.refs_2_, bf16[384,384]{1,0:T(8,128)(2,1)S(1)} %collective-permute-done.6.refs_3_), custom_call_target="tpu_custom_call" | custom-call | flops 1 | bytes 1 | tf_op jit(solution)/shard_map/pallas_call | solution.py:208
  79.6 1.2 collective-permute-start.7
  80.7 12.9 %shard_map.363 = (bf16[3,1,512,64]{3,2,1,0:T(8,128)(2,1)}, f32[512,192]{1,0:T(8,128)}, f32[512,192]{1,0:T(8,128)}, bf16[768,384]{1,0:T(8,128)(2,1)}, bf16[256,384]{1,0:T(8,128)(2,1)}) custom-call(s32[8,128]{1,0:T(8,128)} %pad_bitcast_fusion.refs_3_.refs_0_, bf16[192,384]{1,0:T(8,128)(2,1)} %bitcast.17, bf16[192,384]{1,0:T(8,128)(2,1)} %bitcast.20, ...), custom_call_target="tpu_custom_call" | custom-call | flops 1 | bytes 1 | tf_op jit(solution)/shard_map/pallas_call | solution.py:208
  93.7 1.8 %shard_map.364.refs_0_ = bf16[384,384]{1,0:T(8,128)(2,1)} custom-call(bf16[384,384]{1,0:T(8,128)(2,1)} %shard_map.362.refs_0_, bf16[384,384]{1,0:T(8,128)(2,1)S(1)} %collective-permute-done.7.refs_1_), custom_call_target="tpu_custom_call" | custom-call | flops 1 | bytes 1 | tf_op jit(solution)/shard_map/pallas_call | solution.py:208
  95.5 0.1 collective-permute-start.8
  95.5 1.3 collective-permute-start.12
  96.8 0.9 collective-permute-done.8.refs_10_.refs_2_
  97.8 4.2 %shard_map.365 = (bf16[272,384]{1,0:T(8,128)(2,1)}, bf16[272,384]{1,0:T(8,128)(2,1)}, bf16[272,384]{1,0:T(8,128)(2,1)}, bf16[272,384]{1,0:T(8,128)(2,1)}) custom-call(bf16[512,384]{1,0:T(8,128)(2,1)} %bitcast.15, bf16[512,384]{1,0:T(8,128)(2,1)} %refs_1_.2, bf16[3,2,512,64]{3,2,1,0:T(8,128)(2,1)} %get-tuple-element.125.refs_10_.refs_2_, ...), custom_call_target="tpu_custom_call" | custom-call | flops 1 | bytes 1 | tf_op jit(solution)/shard_map/pallas_call | solution.py:208
  102.0 0.6 collective-permute-start.9
  102.6 0.9 collective-permute-start.10
  103.5 2.1 %collective-permute-start.11 = (bf16[272,384]{1,0:T(8,128)(2,1)}, bf16[272,384]{1,0:T(8,128)(2,1)S(1)}, u32[]{:S(2)}, u32[]{:S(2)}) collective-permute-start(bf16[272,384]{1,0:T(8,128)(2,1)} %get-tuple-element.145), channel_id=1, source_target_pairs={{0,6},{2,4},{4,2},{6,0},{8,14},{10,12},{12,10},{14,8},{16,22},{18,... | collective-permute-start | bytes 626696 | tf_op jit(solution)/shard_map/ppermute | solution.py:748
  105.5 11.6 %shard_map.366 = (bf16[512,384]{1,0:T(8,128)(2,1)}, bf16[512,384]{1,0:T(8,128)(2,1)S(1)}) custom-call(s32[16]{0:T(128)S(1)} %copy-done.6, s32[16]{0:T(128)S(1)} %copy-done.7, bf16[16,32,384]{2,1,0:T(8,128)(2,1)} %copy-done.1, bf16[16,32,384]{2,1,0:T(8,128)(2,1)} %copy-done.4, bf16[2,3,64,1024]{3,2,1,0:T(8,128)(2,1)} %get-tuple-element.116.refs_11_.refs_8_.refs_4_, ...), custom_call_target="tpu_custom_call" | custom-call | flops 1 | bytes 1 | tf_op jit(solution)/shard_map/pallas_call | solution.py:208
  117.2 1.8 %shard_map.367.refs_0_ = bf16[272,384]{1,0:T(8,128)(2,1)} custom-call(bf16[272,384]{1,0:T(8,128)(2,1)} %get-tuple-element.142.refs_0_, bf16[272,384]{1,0:T(8,128)(2,1)S(1)} %collective-permute-done.9.refs_1_, bf16[272,384]{1,0:T(8,128)(2,1)S(1)} %collective-permute-done.10.refs_2_, bf16[272,384]{1,0:T(8,128)(2,1)S(1)} %collective-permute-done.11.refs_3_), custom_call_target="tpu_custom_call" | custom-call | flops 1 | bytes 1 | tf_op jit(solution)/shard_map/pallas_call | solution.py:208
  119.0 1.8 %shard_map.368.refs_0_ = bf16[384,384]{1,0:T(8,128)(2,1)} custom-call(bf16[384,384]{1,0:T(8,128)(2,1)} %shard_map.364.refs_0_, bf16[384,384]{1,0:T(8,128)(2,1)S(1)} %collective-permute-done.12.refs_1_), custom_call_target="tpu_custom_call" | custom-call | flops 1 | bytes 1 | tf_op jit(solution)/shard_map/pallas_call | solution.py:208
  120.8 0.0 copy-start.5
  120.8 0.1 collective-permute-start.13
  120.9 0.9 collective-permute-start.18
  121.8 1.2 collective-permute-start.17
  123.0 1.5 collective-permute-start.16
  124.4 0.9 collective-permute-start.14
  125.4 4.6 %shard_map.369 = (f32[512,384]{1,0:T(8,128)}, bf16[512,384]{1,0:T(8,128)(2,1)S(1)}) custom-call(bf16[512,384]{1,0:T(8,128)(2,1)} %get-tuple-element.147.refs_0_, bf16[512,384]{1,0:T(8,128)(2,1)S(1)} %get-tuple-element.149.refs_1_, bf16[512,384]{1,0:T(8,128)(2,1)S(1)} %collective-permute-done.13.refs_2_, bf16[384]{0:T(512)(128)(2,1)} %refs_3_.4, ...), custom_call_target="tpu_custom_call" | custom-call | flops 1 | bytes 1 | tf_op jit(solution)/shard_map/pallas_call | solution.py:208
  130.0 1.3 collective-permute-done.14.refs_1_
  131.3 1.7 %shard_map.370.refs_0_ = bf16[272,384]{1,0:T(8,128)(2,1)} custom-call(bf16[272,384]{1,0:T(8,128)(2,1)} %shard_map.367.refs_0_, bf16[272,384]{1,0:T(8,128)(2,1)S(1)} %collective-permute-done.14.refs_1_), custom_call_target="tpu_custom_call" | custom-call | flops 1 | bytes 1 | tf_op jit(solution)/shard_map/pallas_call | solution.py:208
  133.0 1.3 collective-permute-start.19
  134.3 3.1 %collective-permute-done.17.refs_2_ = bf16[384,384]{1,0:T(8,128)(2,1)S(1)} collective-permute-done((bf16[384,384]{1,0:T(8,128)(2,1)}, bf16[384,384]{1,0:T(8,128)(2,1)S(1)}, u32[]{:S(2)}, u32[]{:S(2)}) %collective-permute-start.17) | collective-permute-done | bytes 294944 | tf_op jit(solution)/shard_map/ppermute | solution.py:748
  137.4 1.8 %shard_map.371 = (f32[384,768]{1,0:T(8,128)}, f32[768,384]{1,0:T(8,128)}) custom-call(bf16[384,384]{1,0:T(8,128)(2,1)S(1)} %copy-done.5, bf16[384,384]{1,0:T(8,128)(2,1)S(1)} %collective-permute-done.16.refs_1_, bf16[384,384]{1,0:T(8,128)(2,1)S(1)} %collective-permute-done.17.refs_2_, bf16[384,384]{1,0:T(8,128)(2,1)S(1)} %collective-permute-done.18.refs_3_), custom_call_target="tpu_custom_call" | custom-call | flops 99999997952 | bytes 1 | tf_op jit(solution)/shard_map/pallas_call | solution.py:208
  139.2 2.3 %shard_map.372 = bf16[512,384]{1,0:T(8,128)(2,1)} custom-call(f32[512,384]{1,0:T(8,128)} %get-tuple-element.156.refs_0_, bf16[768,384]{1,0:T(8,128)(2,1)} %get-tuple-element.138.refs_1_, bf16[768,384]{1,0:T(8,128)(2,1)} %copy-done.2), custom_call_target="tpu_custom_call" | custom-call | flops 1 | bytes 1 | tf_op jit(solution)/shard_map/pallas_call | solution.py:208
  141.5 2.6 %shard_map.373 = bf16[512,384]{1,0:T(8,128)(2,1)} custom-call(bf16[512,384]{1,0:T(8,128)(2,1)S(1)} %get-tuple-element.153.refs_0_, bf16[512,384]{1,0:T(8,128)(2,1)S(1)} %collective-permute-done.15.refs_1_, bf16[384]{0:T(512)(128)(2,1)} %refs_2_.2, f32[512,384]{1,0:T(8,128)} %get-tuple-element.151.refs_3_, bf16[384]{0:T(512)(128)(2,1)} %refs_4_.5, ...), custom_call_target="tpu_custom_call" | custom-call | flops 1 | bytes 1 | tf_op jit(solution)/shard_map/pallas_call | solution.py:208
  144.0 0.4 collective-permute-done.19.refs_1_
  144.4 1.7 %shard_map.374.refs_0_ = bf16[272,384]{1,0:T(8,128)(2,1)} custom-call(bf16[272,384]{1,0:T(8,128)(2,1)} %shard_map.370.refs_0_, bf16[272,384]{1,0:T(8,128)(2,1)S(1)} %collective-permute-done.19.refs_1_), custom_call_target="tpu_custom_call" | custom-call | flops 1 | bytes 1 | tf_op jit(solution)/shard_map/pallas_call | solution.py:208
  146.1 0.9 collective-permute-start.22
  147.1 1.2 collective-permute-start.21
  148.2 1.5 collective-permute-start.20
  149.7 5.7 %collective-permute-done.22.refs_3_ = bf16[272,384]{1,0:T(8,128)(2,1)S(1)} collective-permute-done((bf16[272,384]{1,0:T(8,128)(2,1)}, bf16[272,384]{1,0:T(8,128)(2,1)S(1)}, u32[]{:S(2)}, u32[]{:S(2)}) %collective-permute-start.22) | collective-permute-done | bytes 208928 | tf_op jit(solution)/shard_map/ppermute | solution.py:748
  155.4 3.1 %collective-permute-done.21.refs_2_ = bf16[272,384]{1,0:T(8,128)(2,1)S(1)} collective-permute-done((bf16[272,384]{1,0:T(8,128)(2,1)}, bf16[272,384]{1,0:T(8,128)(2,1)S(1)}, u32[]{:S(2)}, u32[]{:S(2)}) %collective-permute-start.21) | collective-permute-done | bytes 208928 | tf_op jit(solution)/shard_map/ppermute | solution.py:748
  158.5 0.9 copy-done.3
  159.4 1.1 shard_map.375.refs_0_
  160.6 0.1 collective-permute-start.23
  160.6 2.4 %shard_map.376 = (f32[192,384]{1,0:T(8,128)}, f32[192,384]{1,0:T(8,128)}, f32[192,384]{1,0:T(8,128)}, f32[192,384]{1,0:T(8,128)}, f32[768]{0:T(1024)}, /*index=5...) custom-call(bf16[272,384]{1,0:T(8,128)(2,1)S(1)} %copy-done.3, ...), custom_call_target="tpu_custom_call" | custom-call | flops 1 | bytes 1 | tf_op jit(solution)/shard_map/pallas_call | solution.py:208
  163.1 1.0 shard_map.377
  (33 shorter events, 0.1 us)
Async XLA Ops:
  0.7 1.0 copy-start
  1.7 10.1 %copy-start.9 = (s32[1023]{0:T(1024)S(1)}, s32[1023]{0:T(1024)}, u32[]{:S(2)}) copy-start(s32[1023]{0:T(1024)} %param.25) | copy-start | bytes 12280
  1.7 10.7 %copy-start.6 = (s32[16]{0:T(128)S(1)}, s32[16]{0:T(128)}, u32[]{:S(2)}) copy-start(s32[16]{0:T(128)} %refs_0_.8) | copy-start | bytes 196
  3.4 23.0 %all-to-all-start = ((bf16[16,32,384]{2,1,0:T(8,128)(2,1)}), bf16[16,32,384]{2,1,0:T(8,128)(2,1)S(1)}, u32[]{:S(2)}, u32[]{:S(2)}) async-start(bf16[16,32,384]{2,1,0:T(8,128)(2,1)} %pad_maximum_fusion), calls=%async_computation | async-start | bytes 786432 | tf_op jit(solution)/shard_map/all_to_all | solution.py:741
  26.4 0.7 copy-start.8
  29.0 18.9 %all-to-all-start.1 = ((bf16[16,32,384]{2,1,0:T(8,128)(2,1)}), bf16[16,32,384]{2,1,0:T(8,128)(2,1)S(1)}, u32[]{:S(2)}, u32[]{:S(2)}) async-start(bf16[16,32,384]{2,1,0:T(8,128)(2,1)} %shard_map.358), calls=%async_computation.1 | async-start | bytes 786432 | tf_op jit(solution)/shard_map/all_to_all | solution.py:741
  35.9 1.8 %collective-permute-start = (bf16[512,384]{1,0:T(8,128)(2,1)S(1)}, bf16[512,384]{1,0:T(8,128)(2,1)S(1)}, u32[]{:S(2)}, u32[]{:S(2)}) collective-permute-start(bf16[512,384]{1,0:T(8,128)(2,1)S(1)} %get-tuple-element.101.refs_1_), channel_id=1, source_target_pairs={{0,1},{1,0},{2,3},{3,2},{4,5},{5,4},{6,7},{7,6},{8,9},{9,8},{10,11... | collective-permute-start | bytes 1179656 | tf_op jit(solution)/shard_map/ppermute | solution.py:737
  43.3 4.6 %collective-permute-start.1 = (bf16[512,384]{1,0:T(8,128)(2,1)S(1)}, bf16[512,384]{1,0:T(8,128)(2,1)S(1)}, u32[]{:S(2)}, u32[]{:S(2)}) collective-permute-start(bf16[512,384]{1,0:T(8,128)(2,1)S(1)} %get-tuple-element.102.refs_1_), channel_id=1, source_target_pairs={{0,1},{1,0},{2,3},{3,2},{4,5},{5,4},{6,7},{7,6},{8,9},{9,8},{10,11... | collective-permute-start | bytes 1179656 | tf_op jit(solution)/shard_map/ppermute | solution.py:737
  47.9 8.6 %copy-start.1 = (bf16[16,32,384]{2,1,0:T(8,128)(2,1)}, bf16[16,32,384]{2,1,0:T(8,128)(2,1)S(1)}, u32[]{:S(2)}) copy-start(bf16[16,32,384]{2,1,0:T(8,128)(2,1)S(1)} %all-to-all-done.1.refs_8_.refs_2_) | copy-start | bytes 1179652
  47.9 1.7 %collective-permute-start.2 = (bf16[16,32,384]{2,1,0:T(8,128)(2,1)S(1)}, bf16[16,32,384]{2,1,0:T(8,128)(2,1)S(1)}, u32[]{:S(2)}, u32[]{:S(2)}) collective-permute-start(bf16[16,32,384]{2,1,0:T(8,128)(2,1)S(1)} %all-to-all-done.1.refs_8_.refs_2_), channel_id=1, source_target_pairs={{0,1},{1,0},{2,3},{3,2},{4,5},{5,4},{6,7},{7,6},{8,9},{9,8},{10,11... | collective-permute-start | bytes 1179656 | tf_op jit(solution)/shard_map/ppermute | solution.py:737
  49.6 6.8 %copy-start.4 = (bf16[16,32,384]{2,1,0:T(8,128)(2,1)}, bf16[16,32,384]{2,1,0:T(8,128)(2,1)S(1)}, u32[]{:S(2)}) copy-start(bf16[16,32,384]{2,1,0:T(8,128)(2,1)S(1)} %collective-permute-done.2.refs_9_.refs_3_) | copy-start | bytes 1179652
  56.5 3.7 %collective-permute-start.3 = (bf16[512,384]{1,0:T(8,128)(2,1)S(1)}, bf16[512,384]{1,0:T(8,128)(2,1)S(1)}, u32[]{:S(2)}, u32[]{:S(2)}) collective-permute-start(bf16[512,384]{1,0:T(8,128)(2,1)S(1)} %get-tuple-element.109.refs_1_), channel_id=1, source_target_pairs={{0,1},{1,0},{2,3},{3,2},{4,5},{5,4},{6,7},{7,6},{8,9},{9,8},{10,11... | collective-permute-start | bytes 1179656 | tf_op jit(solution)/shard_map/ppermute | solution.py:737
  56.7 21.0 %collective-permute-start.4 = (bf16[384,384]{1,0:T(8,128)(2,1)}, bf16[384,384]{1,0:T(8,128)(2,1)S(1)}, u32[]{:S(2)}, u32[]{:S(2)}) collective-permute-start(bf16[384,384]{1,0:T(8,128)(2,1)} %get-tuple-element.120), channel_id=1, source_target_pairs={{0,2},{2,0},{4,6},{6,4},{8,10},{10,8},{12,14},{14,12},{16,18},{18,... | collective-permute-start | bytes 884744 | tf_op jit(solution)/shard_map/ppermute | solution.py:748
  57.2 20.4 %collective-permute-start.5 = (bf16[384,384]{1,0:T(8,128)(2,1)}, bf16[384,384]{1,0:T(8,128)(2,1)S(1)}, u32[]{:S(2)}, u32[]{:S(2)}) collective-permute-start(bf16[384,384]{1,0:T(8,128)(2,1)} %get-tuple-element.121), channel_id=1, source_target_pairs={{0,4},{2,6},{4,0},{6,2},{8,12},{10,14},{12,8},{14,10},{16,20},{18,... | collective-permute-start | bytes 884744 | tf_op jit(solution)/shard_map/ppermute | solution.py:748
  58.1 19.6 %collective-permute-start.6 = (bf16[384,384]{1,0:T(8,128)(2,1)}, bf16[384,384]{1,0:T(8,128)(2,1)S(1)}, u32[]{:S(2)}, u32[]{:S(2)}) collective-permute-start(bf16[384,384]{1,0:T(8,128)(2,1)} %get-tuple-element.122), channel_id=1, source_target_pairs={{0,6},{2,4},{4,2},{6,0},{8,14},{10,12},{12,10},{14,8},{16,22},{18,... | collective-permute-start | bytes 884744 | tf_op jit(solution)/shard_map/ppermute | solution.py:748
  79.6 14.1 %collective-permute-start.7 = (bf16[384,384]{1,0:T(8,128)(2,1)}, bf16[384,384]{1,0:T(8,128)(2,1)S(1)}, u32[]{:S(2)}, u32[]{:S(2)}) collective-permute-start(bf16[384,384]{1,0:T(8,128)(2,1)} %shard_map.362.refs_0_), channel_id=1, source_target_pairs={{0,8},{2,10},{4,12},{6,14},{8,0},{10,2},{12,4},{14,6},{16,24},{18,... | collective-permute-start | bytes 884744 | tf_op jit(solution)/shard_map/ppermute | solution.py:864
  95.5 2.3 %collective-permute-start.8 = (bf16[768,384]{1,0:T(8,128)(2,1)}, bf16[768,384]{1,0:T(8,128)(2,1)S(1)}, u32[]{:S(2)}, u32[]{:S(2)}) collective-permute-start(bf16[768,384]{1,0:T(8,128)(2,1)} %get-tuple-element.138.refs_1_), channel_id=1, source_target_pairs={{0,1},{1,0},{2,3},{3,2},{4,5},{5,4},{6,7},{7,6},{8,9},{9,8},{10,11... | collective-permute-start | bytes 1769480 | tf_op jit(solution)/shard_map/ppermute | solution.py:737
  95.5 23.4 %collective-permute-start.12 = (bf16[384,384]{1,0:T(8,128)(2,1)}, bf16[384,384]{1,0:T(8,128)(2,1)S(1)}, u32[]{:S(2)}, u32[]{:S(2)}) collective-permute-start(bf16[384,384]{1,0:T(8,128)(2,1)} %shard_map.364.refs_0_), channel_id=1, source_target_pairs={{0,16},{2,18},{4,20},{6,22},{8,24},{10,26},{12,28},{14,30},{16,0},... | collective-permute-start | bytes 884744 | tf_op jit(solution)/shard_map/ppermute | solution.py:864
  97.7 4.2 %copy-start.2 = (bf16[768,384]{1,0:T(8,128)(2,1)}, bf16[768,384]{1,0:T(8,128)(2,1)S(1)}, u32[]{:S(2)}) copy-start(bf16[768,384]{1,0:T(8,128)(2,1)S(1)} %collective-permute-done.8.refs_10_.refs_2_) | copy-start | bytes 1769476
  97.8 7.8 %copy-start.7 = (s32[16]{0:T(128)S(1)}, s32[16]{0:T(128)}, u32[]{:S(2)}) copy-start(s32[16]{0:T(128)} %refs_1_.3) | copy-start | bytes 196
  102.0 15.2 %collective-permute-start.9 = (bf16[272,384]{1,0:T(8,128)(2,1)}, bf16[272,384]{1,0:T(8,128)(2,1)S(1)}, u32[]{:S(2)}, u32[]{:S(2)}) collective-permute-start(bf16[272,384]{1,0:T(8,128)(2,1)} %get-tuple-element.143), channel_id=1, source_target_pairs={{0,2},{2,0},{4,6},{6,4},{8,10},{10,8},{12,14},{14,12},{16,18},{18,... | collective-permute-start | bytes 626696 | tf_op jit(solution)/shard_map/ppermute | solution.py:748
  102.6 14.6 %collective-permute-start.10 = (bf16[272,384]{1,0:T(8,128)(2,1)}, bf16[272,384]{1,0:T(8,128)(2,1)S(1)}, u32[]{:S(2)}, u32[]{:S(2)}) collective-permute-start(bf16[272,384]{1,0:T(8,128)(2,1)} %get-tuple-element.144), channel_id=1, source_target_pairs={{0,4},{2,6},{4,0},{6,2},{8,12},{10,14},{12,8},{14,10},{16,20},{18,... | collective-permute-start | bytes 626696 | tf_op jit(solution)/shard_map/ppermute | solution.py:748
  103.5 13.7 %collective-permute-start.11 = (bf16[272,384]{1,0:T(8,128)(2,1)}, bf16[272,384]{1,0:T(8,128)(2,1)S(1)}, u32[]{:S(2)}, u32[]{:S(2)}) collective-permute-start(bf16[272,384]{1,0:T(8,128)(2,1)} %get-tuple-element.145), channel_id=1, source_target_pairs={{0,6},{2,4},{4,2},{6,0},{8,14},{10,12},{12,10},{14,8},{16,22},{18,... | collective-permute-start | bytes 626696 | tf_op jit(solution)/shard_map/ppermute | solution.py:748
  120.8 16.6 %copy-start.5 = (bf16[384,384]{1,0:T(8,128)(2,1)S(1)}, bf16[384,384]{1,0:T(8,128)(2,1)}, u32[]{:S(2)}) copy-start(bf16[384,384]{1,0:T(8,128)(2,1)} %shard_map.368.refs_0_) | copy-start | bytes 884740
  120.8 4.6 %collective-permute-start.13 = (bf16[512,384]{1,0:T(8,128)(2,1)S(1)}, bf16[512,384]{1,0:T(8,128)(2,1)S(1)}, u32[]{:S(2)}, u32[]{:S(2)}) collective-permute-start(bf16[512,384]{1,0:T(8,128)(2,1)S(1)} %get-tuple-element.149.refs_1_), channel_id=1, source_target_pairs={{0,1},{1,0},{2,3},{3,2},{4,5},{5,4},{6,7},{7,6},{8,9},{9,8},{10,11... | collective-permute-start | bytes 1179656 | tf_op jit(solution)/shard_map/ppermute | solution.py:737
  120.9 13.4 %collective-permute-start.18 = (bf16[384,384]{1,0:T(8,128)(2,1)}, bf16[384,384]{1,0:T(8,128)(2,1)S(1)}, u32[]{:S(2)}, u32[]{:S(2)}) collective-permute-start(bf16[384,384]{1,0:T(8,128)(2,1)} %shard_map.368.refs_0_), channel_id=1, source_target_pairs={{0,6},{2,4},{4,2},{6,0},{8,14},{10,12},{12,10},{14,8},{16,22},{18,... | collective-permute-start | bytes 884744 | tf_op jit(solution)/shard_map/ppermute | solution.py:748
  121.8 15.6 %collective-permute-start.17 = (bf16[384,384]{1,0:T(8,128)(2,1)}, bf16[384,384]{1,0:T(8,128)(2,1)S(1)}, u32[]{:S(2)}, u32[]{:S(2)}) collective-permute-start(bf16[384,384]{1,0:T(8,128)(2,1)} %shard_map.368.refs_0_), channel_id=1, source_target_pairs={{0,4},{2,6},{4,0},{6,2},{8,12},{10,14},{12,8},{14,10},{16,20},{18,... | collective-permute-start | bytes 884744 | tf_op jit(solution)/shard_map/ppermute | solution.py:748
  123.0 14.4 %collective-permute-start.16 = (bf16[384,384]{1,0:T(8,128)(2,1)}, bf16[384,384]{1,0:T(8,128)(2,1)S(1)}, u32[]{:S(2)}, u32[]{:S(2)}) collective-permute-start(bf16[384,384]{1,0:T(8,128)(2,1)} %shard_map.368.refs_0_), channel_id=1, source_target_pairs={{0,2},{2,0},{4,6},{6,4},{8,10},{10,8},{12,14},{14,12},{16,18},{18,... | collective-permute-start | bytes 884744 | tf_op jit(solution)/shard_map/ppermute | solution.py:748
  124.4 6.9 %collective-permute-start.14 = (bf16[272,384]{1,0:T(8,128)(2,1)}, bf16[272,384]{1,0:T(8,128)(2,1)S(1)}, u32[]{:S(2)}, u32[]{:S(2)}) collective-permute-start(bf16[272,384]{1,0:T(8,128)(2,1)} %shard_map.367.refs_0_), channel_id=1, source_target_pairs={{0,8},{2,10},{4,12},{6,14},{8,0},{10,2},{12,4},{14,6},{16,24},{18,... | collective-permute-start | bytes 626696 | tf_op jit(solution)/shard_map/ppermute | solution.py:864
  133.0 11.5 %collective-permute-start.19 = (bf16[272,384]{1,0:T(8,128)(2,1)}, bf16[272,384]{1,0:T(8,128)(2,1)S(1)}, u32[]{:S(2)}, u32[]{:S(2)}) collective-permute-start(bf16[272,384]{1,0:T(8,128)(2,1)} %shard_map.370.refs_0_), channel_id=1, source_target_pairs={{0,16},{2,18},{4,20},{6,22},{8,24},{10,26},{12,28},{14,30},{16,0},... | collective-permute-start | bytes 626696 | tf_op jit(solution)/shard_map/ppermute | solution.py:864
  134.3 7.2 %collective-permute-start.15 = (bf16[512,384]{1,0:T(8,128)(2,1)S(1)}, bf16[512,384]{1,0:T(8,128)(2,1)S(1)}, u32[]{:S(2)}, u32[]{:S(2)}) collective-permute-start(bf16[512,384]{1,0:T(8,128)(2,1)S(1)} %get-tuple-element.153.refs_0_), channel_id=1, source_target_pairs={{0,1},{1,0},{2,3},{3,2},{4,5},{5,4},{6,7},{7,6},{8,9},{9,8},{10,11... | collective-permute-start | bytes 1179656 | tf_op jit(solution)/shard_map/ppermute | solution.py:737
  146.1 9.2 %collective-permute-start.22 = (bf16[272,384]{1,0:T(8,128)(2,1)}, bf16[272,384]{1,0:T(8,128)(2,1)S(1)}, u32[]{:S(2)}, u32[]{:S(2)}) collective-permute-start(bf16[272,384]{1,0:T(8,128)(2,1)} %shard_map.374.refs_0_), channel_id=1, source_target_pairs={{0,6},{2,4},{4,2},{6,0},{8,14},{10,12},{12,10},{14,8},{16,22},{18,... | collective-permute-start | bytes 626696 | tf_op jit(solution)/shard_map/ppermute | solution.py:748
  147.1 11.4 %collective-permute-start.21 = (bf16[272,384]{1,0:T(8,128)(2,1)}, bf16[272,384]{1,0:T(8,128)(2,1)S(1)}, u32[]{:S(2)}, u32[]{:S(2)}) collective-permute-start(bf16[272,384]{1,0:T(8,128)(2,1)} %shard_map.374.refs_0_), channel_id=1, source_target_pairs={{0,4},{2,6},{4,0},{6,2},{8,12},{10,14},{12,8},{14,10},{16,20},{18,... | collective-permute-start | bytes 626696 | tf_op jit(solution)/shard_map/ppermute | solution.py:748
  148.2 10.3 %collective-permute-start.20 = (bf16[272,384]{1,0:T(8,128)(2,1)}, bf16[272,384]{1,0:T(8,128)(2,1)S(1)}, u32[]{:S(2)}, u32[]{:S(2)}) collective-permute-start(bf16[272,384]{1,0:T(8,128)(2,1)} %shard_map.374.refs_0_), channel_id=1, source_target_pairs={{0,2},{2,0},{4,6},{6,4},{8,10},{10,8},{12,14},{14,12},{16,18},{18,... | collective-permute-start | bytes 626696 | tf_op jit(solution)/shard_map/ppermute | solution.py:748
  158.5 0.9 copy-start.3
  160.6 2.5 %collective-permute-start.23 = (bf16[256,384]{1,0:T(8,128)(2,1)S(1)}, bf16[256,384]{1,0:T(8,128)(2,1)S(1)}, u32[]{:S(2)}, u32[]{:S(2)}) collective-permute-start(bf16[256,384]{1,0:T(8,128)(2,1)S(1)} %shard_map.375.refs_0_), channel_id=1, source_target_pairs={{0,1},{1,0},{2,3},{3,2},{4,5},{5,4},{6,7},{7,6},{8,9},{9,8},{10,11... | collective-permute-start | bytes 589832 | tf_op jit(solution)/shard_map/ppermute | solution.py:737

commit v4 on v3

--- a/solution.py
+++ b/solution.py
@@ -308,49 +308,43 @@
     )
 
 
-def attend(length, q, k, v, tab, wout, ctx, attn_out, far_scratch, prob_out):
-    heads, rows, _ = q.shape
+def attend(length, count, q, k, v, tab, ctx, far_scratch, prob_out):
+    rows = q.shape[1]
     window = rows + BLOCK
     scale = 1.0 / math.sqrt(3.0 * HEAD_DIM)
     key_ok = lax.broadcasted_iota(jnp.int32, (1, rows), 1) < length
+    blocks = [slice(i * BLOCK, (i + 1) * BLOCK) for i in range(rows // BLOCK)]
 
     def head(h, carry):
-        keys = k[h]
-        values = v[h]
-        for b in range(rows // BLOCK):
-            j0 = b * BLOCK
-            w0 = rows - BLOCK - j0
-            far = mm(k[h, j0 : j0 + BLOCK, :], tab[0, h, :, w0 : w0 + window])
+        for here in blocks:
+            w0 = rows - BLOCK - here.start
+            far = mm(k[h, here, :], tab[0, h, :, w0 : w0 + window])
             far = pltpu.roll(far, window - BLOCK, 1, stride=1, stride_axis=0)[:, :rows]
-            far_scratch[:, j0 : j0 + BLOCK] = far.T
-        for a in range(rows // BLOCK):
-            i0 = a * BLOCK
-            w0 = rows - BLOCK - i0
-            block_q = q[h, i0 : i0 + BLOCK, :]
-            near = mm(block_q, tab[1, h, :, w0 : w0 + window])
+            far_scratch[:, here] = far.T
+        for here in blocks:
+            w0 = rows - BLOCK - here.start
+            near = mm(q[h, here, :], tab[1, h, :, w0 : w0 + window])
             near = pltpu.roll(near, window - BLOCK, 1, stride=1, stride_axis=0)[:, :rows]
-            score = (mm(block_q, keys, NT) + near + far_scratch[i0 : i0 + BLOCK, :]) * scale
+            far_scratch[here, :] += near
+        for here in blocks:
+            score = (mm(q[h, here, :], k[h], NT) + far_scratch[here, :]) * scale
             score = jnp.where(key_ok, score, -1e30)
             top = jnp.max(score, axis=1, keepdims=True)
             weights = jnp.exp(score - top)
-            row_ok = i0 + lax.broadcasted_iota(jnp.int32, (BLOCK, 1), 0) < length
+            row_ok = here.start + lax.broadcasted_iota(jnp.int32, (BLOCK, 1), 0) < length
             norm = jnp.where(row_ok, 1.0 / jnp.sum(weights, axis=1, keepdims=True), 0.0)
             prob = (weights * norm).astype(LOW)
             if prob_out is not None:
-                prob_out[h, i0 : i0 + BLOCK, :] = prob
-            ctx[h, i0 : i0 + BLOCK, :] = mm(prob, values).astype(LOW)
+                prob_out[h, here, :] = prob
+            ctx[h, here, :] = mm(prob, v[h]).astype(LOW)
         return carry
 
-    lax.fori_loop(0, heads, head, 0)
-    total = mm(ctx[0], wout[0:HEAD_DIM, :])
-    for h in range(1, heads):
-        total += mm(ctx[h], wout[h * HEAD_DIM : (h + 1) * HEAD_DIM, :])
-    attn_out[...] = total.astype(LOW)
-
-
-def attention_forward(
-    lengths, x, relative, table, wq, bq, wk, bk, wv, bv, wout,
-    q_out, k_out, v_out, tab_out, prob_out, ctx_out, attn_out, far_scratch,
+    lax.fori_loop(0, count, head, 0)
+
+
+def attention_first(
+    lengths, x, relative, table, wq, bq, wk, bk, wv, bv,
+    q_out, k_out, v_out, tab_out, prob_out, ctx_out, far_scratch,
 ):
     length = lengths[lax.axis_index("dp")]
     project(x[...], (wq, wk, wv), (bq, bk, bv), (q_out, k_out, v_out))
@@ -363,7 +357,19 @@
         for h in range(q_out.shape[0]):
             tab_out[slot, h] = spread[h * HEAD_DIM : (h + 1) * HEAD_DIM]
     send(tab_out)
-    attend(length, q_out, k_out, v_out, tab_out, wout, ctx_out, attn_out, far_scratch, prob_out)
+    attend(length, ctx_out.shape[0], q_out, k_out, v_out, tab_out, ctx_out, far_scratch, prob_out)
+
+
+def attention_rest(
+    lengths, q, k, v, tab, wout, ctx_before, prob_out, ctx_out, attn_out, far_scratch
+):
+    length = lengths[lax.axis_index("dp")]
+    ready(q, k, v, tab)
+    attend(length, q.shape[0], q, k, v, tab, ctx_out, far_scratch, prob_out)
+    send(prob_out)
+    heads = [ctx_before[h] for h in range(ctx_before.shape[0])]
+    heads += [ctx_out[h] for h in range(q.shape[0])]
+    attn_out[...] = mm(jnp.concatenate(heads, axis=1), wout[...]).astype(LOW)
 
 
 def attention_dealt(
@@ -375,7 +381,9 @@
     send(x_out)
     project(x_out[...], (wq, wk, wv), (bq, bk, bv), (q, k, v))
     ready(tab)
-    attend(length, q, k, v, tab, wout, ctx, attn_out, far_scratch, None)
+    attend(length, q.shape[0], q, k, v, tab, ctx, far_scratch, None)
+    heads = [ctx[h] for h in range(q.shape[0])]
+    attn_out[...] = mm(jnp.concatenate(heads, axis=1), wout[...]).astype(LOW)
 
 
 def row_norm(values):
@@ -391,31 +399,36 @@
 
 
 def ffn_forward(
-    keep, x, mine, theirs, bout, gain, shift, wup, bup, wdown, normed_out, down_out,
-    inverse_out=None, hidden_out=None, act_out=None, slope_out=None,
+    keep, x, mine, theirs, bout, gain, shift, wup, bup, wdown, normed_out, down_out, *rest
 ):
+    low_scratch, act_scratch = rest[-2:]
+    if keep:
+        inverse_out, hidden_out, act_out, slope_out = rest[:4]
     rows = x.shape[0]
-    ready(x, mine, theirs, bout, gain, shift, wup, bup, wdown)
-
-    def block(i, carry):
-        here = pl.ds(pl.multiple_of(i * BLOCK, BLOCK), BLOCK)
+    blocks = [slice(i * BLOCK, (i + 1) * BLOCK) for i in range(rows // BLOCK)]
+    for here in blocks:
         attn = mine[here, :].astype(WIDE) + theirs[here, :].astype(WIDE) + wide_row(bout)
         normed, inverse = row_norm(x[here, :].astype(WIDE) + attn)
         normed_out[here, :] = normed
         low = (normed * wide_row(gain) + wide_row(shift)).astype(LOW)
-        u = mm(low, wup[...]) + wide_row(bup)
-        cdf = 0.5 * (1.0 + lax.erf(u * ROOT_HALF))
-        act = (u * cdf).astype(LOW)
+        low_scratch[here, :] = low
         if keep:
             inverse_out[here, :] = inverse
             hidden_out[here, :] = low
+    send(normed_out)
+    for here in blocks:
+        u = mm(low_scratch[here, :], wup[...]) + wide_row(bup)
+        cdf = 0.5 * (1.0 + lax.erf(u * ROOT_HALF))
+        act = (u * cdf).astype(LOW)
+        act_scratch[here, :] = act
+        if keep:
             act_out[here, :] = act
             density = jnp.exp(-0.5 * u * u) * INV_ROOT_TAU
             slope_out[here, :] = (cdf + u * density).astype(LOW)
-        down_out[here, :] = mm(act, wdown[...]).astype(LOW)
-        return carry
-
-    lax.fori_loop(0, rows // BLOCK, block, 0)
+    if keep:
+        send(inverse_out, hidden_out, act_out, slope_out)
+    for here in blocks:
+        down_out[here, :] = mm(act_scratch[here, :], wdown[...]).astype(LOW)
 
 
 def wide_row(vector):
@@ -494,58 +507,54 @@
     put_zeros(buffer_out, chunk, 2 * units)
 
 
-def head_backward(h, q, k, v, tab, prob, gctx, anti, g_out, gpq_out, gpk_out, gs_scratch, gp_scratch):
+def head_backward(
+    h, q, k, v, tab, prob, gctx, anti, g_out, gpq_out, gpk_out,
+    gs_scratch, gp_scratch, turned_scratch, moved_scratch,
+):
     rows = q.shape[1]
     span = tab.shape[3]
     window = rows + BLOCK
     scale = 1.0 / math.sqrt(3.0 * HEAD_DIM)
-    blocks = rows // BLOCK
+    blocks = [slice(i * BLOCK, (i + 1) * BLOCK) for i in range(rows // BLOCK)]
     pad = jnp.zeros((BLOCK, BLOCK), WIDE)
-    keys = k[h]
-    queries = q[h]
+    for here in blocks:
+        weights = prob[h, here, :].astype(WIDE)
+        gprob = mm(gctx[h, here, :], v[h], NT)
+        dots = jnp.sum(weights * gprob, axis=1, keepdims=True)
+        gs_scratch[here, :] = (weights * (gprob - dots)).astype(LOW)
+    g_out[2, h] = mm(prob[h], gctx[h], TN).astype(LOW)
+    for slot, (source, other) in enumerate(((q, k), (k, q))):
+        for here in blocks:
+            if slot == 0:
+                turned = mm(anti, gs_scratch[here, :])
+            else:
+                turned = mm(anti, gs_scratch[:, here], NT)
+            turned_scratch[slot, here, :] = turned.astype(LOW)
+            moved_scratch[slot, here, :] = pltpu.roll(
+                jnp.concatenate([turned, pad], axis=1), 1, 1, stride=1, stride_axis=0
+            ).astype(LOW)
     gp_scratch[...] = jnp.zeros((2, HEAD_DIM, span), WIDE)
-    for i in range(blocks):
-        i0 = i * BLOCK
-        w0 = rows - BLOCK - i0
-        weights = prob[h, i0 : i0 + BLOCK, :].astype(WIDE)
-        gprob = mm(gctx[h, i0 : i0 + BLOCK, :], v[h], NT)
-        dots = jnp.sum(weights * gprob, axis=1, keepdims=True)
-        gs = (weights * (gprob - dots)).astype(LOW)
-        gs_scratch[i0 : i0 + BLOCK, :] = gs
-        turned = mm(anti, gs)
-        moved = pltpu.roll(
-            jnp.concatenate([turned, pad], axis=1), 1, 1, stride=1, stride_axis=0
-        ).astype(LOW)
-        table_here = tab[1, h, :, w0 : w0 + window]
-        gq = (mm(turned.astype(LOW), keys) + mm(moved, table_here, NT)) * scale
-        g_out[0, h, i0 : i0 + BLOCK, :] = mm(anti, gq.astype(LOW)).astype(LOW)
-        turned_q = mm(anti, q[h, i0 : i0 + BLOCK, :]).astype(LOW)
-        gp_scratch[1, :, w0 : w0 + window] += mm(turned_q, moved, TN)
-    for b in range(blocks):
-        j0 = b * BLOCK
-        w0 = rows - BLOCK - j0
-        turned = mm(anti, gs_scratch[:, j0 : j0 + BLOCK], NT)
-        moved = pltpu.roll(
-            jnp.concatenate([turned, pad], axis=1), 1, 1, stride=1, stride_axis=0
-        ).astype(LOW)
-        table_here = tab[0, h, :, w0 : w0 + window]
-        gk = (mm(turned.astype(LOW), queries) + mm(moved, table_here, NT)) * scale
-        g_out[1, h, j0 : j0 + BLOCK, :] = mm(anti, gk.astype(LOW)).astype(LOW)
-        turned_k = mm(anti, k[h, j0 : j0 + BLOCK, :]).astype(LOW)
-        gp_scratch[0, :, w0 : w0 + window] += mm(turned_k, moved, TN)
-    g_out[2, h] = mm(prob[h], gctx[h], TN).astype(LOW)
+    for slot, (source, other) in enumerate(((q, k), (k, q))):
+        for here in blocks:
+            w0 = rows - BLOCK - here.start
+            moved = moved_scratch[slot, here, :]
+            table_here = tab[1 - slot, h, :, w0 : w0 + window]
+            grad = (mm(turned_scratch[slot, here, :], other[h]) + mm(moved, table_here, NT)) * scale
+            g_out[slot, h, here, :] = mm(anti, grad.astype(LOW)).astype(LOW)
+            turned = mm(anti, source[h, here, :]).astype(LOW)
+            gp_scratch[1 - slot, :, w0 : w0 + window] += mm(turned, moved, TN)
     gpq_out[h] = gp_scratch[0].astype(LOW)
     gpk_out[h] = gp_scratch[1].astype(LOW)
 
 
 def attention_backward(
-    wout, mine, theirs, gf, normed, inverse, gain, ctx, q, k, v, tab, prob,
+    wout, mine, theirs, gf, normed, inverse, gain, ctx, ctx_last, q, k, v, tab, prob,
     gp_out, wout_out, small_out, gctx_out, g_out, gpq_out, gpk_out,
-    gpb_scratch, gs_scratch, gp_scratch, gctx_scratch,
+    gpb_scratch, gctx_scratch, *scratch,
 ):
-    heads, rows, _ = ctx.shape
+    first, rows, _ = ctx.shape
+    heads = first + 1
     width = gp_out.shape[1]
-    first = q.shape[0]
     blocks = rows // BLOCK
     sums = [jnp.zeros((1, width), WIDE) for _ in range(3)]
     for i in range(blocks):
@@ -565,19 +574,21 @@
             if h < first:
                 gctx_scratch[h, here, :] = part
             else:
-                gctx_out[h - first, here, :] = part
+                gctx_out[0, here, :] = part
     small_out[...] = jnp.zeros(small_out.shape, WIDE)
     for n in range(3):
         small_out[2 + n : 3 + n, :] = sums[n]
     for h in range(heads):
-        wout_out[h * HEAD_DIM : (h + 1) * HEAD_DIM, :] = mm(ctx[h], gpb_scratch[...], TN).astype(LOW)
+        wout_out[h * HEAD_DIM : (h + 1) * HEAD_DIM, :] = mm(
+            ctx[h] if h < first else ctx_last[0], gpb_scratch[...], TN
+        ).astype(LOW)
     send(gp_out, small_out, wout_out, gctx_out)
     anti = anti_diagonal()
     ready(q, k, v, tab, prob)
 
     def head(h, carry):
         head_backward(
-            h, q, k, v, tab, prob, gctx_scratch, anti, g_out, gpq_out, gpk_out, gs_scratch, gp_scratch
+            h, q, k, v, tab, prob, gctx_scratch, anti, g_out, gpq_out, gpk_out, *scratch
         )
         return carry
 
@@ -587,7 +598,7 @@
 def attention_backward_last(
     table, wq, wk, wv, gctx, q, k, v, tab, prob, before, gpq_before, gpk_before,
     g_out, gpq_out, gpk_out, send_out, keep_out,
-    gs_scratch, gp_scratch, gpq_scratch, gpk_scratch, rel_scratch,
+    gpq_scratch, gpk_scratch, rel_scratch, *scratch,
 ):
     side = lax.axis_index("tensor")
     buckets = rel_scratch.shape[0]
@@ -595,7 +606,7 @@
     scale = 1.0 / math.sqrt(3.0 * HEAD_DIM)
     anti = anti_diagonal()
     head_backward(
-        0, q, k, v, tab, prob, gctx, anti, g_out, gpq_scratch, gpk_scratch, gs_scratch, gp_scratch
+        0, q, k, v, tab, prob, gctx, anti, g_out, gpq_scratch, gpk_scratch, *scratch
     )
     send(g_out)
     hot = one_hot(table, buckets)
@@ -663,14 +674,6 @@
         here = slice(i * BLOCK, (i + 1) * BLOCK)
         both = mine[here, :].astype(WIDE) + theirs[here, :].astype(WIDE)
         grad_out[here, :] = (gp[here, :] + both).astype(LOW)
-
-
-def add_up(*refs):
-    parts, sum_out = refs[:-1], refs[-1]
-    acc = parts[0][...].astype(WIDE)
-    for other in parts[1:]:
-        acc += other[...].astype(WIDE)
-    sum_out[...] = acc.astype(LOW)
 
 
 def chunks(gathered, first, count):
@@ -786,6 +789,7 @@
     total = dealing.shape[0]
     part = w_query.shape[1]
     heads = part // HEAD_DIM
+    before = heads - 1
     units = w_up.shape[1]
     half = rows // 2
     span = 2 * rows
@@ -814,12 +818,12 @@
     table = table.reshape(span // BLOCK, BLOCK)
     projections = (w_query.T, b_query, w_key.T, b_key, w_value.T, b_value, w_out)
     head_shape = (heads, rows, HEAD_DIM)
-    q, k, v, tab, prob, ctx, attn_part = run(
-        attention_forward,
+    q, k, v, tab, prob, ctx = run(
+        attention_first,
         [(head_shape, LOW)] * 3
-        + [((2, heads, HEAD_DIM, span), LOW), ((heads, rows, rows), LOW)]
-        + [(head_shape, LOW), Here((rows, width), LOW)],
-        (lengths, x, relative, table) + projections,
+        + [((2, heads, HEAD_DIM, span), LOW), ((before, rows, rows), LOW),
+           ((before, rows, HEAD_DIM), LOW)],
+        (lengths, x, relative, table) + projections[:6],
         scratch=[pltpu.VMEM((rows, rows), WIDE)],
         smem=1,
     )
@@ -830,6 +834,15 @@
     sequence.last = turned
     dealt_mine = exchange(turned)
     dealt_theirs = swap(dealt_mine)
+    prob_last, ctx_last, attn_part = run(
+        attention_rest,
+        [((1, rows, rows), LOW), ((1, rows, HEAD_DIM), LOW), Here((rows, width), LOW)],
+        (lengths,)
+        + tuple(Part(array, 0, before, 1) for array in (q, k, v))
+        + (Part(tab, 1, before, 1), w_out, ctx),
+        scratch=[pltpu.VMEM((rows, rows), WIDE)],
+        smem=1,
+    )
     attn_got = swap(attn_part)
     ffn_weights = (b_out, attn_gain, attn_shift, w_up, b_up, w_down)
     normed, down_part, inverse, hidden, act, slope = run(
@@ -837,6 +850,7 @@
         [((rows, width), WIDE), Here((rows, width), LOW), ((rows, 1), WIDE), ((rows, width), LOW),
          ((rows, units), LOW), ((rows, units), LOW)],
         (x, Here(attn_part), Here(attn_got)) + ffn_weights,
+        scratch=[pltpu.VMEM((rows, width), LOW), pltpu.VMEM((rows, units), LOW)],
     )
     down_got = swap(down_part)
     hidden_part, gf, small_ffn, near_one = run(
@@ -856,8 +870,11 @@
     near_one[1:] = trade(near_one[1:], near_groups)
 
     def total_of(own, got):
-        (out,) = run(add_up, [(own.shape, LOW)], (own,) + tuple(Here(array) for array in got))
-        return out
+        acc = after(own, sequence.last).astype(WIDE)
+        for other in got:
+            acc += other.astype(WIDE)
+        sequence.last = acc.astype(LOW)
+        return sequence.last
 
     def far_step(array, step):
         reach = inner << step
@@ -868,21 +885,25 @@
     def gather_near(line):
         return Stack([line] + trade([line] * (inner - 1), near_groups))
 
-    before = heads - 1
+    head_scratch = [
+        pltpu.VMEM((rows, rows), LOW),
+        pltpu.VMEM((2, HEAD_DIM, span), WIDE),
+        pltpu.VMEM((2, rows, rows), LOW),
+        pltpu.VMEM((2, rows, rows + BLOCK), LOW),
+    ]
     gp, wout_grad, small_attn, gctx, g_before, gpq_before, gpk_before = run(
         attention_backward,
         [((rows, width), WIDE), ((part, width), LOW), ((8, width), WIDE),
          ((1, rows, HEAD_DIM), LOW), ((3, before, rows, HEAD_DIM), LOW),
          ((before, HEAD_DIM, span), LOW), ((before, HEAD_DIM, span), LOW)],
-        (w_out, Here(hidden_part), Here(hidden_got), gf, normed, inverse, attn_gain, ctx)
+        (w_out, Here(hidden_part), Here(hidden_got), gf, normed, inverse, attn_gain, ctx, ctx_last)
         + tuple(Part(array, 0, 0, before) for array in (q, k, v))
-        + (Part(tab, 1, 0, before), Part(prob, 0, 0, before)),
+        + (Part(tab, 1, 0, before), prob),
         scratch=[
             pltpu.VMEM((rows, width), LOW),
-            pltpu.VMEM((rows, rows), LOW),
-            pltpu.VMEM((2, HEAD_DIM, span), WIDE),
             pltpu.VMEM((before, rows, HEAD_DIM), LOW),
-        ],
+        ]
+        + head_scratch,
     )
     line_one = total_of(near_one[0], near_one[1:])
     got_one = far_step(line_one, 0)
@@ -892,14 +913,13 @@
          ((rows + half, width), LOW), ((half, width), LOW)],
         (table, w_query.T, w_key.T, w_value.T, gctx)
         + tuple(Part(array, 0, before, 1) for array in (q, k, v))
-        + (Part(tab, 1, before, 1), Part(prob, 0, before, 1), g_before, gpq_before, gpk_before),
+        + (Part(tab, 1, before, 1), prob_last, g_before, gpq_before, gpk_before),
         scratch=[
-            pltpu.VMEM((rows, rows), LOW),
-            pltpu.VMEM((2, HEAD_DIM, span), WIDE),
             pltpu.VMEM((1, HEAD_DIM, span), LOW),
             pltpu.VMEM((1, HEAD_DIM, span), LOW),
             pltpu.VMEM((rows, width), WIDE),
-        ],
+        ]
+        + head_scratch,
     )
     for step in range(1, steps):
         line_one = total_of(line_one, [got_one])
@@ -929,6 +949,7 @@
         with_statics(ffn_forward, False),
         [((rows, width), WIDE), Here((rows, width), LOW)],
         (x_dealt, Here(attn_dealt), Here(attn_dealt_got)) + ffn_weights,
+        scratch=[pltpu.VMEM((rows, width), LOW), pltpu.VMEM((rows, units), LOW)],
     )
     for step in range(1, steps):
         line_two = total_of(line_two, [got_two])

time: 165 us -> 149 us (0.903)
  Pallas kernels: 101 us -> 82.2 us
  waiting for transfers between devices: 22.5 us -> 26.1 us
  local copies, waits for them, and re-layouts: 4.26 us -> 2.45 us
    pallas_call x20 -> x15, Pallas kernels: 98.9 us -> 80.4 us  [call(): pl.pallas_call(kernel, out_shape=results, in_specs=[pl.BlockSpec(memory_s...]
    ppermute x12, waiting for transfers between devices: 12 us -> 16.2 us  [trade(): got.append(lax.ppermute(array, 'dp', pairs))]
    all_to_all x2, waiting for transfers between devices: 4.44 us -> 2.11 us  [exchange(): return lax.all_to_all(array, 'dp', split_axis=0, concat_axis=0, tiled=True)]
    unnamed x20 -> x18, local copies, waits for them, and re-layouts: 2.69 us -> 0.78 us
  transfers between devices with their start and end apart: 26 -> 26, of which waited for: 9 -> 12; matrix products, arithmetic and copies ran while one was open for 0% -> 1% of each run, Pallas kernels for 50% -> 45%
where the time goes in v4:
time: 149 us; the launch traced here: 148 us
  Pallas kernels  82.2 us (55%)
  starting transfers between devices  34.9 us (23%)
  waiting for transfers between devices  26.1 us (18%)
  local copies, waits for them, and re-layouts  2.45 us (2%)
    pallas_call x15, Pallas kernels, call(): pl.pallas_call(kernel, out_shape=results, in_specs=[pl.BlockSpec(memory_s...  80.4 us
    ppermute x12, waiting for transfers between devices, trade(): got.append(lax.ppermute(array, 'dp', pairs))  16.2 us
    all_to_all x2, starting transfers between devices, exchange(): return lax.all_to_all(array, 'dp', split_axis=0, concat_axis=0, tiled=True)  14.3 us
    ppermute x12, starting transfers between devices, trade(): got.append(lax.ppermute(array, 'dp', pairs))  14.1 us
    ppermute x4, starting transfers between devices, far_step(): return lax.ppermute(array, 'dp', [(p, p ^ reach) for p in range(total)])  5.77 us
    ppermute x8, waiting for transfers between devices, swap(): return lax.ppermute(array, 'tensor', [(0, 1), (1, 0)])  5.64 us
  transfers between devices with their start and end apart: 26, of which 12 were waited for; matrix products, arithmetic and copies ran while one was open for 1% of the time, Pallas kernels for 45%

profile of v4, /device:TPU:0, one launch (start us, length us, event | category | flops | bytes accessed | tf_op | source)
XLA Modules:
  0.0 148.2 jit_solution(5664115353699160533)
XLA Ops:
  0.7 1.1 constant_dynamic-slice_fusion
  1.8 0.8 pad_maximum_fusion
  2.5 8.3 %all-to-all-start = ((bf16[16,32,384]{2,1,0:T(8,128)(2,1)}), bf16[16,32,384]{2,1,0:T(8,128)(2,1)S(1)}, u32[]{:S(2)}, u32[]{:S(2)}) async-start(bf16[16,32,384]{2,1,0:T(8,128)(2,1)} %pad_maximum_fusion), calls=%async_computation | async-start | bytes 786432 | tf_op jit(solution)/shard_map/all_to_all | solution.py:744
  10.9 0.6 pad_bitcast_fusion.refs_3_.refs_0_
  11.5 11.0 %shard_map.357 = (bf16[3,512,64]{2,1,0:T(8,128)(2,1)}, bf16[3,512,64]{2,1,0:T(8,128)(2,1)}, bf16[3,512,64]{2,1,0:T(8,128)(2,1)}, bf16[2,3,64,1024]{3,2,1,0:T(8,1...) custom-call(s32[16]{0:T(128)S(1)} %copy-done.3, bf16[512,384]{1,0:T(8,128)(2,1)} %bitcast.13, ...), custom_call_target="tpu_custom_call" | custom-call | flops 1 | bytes 1 | tf_op jit(solution)/shard_map/pallas_call | solution.py:208
  22.5 1.0 all-to-all-done.refs_1_
  23.5 0.7 copy-done.5
  24.3 1.8 %shard_map.358 = bf16[16,32,384]{2,1,0:T(8,128)(2,1)} custom-call(s32[16]{0:T(128)} %refs_1_.3, bf16[16,32,384]{2,1,0:T(8,128)(2,1)} %copy-done.5), custom_call_target="tpu_custom_call" | custom-call | tf_op jit(solution)/shard_map/pallas_call | solution.py:248
  26.1 5.9 %all-to-all-start.1 = ((bf16[16,32,384]{2,1,0:T(8,128)(2,1)}), bf16[16,32,384]{2,1,0:T(8,128)(2,1)S(1)}, u32[]{:S(2)}, u32[]{:S(2)}) async-start(bf16[16,32,384]{2,1,0:T(8,128)(2,1)} %shard_map.358), calls=%async_computation.1 | async-start | bytes 786432 | tf_op jit(solution)/shard_map/all_to_all | solution.py:744
  32.0 5.1 %shard_map.359 = (bf16[1,512,512]{2,1,0:T(8,128)(2,1)}, bf16[1,512,64]{2,1,0:T(8,128)(2,1)}, bf16[512,384]{1,0:T(8,128)(2,1)S(1)}) custom-call(s32[16]{0:T(128)S(1)} %copy-done.3, bf16[3,512,64]{2,1,0:T(8,128)(2,1)} %get-tuple-element.103.refs_1_.refs_9_.refs_5_, bf16[3,512,64]{2,1,0:T(8,128)(2,1)} %get-tuple-element.104.refs_2_.refs_10_.refs_6_, ...), custom_call_target="tpu_custom_call" | custom-call | flops 1 | bytes 1 | tf_op jit(solution)/shard_map/pallas_call | solution.py:208
  37.0 0.1 collective-permute-start
  37.1 1.7 %collective-permute-done.refs_2_ = bf16[512,384]{1,0:T(8,128)(2,1)S(1)} collective-permute-done((bf16[512,384]{1,0:T(8,128)(2,1)S(1)}, bf16[512,384]{1,0:T(8,128)(2,1)S(1)}, u32[]{:S(2)}, u32[]{:S(2)}) %collective-permute-start) | collective-permute-done | bytes 393248 | tf_op jit(solution)/shard_map/ppermute | solution.py:740
  38.8 3.8 %shard_map.360 = (f32[512,384]{1,0:T(8,128)}, bf16[512,384]{1,0:T(8,128)(2,1)S(1)}, f32[512,1]{1,0:T(8,128)}, bf16[512,384]{1,0:T(8,128)(2,1)}, bf16[512,768]{1,0:T(8,128)(2,1)}, /*index=5*/bf16[512,768]{1,0:T(8,128)(2,1)}) custom-call(bf16[512,384]{1,0:T(8,128)(2,1)} %bitcast.14, bf16[512,384]{1,0:T(8,128)(2,1)S(1)} %get-tuple-element.110.refs_1_, ...), custom_call_target="tpu_custom_call" | custom-call | flops 1 | bytes 1 | tf_op jit(solution)/shard_map/pallas_call | solution.py:208
  42.7 0.2 collective-permute-start.1
  42.9 1.1 all-to-all-done.1.refs_8_.refs_2_
  44.0 0.4 collective-permute-done.1.refs_2_
  44.5 1.3 collective-permute-done.2.refs_9_.refs_3_
  45.7 6.8 %shard_map.361 = (bf16[512,384]{1,0:T(8,128)(2,1)S(1)}, f32[512,384]{1,0:T(8,128)}, f32[8,384]{1,0:T(8,128)}, bf16[384,384]{1,0:T(8,128)(2,1)}, bf16[384,384]{1,...) custom-call(s32[16]{0:T(128)S(1)} %copy-done.3, bf16[512,384]{1,0:T(8,128)(2,1)S(1)} %get-tuple-element.111.refs_1_, ...), custom_call_target="tpu_custom_call" | custom-call | flops 1 | bytes 1 | tf_op jit(solution)/shard_map/pallas_call | solution.py:208
  52.6 0.2 collective-permute-start.3
  52.8 1.2 collective-permute-start.4
  54.0 1.5 collective-permute-start.5
  55.5 0.8 collective-permute-start.6
  56.3 13.3 %shard_map.362 = (f32[512,384]{1,0:T(8,128)}, bf16[192,384]{1,0:T(8,128)(2,1)}, f32[8,384]{1,0:T(8,128)}, bf16[1,512,64]{2,1,0:T(8,128)(2,1)}, bf16[3,2,512,64]{...) custom-call(bf16[192,384]{1,0:T(8,128)(2,1)} %refs_11_.1, ...), custom_call_target="tpu_custom_call" | custom-call | flops 1 | bytes 1 | tf_op jit(solution)/shard_map/pallas_call | solution.py:208
  69.6 0.2 add_convert_fusion.2
  69.8 1.5 collective-permute-start.7
  71.2 10.5 %shard_map.363 = (bf16[3,1,512,64]{3,2,1,0:T(8,128)(2,1)}, f32[512,192]{1,0:T(8,128)}, f32[512,192]{1,0:T(8,128)}, bf16[768,384]{1,0:T(8,128)(2,1)}, bf16[256,384]{1,0:T(8,128)(2,1)}) custom-call(s32[8,128]{1,0:T(8,128)} %pad_bitcast_fusion.refs_3_.refs_0_, bf16[192,384]{1,0:T(8,128)(2,1)} %bitcast.17, bf16[192,384]{1,0:T(8,128)(2,1)} %bitcast.20, ...), custom_call_target="tpu_custom_call" | custom-call | flops 1 | bytes 1 | tf_op jit(solution)/shard_map/pallas_call | solution.py:208
  81.8 0.1 add_convert_fusion.1
  81.9 0.1 collective-permute-start.8
  81.9 2.2 %collective-permute-done.8.refs_10_.refs_2_ = bf16[768,384]{1,0:T(8,128)(2,1)S(1)} collective-permute-done((bf16[768,384]{1,0:T(8,128)(2,1)}, bf16[768,384]{1,0:T(8,128)(2,1)S(1)}, u32[]{:S(2)}, u32[]{:S(2)}) %collective-permute-start.8) | collective-permute-done | bytes 589856 | tf_op jit(solution)/shard_map/ppermute | solution.py:740
  84.1 4.2 %shard_map.364 = (bf16[272,384]{1,0:T(8,128)(2,1)}, bf16[272,384]{1,0:T(8,128)(2,1)}, bf16[272,384]{1,0:T(8,128)(2,1)}, bf16[272,384]{1,0:T(8,128)(2,1)}) custom-call(bf16[512,384]{1,0:T(8,128)(2,1)} %bitcast.15, bf16[512,384]{1,0:T(8,128)(2,1)} %refs_1_.2, bf16[3,2,512,64]{3,2,1,0:T(8,128)(2,1)} %get-tuple-element.131.refs_10_.refs_2_, ...), custom_call_target="tpu_custom_call" | custom-call | flops 1 | bytes 1 | tf_op jit(solution)/shard_map/pallas_call | solution.py:208
  88.4 1.4 collective-permute-start.9
  89.7 1.5 collective-permute-start.10
  91.2 0.7 collective-permute-start.11
  91.9 2.4 %collective-permute-start.12 = (bf16[384,384]{1,0:T(8,128)(2,1)S(1)}, bf16[384,384]{1,0:T(8,128)(2,1)S(1)}, u32[]{:S(2)}, u32[]{:S(2)}) collective-permute-start(bf16[384,384]{1,0:T(8,128)(2,1)S(1)} %add_convert_fusion.1), channel_id=1, source_target_pairs={{0,16},{2,18},{4,20},{6,22},{8,24},{10,26},{12,28},{14,30},{16,0},... | collective-permute-start | bytes 884744 | tf_op jit(solution)/shard_map/ppermute | solution.py:881
  94.3 11.7 %shard_map.365 = (bf16[512,384]{1,0:T(8,128)(2,1)}, bf16[512,384]{1,0:T(8,128)(2,1)S(1)}) custom-call(s32[16]{0:T(128)S(1)} %copy-done.3, s32[16]{0:T(128)S(1)} %copy-done.4, bf16[16,32,384]{2,1,0:T(8,128)(2,1)} %copy-done, bf16[16,32,384]{2,1,0:T(8,128)(2,1)} %copy-done.2, bf16[2,3,64,1024]{3,2,1,0:T(8,128)(2,1)} %get-tuple-element.106.refs_4_.refs_12_.refs_8_, ...), custom_call_target="tpu_custom_call" | custom-call | flops 1 | bytes 1 | tf_op jit(solution)/shard_map/pallas_call | solution.py:208
  106.1 0.1 add_convert_fusion.5
  106.2 1.1 collective-permute-done.12
  107.3 0.1 add_convert_fusion.refs_0_
  107.4 0.1 collective-permute-start.13
  107.5 0.1 collective-permute-start.14
  107.6 2.3 %collective-permute-start.18 = (bf16[384,384]{1,0:T(8,128)(2,1)S(1)}, bf16[384,384]{1,0:T(8,128)(2,1)S(1)}, u32[]{:S(2)}, u32[]{:S(2)}) collective-permute-start(bf16[384,384]{1,0:T(8,128)(2,1)S(1)} %add_convert_fusion.refs_0_), channel_id=1, source_target_pairs={{0,6},{2,4},{4,2},{6,0},{8,14},{10,12},{12,10},{14,8},{16,22},{18,... | collective-permute-start | bytes 884744 | tf_op jit(solution)/shard_map/ppermute | solution.py:751
  109.8 0.6 collective-permute-start.17
  110.4 0.7 collective-permute-start.16
  111.1 2.8 %shard_map.366 = (f32[512,384]{1,0:T(8,128)}, bf16[512,384]{1,0:T(8,128)(2,1)S(1)}) custom-call(bf16[512,384]{1,0:T(8,128)(2,1)} %get-tuple-element.153.refs_0_, bf16[512,384]{1,0:T(8,128)(2,1)S(1)} %get-tuple-element.155.refs_1_, bf16[512,384]{1,0:T(8,128)(2,1)S(1)} %collective-permute-done.13.refs_2_, bf16[384]{0:T(512)(128)(2,1)} %refs_3_.4, ...), custom_call_target="tpu_custom_call" | custom-call | flops 1 | bytes 1 | tf_op jit(solution)/shard_map/pallas_call | solution.py:208
  114.0 1.1 collective-permute-done.14
  115.1 0.1 add_convert_fusion.4
  115.1 1.9 %collective-permute-start.19 = (bf16[272,384]{1,0:T(8,128)(2,1)S(1)}, bf16[272,384]{1,0:T(8,128)(2,1)S(1)}, u32[]{:S(2)}, u32[]{:S(2)}) collective-permute-start(bf16[272,384]{1,0:T(8,128)(2,1)S(1)} %add_convert_fusion.4), channel_id=1, source_target_pairs={{0,16},{2,18},{4,20},{6,22},{8,24},{10,26},{12,28},{14,30},{16,0},... | collective-permute-start | bytes 626696 | tf_op jit(solution)/shard_map/ppermute | solution.py:881
  117.0 1.5 collective-permute-done.18.refs_3_
  118.5 5.7 %collective-permute-done.17.refs_2_ = bf16[384,384]{1,0:T(8,128)(2,1)S(1)} collective-permute-done((bf16[384,384]{1,0:T(8,128)(2,1)S(1)}, bf16[384,384]{1,0:T(8,128)(2,1)S(1)}, u32[]{:S(2)}, u32[]{:S(2)}) %collective-permute-start.17) | collective-permute-done | bytes 294944 | tf_op jit(solution)/shard_map/ppermute | solution.py:751
  124.1 0.0 collective-permute-done.16.refs_1_
  124.2 1.8 %shard_map.367 = (f32[384,768]{1,0:T(8,128)}, f32[768,384]{1,0:T(8,128)}) custom-call(bf16[384,384]{1,0:T(8,128)(2,1)S(1)} %add_convert_fusion.refs_0_, bf16[384,384]{1,0:T(8,128)(2,1)S(1)} %collective-permute-done.16.refs_1_, bf16[384,384]{1,0:T(8,128)(2,1)S(1)} %collective-permute-done.17.refs_2_, bf16[384,384]{1,0:T(8,128)(2,1)S(1)} %collective-permute-done.18.refs_3_), custom_call_target="tpu_custom_call" | custom-call | flops 99999997952 | bytes 1 | tf_op jit(solution)/shard_map/pallas_call | solution.py:208
  126.0 2.3 %shard_map.368 = bf16[512,384]{1,0:T(8,128)(2,1)} custom-call(f32[512,384]{1,0:T(8,128)} %get-tuple-element.162.refs_0_, bf16[768,384]{1,0:T(8,128)(2,1)} %get-tuple-element.144.refs_1_, bf16[768,384]{1,0:T(8,128)(2,1)} %copy-done.1), custom_call_target="tpu_custom_call" | custom-call | flops 1 | bytes 1 | tf_op jit(solution)/shard_map/pallas_call | solution.py:208
  128.2 2.6 %shard_map.369 = bf16[512,384]{1,0:T(8,128)(2,1)} custom-call(bf16[512,384]{1,0:T(8,128)(2,1)S(1)} %get-tuple-element.159.refs_0_, bf16[512,384]{1,0:T(8,128)(2,1)S(1)} %collective-permute-done.15.refs_1_, bf16[384]{0:T(512)(128)(2,1)} %refs_2_.2, f32[512,384]{1,0:T(8,128)} %get-tuple-element.157.refs_3_, bf16[384]{0:T(512)(128)(2,1)} %refs_4_.5, ...), custom_call_target="tpu_custom_call" | custom-call | flops 1 | bytes 1 | tf_op jit(solution)/shard_map/pallas_call | solution.py:208
  130.8 0.1 add_convert_fusion.3.refs_0_
  130.9 1.8 %collective-permute-start.22 = (bf16[272,384]{1,0:T(8,128)(2,1)S(1)}, bf16[272,384]{1,0:T(8,128)(2,1)S(1)}, u32[]{:S(2)}, u32[]{:S(2)}) collective-permute-start(bf16[272,384]{1,0:T(8,128)(2,1)S(1)} %add_convert_fusion.3.refs_0_), channel_id=1, source_target_pairs={{0,6},{2,4},{4,2},{6,0},{8,14},{10,12},{12,10},{14,8},{16,22},{18,... | collective-permute-start | bytes 626696 | tf_op jit(solution)/shard_map/ppermute | solution.py:751
  132.7 1.1 collective-permute-start.21
  133.7 0.7 collective-permute-start.20
  134.4 5.5 %collective-permute-done.22.refs_3_ = bf16[272,384]{1,0:T(8,128)(2,1)S(1)} collective-permute-done((bf16[272,384]{1,0:T(8,128)(2,1)S(1)}, bf16[272,384]{1,0:T(8,128)(2,1)S(1)}, u32[]{:S(2)}, u32[]{:S(2)}) %collective-permute-start.22) | collective-permute-done | bytes 208928 | tf_op jit(solution)/shard_map/ppermute | solution.py:751
  139.9 3.5 %collective-permute-done.21.refs_2_ = bf16[272,384]{1,0:T(8,128)(2,1)S(1)} collective-permute-done((bf16[272,384]{1,0:T(8,128)(2,1)S(1)}, bf16[272,384]{1,0:T(8,128)(2,1)S(1)}, u32[]{:S(2)}, u32[]{:S(2)}) %collective-permute-start.21) | collective-permute-done | bytes 208928 | tf_op jit(solution)/shard_map/ppermute | solution.py:751
  143.4 0.0 collective-permute-done.20.refs_1_
  143.4 1.1 shard_map.370.refs_0_
  144.5 0.1 collective-permute-start.23
  144.6 2.4 %shard_map.371 = (f32[192,384]{1,0:T(8,128)}, f32[192,384]{1,0:T(8,128)}, f32[192,384]{1,0:T(8,128)}, f32[192,384]{1,0:T(8,128)}, f32[768]{0:T(1024)}, /*index=5...) custom-call(bf16[272,384]{1,0:T(8,128)(2,1)S(1)} %add_convert_fusion, ...), custom_call_target="tpu_custom_call" | custom-call | flops 1 | bytes 1 | tf_op jit(solution)/shard_map/pallas_call | solution.py:208
  147.0 1.0 shard_map.372
  (31 shorter events, 0.1 us)
Async XLA Ops:
  0.7 10.2 %copy-start.8 = (s32[1023]{0:T(1024)S(1)}, s32[1023]{0:T(1024)}, u32[]{:S(2)}) copy-start(s32[1023]{0:T(1024)} %param.25) | copy-start | bytes 12280
  0.7 10.8 %copy-start.3 = (s32[16]{0:T(128)S(1)}, s32[16]{0:T(128)}, u32[]{:S(2)}) copy-start(s32[16]{0:T(128)} %refs_0_.10) | copy-start | bytes 196
  2.5 21.0 %all-to-all-start = ((bf16[16,32,384]{2,1,0:T(8,128)(2,1)}), bf16[16,32,384]{2,1,0:T(8,128)(2,1)S(1)}, u32[]{:S(2)}, u32[]{:S(2)}) async-start(bf16[16,32,384]{2,1,0:T(8,128)(2,1)} %pad_maximum_fusion), calls=%async_computation | async-start | bytes 786432 | tf_op jit(solution)/shard_map/all_to_all | solution.py:744
  23.5 0.7 copy-start.5
  26.1 18.0 %all-to-all-start.1 = ((bf16[16,32,384]{2,1,0:T(8,128)(2,1)}), bf16[16,32,384]{2,1,0:T(8,128)(2,1)S(1)}, u32[]{:S(2)}, u32[]{:S(2)}) async-start(bf16[16,32,384]{2,1,0:T(8,128)(2,1)} %shard_map.358), calls=%async_computation.1 | async-start | bytes 786432 | tf_op jit(solution)/shard_map/all_to_all | solution.py:744
  37.0 1.8 %collective-permute-start = (bf16[512,384]{1,0:T(8,128)(2,1)S(1)}, bf16[512,384]{1,0:T(8,128)(2,1)S(1)}, u32[]{:S(2)}, u32[]{:S(2)}) collective-permute-start(bf16[512,384]{1,0:T(8,128)(2,1)S(1)} %get-tuple-element.110.refs_1_), channel_id=1, source_target_pairs={{0,1},{1,0},{2,3},{3,2},{4,5},{5,4},{6,7},{7,6},{8,9},{9,8},{10,11... | collective-permute-start | bytes 1179656 | tf_op jit(solution)/shard_map/ppermute | solution.py:740
  42.7 1.8 %collective-permute-start.1 = (bf16[512,384]{1,0:T(8,128)(2,1)S(1)}, bf16[512,384]{1,0:T(8,128)(2,1)S(1)}, u32[]{:S(2)}, u32[]{:S(2)}) collective-permute-start(bf16[512,384]{1,0:T(8,128)(2,1)S(1)} %get-tuple-element.111.refs_1_), channel_id=1, source_target_pairs={{0,1},{1,0},{2,3},{3,2},{4,5},{5,4},{6,7},{7,6},{8,9},{9,8},{10,11... | collective-permute-start | bytes 1179656 | tf_op jit(solution)/shard_map/ppermute | solution.py:740
  44.0 8.6 %copy-start = (bf16[16,32,384]{2,1,0:T(8,128)(2,1)}, bf16[16,32,384]{2,1,0:T(8,128)(2,1)S(1)}, u32[]{:S(2)}) copy-start(bf16[16,32,384]{2,1,0:T(8,128)(2,1)S(1)} %all-to-all-done.1.refs_8_.refs_2_) | copy-start | bytes 1179652
  44.0 1.7 %collective-permute-start.2 = (bf16[16,32,384]{2,1,0:T(8,128)(2,1)S(1)}, bf16[16,32,384]{2,1,0:T(8,128)(2,1)S(1)}, u32[]{:S(2)}, u32[]{:S(2)}) collective-permute-start(bf16[16,32,384]{2,1,0:T(8,128)(2,1)S(1)} %all-to-all-done.1.refs_8_.refs_2_), channel_id=1, source_target_pairs={{0,1},{1,0},{2,3},{3,2},{4,5},{5,4},{6,7},{7,6},{8,9},{9,8},{10,11... | collective-permute-start | bytes 1179656 | tf_op jit(solution)/shard_map/ppermute | solution.py:740
  45.7 6.8 %copy-start.2 = (bf16[16,32,384]{2,1,0:T(8,128)(2,1)}, bf16[16,32,384]{2,1,0:T(8,128)(2,1)S(1)}, u32[]{:S(2)}) copy-start(bf16[16,32,384]{2,1,0:T(8,128)(2,1)S(1)} %collective-permute-done.2.refs_9_.refs_3_) | copy-start | bytes 1179652
  52.6 3.7 %collective-permute-start.3 = (bf16[512,384]{1,0:T(8,128)(2,1)S(1)}, bf16[512,384]{1,0:T(8,128)(2,1)S(1)}, u32[]{:S(2)}, u32[]{:S(2)}) collective-permute-start(bf16[512,384]{1,0:T(8,128)(2,1)S(1)} %get-tuple-element.118.refs_1_), channel_id=1, source_target_pairs={{0,1},{1,0},{2,3},{3,2},{4,5},{5,4},{6,7},{7,6},{8,9},{9,8},{10,11... | collective-permute-start | bytes 1179656 | tf_op jit(solution)/shard_map/ppermute | solution.py:740
  52.8 16.8 %collective-permute-start.4 = (bf16[384,384]{1,0:T(8,128)(2,1)}, bf16[384,384]{1,0:T(8,128)(2,1)S(1)}, u32[]{:S(2)}, u32[]{:S(2)}) collective-permute-start(bf16[384,384]{1,0:T(8,128)(2,1)} %get-tuple-element.126), channel_id=1, source_target_pairs={{0,2},{2,0},{4,6},{6,4},{8,10},{10,8},{12,14},{14,12},{16,18},{18,... | collective-permute-start | bytes 884744 | tf_op jit(solution)/shard_map/ppermute | solution.py:751
  54.0 15.6 %collective-permute-start.5 = (bf16[384,384]{1,0:T(8,128)(2,1)}, bf16[384,384]{1,0:T(8,128)(2,1)S(1)}, u32[]{:S(2)}, u32[]{:S(2)}) collective-permute-start(bf16[384,384]{1,0:T(8,128)(2,1)} %get-tuple-element.127), channel_id=1, source_target_pairs={{0,4},{2,6},{4,0},{6,2},{8,12},{10,14},{12,8},{14,10},{16,20},{18,... | collective-permute-start | bytes 884744 | tf_op jit(solution)/shard_map/ppermute | solution.py:751
  55.5 14.1 %collective-permute-start.6 = (bf16[384,384]{1,0:T(8,128)(2,1)}, bf16[384,384]{1,0:T(8,128)(2,1)S(1)}, u32[]{:S(2)}, u32[]{:S(2)}) collective-permute-start(bf16[384,384]{1,0:T(8,128)(2,1)} %get-tuple-element.128), channel_id=1, source_target_pairs={{0,6},{2,4},{4,2},{6,0},{8,14},{10,12},{12,10},{14,8},{16,22},{18,... | collective-permute-start | bytes 884744 | tf_op jit(solution)/shard_map/ppermute | solution.py:751
  56.3 13.3 %copy-start.6 = (bf16[384,384]{1,0:T(8,128)(2,1)S(1)}, bf16[384,384]{1,0:T(8,128)(2,1)}, u32[]{:S(2)}) copy-start(bf16[384,384]{1,0:T(8,128)(2,1)} %get-tuple-element.125) | copy-start | bytes 884740
  69.8 12.0 %collective-permute-start.7 = (bf16[384,384]{1,0:T(8,128)(2,1)S(1)}, bf16[384,384]{1,0:T(8,128)(2,1)S(1)}, u32[]{:S(2)}, u32[]{:S(2)}) collective-permute-start(bf16[384,384]{1,0:T(8,128)(2,1)S(1)} %add_convert_fusion.2), channel_id=1, source_target_pairs={{0,8},{2,10},{4,12},{6,14},{8,0},{10,2},{12,4},{14,6},{16,24},{18,... | collective-permute-start | bytes 884744 | tf_op jit(solution)/shard_map/ppermute | solution.py:881
  81.9 2.3 %collective-permute-start.8 = (bf16[768,384]{1,0:T(8,128)(2,1)}, bf16[768,384]{1,0:T(8,128)(2,1)S(1)}, u32[]{:S(2)}, u32[]{:S(2)}) collective-permute-start(bf16[768,384]{1,0:T(8,128)(2,1)} %get-tuple-element.144.refs_1_), channel_id=1, source_target_pairs={{0,1},{1,0},{2,3},{3,2},{4,5},{5,4},{6,7},{7,6},{8,9},{9,8},{10,11... | collective-permute-start | bytes 1769480 | tf_op jit(solution)/shard_map/ppermute | solution.py:740
  84.1 4.2 %copy-start.1 = (bf16[768,384]{1,0:T(8,128)(2,1)}, bf16[768,384]{1,0:T(8,128)(2,1)S(1)}, u32[]{:S(2)}) copy-start(bf16[768,384]{1,0:T(8,128)(2,1)S(1)} %collective-permute-done.8.refs_10_.refs_2_) | copy-start | bytes 1769476
  84.1 10.2 %copy-start.4 = (s32[16]{0:T(128)S(1)}, s32[16]{0:T(128)}, u32[]{:S(2)}) copy-start(s32[16]{0:T(128)} %refs_1_.3) | copy-start | bytes 196
  88.4 17.7 %copy-start.7 = (bf16[272,384]{1,0:T(8,128)(2,1)S(1)}, bf16[272,384]{1,0:T(8,128)(2,1)}, u32[]{:S(2)}) copy-start(bf16[272,384]{1,0:T(8,128)(2,1)} %get-tuple-element.148) | copy-start | bytes 626692
  88.4 17.7 %collective-permute-start.9 = (bf16[272,384]{1,0:T(8,128)(2,1)}, bf16[272,384]{1,0:T(8,128)(2,1)S(1)}, u32[]{:S(2)}, u32[]{:S(2)}) collective-permute-start(bf16[272,384]{1,0:T(8,128)(2,1)} %get-tuple-element.149), channel_id=1, source_target_pairs={{0,2},{2,0},{4,6},{6,4},{8,10},{10,8},{12,14},{14,12},{16,18},{18,... | collective-permute-start | bytes 626696 | tf_op jit(solution)/shard_map/ppermute | solution.py:751
  89.7 16.3 %collective-permute-start.10 = (bf16[272,384]{1,0:T(8,128)(2,1)}, bf16[272,384]{1,0:T(8,128)(2,1)S(1)}, u32[]{:S(2)}, u32[]{:S(2)}) collective-permute-start(bf16[272,384]{1,0:T(8,128)(2,1)} %get-tuple-element.150), channel_id=1, source_target_pairs={{0,4},{2,6},{4,0},{6,2},{8,12},{10,14},{12,8},{14,10},{16,20},{18,... | collective-permute-start | bytes 626696 | tf_op jit(solution)/shard_map/ppermute | solution.py:751
  91.2 14.9 %collective-permute-start.11 = (bf16[272,384]{1,0:T(8,128)(2,1)}, bf16[272,384]{1,0:T(8,128)(2,1)S(1)}, u32[]{:S(2)}, u32[]{:S(2)}) collective-permute-start(bf16[272,384]{1,0:T(8,128)(2,1)} %get-tuple-element.151), channel_id=1, source_target_pairs={{0,6},{2,4},{4,2},{6,0},{8,14},{10,12},{12,10},{14,8},{16,22},{18,... | collective-permute-start | bytes 626696 | tf_op jit(solution)/shard_map/ppermute | solution.py:751
  91.9 15.4 %collective-permute-start.12 = (bf16[384,384]{1,0:T(8,128)(2,1)S(1)}, bf16[384,384]{1,0:T(8,128)(2,1)S(1)}, u32[]{:S(2)}, u32[]{:S(2)}) collective-permute-start(bf16[384,384]{1,0:T(8,128)(2,1)S(1)} %add_convert_fusion.1), channel_id=1, source_target_pairs={{0,16},{2,18},{4,20},{6,22},{8,24},{10,26},{12,28},{14,30},{16,0},... | collective-permute-start | bytes 884744 | tf_op jit(solution)/shard_map/ppermute | solution.py:881
  107.4 3.7 %collective-permute-start.13 = (bf16[512,384]{1,0:T(8,128)(2,1)S(1)}, bf16[512,384]{1,0:T(8,128)(2,1)S(1)}, u32[]{:S(2)}, u32[]{:S(2)}) collective-permute-start(bf16[512,384]{1,0:T(8,128)(2,1)S(1)} %get-tuple-element.155.refs_1_), channel_id=1, source_target_pairs={{0,1},{1,0},{2,3},{3,2},{4,5},{5,4},{6,7},{7,6},{8,9},{9,8},{10,11... | collective-permute-start | bytes 1179656 | tf_op jit(solution)/shard_map/ppermute | solution.py:740
  107.5 7.6 %collective-permute-start.14 = (bf16[272,384]{1,0:T(8,128)(2,1)S(1)}, bf16[272,384]{1,0:T(8,128)(2,1)S(1)}, u32[]{:S(2)}, u32[]{:S(2)}) collective-permute-start(bf16[272,384]{1,0:T(8,128)(2,1)S(1)} %add_convert_fusion.5), channel_id=1, source_target_pairs={{0,8},{2,10},{4,12},{6,14},{8,0},{10,2},{12,4},{14,6},{16,24},{18,... | collective-permute-start | bytes 626696 | tf_op jit(solution)/shard_map/ppermute | solution.py:881
  107.6 10.9 %collective-permute-start.18 = (bf16[384,384]{1,0:T(8,128)(2,1)S(1)}, bf16[384,384]{1,0:T(8,128)(2,1)S(1)}, u32[]{:S(2)}, u32[]{:S(2)}) collective-permute-start(bf16[384,384]{1,0:T(8,128)(2,1)S(1)} %add_convert_fusion.refs_0_), channel_id=1, source_target_pairs={{0,6},{2,4},{4,2},{6,0},{8,14},{10,12},{12,10},{14,8},{16,22},{18,... | collective-permute-start | bytes 884744 | tf_op jit(solution)/shard_map/ppermute | solution.py:751
  109.8 14.3 %collective-permute-start.17 = (bf16[384,384]{1,0:T(8,128)(2,1)S(1)}, bf16[384,384]{1,0:T(8,128)(2,1)S(1)}, u32[]{:S(2)}, u32[]{:S(2)}) collective-permute-start(bf16[384,384]{1,0:T(8,128)(2,1)S(1)} %add_convert_fusion.refs_0_), channel_id=1, source_target_pairs={{0,4},{2,6},{4,0},{6,2},{8,12},{10,14},{12,8},{14,10},{16,20},{18,... | collective-permute-start | bytes 884744 | tf_op jit(solution)/shard_map/ppermute | solution.py:751
  110.4 13.8 %collective-permute-start.16 = (bf16[384,384]{1,0:T(8,128)(2,1)S(1)}, bf16[384,384]{1,0:T(8,128)(2,1)S(1)}, u32[]{:S(2)}, u32[]{:S(2)}) collective-permute-start(bf16[384,384]{1,0:T(8,128)(2,1)S(1)} %add_convert_fusion.refs_0_), channel_id=1, source_target_pairs={{0,2},{2,0},{4,6},{6,4},{8,10},{10,8},{12,14},{14,12},{16,18},{18,... | collective-permute-start | bytes 884744 | tf_op jit(solution)/shard_map/ppermute | solution.py:751
  115.1 15.7 %collective-permute-start.19 = (bf16[272,384]{1,0:T(8,128)(2,1)S(1)}, bf16[272,384]{1,0:T(8,128)(2,1)S(1)}, u32[]{:S(2)}, u32[]{:S(2)}) collective-permute-start(bf16[272,384]{1,0:T(8,128)(2,1)S(1)} %add_convert_fusion.4), channel_id=1, source_target_pairs={{0,16},{2,18},{4,20},{6,22},{8,24},{10,26},{12,28},{14,30},{16,0},... | collective-permute-start | bytes 626696 | tf_op jit(solution)/shard_map/ppermute | solution.py:881
  117.0 11.2 %collective-permute-start.15 = (bf16[512,384]{1,0:T(8,128)(2,1)S(1)}, bf16[512,384]{1,0:T(8,128)(2,1)S(1)}, u32[]{:S(2)}, u32[]{:S(2)}) collective-permute-start(bf16[512,384]{1,0:T(8,128)(2,1)S(1)} %get-tuple-element.159.refs_0_), channel_id=1, source_target_pairs={{0,1},{1,0},{2,3},{3,2},{4,5},{5,4},{6,7},{7,6},{8,9},{9,8},{10,11... | collective-permute-start | bytes 1179656 | tf_op jit(solution)/shard_map/ppermute | solution.py:740
  130.9 9.0 %collective-permute-start.22 = (bf16[272,384]{1,0:T(8,128)(2,1)S(1)}, bf16[272,384]{1,0:T(8,128)(2,1)S(1)}, u32[]{:S(2)}, u32[]{:S(2)}) collective-permute-start(bf16[272,384]{1,0:T(8,128)(2,1)S(1)} %add_convert_fusion.3.refs_0_), channel_id=1, source_target_pairs={{0,6},{2,4},{4,2},{6,0},{8,14},{10,12},{12,10},{14,8},{16,22},{18,... | collective-permute-start | bytes 626696 | tf_op jit(solution)/shard_map/ppermute | solution.py:751
  132.7 10.7 %collective-permute-start.21 = (bf16[272,384]{1,0:T(8,128)(2,1)S(1)}, bf16[272,384]{1,0:T(8,128)(2,1)S(1)}, u32[]{:S(2)}, u32[]{:S(2)}) collective-permute-start(bf16[272,384]{1,0:T(8,128)(2,1)S(1)} %add_convert_fusion.3.refs_0_), channel_id=1, source_target_pairs={{0,4},{2,6},{4,0},{6,2},{8,12},{10,14},{12,8},{14,10},{16,20},{18,... | collective-permute-start | bytes 626696 | tf_op jit(solution)/shard_map/ppermute | solution.py:751
  133.7 9.7 %collective-permute-start.20 = (bf16[272,384]{1,0:T(8,128)(2,1)S(1)}, bf16[272,384]{1,0:T(8,128)(2,1)S(1)}, u32[]{:S(2)}, u32[]{:S(2)}) collective-permute-start(bf16[272,384]{1,0:T(8,128)(2,1)S(1)} %add_convert_fusion.3.refs_0_), channel_id=1, source_target_pairs={{0,2},{2,0},{4,6},{6,4},{8,10},{10,8},{12,14},{14,12},{16,18},{18,... | collective-permute-start | bytes 626696 | tf_op jit(solution)/shard_map/ppermute | solution.py:751
  144.5 2.5 %collective-permute-start.23 = (bf16[256,384]{1,0:T(8,128)(2,1)S(1)}, bf16[256,384]{1,0:T(8,128)(2,1)S(1)}, u32[]{:S(2)}, u32[]{:S(2)}) collective-permute-start(bf16[256,384]{1,0:T(8,128)(2,1)S(1)} %shard_map.370.refs_0_), channel_id=1, source_target_pairs={{0,1},{1,0},{2,3},{3,2},{4,5},{5,4},{6,7},{7,6},{8,9},{9,8},{10,11... | collective-permute-start | bytes 589832 | tf_op jit(solution)/shard_map/ppermute | solution.py:740

commit v5 on v4

--- a/solution.py
+++ b/solution.py
@@ -252,6 +252,7 @@
             pl.BlockSpec(memory_space=pltpu.SMEM if i < smem else pltpu.VMEM) for i in range(len(args))
         ],
         out_specs=[pl.BlockSpec(memory_space=pltpu.VMEM) for _ in outs],
+        compiler_params=pltpu.CompilerParams(vmem_limit_bytes=4 * 1024 * 1024),
     )(*args)
 
 
@@ -344,19 +345,20 @@
 
 def attention_first(
     lengths, x, relative, table, wq, bq, wk, bk, wv, bv,
-    q_out, k_out, v_out, tab_out, prob_out, ctx_out, far_scratch,
+    q_out, k_out, v_out, tab_out, hot_out, prob_out, ctx_out, far_scratch,
 ):
     length = lengths[lax.axis_index("dp")]
     project(x[...], (wq, wk, wv), (bq, bk, bv), (q_out, k_out, v_out))
     send(q_out, k_out, v_out)
     rel = relative[...]
     hot = one_hot(table, relative.shape[0])
+    hot_out[...] = hot
     for slot, (weight, bias) in enumerate(((wq, bq), (wk, bk))):
         low = (mm(rel, weight[...], NT) + bias[...].astype(WIDE)[None, :]).astype(LOW)
         spread = mm(low, hot, TN).astype(LOW)
         for h in range(q_out.shape[0]):
             tab_out[slot, h] = spread[h * HEAD_DIM : (h + 1) * HEAD_DIM]
-    send(tab_out)
+    send(tab_out, hot_out)
     attend(length, ctx_out.shape[0], q_out, k_out, v_out, tab_out, ctx_out, far_scratch, prob_out)
 
 
@@ -596,7 +598,7 @@
 
 
 def attention_backward_last(
-    table, wq, wk, wv, gctx, q, k, v, tab, prob, before, gpq_before, gpk_before,
+    hot, wq, wk, wv, gctx, q, k, v, tab, prob, before, gpq_before, gpk_before,
     g_out, gpq_out, gpk_out, send_out, keep_out,
     gpq_scratch, gpk_scratch, rel_scratch, *scratch,
 ):
@@ -609,12 +611,11 @@
         0, q, k, v, tab, prob, gctx, anti, g_out, gpq_scratch, gpk_scratch, *scratch
     )
     send(g_out)
-    hot = one_hot(table, buckets)
     for first, here, out in (
         (gpq_before, gpq_scratch, gpq_out), (gpk_before, gpk_scratch, gpk_out)
     ):
         parts = [first[h] for h in range(first.shape[0])] + [here[0]]
-        out[...] = mm(hot, jnp.concatenate(parts, axis=0), NT) * scale
+        out[...] = mm(hot[...], jnp.concatenate(parts, axis=0), NT) * scale
     rel_scratch[...] = mm(gpq_out[...].astype(LOW), wq[...]) + mm(gpk_out[...].astype(LOW), wk[...])
     send(gpq_out, gpk_out)
     rows = buckets
@@ -818,10 +819,10 @@
     table = table.reshape(span // BLOCK, BLOCK)
     projections = (w_query.T, b_query, w_key.T, b_key, w_value.T, b_value, w_out)
     head_shape = (heads, rows, HEAD_DIM)
-    q, k, v, tab, prob, ctx = run(
+    q, k, v, tab, hot, prob, ctx = run(
         attention_first,
         [(head_shape, LOW)] * 3
-        + [((2, heads, HEAD_DIM, span), LOW), ((before, rows, rows), LOW),
+        + [((2, heads, HEAD_DIM, span), LOW), ((relative.shape[0], span), LOW), ((before, rows, rows), LOW),
            ((before, rows, HEAD_DIM), LOW)],
         (lengths, x, relative, table) + projections[:6],
         scratch=[pltpu.VMEM((rows, rows), WIDE)],
@@ -911,7 +912,7 @@
         attention_backward_last,
         [((3, 1, rows, HEAD_DIM), LOW), ((rows, part), WIDE), ((rows, part), WIDE),
          ((rows + half, width), LOW), ((half, width), LOW)],
-        (table, w_query.T, w_key.T, w_value.T, gctx)
+        (hot, w_query.T, w_key.T, w_value.T, gctx)
         + tuple(Part(array, 0, before, 1) for array in (q, k, v))
         + (Part(tab, 1, before, 1), prob_last, g_before, gpq_before, gpk_before),
         scratch=[
@@ -954,21 +955,23 @@
     for step in range(1, steps):
         line_two = total_of(line_two, [got_two])
         got_two = far_step(line_two, step)
-    g_up, g_down = run(
-        unpack_ffn, [((width, units), WIDE), ((units, width), WIDE)], (all_one,),
-        flops=10**11,
-    )
     down_dealt_got = swap(after(down_dealt, line_two))
     (grad_tokens,) = run(
         finish_tokens,
         [((rows, width), LOW)],
         (gp, Part(send_part, 0, 0, rows), Part(send_got, 0, 0, rows)),
+        flops=6 * 10**9,
     )
     (y,) = run(
         finish_dealt,
         [((rows, width), LOW)],
         (Here(down_dealt), Here(down_dealt_got), b_down, normed_dealt, attn_gain, attn_shift,
          ffn_gain, ffn_shift),
+        flops=6 * 10**9,
+    )
+    g_up, g_down = run(
+        unpack_ffn, [((width, units), WIDE), ((units, width), WIDE)], (all_one,),
+        flops=6 * 10**9,
     )
     line_two = total_of(line_two, [got_two])
     all_two = gather_near(line_two)

time: 149 us -> 144 us (0.966)
  waiting for transfers between devices: 26.1 us -> 22.5 us
    ppermute x12, waiting for transfers between devices: 16.2 us -> 11.4 us  [trade(): got.append(lax.ppermute(array, 'dp', pairs))]
  transfers between devices with their start and end apart: 26 -> 26, of which waited for: 12 -> 13; matrix products, arithmetic and copies ran while one was open for 1% -> 1% of each run, Pallas kernels for 45% -> 47%
where the time goes in v5:
time: 144 us; the launch traced here: 143 us
  Pallas kernels  81.5 us (57%)
  starting transfers between devices  35.3 us (25%)
  waiting for transfers between devices  22.5 us (16%)
  local copies, waits for them, and re-layouts  1.7 us (1%)
    pallas_call x15, Pallas kernels, call(): pl.pallas_call(kernel, out_shape=results, in_specs=[pl.BlockSpec(memory_s...  80.2 us
    all_to_all x2, starting transfers between devices, exchange(): return lax.all_to_all(array, 'dp', split_axis=0, concat_axis=0, tiled=True)  14.6 us
    ppermute x12, starting transfers between devices, trade(): got.append(lax.ppermute(array, 'dp', pairs))  14.1 us
    ppermute x12, waiting for transfers between devices, trade(): got.append(lax.ppermute(array, 'dp', pairs))  11.4 us
    ppermute x4, starting transfers between devices, far_step(): return lax.ppermute(array, 'dp', [(p, p ^ reach) for p in range(total)])  5.85 us
    ppermute x8, waiting for transfers between devices, swap(): return lax.ppermute(array, 'tensor', [(0, 1), (1, 0)])  5.64 us
    ppermute x4, waiting for transfers between devices, far_step(): return lax.ppermute(array, 'dp', [(p, p ^ reach) for p in range(total)])  3.49 us
  transfers between devices with their start and end apart: 26, of which 13 were waited for; matrix products, arithmetic and copies ran while one was open for 1% of the time, Pallas kernels for 47%

profile of v5, /device:TPU:0, one launch (start us, length us, event | category | flops | bytes accessed | tf_op | source)
XLA Modules:
  0.0 143.4 jit_solution(8590638058131931322)
XLA Ops:
  0.7 1.1 constant_dynamic-slice_fusion
  1.8 0.8 pad_maximum_fusion
  2.5 8.5 %all-to-all-start = ((bf16[16,32,384]{2,1,0:T(8,128)(2,1)}), bf16[16,32,384]{2,1,0:T(8,128)(2,1)S(1)}, u32[]{:S(2)}, u32[]{:S(2)}) async-start(bf16[16,32,384]{2,1,0:T(8,128)(2,1)} %pad_maximum_fusion), calls=%async_computation | async-start | bytes 786432 | tf_op jit(solution)/shard_map/all_to_all | solution.py:745
  11.0 0.6 pad_bitcast_fusion.refs_3_
  11.6 11.2 %shard_map.357 = (bf16[3,512,64]{2,1,0:T(8,128)(2,1)}, bf16[3,512,64]{2,1,0:T(8,128)(2,1)}, bf16[3,512,64]{2,1,0:T(8,128)(2,1)}, bf16[2,3,64,1024]{3,2,1,0:T(8,1...) custom-call(s32[16]{0:T(128)S(1)} %copy-done.3, ...), custom_call_target="tpu_custom_call" | custom-call | flops 1 | bytes 1 | tf_op jit(solution)/shard_map/pallas_call | solution.py:208
  22.8 0.8 all-to-all-done.refs_1_
  23.7 1.3 shard_map.358
  25.0 6.1 %all-to-all-start.1 = ((bf16[16,32,384]{2,1,0:T(8,128)(2,1)}), bf16[16,32,384]{2,1,0:T(8,128)(2,1)S(1)}, u32[]{:S(2)}, u32[]{:S(2)}) async-start(bf16[16,32,384]{2,1,0:T(8,128)(2,1)} %shard_map.358), calls=%async_computation.1 | async-start | bytes 786432 | tf_op jit(solution)/shard_map/all_to_all | solution.py:745
  31.1 5.1 %shard_map.359 = (bf16[1,512,512]{2,1,0:T(8,128)(2,1)}, bf16[1,512,64]{2,1,0:T(8,128)(2,1)}, bf16[512,384]{1,0:T(8,128)(2,1)S(1)}) custom-call(s32[16]{0:T(128)S(1)} %copy-done.3, bf16[3,512,64]{2,1,0:T(8,128)(2,1)} %get-tuple-element.104.refs_1_.refs_9_.refs_5_, bf16[3,512,64]{2,1,0:T(8,128)(2,1)} %get-tuple-element.105.refs_2_.refs_10_.refs_6_, ...), custom_call_target="tpu_custom_call" | custom-call | flops 1 | bytes 1 | tf_op jit(solution)/shard_map/pallas_call | solution.py:208
  36.2 0.1 collective-permute-start
  36.2 1.7 %collective-permute-done.refs_2_ = bf16[512,384]{1,0:T(8,128)(2,1)S(1)} collective-permute-done((bf16[512,384]{1,0:T(8,128)(2,1)S(1)}, bf16[512,384]{1,0:T(8,128)(2,1)S(1)}, u32[]{:S(2)}, u32[]{:S(2)}) %collective-permute-start) | collective-permute-done | bytes 393248 | tf_op jit(solution)/shard_map/ppermute | solution.py:741
  38.0 3.8 %shard_map.360 = (f32[512,384]{1,0:T(8,128)}, bf16[512,384]{1,0:T(8,128)(2,1)S(1)}, f32[512,1]{1,0:T(8,128)}, bf16[512,384]{1,0:T(8,128)(2,1)}, bf16[512,768]{1,0:T(8,128)(2,1)}, /*index=5*/bf16[512,768]{1,0:T(8,128)(2,1)}) custom-call(bf16[512,384]{1,0:T(8,128)(2,1)} %bitcast.14, bf16[512,384]{1,0:T(8,128)(2,1)S(1)} %get-tuple-element.111.refs_1_, ...), custom_call_target="tpu_custom_call" | custom-call | flops 1 | bytes 1 | tf_op jit(solution)/shard_map/pallas_call | solution.py:208
  41.8 0.2 collective-permute-start.1
  42.0 1.1 all-to-all-done.1.refs_8_.refs_2_
  43.1 0.5 collective-permute-done.1.refs_2_
  43.6 1.2 collective-permute-done.2.refs_9_.refs_3_
  44.8 6.8 %shard_map.361 = (bf16[512,384]{1,0:T(8,128)(2,1)S(1)}, f32[512,384]{1,0:T(8,128)}, f32[8,384]{1,0:T(8,128)}, bf16[384,384]{1,0:T(8,128)(2,1)}, bf16[384,384]{1,...) custom-call(s32[16]{0:T(128)S(1)} %copy-done.3, bf16[512,384]{1,0:T(8,128)(2,1)S(1)} %get-tuple-element.112.refs_1_, ...), custom_call_target="tpu_custom_call" | custom-call | flops 1 | bytes 1 | tf_op jit(solution)/shard_map/pallas_call | solution.py:208
  51.7 0.2 collective-permute-start.3
  51.9 1.2 collective-permute-start.4
  53.1 1.5 %collective-permute-start.5 = (bf16[384,384]{1,0:T(8,128)(2,1)}, bf16[384,384]{1,0:T(8,128)(2,1)S(1)}, u32[]{:S(2)}, u32[]{:S(2)}) collective-permute-start(bf16[384,384]{1,0:T(8,128)(2,1)} %get-tuple-element.128), channel_id=1, source_target_pairs={{0,4},{2,6},{4,0},{6,2},{8,12},{10,14},{12,8},{14,10},{16,20},{18,... | collective-permute-start | bytes 884744 | tf_op jit(solution)/shard_map/ppermute | solution.py:752
  54.6 0.8 collective-permute-start.6
  55.4 13.2 %shard_map.362 = (f32[512,384]{1,0:T(8,128)}, bf16[192,384]{1,0:T(8,128)(2,1)}, f32[8,384]{1,0:T(8,128)}, bf16[1,512,64]{2,1,0:T(8,128)(2,1)}, bf16[3,2,512,64]{...) custom-call(bf16[192,384]{1,0:T(8,128)(2,1)} %refs_11_.1, ...), custom_call_target="tpu_custom_call" | custom-call | flops 1 | bytes 1 | tf_op jit(solution)/shard_map/pallas_call | solution.py:208
  68.6 0.1 collective-permute-done.5
  68.7 0.2 add_convert_fusion.2
  68.8 1.5 %collective-permute-start.7 = (bf16[384,384]{1,0:T(8,128)(2,1)S(1)}, bf16[384,384]{1,0:T(8,128)(2,1)S(1)}, u32[]{:S(2)}, u32[]{:S(2)}) collective-permute-start(bf16[384,384]{1,0:T(8,128)(2,1)S(1)} %add_convert_fusion.2), channel_id=1, source_target_pairs={{0,8},{2,10},{4,12},{6,14},{8,0},{10,2},{12,4},{14,6},{16,24},{18,... | collective-permute-start | bytes 884744 | tf_op jit(solution)/shard_map/ppermute | solution.py:882
  70.4 10.3 %shard_map.363 = (bf16[3,1,512,64]{3,2,1,0:T(8,128)(2,1)}, f32[512,192]{1,0:T(8,128)}, f32[512,192]{1,0:T(8,128)}, bf16[768,384]{1,0:T(8,128)(2,1)}, bf16[256,384]{1,0:T(8,128)(2,1)}) custom-call(bf16[512,1024]{1,0:T(8,128)(2,1)} %get-tuple-element.131.refs_0_, bf16[192,384]{1,0:T(8,128)(2,1)} %bitcast.17, bf16[192,384]{1,0:T(8,128)(2,1)} %bitcast.20, ...), custom_call_target="tpu_custom_call" | custom-call | flops 1 | bytes 1 | tf_op jit(solution)/shard_map/pallas_call | solution.py:208
  80.7 0.1 add_convert_fusion.1
  80.7 0.1 collective-permute-start.8
  80.8 2.2 %collective-permute-done.8.refs_10_.refs_2_ = bf16[768,384]{1,0:T(8,128)(2,1)S(1)} collective-permute-done((bf16[768,384]{1,0:T(8,128)(2,1)}, bf16[768,384]{1,0:T(8,128)(2,1)S(1)}, u32[]{:S(2)}, u32[]{:S(2)}) %collective-permute-start.8) | collective-permute-done | bytes 589856 | tf_op jit(solution)/shard_map/ppermute | solution.py:741
  83.0 4.2 %shard_map.364 = (bf16[272,384]{1,0:T(8,128)(2,1)}, bf16[272,384]{1,0:T(8,128)(2,1)}, bf16[272,384]{1,0:T(8,128)(2,1)}, bf16[272,384]{1,0:T(8,128)(2,1)}) custom-call(bf16[512,384]{1,0:T(8,128)(2,1)} %bitcast.15, bf16[512,384]{1,0:T(8,128)(2,1)} %refs_1_.2, bf16[3,2,512,64]{3,2,1,0:T(8,128)(2,1)} %get-tuple-element.133.refs_10_.refs_2_, ...), custom_call_target="tpu_custom_call" | custom-call | flops 1 | bytes 1 | tf_op jit(solution)/shard_map/pallas_call | solution.py:208
  87.2 1.3 collective-permute-start.9
  88.5 1.5 %collective-permute-start.10 = (bf16[272,384]{1,0:T(8,128)(2,1)}, bf16[272,384]{1,0:T(8,128)(2,1)S(1)}, u32[]{:S(2)}, u32[]{:S(2)}) collective-permute-start(bf16[272,384]{1,0:T(8,128)(2,1)} %get-tuple-element.152), channel_id=1, source_target_pairs={{0,4},{2,6},{4,0},{6,2},{8,12},{10,14},{12,8},{14,10},{16,20},{18,... | collective-permute-start | bytes 626696 | tf_op jit(solution)/shard_map/ppermute | solution.py:752
  90.0 0.8 collective-permute-start.11
  90.8 2.4 %collective-permute-start.12 = (bf16[384,384]{1,0:T(8,128)(2,1)S(1)}, bf16[384,384]{1,0:T(8,128)(2,1)S(1)}, u32[]{:S(2)}, u32[]{:S(2)}) collective-permute-start(bf16[384,384]{1,0:T(8,128)(2,1)S(1)} %add_convert_fusion.1), channel_id=1, source_target_pairs={{0,16},{2,18},{4,20},{6,22},{8,24},{10,26},{12,28},{14,30},{16,0},... | collective-permute-start | bytes 884744 | tf_op jit(solution)/shard_map/ppermute | solution.py:882
  93.2 11.7 %shard_map.365 = (bf16[512,384]{1,0:T(8,128)(2,1)}, bf16[512,384]{1,0:T(8,128)(2,1)S(1)}) custom-call(s32[16]{0:T(128)S(1)} %copy-done.3, s32[16]{0:T(128)S(1)} %copy-done.4, bf16[16,32,384]{2,1,0:T(8,128)(2,1)} %copy-done, bf16[16,32,384]{2,1,0:T(8,128)(2,1)} %copy-done.1, bf16[2,3,64,1024]{3,2,1,0:T(8,128)(2,1)} %get-tuple-element.107.refs_4_.refs_12_.refs_8_, ...), custom_call_target="tpu_custom_call" | custom-call | flops 1 | bytes 1 | tf_op jit(solution)/shard_map/pallas_call | solution.py:208
  104.9 0.1 add_convert_fusion.5
  105.1 1.2 collective-permute-done.12
  106.2 0.1 add_convert_fusion.refs_0_
  106.3 0.1 collective-permute-start.13
  106.4 0.1 collective-permute-start.14
  106.5 2.2 %collective-permute-start.18 = (bf16[384,384]{1,0:T(8,128)(2,1)S(1)}, bf16[384,384]{1,0:T(8,128)(2,1)S(1)}, u32[]{:S(2)}, u32[]{:S(2)}) collective-permute-start(bf16[384,384]{1,0:T(8,128)(2,1)S(1)} %add_convert_fusion.refs_0_), channel_id=1, source_target_pairs={{0,6},{2,4},{4,2},{6,0},{8,14},{10,12},{12,10},{14,8},{16,22},{18,... | collective-permute-start | bytes 884744 | tf_op jit(solution)/shard_map/ppermute | solution.py:752
  108.6 0.6 collective-permute-start.17
  109.2 0.8 collective-permute-start.16
  110.0 2.8 %shard_map.366 = (f32[512,384]{1,0:T(8,128)}, bf16[512,384]{1,0:T(8,128)(2,1)S(1)}) custom-call(bf16[512,384]{1,0:T(8,128)(2,1)} %get-tuple-element.155.refs_0_, bf16[512,384]{1,0:T(8,128)(2,1)S(1)} %get-tuple-element.157.refs_1_, bf16[512,384]{1,0:T(8,128)(2,1)S(1)} %collective-permute-done.13.refs_2_, bf16[384]{0:T(512)(128)(2,1)} %refs_3_.4, ...), custom_call_target="tpu_custom_call" | custom-call | flops 1 | bytes 1 | tf_op jit(solution)/shard_map/pallas_call | solution.py:208
  112.9 1.1 collective-permute-done.14
  114.0 0.1 add_convert_fusion.4
  114.0 1.9 %collective-permute-start.19 = (bf16[272,384]{1,0:T(8,128)(2,1)S(1)}, bf16[272,384]{1,0:T(8,128)(2,1)S(1)}, u32[]{:S(2)}, u32[]{:S(2)}) collective-permute-start(bf16[272,384]{1,0:T(8,128)(2,1)S(1)} %add_convert_fusion.4), channel_id=1, source_target_pairs={{0,16},{2,18},{4,20},{6,22},{8,24},{10,26},{12,28},{14,30},{16,0},... | collective-permute-start | bytes 626696 | tf_op jit(solution)/shard_map/ppermute | solution.py:882
  115.9 2.2 %shard_map.367 = bf16[512,384]{1,0:T(8,128)(2,1)} custom-call(f32[512,384]{1,0:T(8,128)} %get-tuple-element.162.refs_0_, bf16[768,384]{1,0:T(8,128)(2,1)} %get-tuple-element.146.refs_1_, bf16[768,384]{1,0:T(8,128)(2,1)} %copy-done.2), custom_call_target="tpu_custom_call" | custom-call | flops 6000000000 | bytes 1 | tf_op jit(solution)/shard_map/pallas_call | solution.py:208
  118.2 2.6 %shard_map.368 = bf16[512,384]{1,0:T(8,128)(2,1)} custom-call(bf16[512,384]{1,0:T(8,128)(2,1)S(1)} %get-tuple-element.161.refs_0_, bf16[512,384]{1,0:T(8,128)(2,1)S(1)} %collective-permute-done.15.refs_1_, bf16[384]{0:T(512)(128)(2,1)} %refs_2_.2, f32[512,384]{1,0:T(8,128)} %get-tuple-element.159.refs_3_, bf16[384]{0:T(512)(128)(2,1)} %refs_4_.5, ...), custom_call_target="tpu_custom_call" | custom-call | flops 6000000000 | bytes 1 | tf_op jit(solution)/shard_map/pallas_call | solution.py:208
  120.7 2.3 %collective-permute-done.17.refs_2_ = bf16[384,384]{1,0:T(8,128)(2,1)S(1)} collective-permute-done((bf16[384,384]{1,0:T(8,128)(2,1)S(1)}, bf16[384,384]{1,0:T(8,128)(2,1)S(1)}, u32[]{:S(2)}, u32[]{:S(2)}) %collective-permute-start.17) | collective-permute-done | bytes 294944 | tf_op jit(solution)/shard_map/ppermute | solution.py:752
  123.0 0.0 collective-permute-done.16.refs_1_
  123.1 1.8 %shard_map.369 = (f32[384,768]{1,0:T(8,128)}, f32[768,384]{1,0:T(8,128)}) custom-call(bf16[384,384]{1,0:T(8,128)(2,1)S(1)} %add_convert_fusion.refs_0_, bf16[384,384]{1,0:T(8,128)(2,1)S(1)} %collective-permute-done.16.refs_1_, bf16[384,384]{1,0:T(8,128)(2,1)S(1)} %collective-permute-done.17.refs_2_, bf16[384,384]{1,0:T(8,128)(2,1)S(1)} %collective-permute-done.18.refs_3_), custom_call_target="tpu_custom_call" | custom-call | flops 6000000000 | bytes 1 | tf_op jit(solution)/shard_map/pallas_call | solution.py:208
  124.8 1.2 collective-permute-done.19
  126.1 0.1 add_convert_fusion.3.refs_0_
  126.1 2.2 %collective-permute-start.22 = (bf16[272,384]{1,0:T(8,128)(2,1)S(1)}, bf16[272,384]{1,0:T(8,128)(2,1)S(1)}, u32[]{:S(2)}, u32[]{:S(2)}) collective-permute-start(bf16[272,384]{1,0:T(8,128)(2,1)S(1)} %add_convert_fusion.3.refs_0_), channel_id=1, source_target_pairs={{0,6},{2,4},{4,2},{6,0},{8,14},{10,12},{12,10},{14,8},{16,22},{18,... | collective-permute-start | bytes 626696 | tf_op jit(solution)/shard_map/ppermute | solution.py:752
  128.3 0.6 collective-permute-start.21
  128.9 0.8 collective-permute-start.20
  129.7 5.5 %collective-permute-done.22.refs_3_ = bf16[272,384]{1,0:T(8,128)(2,1)S(1)} collective-permute-done((bf16[272,384]{1,0:T(8,128)(2,1)S(1)}, bf16[272,384]{1,0:T(8,128)(2,1)S(1)}, u32[]{:S(2)}, u32[]{:S(2)}) %collective-permute-start.22) | collective-permute-done | bytes 208928 | tf_op jit(solution)/shard_map/ppermute | solution.py:752
  135.2 3.4 %collective-permute-done.21.refs_2_ = bf16[272,384]{1,0:T(8,128)(2,1)S(1)} collective-permute-done((bf16[272,384]{1,0:T(8,128)(2,1)S(1)}, bf16[272,384]{1,0:T(8,128)(2,1)S(1)}, u32[]{:S(2)}, u32[]{:S(2)}) %collective-permute-start.21) | collective-permute-done | bytes 208928 | tf_op jit(solution)/shard_map/ppermute | solution.py:752
  138.6 0.0 collective-permute-done.20.refs_1_
  138.7 1.1 shard_map.370.refs_0_
  139.8 0.1 collective-permute-start.23
  139.9 2.4 %shard_map.371 = (f32[192,384]{1,0:T(8,128)}, f32[192,384]{1,0:T(8,128)}, f32[192,384]{1,0:T(8,128)}, f32[192,384]{1,0:T(8,128)}, f32[768]{0:T(1024)}, /*index=5...) custom-call(bf16[272,384]{1,0:T(8,128)(2,1)S(1)} %add_convert_fusion, ...), custom_call_target="tpu_custom_call" | custom-call | flops 1 | bytes 1 | tf_op jit(solution)/shard_map/pallas_call | solution.py:208
  142.3 1.0 shard_map.372
  (29 shorter events, 0.1 us)
Async XLA Ops:
  0.7 10.4 %copy-start.7 = (s32[1023]{0:T(1024)S(1)}, s32[1023]{0:T(1024)}, u32[]{:S(2)}) copy-start(s32[1023]{0:T(1024)} %param.25) | copy-start | bytes 12280
  0.7 11.0 %copy-start.3 = (s32[16]{0:T(128)S(1)}, s32[16]{0:T(128)}, u32[]{:S(2)}) copy-start(s32[16]{0:T(128)} %refs_0_.10) | copy-start | bytes 196
  2.5 21.1 %copy-start.4 = (s32[16]{0:T(128)S(1)}, s32[16]{0:T(128)}, u32[]{:S(2)}) copy-start(s32[16]{0:T(128)} %refs_1_.3) | copy-start | bytes 196
  2.5 21.1 %all-to-all-start = ((bf16[16,32,384]{2,1,0:T(8,128)(2,1)}), bf16[16,32,384]{2,1,0:T(8,128)(2,1)S(1)}, u32[]{:S(2)}, u32[]{:S(2)}) async-start(bf16[16,32,384]{2,1,0:T(8,128)(2,1)} %pad_maximum_fusion), calls=%async_computation | async-start | bytes 786432 | tf_op jit(solution)/shard_map/all_to_all | solution.py:745
  25.0 18.1 %all-to-all-start.1 = ((bf16[16,32,384]{2,1,0:T(8,128)(2,1)}), bf16[16,32,384]{2,1,0:T(8,128)(2,1)S(1)}, u32[]{:S(2)}, u32[]{:S(2)}) async-start(bf16[16,32,384]{2,1,0:T(8,128)(2,1)} %shard_map.358), calls=%async_computation.1 | async-start | bytes 786432 | tf_op jit(solution)/shard_map/all_to_all | solution.py:745
  36.2 1.8 %collective-permute-start = (bf16[512,384]{1,0:T(8,128)(2,1)S(1)}, bf16[512,384]{1,0:T(8,128)(2,1)S(1)}, u32[]{:S(2)}, u32[]{:S(2)}) collective-permute-start(bf16[512,384]{1,0:T(8,128)(2,1)S(1)} %get-tuple-element.111.refs_1_), channel_id=1, source_target_pairs={{0,1},{1,0},{2,3},{3,2},{4,5},{5,4},{6,7},{7,6},{8,9},{9,8},{10,11... | collective-permute-start | bytes 1179656 | tf_op jit(solution)/shard_map/ppermute | solution.py:741
  41.8 1.8 %collective-permute-start.1 = (bf16[512,384]{1,0:T(8,128)(2,1)S(1)}, bf16[512,384]{1,0:T(8,128)(2,1)S(1)}, u32[]{:S(2)}, u32[]{:S(2)}) collective-permute-start(bf16[512,384]{1,0:T(8,128)(2,1)S(1)} %get-tuple-element.112.refs_1_), channel_id=1, source_target_pairs={{0,1},{1,0},{2,3},{3,2},{4,5},{5,4},{6,7},{7,6},{8,9},{9,8},{10,11... | collective-permute-start | bytes 1179656 | tf_op jit(solution)/shard_map/ppermute | solution.py:741
  43.1 8.6 %copy-start = (bf16[16,32,384]{2,1,0:T(8,128)(2,1)}, bf16[16,32,384]{2,1,0:T(8,128)(2,1)S(1)}, u32[]{:S(2)}) copy-start(bf16[16,32,384]{2,1,0:T(8,128)(2,1)S(1)} %all-to-all-done.1.refs_8_.refs_2_) | copy-start | bytes 1179652
  43.1 1.7 %collective-permute-start.2 = (bf16[16,32,384]{2,1,0:T(8,128)(2,1)S(1)}, bf16[16,32,384]{2,1,0:T(8,128)(2,1)S(1)}, u32[]{:S(2)}, u32[]{:S(2)}) collective-permute-start(bf16[16,32,384]{2,1,0:T(8,128)(2,1)S(1)} %all-to-all-done.1.refs_8_.refs_2_), channel_id=1, source_target_pairs={{0,1},{1,0},{2,3},{3,2},{4,5},{5,4},{6,7},{7,6},{8,9},{9,8},{10,11... | collective-permute-start | bytes 1179656 | tf_op jit(solution)/shard_map/ppermute | solution.py:741
  44.8 6.8 %copy-start.1 = (bf16[16,32,384]{2,1,0:T(8,128)(2,1)}, bf16[16,32,384]{2,1,0:T(8,128)(2,1)S(1)}, u32[]{:S(2)}) copy-start(bf16[16,32,384]{2,1,0:T(8,128)(2,1)S(1)} %collective-permute-done.2.refs_9_.refs_3_) | copy-start | bytes 1179652
  51.7 3.7 %collective-permute-start.3 = (bf16[512,384]{1,0:T(8,128)(2,1)S(1)}, bf16[512,384]{1,0:T(8,128)(2,1)S(1)}, u32[]{:S(2)}, u32[]{:S(2)}) collective-permute-start(bf16[512,384]{1,0:T(8,128)(2,1)S(1)} %get-tuple-element.119.refs_1_), channel_id=1, source_target_pairs={{0,1},{1,0},{2,3},{3,2},{4,5},{5,4},{6,7},{7,6},{8,9},{9,8},{10,11... | collective-permute-start | bytes 1179656 | tf_op jit(solution)/shard_map/ppermute | solution.py:741
  51.9 16.7 %collective-permute-start.4 = (bf16[384,384]{1,0:T(8,128)(2,1)}, bf16[384,384]{1,0:T(8,128)(2,1)S(1)}, u32[]{:S(2)}, u32[]{:S(2)}) collective-permute-start(bf16[384,384]{1,0:T(8,128)(2,1)} %get-tuple-element.127), channel_id=1, source_target_pairs={{0,2},{2,0},{4,6},{6,4},{8,10},{10,8},{12,14},{14,12},{16,18},{18,... | collective-permute-start | bytes 884744 | tf_op jit(solution)/shard_map/ppermute | solution.py:752
  53.1 15.5 %collective-permute-start.5 = (bf16[384,384]{1,0:T(8,128)(2,1)}, bf16[384,384]{1,0:T(8,128)(2,1)S(1)}, u32[]{:S(2)}, u32[]{:S(2)}) collective-permute-start(bf16[384,384]{1,0:T(8,128)(2,1)} %get-tuple-element.128), channel_id=1, source_target_pairs={{0,4},{2,6},{4,0},{6,2},{8,12},{10,14},{12,8},{14,10},{16,20},{18,... | collective-permute-start | bytes 884744 | tf_op jit(solution)/shard_map/ppermute | solution.py:752
  54.6 14.1 %collective-permute-start.6 = (bf16[384,384]{1,0:T(8,128)(2,1)}, bf16[384,384]{1,0:T(8,128)(2,1)S(1)}, u32[]{:S(2)}, u32[]{:S(2)}) collective-permute-start(bf16[384,384]{1,0:T(8,128)(2,1)} %get-tuple-element.129), channel_id=1, source_target_pairs={{0,6},{2,4},{4,2},{6,0},{8,14},{10,12},{12,10},{14,8},{16,22},{18,... | collective-permute-start | bytes 884744 | tf_op jit(solution)/shard_map/ppermute | solution.py:752
  55.4 13.3 %copy-start.5 = (bf16[384,384]{1,0:T(8,128)(2,1)S(1)}, bf16[384,384]{1,0:T(8,128)(2,1)}, u32[]{:S(2)}) copy-start(bf16[384,384]{1,0:T(8,128)(2,1)} %get-tuple-element.126) | copy-start | bytes 884740
  68.8 11.8 %collective-permute-start.7 = (bf16[384,384]{1,0:T(8,128)(2,1)S(1)}, bf16[384,384]{1,0:T(8,128)(2,1)S(1)}, u32[]{:S(2)}, u32[]{:S(2)}) collective-permute-start(bf16[384,384]{1,0:T(8,128)(2,1)S(1)} %add_convert_fusion.2), channel_id=1, source_target_pairs={{0,8},{2,10},{4,12},{6,14},{8,0},{10,2},{12,4},{14,6},{16,24},{18,... | collective-permute-start | bytes 884744 | tf_op jit(solution)/shard_map/ppermute | solution.py:882
  80.7 2.3 %collective-permute-start.8 = (bf16[768,384]{1,0:T(8,128)(2,1)}, bf16[768,384]{1,0:T(8,128)(2,1)S(1)}, u32[]{:S(2)}, u32[]{:S(2)}) collective-permute-start(bf16[768,384]{1,0:T(8,128)(2,1)} %get-tuple-element.146.refs_1_), channel_id=1, source_target_pairs={{0,1},{1,0},{2,3},{3,2},{4,5},{5,4},{6,7},{7,6},{8,9},{9,8},{10,11... | collective-permute-start | bytes 1769480 | tf_op jit(solution)/shard_map/ppermute | solution.py:741
  83.0 4.2 %copy-start.2 = (bf16[768,384]{1,0:T(8,128)(2,1)}, bf16[768,384]{1,0:T(8,128)(2,1)S(1)}, u32[]{:S(2)}) copy-start(bf16[768,384]{1,0:T(8,128)(2,1)S(1)} %collective-permute-done.8.refs_10_.refs_2_) | copy-start | bytes 1769476
  87.2 17.7 %copy-start.6 = (bf16[272,384]{1,0:T(8,128)(2,1)S(1)}, bf16[272,384]{1,0:T(8,128)(2,1)}, u32[]{:S(2)}) copy-start(bf16[272,384]{1,0:T(8,128)(2,1)} %get-tuple-element.150) | copy-start | bytes 626692
  87.2 17.7 %collective-permute-start.9 = (bf16[272,384]{1,0:T(8,128)(2,1)}, bf16[272,384]{1,0:T(8,128)(2,1)S(1)}, u32[]{:S(2)}, u32[]{:S(2)}) collective-permute-start(bf16[272,384]{1,0:T(8,128)(2,1)} %get-tuple-element.151), channel_id=1, source_target_pairs={{0,2},{2,0},{4,6},{6,4},{8,10},{10,8},{12,14},{14,12},{16,18},{18,... | collective-permute-start | bytes 626696 | tf_op jit(solution)/shard_map/ppermute | solution.py:752
  88.5 16.4 %collective-permute-start.10 = (bf16[272,384]{1,0:T(8,128)(2,1)}, bf16[272,384]{1,0:T(8,128)(2,1)S(1)}, u32[]{:S(2)}, u32[]{:S(2)}) collective-permute-start(bf16[272,384]{1,0:T(8,128)(2,1)} %get-tuple-element.152), channel_id=1, source_target_pairs={{0,4},{2,6},{4,0},{6,2},{8,12},{10,14},{12,8},{14,10},{16,20},{18,... | collective-permute-start | bytes 626696 | tf_op jit(solution)/shard_map/ppermute | solution.py:752
  90.0 15.0 %collective-permute-start.11 = (bf16[272,384]{1,0:T(8,128)(2,1)}, bf16[272,384]{1,0:T(8,128)(2,1)S(1)}, u32[]{:S(2)}, u32[]{:S(2)}) collective-permute-start(bf16[272,384]{1,0:T(8,128)(2,1)} %get-tuple-element.153), channel_id=1, source_target_pairs={{0,6},{2,4},{4,2},{6,0},{8,14},{10,12},{12,10},{14,8},{16,22},{18,... | collective-permute-start | bytes 626696 | tf_op jit(solution)/shard_map/ppermute | solution.py:752
  90.8 15.4 %collective-permute-start.12 = (bf16[384,384]{1,0:T(8,128)(2,1)S(1)}, bf16[384,384]{1,0:T(8,128)(2,1)S(1)}, u32[]{:S(2)}, u32[]{:S(2)}) collective-permute-start(bf16[384,384]{1,0:T(8,128)(2,1)S(1)} %add_convert_fusion.1), channel_id=1, source_target_pairs={{0,16},{2,18},{4,20},{6,22},{8,24},{10,26},{12,28},{14,30},{16,0},... | collective-permute-start | bytes 884744 | tf_op jit(solution)/shard_map/ppermute | solution.py:882
  106.3 3.7 %collective-permute-start.13 = (bf16[512,384]{1,0:T(8,128)(2,1)S(1)}, bf16[512,384]{1,0:T(8,128)(2,1)S(1)}, u32[]{:S(2)}, u32[]{:S(2)}) collective-permute-start(bf16[512,384]{1,0:T(8,128)(2,1)S(1)} %get-tuple-element.157.refs_1_), channel_id=1, source_target_pairs={{0,1},{1,0},{2,3},{3,2},{4,5},{5,4},{6,7},{7,6},{8,9},{9,8},{10,11... | collective-permute-start | bytes 1179656 | tf_op jit(solution)/shard_map/ppermute | solution.py:741
  106.4 7.6 %collective-permute-start.14 = (bf16[272,384]{1,0:T(8,128)(2,1)S(1)}, bf16[272,384]{1,0:T(8,128)(2,1)S(1)}, u32[]{:S(2)}, u32[]{:S(2)}) collective-permute-start(bf16[272,384]{1,0:T(8,128)(2,1)S(1)} %add_convert_fusion.5), channel_id=1, source_target_pairs={{0,8},{2,10},{4,12},{6,14},{8,0},{10,2},{12,4},{14,6},{16,24},{18,... | collective-permute-start | bytes 626696 | tf_op jit(solution)/shard_map/ppermute | solution.py:882
  106.5 14.3 %collective-permute-start.18 = (bf16[384,384]{1,0:T(8,128)(2,1)S(1)}, bf16[384,384]{1,0:T(8,128)(2,1)S(1)}, u32[]{:S(2)}, u32[]{:S(2)}) collective-permute-start(bf16[384,384]{1,0:T(8,128)(2,1)S(1)} %add_convert_fusion.refs_0_), channel_id=1, source_target_pairs={{0,6},{2,4},{4,2},{6,0},{8,14},{10,12},{12,10},{14,8},{16,22},{18,... | collective-permute-start | bytes 884744 | tf_op jit(solution)/shard_map/ppermute | solution.py:752
  108.6 14.4 %collective-permute-start.17 = (bf16[384,384]{1,0:T(8,128)(2,1)S(1)}, bf16[384,384]{1,0:T(8,128)(2,1)S(1)}, u32[]{:S(2)}, u32[]{:S(2)}) collective-permute-start(bf16[384,384]{1,0:T(8,128)(2,1)S(1)} %add_convert_fusion.refs_0_), channel_id=1, source_target_pairs={{0,4},{2,6},{4,0},{6,2},{8,12},{10,14},{12,8},{14,10},{16,20},{18,... | collective-permute-start | bytes 884744 | tf_op jit(solution)/shard_map/ppermute | solution.py:752
  109.2 13.9 %collective-permute-start.16 = (bf16[384,384]{1,0:T(8,128)(2,1)S(1)}, bf16[384,384]{1,0:T(8,128)(2,1)S(1)}, u32[]{:S(2)}, u32[]{:S(2)}) collective-permute-start(bf16[384,384]{1,0:T(8,128)(2,1)S(1)} %add_convert_fusion.refs_0_), channel_id=1, source_target_pairs={{0,2},{2,0},{4,6},{6,4},{8,10},{10,8},{12,14},{14,12},{16,18},{18,... | collective-permute-start | bytes 884744 | tf_op jit(solution)/shard_map/ppermute | solution.py:752
  114.0 12.1 %collective-permute-start.19 = (bf16[272,384]{1,0:T(8,128)(2,1)S(1)}, bf16[272,384]{1,0:T(8,128)(2,1)S(1)}, u32[]{:S(2)}, u32[]{:S(2)}) collective-permute-start(bf16[272,384]{1,0:T(8,128)(2,1)S(1)} %add_convert_fusion.4), channel_id=1, source_target_pairs={{0,16},{2,18},{4,20},{6,22},{8,24},{10,26},{12,28},{14,30},{16,0},... | collective-permute-start | bytes 626696 | tf_op jit(solution)/shard_map/ppermute | solution.py:882
  115.9 2.3 %collective-permute-start.15 = (bf16[512,384]{1,0:T(8,128)(2,1)S(1)}, bf16[512,384]{1,0:T(8,128)(2,1)S(1)}, u32[]{:S(2)}, u32[]{:S(2)}) collective-permute-start(bf16[512,384]{1,0:T(8,128)(2,1)S(1)} %get-tuple-element.161.refs_0_), channel_id=1, source_target_pairs={{0,1},{1,0},{2,3},{3,2},{4,5},{5,4},{6,7},{7,6},{8,9},{9,8},{10,11... | collective-permute-start | bytes 1179656 | tf_op jit(solution)/shard_map/ppermute | solution.py:741
  126.1 9.0 %collective-permute-start.22 = (bf16[272,384]{1,0:T(8,128)(2,1)S(1)}, bf16[272,384]{1,0:T(8,128)(2,1)S(1)}, u32[]{:S(2)}, u32[]{:S(2)}) collective-permute-start(bf16[272,384]{1,0:T(8,128)(2,1)S(1)} %add_convert_fusion.3.refs_0_), channel_id=1, source_target_pairs={{0,6},{2,4},{4,2},{6,0},{8,14},{10,12},{12,10},{14,8},{16,22},{18,... | collective-permute-start | bytes 626696 | tf_op jit(solution)/shard_map/ppermute | solution.py:752
  128.3 10.3 %collective-permute-start.21 = (bf16[272,384]{1,0:T(8,128)(2,1)S(1)}, bf16[272,384]{1,0:T(8,128)(2,1)S(1)}, u32[]{:S(2)}, u32[]{:S(2)}) collective-permute-start(bf16[272,384]{1,0:T(8,128)(2,1)S(1)} %add_convert_fusion.3.refs_0_), channel_id=1, source_target_pairs={{0,4},{2,6},{4,0},{6,2},{8,12},{10,14},{12,8},{14,10},{16,20},{18,... | collective-permute-start | bytes 626696 | tf_op jit(solution)/shard_map/ppermute | solution.py:752
  128.9 9.8 %collective-permute-start.20 = (bf16[272,384]{1,0:T(8,128)(2,1)S(1)}, bf16[272,384]{1,0:T(8,128)(2,1)S(1)}, u32[]{:S(2)}, u32[]{:S(2)}) collective-permute-start(bf16[272,384]{1,0:T(8,128)(2,1)S(1)} %add_convert_fusion.3.refs_0_), channel_id=1, source_target_pairs={{0,2},{2,0},{4,6},{6,4},{8,10},{10,8},{12,14},{14,12},{16,18},{18,... | collective-permute-start | bytes 626696 | tf_op jit(solution)/shard_map/ppermute | solution.py:752
  139.8 2.5 %collective-permute-start.23 = (bf16[256,384]{1,0:T(8,128)(2,1)S(1)}, bf16[256,384]{1,0:T(8,128)(2,1)S(1)}, u32[]{:S(2)}, u32[]{:S(2)}) collective-permute-start(bf16[256,384]{1,0:T(8,128)(2,1)S(1)} %shard_map.370.refs_0_), channel_id=1, source_target_pairs={{0,1},{1,0},{2,3},{3,2},{4,5},{5,4},{6,7},{7,6},{8,9},{9,8},{10,11... | collective-permute-start | bytes 589832 | tf_op jit(solution)/shard_map/ppermute | solution.py:741

commit v6 on v5

--- a/solution.py
+++ b/solution.py
@@ -941,11 +941,12 @@
         scratch=[pltpu.VMEM(head_shape, LOW) for _ in range(4)] + [pltpu.VMEM((rows, rows), WIDE)],
         smem=2,
     )
+    line_one, *near_two[1:] = lax.optimization_barrier((line_one, *near_two[1:]))
+    line_one = total_of(line_one, [got_one])
     line_two = total_of(near_two[0], near_two[1:])
     got_two = far_step(line_two, 0)
-    line_one = total_of(line_one, [got_one])
     all_one = gather_near(line_one)
-    attn_dealt_got = swap(after(attn_dealt, line_one))
+    attn_dealt_got = swap(after(attn_dealt, line_two))
     normed_dealt, down_dealt = run(
         with_statics(ffn_forward, False),
         [((rows, width), WIDE), Here((rows, width), LOW)],

time: 144 us -> 141 us (0.979)
  waiting for transfers between devices: 22.5 us -> 18.3 us
    ppermute x8, waiting for transfers between devices: 5.64 us -> 3.44 us  [swap(): return lax.ppermute(array, 'tensor', [(0, 1), (1, 0)])]
    ppermute x4, waiting for transfers between devices: 3.49 us -> 1.56 us  [far_step(): return lax.ppermute(array, 'dp', [(p, p ^ reach) for p in range(total)])]
  transfers between devices with their start and end apart: 26 -> 26, of which waited for: 13 -> 11; matrix products, arithmetic and copies ran while one was open for 1% -> 0% of each run, Pallas kernels for 47% -> 51%
where the time goes in v6:
time: 141 us; the launch traced here: 140 us
  Pallas kernels  81.5 us (58%)
  starting transfers between devices  36.1 us (26%)
  waiting for transfers between devices  18.3 us (13%)
  local copies, waits for them, and re-layouts  1.7 us (1%)
    pallas_call x15, Pallas kernels, call(): pl.pallas_call(kernel, out_shape=results, in_specs=[pl.BlockSpec(memory_s...  80.2 us
    all_to_all x2, starting transfers between devices, exchange(): return lax.all_to_all(array, 'dp', split_axis=0, concat_axis=0, tiled=True)  14.6 us
    ppermute x12, starting transfers between devices, trade(): got.append(lax.ppermute(array, 'dp', pairs))  14.1 us
    ppermute x12, waiting for transfers between devices, trade(): got.append(lax.ppermute(array, 'dp', pairs))  11.3 us
    ppermute x4, starting transfers between devices, far_step(): return lax.ppermute(array, 'dp', [(p, p ^ reach) for p in range(total)])  6.8 us
    ppermute x8, waiting for transfers between devices, swap(): return lax.ppermute(array, 'tensor', [(0, 1), (1, 0)])  3.44 us
  transfers between devices with their start and end apart: 26, of which 11 were waited for; matrix products, arithmetic and copies ran while one was open for 0% of the time, Pallas kernels for 51%

profile of v6, /device:TPU:0, one launch (start us, length us, event | category | flops | bytes accessed | tf_op | source)
XLA Modules:
  0.0 140.1 jit_solution(2305741498317663633)
XLA Ops:
  0.7 1.1 constant_dynamic-slice_fusion
  1.8 0.8 pad_maximum_fusion
  2.5 8.5 %all-to-all-start = ((bf16[16,32,384]{2,1,0:T(8,128)(2,1)}), bf16[16,32,384]{2,1,0:T(8,128)(2,1)S(1)}, u32[]{:S(2)}, u32[]{:S(2)}) async-start(bf16[16,32,384]{2,1,0:T(8,128)(2,1)} %pad_maximum_fusion), calls=%async_computation | async-start | bytes 786432 | tf_op jit(solution)/shard_map/all_to_all | solution.py:745
  11.0 0.6 pad_bitcast_fusion.refs_3_
  11.6 11.2 %shard_map.357 = (bf16[3,512,64]{2,1,0:T(8,128)(2,1)}, bf16[3,512,64]{2,1,0:T(8,128)(2,1)}, bf16[3,512,64]{2,1,0:T(8,128)(2,1)}, bf16[2,3,64,1024]{3,2,1,0:T(8,1...) custom-call(s32[16]{0:T(128)S(1)} %copy-done.3, ...), custom_call_target="tpu_custom_call" | custom-call | flops 1 | bytes 1 | tf_op jit(solution)/shard_map/pallas_call | solution.py:208
  22.8 0.8 all-to-all-done.refs_1_
  23.7 1.3 shard_map.358
  25.0 6.1 %all-to-all-start.1 = ((bf16[16,32,384]{2,1,0:T(8,128)(2,1)}), bf16[16,32,384]{2,1,0:T(8,128)(2,1)S(1)}, u32[]{:S(2)}, u32[]{:S(2)}) async-start(bf16[16,32,384]{2,1,0:T(8,128)(2,1)} %shard_map.358), calls=%async_computation.1 | async-start | bytes 786432 | tf_op jit(solution)/shard_map/all_to_all | solution.py:745
  31.1 5.1 %shard_map.359 = (bf16[1,512,512]{2,1,0:T(8,128)(2,1)}, bf16[1,512,64]{2,1,0:T(8,128)(2,1)}, bf16[512,384]{1,0:T(8,128)(2,1)S(1)}) custom-call(s32[16]{0:T(128)S(1)} %copy-done.3, bf16[3,512,64]{2,1,0:T(8,128)(2,1)} %get-tuple-element.108.refs_1_.refs_9_.refs_5_, bf16[3,512,64]{2,1,0:T(8,128)(2,1)} %get-tuple-element.109.refs_2_.refs_10_.refs_6_, ...), custom_call_target="tpu_custom_call" | custom-call | flops 1 | bytes 1 | tf_op jit(solution)/shard_map/pallas_call | solution.py:208
  36.2 0.1 collective-permute-start
  36.2 1.7 %collective-permute-done.refs_2_ = bf16[512,384]{1,0:T(8,128)(2,1)S(1)} collective-permute-done((bf16[512,384]{1,0:T(8,128)(2,1)S(1)}, bf16[512,384]{1,0:T(8,128)(2,1)S(1)}, u32[]{:S(2)}, u32[]{:S(2)}) %collective-permute-start) | collective-permute-done | bytes 393248 | tf_op jit(solution)/shard_map/ppermute | solution.py:741
  38.0 3.8 %shard_map.360 = (f32[512,384]{1,0:T(8,128)}, bf16[512,384]{1,0:T(8,128)(2,1)S(1)}, f32[512,1]{1,0:T(8,128)}, bf16[512,384]{1,0:T(8,128)(2,1)}, bf16[512,768]{1,0:T(8,128)(2,1)}, /*index=5*/bf16[512,768]{1,0:T(8,128)(2,1)}) custom-call(bf16[512,384]{1,0:T(8,128)(2,1)} %bitcast.14, bf16[512,384]{1,0:T(8,128)(2,1)S(1)} %get-tuple-element.115.refs_1_, ...), custom_call_target="tpu_custom_call" | custom-call | flops 1 | bytes 1 | tf_op jit(solution)/shard_map/pallas_call | solution.py:208
  41.8 0.2 collective-permute-start.1
  42.0 1.1 all-to-all-done.1.refs_8_.refs_2_
  43.1 0.0 collective-permute-start.2
  43.1 0.5 collective-permute-done.1.refs_2_
  43.6 1.2 collective-permute-done.2.refs_9_.refs_3_
  44.8 6.8 %shard_map.361 = (bf16[512,384]{1,0:T(8,128)(2,1)S(1)}, f32[512,384]{1,0:T(8,128)}, f32[8,384]{1,0:T(8,128)}, bf16[384,384]{1,0:T(8,128)(2,1)}, bf16[384,384]{1,...) custom-call(s32[16]{0:T(128)S(1)} %copy-done.3, bf16[512,384]{1,0:T(8,128)(2,1)S(1)} %get-tuple-element.116.refs_1_, ...), custom_call_target="tpu_custom_call" | custom-call | flops 1 | bytes 1 | tf_op jit(solution)/shard_map/pallas_call | solution.py:208
  51.7 0.2 collective-permute-start.3
  51.9 1.2 collective-permute-start.4
  53.1 1.5 %collective-permute-start.5 = (bf16[384,384]{1,0:T(8,128)(2,1)}, bf16[384,384]{1,0:T(8,128)(2,1)S(1)}, u32[]{:S(2)}, u32[]{:S(2)}) collective-permute-start(bf16[384,384]{1,0:T(8,128)(2,1)} %get-tuple-element.132), channel_id=1, source_target_pairs={{0,4},{2,6},{4,0},{6,2},{8,12},{10,14},{12,8},{14,10},{16,20},{18,... | collective-permute-start | bytes 884744 | tf_op jit(solution)/shard_map/ppermute | solution.py:752
  54.6 0.8 collective-permute-start.6
  55.4 0.0 collective-permute-done.3.refs_2_
  55.4 13.2 %shard_map.362 = (f32[512,384]{1,0:T(8,128)}, bf16[192,384]{1,0:T(8,128)(2,1)}, f32[8,384]{1,0:T(8,128)}, bf16[1,512,64]{2,1,0:T(8,128)(2,1)}, bf16[3,2,512,64]{...) custom-call(bf16[192,384]{1,0:T(8,128)(2,1)} %refs_11_.1, ...), custom_call_target="tpu_custom_call" | custom-call | flops 1 | bytes 1 | tf_op jit(solution)/shard_map/pallas_call | solution.py:208
  68.6 0.1 collective-permute-done.5
  68.7 0.2 add_convert_fusion.2
  68.8 1.5 %collective-permute-start.7 = (bf16[384,384]{1,0:T(8,128)(2,1)S(1)}, bf16[384,384]{1,0:T(8,128)(2,1)S(1)}, u32[]{:S(2)}, u32[]{:S(2)}) collective-permute-start(bf16[384,384]{1,0:T(8,128)(2,1)S(1)} %add_convert_fusion.2), channel_id=1, source_target_pairs={{0,8},{2,10},{4,12},{6,14},{8,0},{10,2},{12,4},{14,6},{16,24},{18,... | collective-permute-start | bytes 884744 | tf_op jit(solution)/shard_map/ppermute | solution.py:882
  70.4 10.3 %shard_map.363 = (bf16[3,1,512,64]{3,2,1,0:T(8,128)(2,1)}, f32[512,192]{1,0:T(8,128)}, f32[512,192]{1,0:T(8,128)}, bf16[768,384]{1,0:T(8,128)(2,1)}, bf16[256,384]{1,0:T(8,128)(2,1)}) custom-call(bf16[512,1024]{1,0:T(8,128)(2,1)} %get-tuple-element.135.refs_0_, bf16[192,384]{1,0:T(8,128)(2,1)} %bitcast.17, bf16[192,384]{1,0:T(8,128)(2,1)} %bitcast.20, ...), custom_call_target="tpu_custom_call" | custom-call | flops 1 | bytes 1 | tf_op jit(solution)/shard_map/pallas_call | solution.py:208
  80.7 0.1 add_convert_fusion.1
  80.7 0.1 collective-permute-start.8
  80.8 2.4 %collective-permute-start.12 = (bf16[384,384]{1,0:T(8,128)(2,1)S(1)}, bf16[384,384]{1,0:T(8,128)(2,1)S(1)}, u32[]{:S(2)}, u32[]{:S(2)}) collective-permute-start(bf16[384,384]{1,0:T(8,128)(2,1)S(1)} %add_convert_fusion.1), channel_id=1, source_target_pairs={{0,16},{2,18},{4,20},{6,22},{8,24},{10,26},{12,28},{14,30},{16,0},... | collective-permute-start | bytes 884744 | tf_op jit(solution)/shard_map/ppermute | solution.py:882
  83.3 4.2 %shard_map.364 = (bf16[272,384]{1,0:T(8,128)(2,1)}, bf16[272,384]{1,0:T(8,128)(2,1)}, bf16[272,384]{1,0:T(8,128)(2,1)}, bf16[272,384]{1,0:T(8,128)(2,1)}) custom-call(bf16[512,384]{1,0:T(8,128)(2,1)} %bitcast.15, bf16[512,384]{1,0:T(8,128)(2,1)} %refs_1_.2, bf16[3,2,512,64]{3,2,1,0:T(8,128)(2,1)} %get-tuple-element.137.refs_10_.refs_2_, ...), custom_call_target="tpu_custom_call" | custom-call | flops 1 | bytes 1 | tf_op jit(solution)/shard_map/pallas_call | solution.py:208
  87.5 1.3 collective-permute-start.9
  88.7 1.5 %collective-permute-start.10 = (bf16[272,384]{1,0:T(8,128)(2,1)}, bf16[272,384]{1,0:T(8,128)(2,1)S(1)}, u32[]{:S(2)}, u32[]{:S(2)}) collective-permute-start(bf16[272,384]{1,0:T(8,128)(2,1)} %get-tuple-element.155), channel_id=1, source_target_pairs={{0,4},{2,6},{4,0},{6,2},{8,12},{10,14},{12,8},{14,10},{16,20},{18,... | collective-permute-start | bytes 626696 | tf_op jit(solution)/shard_map/ppermute | solution.py:752
  90.2 0.9 collective-permute-start.11
  91.0 11.7 %shard_map.365 = (bf16[512,384]{1,0:T(8,128)(2,1)}, bf16[512,384]{1,0:T(8,128)(2,1)S(1)}) custom-call(s32[16]{0:T(128)S(1)} %copy-done.3, s32[16]{0:T(128)S(1)} %copy-done.4, bf16[16,32,384]{2,1,0:T(8,128)(2,1)} %copy-done, bf16[16,32,384]{2,1,0:T(8,128)(2,1)} %copy-done.1, bf16[2,3,64,1024]{3,2,1,0:T(8,128)(2,1)} %get-tuple-element.111.refs_4_.refs_12_.refs_8_, ...), custom_call_target="tpu_custom_call" | custom-call | flops 1 | bytes 1 | tf_op jit(solution)/shard_map/pallas_call | solution.py:208
  102.8 0.1 add_convert_fusion.refs_0_
  102.9 0.1 add_convert_fusion.5
  103.0 0.1 collective-permute-start.13
  103.1 0.6 collective-permute-start.14
  103.7 2.1 %collective-permute-start.18 = (bf16[384,384]{1,0:T(8,128)(2,1)S(1)}, bf16[384,384]{1,0:T(8,128)(2,1)S(1)}, u32[]{:S(2)}, u32[]{:S(2)}) collective-permute-start(bf16[384,384]{1,0:T(8,128)(2,1)S(1)} %add_convert_fusion.refs_0_), channel_id=1, source_target_pairs={{0,6},{2,4},{4,2},{6,0},{8,14},{10,12},{12,10},{14,8},{16,22},{18,... | collective-permute-start | bytes 884744 | tf_op jit(solution)/shard_map/ppermute | solution.py:752
  105.8 0.6 collective-permute-start.17
  106.3 0.8 collective-permute-start.16
  107.2 2.8 %shard_map.366 = (f32[512,384]{1,0:T(8,128)}, bf16[512,384]{1,0:T(8,128)(2,1)S(1)}) custom-call(bf16[512,384]{1,0:T(8,128)(2,1)} %get-tuple-element.163.refs_0_, bf16[512,384]{1,0:T(8,128)(2,1)S(1)} %get-tuple-element.165.refs_1_, bf16[512,384]{1,0:T(8,128)(2,1)S(1)} %collective-permute-done.13.refs_2_, bf16[384]{0:T(512)(128)(2,1)} %refs_3_.4, ...), custom_call_target="tpu_custom_call" | custom-call | flops 1 | bytes 1 | tf_op jit(solution)/shard_map/pallas_call | solution.py:208
  110.0 0.6 collective-permute-done.14
  110.6 0.1 add_convert_fusion.4
  110.7 2.2 %collective-permute-start.19 = (bf16[272,384]{1,0:T(8,128)(2,1)S(1)}, bf16[272,384]{1,0:T(8,128)(2,1)S(1)}, u32[]{:S(2)}, u32[]{:S(2)}) collective-permute-start(bf16[272,384]{1,0:T(8,128)(2,1)S(1)} %add_convert_fusion.4), channel_id=1, source_target_pairs={{0,16},{2,18},{4,20},{6,22},{8,24},{10,26},{12,28},{14,30},{16,0},... | collective-permute-start | bytes 626696 | tf_op jit(solution)/shard_map/ppermute | solution.py:882
  112.9 2.2 %shard_map.367 = bf16[512,384]{1,0:T(8,128)(2,1)} custom-call(f32[512,384]{1,0:T(8,128)} %get-tuple-element.170.refs_0_, bf16[768,384]{1,0:T(8,128)(2,1)} %get-tuple-element.150.refs_1_, bf16[768,384]{1,0:T(8,128)(2,1)} %copy-done.2), custom_call_target="tpu_custom_call" | custom-call | flops 6000000000 | bytes 1 | tf_op jit(solution)/shard_map/pallas_call | solution.py:208
  115.2 2.6 %shard_map.368 = bf16[512,384]{1,0:T(8,128)(2,1)} custom-call(bf16[512,384]{1,0:T(8,128)(2,1)S(1)} %get-tuple-element.169.refs_0_, bf16[512,384]{1,0:T(8,128)(2,1)S(1)} %collective-permute-done.15.refs_1_, bf16[384]{0:T(512)(128)(2,1)} %refs_2_.2, f32[512,384]{1,0:T(8,128)} %get-tuple-element.167.refs_3_, bf16[384]{0:T(512)(128)(2,1)} %refs_4_.5, ...), custom_call_target="tpu_custom_call" | custom-call | flops 6000000000 | bytes 1 | tf_op jit(solution)/shard_map/pallas_call | solution.py:208
  117.7 2.2 %collective-permute-done.17.refs_2_ = bf16[384,384]{1,0:T(8,128)(2,1)S(1)} collective-permute-done((bf16[384,384]{1,0:T(8,128)(2,1)S(1)}, bf16[384,384]{1,0:T(8,128)(2,1)S(1)}, u32[]{:S(2)}, u32[]{:S(2)}) %collective-permute-start.17) | collective-permute-done | bytes 294944 | tf_op jit(solution)/shard_map/ppermute | solution.py:752
  120.0 0.0 collective-permute-done.16.refs_1_
  120.0 1.8 %shard_map.369 = (f32[384,768]{1,0:T(8,128)}, f32[768,384]{1,0:T(8,128)}) custom-call(bf16[384,384]{1,0:T(8,128)(2,1)S(1)} %add_convert_fusion.refs_0_, bf16[384,384]{1,0:T(8,128)(2,1)S(1)} %collective-permute-done.16.refs_1_, bf16[384,384]{1,0:T(8,128)(2,1)S(1)} %collective-permute-done.17.refs_2_, bf16[384,384]{1,0:T(8,128)(2,1)S(1)} %collective-permute-done.18.refs_3_), custom_call_target="tpu_custom_call" | custom-call | flops 6000000000 | bytes 1 | tf_op jit(solution)/shard_map/pallas_call | solution.py:208
  121.8 1.0 collective-permute-done.19
  122.8 0.1 add_convert_fusion.3.refs_0_
  122.8 2.1 %collective-permute-start.22 = (bf16[272,384]{1,0:T(8,128)(2,1)S(1)}, bf16[272,384]{1,0:T(8,128)(2,1)S(1)}, u32[]{:S(2)}, u32[]{:S(2)}) collective-permute-start(bf16[272,384]{1,0:T(8,128)(2,1)S(1)} %add_convert_fusion.3.refs_0_), channel_id=1, source_target_pairs={{0,6},{2,4},{4,2},{6,0},{8,14},{10,12},{12,10},{14,8},{16,22},{18,... | collective-permute-start | bytes 626696 | tf_op jit(solution)/shard_map/ppermute | solution.py:752
  125.0 0.6 collective-permute-start.21
  125.5 0.8 collective-permute-start.20
  126.4 5.5 %collective-permute-done.22.refs_3_ = bf16[272,384]{1,0:T(8,128)(2,1)S(1)} collective-permute-done((bf16[272,384]{1,0:T(8,128)(2,1)S(1)}, bf16[272,384]{1,0:T(8,128)(2,1)S(1)}, u32[]{:S(2)}, u32[]{:S(2)}) %collective-permute-start.22) | collective-permute-done | bytes 208928 | tf_op jit(solution)/shard_map/ppermute | solution.py:752
  131.9 3.4 %collective-permute-done.21.refs_2_ = bf16[272,384]{1,0:T(8,128)(2,1)S(1)} collective-permute-done((bf16[272,384]{1,0:T(8,128)(2,1)S(1)}, bf16[272,384]{1,0:T(8,128)(2,1)S(1)}, u32[]{:S(2)}, u32[]{:S(2)}) %collective-permute-start.21) | collective-permute-done | bytes 208928 | tf_op jit(solution)/shard_map/ppermute | solution.py:752
  135.3 0.0 collective-permute-done.20.refs_1_
  135.3 1.1 shard_map.370.refs_0_
  136.5 0.1 collective-permute-start.23
  136.5 2.4 %shard_map.371 = (f32[192,384]{1,0:T(8,128)}, f32[192,384]{1,0:T(8,128)}, f32[192,384]{1,0:T(8,128)}, f32[192,384]{1,0:T(8,128)}, f32[768]{0:T(1024)}, /*index=5...) custom-call(bf16[272,384]{1,0:T(8,128)(2,1)S(1)} %add_convert_fusion, ...), custom_call_target="tpu_custom_call" | custom-call | flops 1 | bytes 1 | tf_op jit(solution)/shard_map/pallas_call | solution.py:208
  139.0 1.0 shard_map.372
  (29 shorter events, 0.1 us)
Async XLA Ops:
  0.7 10.4 %copy-start.7 = (s32[1023]{0:T(1024)S(1)}, s32[1023]{0:T(1024)}, u32[]{:S(2)}) copy-start(s32[1023]{0:T(1024)} %param.25) | copy-start | bytes 12280
  0.7 11.0 %copy-start.3 = (s32[16]{0:T(128)S(1)}, s32[16]{0:T(128)}, u32[]{:S(2)}) copy-start(s32[16]{0:T(128)} %refs_0_.10) | copy-start | bytes 196
  2.5 21.1 %copy-start.4 = (s32[16]{0:T(128)S(1)}, s32[16]{0:T(128)}, u32[]{:S(2)}) copy-start(s32[16]{0:T(128)} %refs_1_.3) | copy-start | bytes 196
  2.5 21.1 %all-to-all-start = ((bf16[16,32,384]{2,1,0:T(8,128)(2,1)}), bf16[16,32,384]{2,1,0:T(8,128)(2,1)S(1)}, u32[]{:S(2)}, u32[]{:S(2)}) async-start(bf16[16,32,384]{2,1,0:T(8,128)(2,1)} %pad_maximum_fusion), calls=%async_computation | async-start | bytes 786432 | tf_op jit(solution)/shard_map/all_to_all | solution.py:745
  25.0 18.1 %all-to-all-start.1 = ((bf16[16,32,384]{2,1,0:T(8,128)(2,1)}), bf16[16,32,384]{2,1,0:T(8,128)(2,1)S(1)}, u32[]{:S(2)}, u32[]{:S(2)}) async-start(bf16[16,32,384]{2,1,0:T(8,128)(2,1)} %shard_map.358), calls=%async_computation.1 | async-start | bytes 786432 | tf_op jit(solution)/shard_map/all_to_all | solution.py:745
  36.2 1.8 %collective-permute-start = (bf16[512,384]{1,0:T(8,128)(2,1)S(1)}, bf16[512,384]{1,0:T(8,128)(2,1)S(1)}, u32[]{:S(2)}, u32[]{:S(2)}) collective-permute-start(bf16[512,384]{1,0:T(8,128)(2,1)S(1)} %get-tuple-element.115.refs_1_), channel_id=1, source_target_pairs={{0,1},{1,0},{2,3},{3,2},{4,5},{5,4},{6,7},{7,6},{8,9},{9,8},{10,11... | collective-permute-start | bytes 1179656 | tf_op jit(solution)/shard_map/ppermute | solution.py:741
  41.8 1.8 %collective-permute-start.1 = (bf16[512,384]{1,0:T(8,128)(2,1)S(1)}, bf16[512,384]{1,0:T(8,128)(2,1)S(1)}, u32[]{:S(2)}, u32[]{:S(2)}) collective-permute-start(bf16[512,384]{1,0:T(8,128)(2,1)S(1)} %get-tuple-element.116.refs_1_), channel_id=1, source_target_pairs={{0,1},{1,0},{2,3},{3,2},{4,5},{5,4},{6,7},{7,6},{8,9},{9,8},{10,11... | collective-permute-start | bytes 1179656 | tf_op jit(solution)/shard_map/ppermute | solution.py:741
  43.1 8.6 %copy-start = (bf16[16,32,384]{2,1,0:T(8,128)(2,1)}, bf16[16,32,384]{2,1,0:T(8,128)(2,1)S(1)}, u32[]{:S(2)}) copy-start(bf16[16,32,384]{2,1,0:T(8,128)(2,1)S(1)} %all-to-all-done.1.refs_8_.refs_2_) | copy-start | bytes 1179652
  43.1 1.7 %collective-permute-start.2 = (bf16[16,32,384]{2,1,0:T(8,128)(2,1)S(1)}, bf16[16,32,384]{2,1,0:T(8,128)(2,1)S(1)}, u32[]{:S(2)}, u32[]{:S(2)}) collective-permute-start(bf16[16,32,384]{2,1,0:T(8,128)(2,1)S(1)} %all-to-all-done.1.refs_8_.refs_2_), channel_id=1, source_target_pairs={{0,1},{1,0},{2,3},{3,2},{4,5},{5,4},{6,7},{7,6},{8,9},{9,8},{10,11... | collective-permute-start | bytes 1179656 | tf_op jit(solution)/shard_map/ppermute | solution.py:741
  44.8 6.8 %copy-start.1 = (bf16[16,32,384]{2,1,0:T(8,128)(2,1)}, bf16[16,32,384]{2,1,0:T(8,128)(2,1)S(1)}, u32[]{:S(2)}) copy-start(bf16[16,32,384]{2,1,0:T(8,128)(2,1)S(1)} %collective-permute-done.2.refs_9_.refs_3_) | copy-start | bytes 1179652
  51.7 3.7 %collective-permute-start.3 = (bf16[512,384]{1,0:T(8,128)(2,1)S(1)}, bf16[512,384]{1,0:T(8,128)(2,1)S(1)}, u32[]{:S(2)}, u32[]{:S(2)}) collective-permute-start(bf16[512,384]{1,0:T(8,128)(2,1)S(1)} %get-tuple-element.123.refs_1_), channel_id=1, source_target_pairs={{0,1},{1,0},{2,3},{3,2},{4,5},{5,4},{6,7},{7,6},{8,9},{9,8},{10,11... | collective-permute-start | bytes 1179656 | tf_op jit(solution)/shard_map/ppermute | solution.py:741
  51.9 16.7 %collective-permute-start.4 = (bf16[384,384]{1,0:T(8,128)(2,1)}, bf16[384,384]{1,0:T(8,128)(2,1)S(1)}, u32[]{:S(2)}, u32[]{:S(2)}) collective-permute-start(bf16[384,384]{1,0:T(8,128)(2,1)} %get-tuple-element.131), channel_id=1, source_target_pairs={{0,2},{2,0},{4,6},{6,4},{8,10},{10,8},{12,14},{14,12},{16,18},{18,... | collective-permute-start | bytes 884744 | tf_op jit(solution)/shard_map/ppermute | solution.py:752
  53.1 15.5 %collective-permute-start.5 = (bf16[384,384]{1,0:T(8,128)(2,1)}, bf16[384,384]{1,0:T(8,128)(2,1)S(1)}, u32[]{:S(2)}, u32[]{:S(2)}) collective-permute-start(bf16[384,384]{1,0:T(8,128)(2,1)} %get-tuple-element.132), channel_id=1, source_target_pairs={{0,4},{2,6},{4,0},{6,2},{8,12},{10,14},{12,8},{14,10},{16,20},{18,... | collective-permute-start | bytes 884744 | tf_op jit(solution)/shard_map/ppermute | solution.py:752
  54.6 14.1 %collective-permute-start.6 = (bf16[384,384]{1,0:T(8,128)(2,1)}, bf16[384,384]{1,0:T(8,128)(2,1)S(1)}, u32[]{:S(2)}, u32[]{:S(2)}) collective-permute-start(bf16[384,384]{1,0:T(8,128)(2,1)} %get-tuple-element.133), channel_id=1, source_target_pairs={{0,6},{2,4},{4,2},{6,0},{8,14},{10,12},{12,10},{14,8},{16,22},{18,... | collective-permute-start | bytes 884744 | tf_op jit(solution)/shard_map/ppermute | solution.py:752
  55.4 13.3 %copy-start.5 = (bf16[384,384]{1,0:T(8,128)(2,1)S(1)}, bf16[384,384]{1,0:T(8,128)(2,1)}, u32[]{:S(2)}) copy-start(bf16[384,384]{1,0:T(8,128)(2,1)} %get-tuple-element.130) | copy-start | bytes 884740
  68.8 11.8 %collective-permute-start.7 = (bf16[384,384]{1,0:T(8,128)(2,1)S(1)}, bf16[384,384]{1,0:T(8,128)(2,1)S(1)}, u32[]{:S(2)}, u32[]{:S(2)}) collective-permute-start(bf16[384,384]{1,0:T(8,128)(2,1)S(1)} %add_convert_fusion.2), channel_id=1, source_target_pairs={{0,8},{2,10},{4,12},{6,14},{8,0},{10,2},{12,4},{14,6},{16,24},{18,... | collective-permute-start | bytes 884744 | tf_op jit(solution)/shard_map/ppermute | solution.py:882
  80.7 2.5 %collective-permute-start.8 = (bf16[768,384]{1,0:T(8,128)(2,1)}, bf16[768,384]{1,0:T(8,128)(2,1)S(1)}, u32[]{:S(2)}, u32[]{:S(2)}) collective-permute-start(bf16[768,384]{1,0:T(8,128)(2,1)} %get-tuple-element.150.refs_1_), channel_id=1, source_target_pairs={{0,1},{1,0},{2,3},{3,2},{4,5},{5,4},{6,7},{7,6},{8,9},{9,8},{10,11... | collective-permute-start | bytes 1769480 | tf_op jit(solution)/shard_map/ppermute | solution.py:741
  80.8 21.9 %collective-permute-start.12 = (bf16[384,384]{1,0:T(8,128)(2,1)S(1)}, bf16[384,384]{1,0:T(8,128)(2,1)S(1)}, u32[]{:S(2)}, u32[]{:S(2)}) collective-permute-start(bf16[384,384]{1,0:T(8,128)(2,1)S(1)} %add_convert_fusion.1), channel_id=1, source_target_pairs={{0,16},{2,18},{4,20},{6,22},{8,24},{10,26},{12,28},{14,30},{16,0},... | collective-permute-start | bytes 884744 | tf_op jit(solution)/shard_map/ppermute | solution.py:882
  83.3 4.2 %copy-start.2 = (bf16[768,384]{1,0:T(8,128)(2,1)}, bf16[768,384]{1,0:T(8,128)(2,1)S(1)}, u32[]{:S(2)}) copy-start(bf16[768,384]{1,0:T(8,128)(2,1)S(1)} %collective-permute-done.8.refs_10_.refs_2_) | copy-start | bytes 1769476
  87.5 15.3 %collective-permute-start.9 = (bf16[272,384]{1,0:T(8,128)(2,1)}, bf16[272,384]{1,0:T(8,128)(2,1)S(1)}, u32[]{:S(2)}, u32[]{:S(2)}) collective-permute-start(bf16[272,384]{1,0:T(8,128)(2,1)} %get-tuple-element.154), channel_id=1, source_target_pairs={{0,2},{2,0},{4,6},{6,4},{8,10},{10,8},{12,14},{14,12},{16,18},{18,... | collective-permute-start | bytes 626696 | tf_op jit(solution)/shard_map/ppermute | solution.py:752
  88.7 14.0 %collective-permute-start.10 = (bf16[272,384]{1,0:T(8,128)(2,1)}, bf16[272,384]{1,0:T(8,128)(2,1)S(1)}, u32[]{:S(2)}, u32[]{:S(2)}) collective-permute-start(bf16[272,384]{1,0:T(8,128)(2,1)} %get-tuple-element.155), channel_id=1, source_target_pairs={{0,4},{2,6},{4,0},{6,2},{8,12},{10,14},{12,8},{14,10},{16,20},{18,... | collective-permute-start | bytes 626696 | tf_op jit(solution)/shard_map/ppermute | solution.py:752
  90.2 12.6 %collective-permute-start.11 = (bf16[272,384]{1,0:T(8,128)(2,1)}, bf16[272,384]{1,0:T(8,128)(2,1)S(1)}, u32[]{:S(2)}, u32[]{:S(2)}) collective-permute-start(bf16[272,384]{1,0:T(8,128)(2,1)} %get-tuple-element.156), channel_id=1, source_target_pairs={{0,6},{2,4},{4,2},{6,0},{8,14},{10,12},{12,10},{14,8},{16,22},{18,... | collective-permute-start | bytes 626696 | tf_op jit(solution)/shard_map/ppermute | solution.py:752
  91.0 11.8 %copy-start.6 = (bf16[272,384]{1,0:T(8,128)(2,1)S(1)}, bf16[272,384]{1,0:T(8,128)(2,1)}, u32[]{:S(2)}) copy-start(bf16[272,384]{1,0:T(8,128)(2,1)} %get-tuple-element.159) | copy-start | bytes 626692
  103.0 4.2 %collective-permute-start.13 = (bf16[512,384]{1,0:T(8,128)(2,1)S(1)}, bf16[512,384]{1,0:T(8,128)(2,1)S(1)}, u32[]{:S(2)}, u32[]{:S(2)}) collective-permute-start(bf16[512,384]{1,0:T(8,128)(2,1)S(1)} %get-tuple-element.165.refs_1_), channel_id=1, source_target_pairs={{0,1},{1,0},{2,3},{3,2},{4,5},{5,4},{6,7},{7,6},{8,9},{9,8},{10,11... | collective-permute-start | bytes 1179656 | tf_op jit(solution)/shard_map/ppermute | solution.py:741
  103.1 7.6 %collective-permute-start.14 = (bf16[272,384]{1,0:T(8,128)(2,1)S(1)}, bf16[272,384]{1,0:T(8,128)(2,1)S(1)}, u32[]{:S(2)}, u32[]{:S(2)}) collective-permute-start(bf16[272,384]{1,0:T(8,128)(2,1)S(1)} %add_convert_fusion.5), channel_id=1, source_target_pairs={{0,8},{2,10},{4,12},{6,14},{8,0},{10,2},{12,4},{14,6},{16,24},{18,... | collective-permute-start | bytes 626696 | tf_op jit(solution)/shard_map/ppermute | solution.py:882
  103.7 14.0 %collective-permute-start.18 = (bf16[384,384]{1,0:T(8,128)(2,1)S(1)}, bf16[384,384]{1,0:T(8,128)(2,1)S(1)}, u32[]{:S(2)}, u32[]{:S(2)}) collective-permute-start(bf16[384,384]{1,0:T(8,128)(2,1)S(1)} %add_convert_fusion.refs_0_), channel_id=1, source_target_pairs={{0,6},{2,4},{4,2},{6,0},{8,14},{10,12},{12,10},{14,8},{16,22},{18,... | collective-permute-start | bytes 884744 | tf_op jit(solution)/shard_map/ppermute | solution.py:752
  105.8 14.2 %collective-permute-start.17 = (bf16[384,384]{1,0:T(8,128)(2,1)S(1)}, bf16[384,384]{1,0:T(8,128)(2,1)S(1)}, u32[]{:S(2)}, u32[]{:S(2)}) collective-permute-start(bf16[384,384]{1,0:T(8,128)(2,1)S(1)} %add_convert_fusion.refs_0_), channel_id=1, source_target_pairs={{0,4},{2,6},{4,0},{6,2},{8,12},{10,14},{12,8},{14,10},{16,20},{18,... | collective-permute-start | bytes 884744 | tf_op jit(solution)/shard_map/ppermute | solution.py:752
  106.3 13.7 %collective-permute-start.16 = (bf16[384,384]{1,0:T(8,128)(2,1)S(1)}, bf16[384,384]{1,0:T(8,128)(2,1)S(1)}, u32[]{:S(2)}, u32[]{:S(2)}) collective-permute-start(bf16[384,384]{1,0:T(8,128)(2,1)S(1)} %add_convert_fusion.refs_0_), channel_id=1, source_target_pairs={{0,2},{2,0},{4,6},{6,4},{8,10},{10,8},{12,14},{14,12},{16,18},{18,... | collective-permute-start | bytes 884744 | tf_op jit(solution)/shard_map/ppermute | solution.py:752
  110.7 12.1 %collective-permute-start.19 = (bf16[272,384]{1,0:T(8,128)(2,1)S(1)}, bf16[272,384]{1,0:T(8,128)(2,1)S(1)}, u32[]{:S(2)}, u32[]{:S(2)}) collective-permute-start(bf16[272,384]{1,0:T(8,128)(2,1)S(1)} %add_convert_fusion.4), channel_id=1, source_target_pairs={{0,16},{2,18},{4,20},{6,22},{8,24},{10,26},{12,28},{14,30},{16,0},... | collective-permute-start | bytes 626696 | tf_op jit(solution)/shard_map/ppermute | solution.py:882
  112.9 2.3 %collective-permute-start.15 = (bf16[512,384]{1,0:T(8,128)(2,1)S(1)}, bf16[512,384]{1,0:T(8,128)(2,1)S(1)}, u32[]{:S(2)}, u32[]{:S(2)}) collective-permute-start(bf16[512,384]{1,0:T(8,128)(2,1)S(1)} %get-tuple-element.169.refs_0_), channel_id=1, source_target_pairs={{0,1},{1,0},{2,3},{3,2},{4,5},{5,4},{6,7},{7,6},{8,9},{9,8},{10,11... | collective-permute-start | bytes 1179656 | tf_op jit(solution)/shard_map/ppermute | solution.py:741
  122.8 9.0 %collective-permute-start.22 = (bf16[272,384]{1,0:T(8,128)(2,1)S(1)}, bf16[272,384]{1,0:T(8,128)(2,1)S(1)}, u32[]{:S(2)}, u32[]{:S(2)}) collective-permute-start(bf16[272,384]{1,0:T(8,128)(2,1)S(1)} %add_convert_fusion.3.refs_0_), channel_id=1, source_target_pairs={{0,6},{2,4},{4,2},{6,0},{8,14},{10,12},{12,10},{14,8},{16,22},{18,... | collective-permute-start | bytes 626696 | tf_op jit(solution)/shard_map/ppermute | solution.py:752
  125.0 10.3 %collective-permute-start.21 = (bf16[272,384]{1,0:T(8,128)(2,1)S(1)}, bf16[272,384]{1,0:T(8,128)(2,1)S(1)}, u32[]{:S(2)}, u32[]{:S(2)}) collective-permute-start(bf16[272,384]{1,0:T(8,128)(2,1)S(1)} %add_convert_fusion.3.refs_0_), channel_id=1, source_target_pairs={{0,4},{2,6},{4,0},{6,2},{8,12},{10,14},{12,8},{14,10},{16,20},{18,... | collective-permute-start | bytes 626696 | tf_op jit(solution)/shard_map/ppermute | solution.py:752
  125.5 9.8 %collective-permute-start.20 = (bf16[272,384]{1,0:T(8,128)(2,1)S(1)}, bf16[272,384]{1,0:T(8,128)(2,1)S(1)}, u32[]{:S(2)}, u32[]{:S(2)}) collective-permute-start(bf16[272,384]{1,0:T(8,128)(2,1)S(1)} %add_convert_fusion.3.refs_0_), channel_id=1, source_target_pairs={{0,2},{2,0},{4,6},{6,4},{8,10},{10,8},{12,14},{14,12},{16,18},{18,... | collective-permute-start | bytes 626696 | tf_op jit(solution)/shard_map/ppermute | solution.py:752
  136.5 2.5 %collective-permute-start.23 = (bf16[256,384]{1,0:T(8,128)(2,1)S(1)}, bf16[256,384]{1,0:T(8,128)(2,1)S(1)}, u32[]{:S(2)}, u32[]{:S(2)}) collective-permute-start(bf16[256,384]{1,0:T(8,128)(2,1)S(1)} %shard_map.370.refs_0_), channel_id=1, source_target_pairs={{0,1},{1,0},{2,3},{3,2},{4,5},{5,4},{6,7},{7,6},{8,9},{9,8},{10,11... | collective-permute-start | bytes 589832 | tf_op jit(solution)/shard_map/ppermute | solution.py:741

commit v7 on v6

--- a/solution.py
+++ b/solution.py
@@ -140,7 +140,8 @@
     results, out_buffers, copies_out = [], [], 0
     for out in outs:
         if isinstance(out, Pieces):
-            results += [pltpu.HBM(out.shape, out.kind)] * out.count
+            here_out.update(range(len(results), len(results) + out.count))
+            results += [jax.ShapeDtypeStruct(out.shape, out.kind)] * out.count
             out_buffers.append(pltpu.VMEM((out.count,) + out.shape, out.kind))
             copies_out += out.count
         elif isinstance(out, Here):

time: 141 us -> 140 us (level)
  no operation moved by 1% of the time
where the time goes in v7:
time: 140 us; the launch traced here: 139 us
  Pallas kernels  80.8 us (58%)
  starting transfers between devices  36 us (26%)
  waiting for transfers between devices  18.2 us (13%)
  local copies, waits for them, and re-layouts  1.69 us (1%)
    pallas_call x15, Pallas kernels, call(): pl.pallas_call(kernel, out_shape=results, in_specs=[pl.BlockSpec(memory_s...  79.5 us
    all_to_all x2, starting transfers between devices, exchange(): return lax.all_to_all(array, 'dp', split_axis=0, concat_axis=0, tiled=True)  14.6 us
    ppermute x12, starting transfers between devices, trade(): got.append(lax.ppermute(array, 'dp', pairs))  14.1 us
    ppermute x12, waiting for transfers between devices, trade(): got.append(lax.ppermute(array, 'dp', pairs))  11.3 us
    ppermute x4, starting transfers between devices, far_step(): return lax.ppermute(array, 'dp', [(p, p ^ reach) for p in range(total)])  6.66 us
    ppermute x8, waiting for transfers between devices, swap(): return lax.ppermute(array, 'tensor', [(0, 1), (1, 0)])  3.44 us
  transfers between devices with their start and end apart: 26, of which 11 were waited for; matrix products, arithmetic and copies ran while one was open for 0% of the time, Pallas kernels for 51%

profile of v7, /device:TPU:0, one launch (start us, length us, event | category | flops | bytes accessed | tf_op | source)
XLA Modules:
  0.0 139.3 jit_solution(3910805919312378962)
XLA Ops:
  0.7 1.1 constant_dynamic-slice_fusion
  1.8 0.8 pad_maximum_fusion
  2.5 8.5 %all-to-all-start = ((bf16[16,32,384]{2,1,0:T(8,128)(2,1)}), bf16[16,32,384]{2,1,0:T(8,128)(2,1)S(1)}, u32[]{:S(2)}, u32[]{:S(2)}) async-start(bf16[16,32,384]{2,1,0:T(8,128)(2,1)} %pad_maximum_fusion), calls=%async_computation | async-start | bytes 786432 | tf_op jit(solution)/shard_map/all_to_all | solution.py:746
  11.0 0.6 pad_bitcast_fusion.refs_3_
  11.6 11.2 %shard_map.357 = (bf16[3,512,64]{2,1,0:T(8,128)(2,1)}, bf16[3,512,64]{2,1,0:T(8,128)(2,1)}, bf16[3,512,64]{2,1,0:T(8,128)(2,1)}, bf16[2,3,64,1024]{3,2,1,0:T(8,1...) custom-call(s32[16]{0:T(128)S(1)} %copy-done.3, ...), custom_call_target="tpu_custom_call" | custom-call | flops 1 | bytes 1 | tf_op jit(solution)/shard_map/pallas_call | solution.py:209
  22.8 0.8 all-to-all-done.refs_1_
  23.7 1.3 shard_map.358
  25.0 6.1 %all-to-all-start.1 = ((bf16[16,32,384]{2,1,0:T(8,128)(2,1)}), bf16[16,32,384]{2,1,0:T(8,128)(2,1)S(1)}, u32[]{:S(2)}, u32[]{:S(2)}) async-start(bf16[16,32,384]{2,1,0:T(8,128)(2,1)} %shard_map.358), calls=%async_computation.1 | async-start | bytes 786432 | tf_op jit(solution)/shard_map/all_to_all | solution.py:746
  31.1 5.1 %shard_map.359 = (bf16[1,512,512]{2,1,0:T(8,128)(2,1)}, bf16[1,512,64]{2,1,0:T(8,128)(2,1)}, bf16[512,384]{1,0:T(8,128)(2,1)S(1)}) custom-call(s32[16]{0:T(128)S(1)} %copy-done.3, bf16[3,512,64]{2,1,0:T(8,128)(2,1)} %get-tuple-element.108.refs_1_.refs_9_.refs_5_, bf16[3,512,64]{2,1,0:T(8,128)(2,1)} %get-tuple-element.109.refs_2_.refs_10_.refs_6_, ...), custom_call_target="tpu_custom_call" | custom-call | flops 1 | bytes 1 | tf_op jit(solution)/shard_map/pallas_call | solution.py:209
  36.2 0.1 collective-permute-start
  36.2 1.7 %collective-permute-done.refs_2_ = bf16[512,384]{1,0:T(8,128)(2,1)S(1)} collective-permute-done((bf16[512,384]{1,0:T(8,128)(2,1)S(1)}, bf16[512,384]{1,0:T(8,128)(2,1)S(1)}, u32[]{:S(2)}, u32[]{:S(2)}) %collective-permute-start) | collective-permute-done | bytes 393248 | tf_op jit(solution)/shard_map/ppermute | solution.py:742
  38.0 3.8 %shard_map.360 = (f32[512,384]{1,0:T(8,128)}, bf16[512,384]{1,0:T(8,128)(2,1)S(1)}, f32[512,1]{1,0:T(8,128)}, bf16[512,384]{1,0:T(8,128)(2,1)}, bf16[512,768]{1,0:T(8,128)(2,1)}, /*index=5*/bf16[512,768]{1,0:T(8,128)(2,1)}) custom-call(bf16[512,384]{1,0:T(8,128)(2,1)} %bitcast.14, bf16[512,384]{1,0:T(8,128)(2,1)S(1)} %get-tuple-element.115.refs_1_, ...), custom_call_target="tpu_custom_call" | custom-call | flops 1 | bytes 1 | tf_op jit(solution)/shard_map/pallas_call | solution.py:209
  41.8 0.2 collective-permute-start.1
  42.0 1.1 all-to-all-done.1.refs_8_.refs_2_
  43.1 0.0 collective-permute-start.2
  43.1 0.5 collective-permute-done.1.refs_2_
  43.6 1.3 collective-permute-done.2.refs_9_.refs_3_
  44.8 6.1 %shard_map.361 = (bf16[512,384]{1,0:T(8,128)(2,1)S(1)}, f32[512,384]{1,0:T(8,128)}, f32[8,384]{1,0:T(8,128)}, bf16[384,384]{1,0:T(8,128)(2,1)S(1)}, bf16[384,384...) custom-call(s32[16]{0:T(128)S(1)} %copy-done.3, ...), custom_call_target="tpu_custom_call" | custom-call | flops 1 | bytes 1 | tf_op jit(solution)/shard_map/pallas_call | solution.py:209
  50.9 0.2 collective-permute-start.3
  51.1 1.2 collective-permute-start.4
  52.3 1.5 %collective-permute-start.5 = (bf16[384,384]{1,0:T(8,128)(2,1)S(1)}, bf16[384,384]{1,0:T(8,128)(2,1)S(1)}, u32[]{:S(2)}, u32[]{:S(2)}) collective-permute-start(bf16[384,384]{1,0:T(8,128)(2,1)S(1)} %get-tuple-element.132), channel_id=1, source_target_pairs={{0,4},{2,6},{4,0},{6,2},{8,12},{10,14},{12,8},{14,10},{16,20},{18,... | collective-permute-start | bytes 884744 | tf_op jit(solution)/shard_map/ppermute | solution.py:753
  53.8 0.8 collective-permute-start.6
  54.6 0.0 collective-permute-done.3.refs_2_
  54.6 13.1 %shard_map.362 = (f32[512,384]{1,0:T(8,128)}, bf16[192,384]{1,0:T(8,128)(2,1)}, f32[8,384]{1,0:T(8,128)}, bf16[1,512,64]{2,1,0:T(8,128)(2,1)}, bf16[3,2,512,64]{...) custom-call(bf16[192,384]{1,0:T(8,128)(2,1)} %refs_11_.1, ...), custom_call_target="tpu_custom_call" | custom-call | flops 1 | bytes 1 | tf_op jit(solution)/shard_map/pallas_call | solution.py:209
  67.8 0.0 collective-permute-done.4
  67.8 0.2 add_convert_fusion.2
  68.0 1.4 collective-permute-start.7
  69.4 10.3 %shard_map.363 = (bf16[3,1,512,64]{3,2,1,0:T(8,128)(2,1)}, f32[512,192]{1,0:T(8,128)}, f32[512,192]{1,0:T(8,128)}, bf16[768,384]{1,0:T(8,128)(2,1)}, bf16[256,384]{1,0:T(8,128)(2,1)}) custom-call(bf16[512,1024]{1,0:T(8,128)(2,1)} %get-tuple-element.135.refs_0_, bf16[192,384]{1,0:T(8,128)(2,1)} %bitcast.17, bf16[192,384]{1,0:T(8,128)(2,1)} %bitcast.20, ...), custom_call_target="tpu_custom_call" | custom-call | flops 1 | bytes 1 | tf_op jit(solution)/shard_map/pallas_call | solution.py:209
  79.7 0.1 add_convert_fusion.1
  79.8 0.1 collective-permute-start.8
  79.8 2.4 %collective-permute-start.12 = (bf16[384,384]{1,0:T(8,128)(2,1)S(1)}, bf16[384,384]{1,0:T(8,128)(2,1)S(1)}, u32[]{:S(2)}, u32[]{:S(2)}) collective-permute-start(bf16[384,384]{1,0:T(8,128)(2,1)S(1)} %add_convert_fusion.1), channel_id=1, source_target_pairs={{0,16},{2,18},{4,20},{6,22},{8,24},{10,26},{12,28},{14,30},{16,0},... | collective-permute-start | bytes 884744 | tf_op jit(solution)/shard_map/ppermute | solution.py:883
  82.3 4.3 %shard_map.364 = (bf16[272,384]{1,0:T(8,128)(2,1)S(1)}, bf16[272,384]{1,0:T(8,128)(2,1)S(1)}, bf16[272,384]{1,0:T(8,128)(2,1)S(1)}, bf16[272,384]{1,0:T(8,128)(2,1)S(1)}) custom-call(bf16[512,384]{1,0:T(8,128)(2,1)} %bitcast.15, bf16[512,384]{1,0:T(8,128)(2,1)} %refs_1_.2, bf16[3,2,512,64]{3,2,1,0:T(8,128)(2,1)} %get-tuple-element.137.refs_10_.refs_2_, ...), custom_call_target="tpu_custom_call" | custom-call | flops 1 | bytes 1 | tf_op jit(solution)/shard_map/pallas_call | solution.py:209
  86.6 1.4 %collective-permute-start.9 = (bf16[272,384]{1,0:T(8,128)(2,1)S(1)}, bf16[272,384]{1,0:T(8,128)(2,1)S(1)}, u32[]{:S(2)}, u32[]{:S(2)}) collective-permute-start(bf16[272,384]{1,0:T(8,128)(2,1)S(1)} %get-tuple-element.154), channel_id=1, source_target_pairs={{0,2},{2,0},{4,6},{6,4},{8,10},{10,8},{12,14},{14,12},{16,18},{18,... | collective-permute-start | bytes 626696 | tf_op jit(solution)/shard_map/ppermute | solution.py:753
  88.0 1.5 %collective-permute-start.10 = (bf16[272,384]{1,0:T(8,128)(2,1)S(1)}, bf16[272,384]{1,0:T(8,128)(2,1)S(1)}, u32[]{:S(2)}, u32[]{:S(2)}) collective-permute-start(bf16[272,384]{1,0:T(8,128)(2,1)S(1)} %get-tuple-element.155), channel_id=1, source_target_pairs={{0,4},{2,6},{4,0},{6,2},{8,12},{10,14},{12,8},{14,10},{16,20},{18,... | collective-permute-start | bytes 626696 | tf_op jit(solution)/shard_map/ppermute | solution.py:753
  89.5 0.7 collective-permute-start.11
  90.2 11.7 %shard_map.365 = (bf16[512,384]{1,0:T(8,128)(2,1)}, bf16[512,384]{1,0:T(8,128)(2,1)S(1)}) custom-call(s32[16]{0:T(128)S(1)} %copy-done.3, s32[16]{0:T(128)S(1)} %copy-done.4, bf16[16,32,384]{2,1,0:T(8,128)(2,1)} %copy-done, bf16[16,32,384]{2,1,0:T(8,128)(2,1)} %copy-done.1, bf16[2,3,64,1024]{3,2,1,0:T(8,128)(2,1)} %get-tuple-element.111.refs_4_.refs_12_.refs_8_, ...), custom_call_target="tpu_custom_call" | custom-call | flops 1 | bytes 1 | tf_op jit(solution)/shard_map/pallas_call | solution.py:209
  102.0 0.1 add_convert_fusion.refs_0_
  102.0 0.1 add_convert_fusion.5
  102.2 0.1 collective-permute-start.13
  102.2 0.6 collective-permute-start.14
  102.9 2.2 %collective-permute-start.18 = (bf16[384,384]{1,0:T(8,128)(2,1)S(1)}, bf16[384,384]{1,0:T(8,128)(2,1)S(1)}, u32[]{:S(2)}, u32[]{:S(2)}) collective-permute-start(bf16[384,384]{1,0:T(8,128)(2,1)S(1)} %add_convert_fusion.refs_0_), channel_id=1, source_target_pairs={{0,6},{2,4},{4,2},{6,0},{8,14},{10,12},{12,10},{14,8},{16,22},{18,... | collective-permute-start | bytes 884744 | tf_op jit(solution)/shard_map/ppermute | solution.py:753
  105.1 0.5 collective-permute-start.17
  105.7 0.7 collective-permute-start.16
  106.4 2.8 %shard_map.366 = (f32[512,384]{1,0:T(8,128)}, bf16[512,384]{1,0:T(8,128)(2,1)S(1)}) custom-call(bf16[512,384]{1,0:T(8,128)(2,1)} %get-tuple-element.163.refs_0_, bf16[512,384]{1,0:T(8,128)(2,1)S(1)} %get-tuple-element.165.refs_1_, bf16[512,384]{1,0:T(8,128)(2,1)S(1)} %collective-permute-done.13.refs_2_, bf16[384]{0:T(512)(128)(2,1)} %refs_3_.4, ...), custom_call_target="tpu_custom_call" | custom-call | flops 1 | bytes 1 | tf_op jit(solution)/shard_map/pallas_call | solution.py:209
  109.2 0.6 collective-permute-done.14
  109.8 0.1 add_convert_fusion.4
  109.9 2.2 %collective-permute-start.19 = (bf16[272,384]{1,0:T(8,128)(2,1)S(1)}, bf16[272,384]{1,0:T(8,128)(2,1)S(1)}, u32[]{:S(2)}, u32[]{:S(2)}) collective-permute-start(bf16[272,384]{1,0:T(8,128)(2,1)S(1)} %add_convert_fusion.4), channel_id=1, source_target_pairs={{0,16},{2,18},{4,20},{6,22},{8,24},{10,26},{12,28},{14,30},{16,0},... | collective-permute-start | bytes 626696 | tf_op jit(solution)/shard_map/ppermute | solution.py:883
  112.1 2.2 %shard_map.367 = bf16[512,384]{1,0:T(8,128)(2,1)} custom-call(f32[512,384]{1,0:T(8,128)} %get-tuple-element.170.refs_0_, bf16[768,384]{1,0:T(8,128)(2,1)} %get-tuple-element.150.refs_1_, bf16[768,384]{1,0:T(8,128)(2,1)} %copy-done.2), custom_call_target="tpu_custom_call" | custom-call | flops 6000000000 | bytes 1 | tf_op jit(solution)/shard_map/pallas_call | solution.py:209
  114.3 2.6 %shard_map.368 = bf16[512,384]{1,0:T(8,128)(2,1)} custom-call(bf16[512,384]{1,0:T(8,128)(2,1)S(1)} %get-tuple-element.169.refs_0_, bf16[512,384]{1,0:T(8,128)(2,1)S(1)} %collective-permute-done.15.refs_1_, bf16[384]{0:T(512)(128)(2,1)} %refs_2_.2, f32[512,384]{1,0:T(8,128)} %get-tuple-element.167.refs_3_, bf16[384]{0:T(512)(128)(2,1)} %refs_4_.5, ...), custom_call_target="tpu_custom_call" | custom-call | flops 6000000000 | bytes 1 | tf_op jit(solution)/shard_map/pallas_call | solution.py:209
  116.9 2.2 %collective-permute-done.17.refs_2_ = bf16[384,384]{1,0:T(8,128)(2,1)S(1)} collective-permute-done((bf16[384,384]{1,0:T(8,128)(2,1)S(1)}, bf16[384,384]{1,0:T(8,128)(2,1)S(1)}, u32[]{:S(2)}, u32[]{:S(2)}) %collective-permute-start.17) | collective-permute-done | bytes 294944 | tf_op jit(solution)/shard_map/ppermute | solution.py:753
  119.1 0.1 collective-permute-done.16.refs_1_
  119.2 1.8 %shard_map.369 = (f32[384,768]{1,0:T(8,128)}, f32[768,384]{1,0:T(8,128)}) custom-call(bf16[384,384]{1,0:T(8,128)(2,1)S(1)} %add_convert_fusion.refs_0_, bf16[384,384]{1,0:T(8,128)(2,1)S(1)} %collective-permute-done.16.refs_1_, bf16[384,384]{1,0:T(8,128)(2,1)S(1)} %collective-permute-done.17.refs_2_, bf16[384,384]{1,0:T(8,128)(2,1)S(1)} %collective-permute-done.18.refs_3_), custom_call_target="tpu_custom_call" | custom-call | flops 6000000000 | bytes 1 | tf_op jit(solution)/shard_map/pallas_call | solution.py:209
  121.0 1.0 collective-permute-done.19
  121.9 0.1 add_convert_fusion.3.refs_0_
  122.0 2.3 %collective-permute-start.22 = (bf16[272,384]{1,0:T(8,128)(2,1)S(1)}, bf16[272,384]{1,0:T(8,128)(2,1)S(1)}, u32[]{:S(2)}, u32[]{:S(2)}) collective-permute-start(bf16[272,384]{1,0:T(8,128)(2,1)S(1)} %add_convert_fusion.3.refs_0_), channel_id=1, source_target_pairs={{0,6},{2,4},{4,2},{6,0},{8,14},{10,12},{12,10},{14,8},{16,22},{18,... | collective-permute-start | bytes 626696 | tf_op jit(solution)/shard_map/ppermute | solution.py:753
  124.3 0.6 collective-permute-start.21
  124.9 0.7 collective-permute-start.20
  125.6 5.5 %collective-permute-done.22.refs_3_ = bf16[272,384]{1,0:T(8,128)(2,1)S(1)} collective-permute-done((bf16[272,384]{1,0:T(8,128)(2,1)S(1)}, bf16[272,384]{1,0:T(8,128)(2,1)S(1)}, u32[]{:S(2)}, u32[]{:S(2)}) %collective-permute-start.22) | collective-permute-done | bytes 208928 | tf_op jit(solution)/shard_map/ppermute | solution.py:753
  131.0 3.4 %collective-permute-done.21.refs_2_ = bf16[272,384]{1,0:T(8,128)(2,1)S(1)} collective-permute-done((bf16[272,384]{1,0:T(8,128)(2,1)S(1)}, bf16[272,384]{1,0:T(8,128)(2,1)S(1)}, u32[]{:S(2)}, u32[]{:S(2)}) %collective-permute-start.21) | collective-permute-done | bytes 208928 | tf_op jit(solution)/shard_map/ppermute | solution.py:753
  134.5 0.0 collective-permute-done.20.refs_1_
  134.5 1.1 shard_map.370.refs_0_
  135.6 0.1 collective-permute-start.23
  135.7 2.4 %shard_map.371 = (f32[192,384]{1,0:T(8,128)}, f32[192,384]{1,0:T(8,128)}, f32[192,384]{1,0:T(8,128)}, f32[192,384]{1,0:T(8,128)}, f32[768]{0:T(1024)}, /*index=5...) custom-call(bf16[272,384]{1,0:T(8,128)(2,1)S(1)} %add_convert_fusion, ...), custom_call_target="tpu_custom_call" | custom-call | flops 1 | bytes 1 | tf_op jit(solution)/shard_map/pallas_call | solution.py:209
  138.1 1.0 shard_map.372
  (25 shorter events, 0.1 us)
Async XLA Ops:
  0.7 10.4 %copy-start.5 = (s32[1023]{0:T(1024)S(1)}, s32[1023]{0:T(1024)}, u32[]{:S(2)}) copy-start(s32[1023]{0:T(1024)} %param.25) | copy-start | bytes 12280
  0.7 11.0 %copy-start.3 = (s32[16]{0:T(128)S(1)}, s32[16]{0:T(128)}, u32[]{:S(2)}) copy-start(s32[16]{0:T(128)} %refs_0_.10) | copy-start | bytes 196
  2.5 21.1 %copy-start.4 = (s32[16]{0:T(128)S(1)}, s32[16]{0:T(128)}, u32[]{:S(2)}) copy-start(s32[16]{0:T(128)} %refs_1_.3) | copy-start | bytes 196
  2.5 21.1 %all-to-all-start = ((bf16[16,32,384]{2,1,0:T(8,128)(2,1)}), bf16[16,32,384]{2,1,0:T(8,128)(2,1)S(1)}, u32[]{:S(2)}, u32[]{:S(2)}) async-start(bf16[16,32,384]{2,1,0:T(8,128)(2,1)} %pad_maximum_fusion), calls=%async_computation | async-start | bytes 786432 | tf_op jit(solution)/shard_map/all_to_all | solution.py:746
  25.0 18.1 %all-to-all-start.1 = ((bf16[16,32,384]{2,1,0:T(8,128)(2,1)}), bf16[16,32,384]{2,1,0:T(8,128)(2,1)S(1)}, u32[]{:S(2)}, u32[]{:S(2)}) async-start(bf16[16,32,384]{2,1,0:T(8,128)(2,1)} %shard_map.358), calls=%async_computation.1 | async-start | bytes 786432 | tf_op jit(solution)/shard_map/all_to_all | solution.py:746
  36.2 1.8 %collective-permute-start = (bf16[512,384]{1,0:T(8,128)(2,1)S(1)}, bf16[512,384]{1,0:T(8,128)(2,1)S(1)}, u32[]{:S(2)}, u32[]{:S(2)}) collective-permute-start(bf16[512,384]{1,0:T(8,128)(2,1)S(1)} %get-tuple-element.115.refs_1_), channel_id=1, source_target_pairs={{0,1},{1,0},{2,3},{3,2},{4,5},{5,4},{6,7},{7,6},{8,9},{9,8},{10,11... | collective-permute-start | bytes 1179656 | tf_op jit(solution)/shard_map/ppermute | solution.py:742
  41.8 1.8 %collective-permute-start.1 = (bf16[512,384]{1,0:T(8,128)(2,1)S(1)}, bf16[512,384]{1,0:T(8,128)(2,1)S(1)}, u32[]{:S(2)}, u32[]{:S(2)}) collective-permute-start(bf16[512,384]{1,0:T(8,128)(2,1)S(1)} %get-tuple-element.116.refs_1_), channel_id=1, source_target_pairs={{0,1},{1,0},{2,3},{3,2},{4,5},{5,4},{6,7},{7,6},{8,9},{9,8},{10,11... | collective-permute-start | bytes 1179656 | tf_op jit(solution)/shard_map/ppermute | solution.py:742
  43.1 7.8 %copy-start = (bf16[16,32,384]{2,1,0:T(8,128)(2,1)}, bf16[16,32,384]{2,1,0:T(8,128)(2,1)S(1)}, u32[]{:S(2)}) copy-start(bf16[16,32,384]{2,1,0:T(8,128)(2,1)S(1)} %all-to-all-done.1.refs_8_.refs_2_) | copy-start | bytes 1179652
  43.1 1.7 %collective-permute-start.2 = (bf16[16,32,384]{2,1,0:T(8,128)(2,1)S(1)}, bf16[16,32,384]{2,1,0:T(8,128)(2,1)S(1)}, u32[]{:S(2)}, u32[]{:S(2)}) collective-permute-start(bf16[16,32,384]{2,1,0:T(8,128)(2,1)S(1)} %all-to-all-done.1.refs_8_.refs_2_), channel_id=1, source_target_pairs={{0,1},{1,0},{2,3},{3,2},{4,5},{5,4},{6,7},{7,6},{8,9},{9,8},{10,11... | collective-permute-start | bytes 1179656 | tf_op jit(solution)/shard_map/ppermute | solution.py:742
  44.8 6.1 %copy-start.1 = (bf16[16,32,384]{2,1,0:T(8,128)(2,1)}, bf16[16,32,384]{2,1,0:T(8,128)(2,1)S(1)}, u32[]{:S(2)}) copy-start(bf16[16,32,384]{2,1,0:T(8,128)(2,1)S(1)} %collective-permute-done.2.refs_9_.refs_3_) | copy-start | bytes 1179652
  50.9 3.7 %collective-permute-start.3 = (bf16[512,384]{1,0:T(8,128)(2,1)S(1)}, bf16[512,384]{1,0:T(8,128)(2,1)S(1)}, u32[]{:S(2)}, u32[]{:S(2)}) collective-permute-start(bf16[512,384]{1,0:T(8,128)(2,1)S(1)} %get-tuple-element.123.refs_1_), channel_id=1, source_target_pairs={{0,1},{1,0},{2,3},{3,2},{4,5},{5,4},{6,7},{7,6},{8,9},{9,8},{10,11... | collective-permute-start | bytes 1179656 | tf_op jit(solution)/shard_map/ppermute | solution.py:742
  51.1 16.6 %collective-permute-start.4 = (bf16[384,384]{1,0:T(8,128)(2,1)S(1)}, bf16[384,384]{1,0:T(8,128)(2,1)S(1)}, u32[]{:S(2)}, u32[]{:S(2)}) collective-permute-start(bf16[384,384]{1,0:T(8,128)(2,1)S(1)} %get-tuple-element.131), channel_id=1, source_target_pairs={{0,2},{2,0},{4,6},{6,4},{8,10},{10,8},{12,14},{14,12},{16,18},{18,... | collective-permute-start | bytes 884744 | tf_op jit(solution)/shard_map/ppermute | solution.py:753
  52.3 15.4 %collective-permute-start.5 = (bf16[384,384]{1,0:T(8,128)(2,1)S(1)}, bf16[384,384]{1,0:T(8,128)(2,1)S(1)}, u32[]{:S(2)}, u32[]{:S(2)}) collective-permute-start(bf16[384,384]{1,0:T(8,128)(2,1)S(1)} %get-tuple-element.132), channel_id=1, source_target_pairs={{0,4},{2,6},{4,0},{6,2},{8,12},{10,14},{12,8},{14,10},{16,20},{18,... | collective-permute-start | bytes 884744 | tf_op jit(solution)/shard_map/ppermute | solution.py:753
  53.8 14.0 %collective-permute-start.6 = (bf16[384,384]{1,0:T(8,128)(2,1)S(1)}, bf16[384,384]{1,0:T(8,128)(2,1)S(1)}, u32[]{:S(2)}, u32[]{:S(2)}) collective-permute-start(bf16[384,384]{1,0:T(8,128)(2,1)S(1)} %get-tuple-element.133), channel_id=1, source_target_pairs={{0,6},{2,4},{4,2},{6,0},{8,14},{10,12},{12,10},{14,8},{16,22},{18,... | collective-permute-start | bytes 884744 | tf_op jit(solution)/shard_map/ppermute | solution.py:753
  68.0 11.7 %collective-permute-start.7 = (bf16[384,384]{1,0:T(8,128)(2,1)S(1)}, bf16[384,384]{1,0:T(8,128)(2,1)S(1)}, u32[]{:S(2)}, u32[]{:S(2)}) collective-permute-start(bf16[384,384]{1,0:T(8,128)(2,1)S(1)} %add_convert_fusion.2), channel_id=1, source_target_pairs={{0,8},{2,10},{4,12},{6,14},{8,0},{10,2},{12,4},{14,6},{16,24},{18,... | collective-permute-start | bytes 884744 | tf_op jit(solution)/shard_map/ppermute | solution.py:883
  79.8 2.5 %collective-permute-start.8 = (bf16[768,384]{1,0:T(8,128)(2,1)}, bf16[768,384]{1,0:T(8,128)(2,1)S(1)}, u32[]{:S(2)}, u32[]{:S(2)}) collective-permute-start(bf16[768,384]{1,0:T(8,128)(2,1)} %get-tuple-element.150.refs_1_), channel_id=1, source_target_pairs={{0,1},{1,0},{2,3},{3,2},{4,5},{5,4},{6,7},{7,6},{8,9},{9,8},{10,11... | collective-permute-start | bytes 1769480 | tf_op jit(solution)/shard_map/ppermute | solution.py:742
  79.8 22.1 %collective-permute-start.12 = (bf16[384,384]{1,0:T(8,128)(2,1)S(1)}, bf16[384,384]{1,0:T(8,128)(2,1)S(1)}, u32[]{:S(2)}, u32[]{:S(2)}) collective-permute-start(bf16[384,384]{1,0:T(8,128)(2,1)S(1)} %add_convert_fusion.1), channel_id=1, source_target_pairs={{0,16},{2,18},{4,20},{6,22},{8,24},{10,26},{12,28},{14,30},{16,0},... | collective-permute-start | bytes 884744 | tf_op jit(solution)/shard_map/ppermute | solution.py:883
  82.3 4.4 %copy-start.2 = (bf16[768,384]{1,0:T(8,128)(2,1)}, bf16[768,384]{1,0:T(8,128)(2,1)S(1)}, u32[]{:S(2)}) copy-start(bf16[768,384]{1,0:T(8,128)(2,1)S(1)} %collective-permute-done.8.refs_10_.refs_2_) | copy-start | bytes 1769476
  86.6 15.3 %collective-permute-start.9 = (bf16[272,384]{1,0:T(8,128)(2,1)S(1)}, bf16[272,384]{1,0:T(8,128)(2,1)S(1)}, u32[]{:S(2)}, u32[]{:S(2)}) collective-permute-start(bf16[272,384]{1,0:T(8,128)(2,1)S(1)} %get-tuple-element.154), channel_id=1, source_target_pairs={{0,2},{2,0},{4,6},{6,4},{8,10},{10,8},{12,14},{14,12},{16,18},{18,... | collective-permute-start | bytes 626696 | tf_op jit(solution)/shard_map/ppermute | solution.py:753
  88.0 13.9 %collective-permute-start.10 = (bf16[272,384]{1,0:T(8,128)(2,1)S(1)}, bf16[272,384]{1,0:T(8,128)(2,1)S(1)}, u32[]{:S(2)}, u32[]{:S(2)}) collective-permute-start(bf16[272,384]{1,0:T(8,128)(2,1)S(1)} %get-tuple-element.155), channel_id=1, source_target_pairs={{0,4},{2,6},{4,0},{6,2},{8,12},{10,14},{12,8},{14,10},{16,20},{18,... | collective-permute-start | bytes 626696 | tf_op jit(solution)/shard_map/ppermute | solution.py:753
  89.5 12.4 %collective-permute-start.11 = (bf16[272,384]{1,0:T(8,128)(2,1)S(1)}, bf16[272,384]{1,0:T(8,128)(2,1)S(1)}, u32[]{:S(2)}, u32[]{:S(2)}) collective-permute-start(bf16[272,384]{1,0:T(8,128)(2,1)S(1)} %get-tuple-element.156), channel_id=1, source_target_pairs={{0,6},{2,4},{4,2},{6,0},{8,14},{10,12},{12,10},{14,8},{16,22},{18,... | collective-permute-start | bytes 626696 | tf_op jit(solution)/shard_map/ppermute | solution.py:753
  102.2 4.2 %collective-permute-start.13 = (bf16[512,384]{1,0:T(8,128)(2,1)S(1)}, bf16[512,384]{1,0:T(8,128)(2,1)S(1)}, u32[]{:S(2)}, u32[]{:S(2)}) collective-permute-start(bf16[512,384]{1,0:T(8,128)(2,1)S(1)} %get-tuple-element.165.refs_1_), channel_id=1, source_target_pairs={{0,1},{1,0},{2,3},{3,2},{4,5},{5,4},{6,7},{7,6},{8,9},{9,8},{10,11... | collective-permute-start | bytes 1179656 | tf_op jit(solution)/shard_map/ppermute | solution.py:742
  102.2 7.6 %collective-permute-start.14 = (bf16[272,384]{1,0:T(8,128)(2,1)S(1)}, bf16[272,384]{1,0:T(8,128)(2,1)S(1)}, u32[]{:S(2)}, u32[]{:S(2)}) collective-permute-start(bf16[272,384]{1,0:T(8,128)(2,1)S(1)} %add_convert_fusion.5), channel_id=1, source_target_pairs={{0,8},{2,10},{4,12},{6,14},{8,0},{10,2},{12,4},{14,6},{16,24},{18,... | collective-permute-start | bytes 626696 | tf_op jit(solution)/shard_map/ppermute | solution.py:883
  102.9 14.0 %collective-permute-start.18 = (bf16[384,384]{1,0:T(8,128)(2,1)S(1)}, bf16[384,384]{1,0:T(8,128)(2,1)S(1)}, u32[]{:S(2)}, u32[]{:S(2)}) collective-permute-start(bf16[384,384]{1,0:T(8,128)(2,1)S(1)} %add_convert_fusion.refs_0_), channel_id=1, source_target_pairs={{0,6},{2,4},{4,2},{6,0},{8,14},{10,12},{12,10},{14,8},{16,22},{18,... | collective-permute-start | bytes 884744 | tf_op jit(solution)/shard_map/ppermute | solution.py:753
  105.1 14.0 %collective-permute-start.17 = (bf16[384,384]{1,0:T(8,128)(2,1)S(1)}, bf16[384,384]{1,0:T(8,128)(2,1)S(1)}, u32[]{:S(2)}, u32[]{:S(2)}) collective-permute-start(bf16[384,384]{1,0:T(8,128)(2,1)S(1)} %add_convert_fusion.refs_0_), channel_id=1, source_target_pairs={{0,4},{2,6},{4,0},{6,2},{8,12},{10,14},{12,8},{14,10},{16,20},{18,... | collective-permute-start | bytes 884744 | tf_op jit(solution)/shard_map/ppermute | solution.py:753
  105.7 13.5 %collective-permute-start.16 = (bf16[384,384]{1,0:T(8,128)(2,1)S(1)}, bf16[384,384]{1,0:T(8,128)(2,1)S(1)}, u32[]{:S(2)}, u32[]{:S(2)}) collective-permute-start(bf16[384,384]{1,0:T(8,128)(2,1)S(1)} %add_convert_fusion.refs_0_), channel_id=1, source_target_pairs={{0,2},{2,0},{4,6},{6,4},{8,10},{10,8},{12,14},{14,12},{16,18},{18,... | collective-permute-start | bytes 884744 | tf_op jit(solution)/shard_map/ppermute | solution.py:753
  109.9 12.1 %collective-permute-start.19 = (bf16[272,384]{1,0:T(8,128)(2,1)S(1)}, bf16[272,384]{1,0:T(8,128)(2,1)S(1)}, u32[]{:S(2)}, u32[]{:S(2)}) collective-permute-start(bf16[272,384]{1,0:T(8,128)(2,1)S(1)} %add_convert_fusion.4), channel_id=1, source_target_pairs={{0,16},{2,18},{4,20},{6,22},{8,24},{10,26},{12,28},{14,30},{16,0},... | collective-permute-start | bytes 626696 | tf_op jit(solution)/shard_map/ppermute | solution.py:883
  112.1 2.3 %collective-permute-start.15 = (bf16[512,384]{1,0:T(8,128)(2,1)S(1)}, bf16[512,384]{1,0:T(8,128)(2,1)S(1)}, u32[]{:S(2)}, u32[]{:S(2)}) collective-permute-start(bf16[512,384]{1,0:T(8,128)(2,1)S(1)} %get-tuple-element.169.refs_0_), channel_id=1, source_target_pairs={{0,1},{1,0},{2,3},{3,2},{4,5},{5,4},{6,7},{7,6},{8,9},{9,8},{10,11... | collective-permute-start | bytes 1179656 | tf_op jit(solution)/shard_map/ppermute | solution.py:742
  122.0 9.0 %collective-permute-start.22 = (bf16[272,384]{1,0:T(8,128)(2,1)S(1)}, bf16[272,384]{1,0:T(8,128)(2,1)S(1)}, u32[]{:S(2)}, u32[]{:S(2)}) collective-permute-start(bf16[272,384]{1,0:T(8,128)(2,1)S(1)} %add_convert_fusion.3.refs_0_), channel_id=1, source_target_pairs={{0,6},{2,4},{4,2},{6,0},{8,14},{10,12},{12,10},{14,8},{16,22},{18,... | collective-permute-start | bytes 626696 | tf_op jit(solution)/shard_map/ppermute | solution.py:753
  124.3 10.2 %collective-permute-start.21 = (bf16[272,384]{1,0:T(8,128)(2,1)S(1)}, bf16[272,384]{1,0:T(8,128)(2,1)S(1)}, u32[]{:S(2)}, u32[]{:S(2)}) collective-permute-start(bf16[272,384]{1,0:T(8,128)(2,1)S(1)} %add_convert_fusion.3.refs_0_), channel_id=1, source_target_pairs={{0,4},{2,6},{4,0},{6,2},{8,12},{10,14},{12,8},{14,10},{16,20},{18,... | collective-permute-start | bytes 626696 | tf_op jit(solution)/shard_map/ppermute | solution.py:753
  124.9 9.6 %collective-permute-start.20 = (bf16[272,384]{1,0:T(8,128)(2,1)S(1)}, bf16[272,384]{1,0:T(8,128)(2,1)S(1)}, u32[]{:S(2)}, u32[]{:S(2)}) collective-permute-start(bf16[272,384]{1,0:T(8,128)(2,1)S(1)} %add_convert_fusion.3.refs_0_), channel_id=1, source_target_pairs={{0,2},{2,0},{4,6},{6,4},{8,10},{10,8},{12,14},{14,12},{16,18},{18,... | collective-permute-start | bytes 626696 | tf_op jit(solution)/shard_map/ppermute | solution.py:753
  135.6 2.5 %collective-permute-start.23 = (bf16[256,384]{1,0:T(8,128)(2,1)S(1)}, bf16[256,384]{1,0:T(8,128)(2,1)S(1)}, u32[]{:S(2)}, u32[]{:S(2)}) collective-permute-start(bf16[256,384]{1,0:T(8,128)(2,1)S(1)} %shard_map.370.refs_0_), channel_id=1, source_target_pairs={{0,1},{1,0},{2,3},{3,2},{4,5},{5,4},{6,7},{7,6},{8,9},{9,8},{10,11... | collective-permute-start | bytes 589832 | tf_op jit(solution)/shard_map/ppermute | solution.py:742

commit v8 on v7

--- a/solution.py
+++ b/solution.py
@@ -600,7 +600,7 @@
 
 def attention_backward_last(
     hot, wq, wk, wv, gctx, q, k, v, tab, prob, before, gpq_before, gpk_before,
-    g_out, gpq_out, gpk_out, send_out, keep_out,
+    g_out, gpq_out, gpk_out, sums_out, send_out, keep_out,
     gpq_scratch, gpk_scratch, rel_scratch, *scratch,
 ):
     side = lax.axis_index("tensor")
@@ -612,13 +612,15 @@
         0, q, k, v, tab, prob, gctx, anti, g_out, gpq_scratch, gpk_scratch, *scratch
     )
     send(g_out)
-    for first, here, out in (
-        (gpq_before, gpq_scratch, gpq_out), (gpk_before, gpk_scratch, gpk_out)
+    for slot, (first, here, out) in enumerate(
+        ((gpq_before, gpq_scratch, gpq_out), (gpk_before, gpk_scratch, gpk_out))
     ):
         parts = [first[h] for h in range(first.shape[0])] + [here[0]]
-        out[...] = mm(hot[...], jnp.concatenate(parts, axis=0), NT) * scale
-    rel_scratch[...] = mm(gpq_out[...].astype(LOW), wq[...]) + mm(gpk_out[...].astype(LOW), wk[...])
-    send(gpq_out, gpk_out)
+        value = mm(hot[...], jnp.concatenate(parts, axis=0), NT) * scale
+        out[...] = value.astype(LOW)
+        sums_out[slot : slot + 1, :] = jnp.sum(value, axis=0, keepdims=True)
+    rel_scratch[...] = mm(gpq_out[...], wq[...]) + mm(gpk_out[...], wk[...])
+    send(gpq_out, gpk_out, sums_out)
     rows = buckets
     send_out[rows:, :] = rel_scratch[
         pl.ds(pl.multiple_of((1 - side) * half, half), half), :
@@ -637,7 +639,7 @@
 
 
 def weight_gradients(
-    chunk, x, relative, before, last, gpq, gpk, wout_grad, small_ffn, small_attn, keep, got,
+    chunk, x, relative, before, last, gpq, gpk, sums, wout_grad, small_ffn, small_attn, keep, got,
     buffer_out,
 ):
     part = gpq.shape[1]
@@ -646,11 +648,11 @@
     gq, gk, gv = (together(slot, before, last) for slot in range(3))
     put(
         buffer_out, chunk, 0,
-        (mm(gq, xv, TN) + mm(gpq[...].astype(LOW), rel, TN)).astype(LOW),
+        (mm(gq, xv, TN) + mm(gpq[...], rel, TN)).astype(LOW),
     )
     put(
         buffer_out, chunk, part,
-        (mm(gk, xv, TN) + mm(gpk[...].astype(LOW), rel, TN)).astype(LOW),
+        (mm(gk, xv, TN) + mm(gpk[...], rel, TN)).astype(LOW),
     )
     put(buffer_out, chunk, 2 * part, mm(gv, xv, TN).astype(LOW))
     put(buffer_out, chunk, 3 * part, wout_grad[...])
@@ -659,8 +661,8 @@
     put(buffer_out, chunk, 4 * part, both)
     count = 4 * part + keep.shape[0]
     bias = [
-        jnp.sum(gq.astype(WIDE), axis=0, keepdims=True) + jnp.sum(gpq[...], axis=0, keepdims=True),
-        jnp.sum(gk.astype(WIDE), axis=0, keepdims=True) + jnp.sum(gpk[...], axis=0, keepdims=True),
+        jnp.sum(gq.astype(WIDE), axis=0, keepdims=True) + sums[0:1, :],
+        jnp.sum(gk.astype(WIDE), axis=0, keepdims=True) + sums[1:2, :],
         jnp.sum(gv.astype(WIDE), axis=0, keepdims=True),
     ]
     second = jnp.concatenate([bias[2], jnp.zeros_like(bias[2])], axis=1)
@@ -909,9 +911,10 @@
     )
     line_one = total_of(near_one[0], near_one[1:])
     got_one = far_step(line_one, 0)
-    g_last, gpq, gpk, send_part, rel_keep = run(
+    g_last, gpq, gpk, sums, send_part, rel_keep = run(
         attention_backward_last,
-        [((3, 1, rows, HEAD_DIM), LOW), ((rows, part), WIDE), ((rows, part), WIDE),
+        [((3, 1, rows, HEAD_DIM), LOW), ((rows, part), LOW), ((rows, part), LOW),
+         ((2, part), WIDE),
          ((rows + half, width), LOW), ((half, width), LOW)],
         (hot, w_query.T, w_key.T, w_value.T, gctx)
         + tuple(Part(array, 0, before, 1) for array in (q, k, v))
@@ -930,7 +933,7 @@
     (near_two,) = run(
         with_statics(weight_gradients, chunk_two),
         [Pieces(inner, (chunk_two, width), LOW)],
-        (x, relative, g_before, g_last, gpq, gpk, wout_grad, small_ffn, small_attn, rel_keep,
+        (x, relative, g_before, g_last, gpq, gpk, sums, wout_grad, small_ffn, small_attn, rel_keep,
          Here(send_got)),
     )
     near_two[1:] = trade(near_two[1:], near_groups)

time: 140 us -> 140 us (level)
  no operation moved by 1% of the time
where the time goes in v8:
time: 140 us; the launch traced here: 139 us
  Pallas kernels  80.9 us (58%)
  starting transfers between devices  36 us (26%)
  waiting for transfers between devices  18.3 us (13%)
  local copies, waits for them, and re-layouts  1.69 us (1%)
    pallas_call x15, Pallas kernels, call(): pl.pallas_call(kernel, out_shape=results, in_specs=[pl.BlockSpec(memory_s...  79.6 us
    all_to_all x2, starting transfers between devices, exchange(): return lax.all_to_all(array, 'dp', split_axis=0, concat_axis=0, tiled=True)  14.6 us
    ppermute x12, starting transfers between devices, trade(): got.append(lax.ppermute(array, 'dp', pairs))  14.1 us
    ppermute x12, waiting for transfers between devices, trade(): got.append(lax.ppermute(array, 'dp', pairs))  11.3 us
    ppermute x4, starting transfers between devices, far_step(): return lax.ppermute(array, 'dp', [(p, p ^ reach) for p in range(total)])  6.65 us
    ppermute x8, waiting for transfers between devices, swap(): return lax.ppermute(array, 'tensor', [(0, 1), (1, 0)])  3.44 us
  transfers between devices with their start and end apart: 26, of which 11 were waited for; matrix products, arithmetic and copies ran while one was open for 0% of the time, Pallas kernels for 51%

profile of v8, /device:TPU:0, one launch (start us, length us, event | category | flops | bytes accessed | tf_op | source)
XLA Modules:
  0.0 139.4 jit_solution(7524914323133693972)
XLA Ops:
  0.7 1.1 constant_dynamic-slice_fusion
  1.8 0.8 pad_maximum_fusion
  2.5 8.5 %all-to-all-start = ((bf16[16,32,384]{2,1,0:T(8,128)(2,1)}), bf16[16,32,384]{2,1,0:T(8,128)(2,1)S(1)}, u32[]{:S(2)}, u32[]{:S(2)}) async-start(bf16[16,32,384]{2,1,0:T(8,128)(2,1)} %pad_maximum_fusion), calls=%async_computation | async-start | bytes 786432 | tf_op jit(solution)/shard_map/all_to_all | solution.py:748
  11.0 0.6 pad_bitcast_fusion.refs_3_
  11.6 11.2 %shard_map.357 = (bf16[3,512,64]{2,1,0:T(8,128)(2,1)}, bf16[3,512,64]{2,1,0:T(8,128)(2,1)}, bf16[3,512,64]{2,1,0:T(8,128)(2,1)}, bf16[2,3,64,1024]{3,2,1,0:T(8,1...) custom-call(s32[16]{0:T(128)S(1)} %copy-done.3, ...), custom_call_target="tpu_custom_call" | custom-call | flops 1 | bytes 1 | tf_op jit(solution)/shard_map/pallas_call | solution.py:209
  22.8 0.8 all-to-all-done.refs_1_
  23.7 1.3 shard_map.358
  25.0 6.1 %all-to-all-start.1 = ((bf16[16,32,384]{2,1,0:T(8,128)(2,1)}), bf16[16,32,384]{2,1,0:T(8,128)(2,1)S(1)}, u32[]{:S(2)}, u32[]{:S(2)}) async-start(bf16[16,32,384]{2,1,0:T(8,128)(2,1)} %shard_map.358), calls=%async_computation.1 | async-start | bytes 786432 | tf_op jit(solution)/shard_map/all_to_all | solution.py:748
  31.1 5.1 %shard_map.359 = (bf16[1,512,512]{2,1,0:T(8,128)(2,1)}, bf16[1,512,64]{2,1,0:T(8,128)(2,1)}, bf16[512,384]{1,0:T(8,128)(2,1)S(1)}) custom-call(s32[16]{0:T(128)S(1)} %copy-done.3, bf16[3,512,64]{2,1,0:T(8,128)(2,1)} %get-tuple-element.109.refs_1_.refs_9_.refs_5_, bf16[3,512,64]{2,1,0:T(8,128)(2,1)} %get-tuple-element.110.refs_2_.refs_10_.refs_6_, ...), custom_call_target="tpu_custom_call" | custom-call | flops 1 | bytes 1 | tf_op jit(solution)/shard_map/pallas_call | solution.py:209
  36.2 0.1 collective-permute-start
  36.2 1.7 %collective-permute-done.refs_2_ = bf16[512,384]{1,0:T(8,128)(2,1)S(1)} collective-permute-done((bf16[512,384]{1,0:T(8,128)(2,1)S(1)}, bf16[512,384]{1,0:T(8,128)(2,1)S(1)}, u32[]{:S(2)}, u32[]{:S(2)}) %collective-permute-start) | collective-permute-done | bytes 393248 | tf_op jit(solution)/shard_map/ppermute | solution.py:744
  38.0 3.8 %shard_map.360 = (f32[512,384]{1,0:T(8,128)}, bf16[512,384]{1,0:T(8,128)(2,1)S(1)}, f32[512,1]{1,0:T(8,128)}, bf16[512,384]{1,0:T(8,128)(2,1)}, bf16[512,768]{1,0:T(8,128)(2,1)}, /*index=5*/bf16[512,768]{1,0:T(8,128)(2,1)}) custom-call(bf16[512,384]{1,0:T(8,128)(2,1)} %bitcast.14, bf16[512,384]{1,0:T(8,128)(2,1)S(1)} %get-tuple-element.116.refs_1_, ...), custom_call_target="tpu_custom_call" | custom-call | flops 1 | bytes 1 | tf_op jit(solution)/shard_map/pallas_call | solution.py:209
  41.8 0.2 collective-permute-start.1
  42.0 1.1 all-to-all-done.1.refs_8_.refs_2_
  43.1 0.0 collective-permute-start.2
  43.1 0.5 collective-permute-done.1.refs_2_
  43.6 1.3 collective-permute-done.2.refs_9_.refs_3_
  44.8 6.1 %shard_map.361 = (bf16[512,384]{1,0:T(8,128)(2,1)S(1)}, f32[512,384]{1,0:T(8,128)}, f32[8,384]{1,0:T(8,128)}, bf16[384,384]{1,0:T(8,128)(2,1)S(1)}, bf16[384,384...) custom-call(s32[16]{0:T(128)S(1)} %copy-done.3, ...), custom_call_target="tpu_custom_call" | custom-call | flops 1 | bytes 1 | tf_op jit(solution)/shard_map/pallas_call | solution.py:209
  50.9 0.2 collective-permute-start.3
  51.1 1.2 collective-permute-start.4
  52.3 1.5 %collective-permute-start.5 = (bf16[384,384]{1,0:T(8,128)(2,1)S(1)}, bf16[384,384]{1,0:T(8,128)(2,1)S(1)}, u32[]{:S(2)}, u32[]{:S(2)}) collective-permute-start(bf16[384,384]{1,0:T(8,128)(2,1)S(1)} %get-tuple-element.133), channel_id=1, source_target_pairs={{0,4},{2,6},{4,0},{6,2},{8,12},{10,14},{12,8},{14,10},{16,20},{18,... | collective-permute-start | bytes 884744 | tf_op jit(solution)/shard_map/ppermute | solution.py:755
  53.8 0.8 collective-permute-start.6
  54.6 0.0 collective-permute-done.3.refs_2_
  54.6 13.1 %shard_map.362 = (f32[512,384]{1,0:T(8,128)}, bf16[192,384]{1,0:T(8,128)(2,1)}, f32[8,384]{1,0:T(8,128)}, bf16[1,512,64]{2,1,0:T(8,128)(2,1)}, bf16[3,2,512,64]{...) custom-call(bf16[192,384]{1,0:T(8,128)(2,1)} %refs_11_.1, ...), custom_call_target="tpu_custom_call" | custom-call | flops 1 | bytes 1 | tf_op jit(solution)/shard_map/pallas_call | solution.py:209
  67.8 0.0 collective-permute-done.5
  67.8 0.2 add_convert_fusion.2
  68.0 1.4 collective-permute-start.7
  69.4 10.3 %shard_map.363 = (bf16[3,1,512,64]{3,2,1,0:T(8,128)(2,1)}, bf16[512,192]{1,0:T(8,128)(2,1)}, bf16[512,192]{1,0:T(8,128)(2,1)}, f32[2,192]{1,0:T(2,128)}, bf16[76...) custom-call(bf16[512,1024]{1,0:T(8,128)(2,1)} %get-tuple-element.136.refs_0_, bf16[192,384]{1,0:T(8,128)(2,1)} %bitcast.17, ...), custom_call_target="tpu_custom_call" | custom-call | flops 1 | bytes 1 | tf_op jit(solution)/shard_map/pallas_call | solution.py:209
  79.7 0.1 add_convert_fusion.1
  79.8 0.1 collective-permute-start.8
  79.9 2.4 %collective-permute-start.12 = (bf16[384,384]{1,0:T(8,128)(2,1)S(1)}, bf16[384,384]{1,0:T(8,128)(2,1)S(1)}, u32[]{:S(2)}, u32[]{:S(2)}) collective-permute-start(bf16[384,384]{1,0:T(8,128)(2,1)S(1)} %add_convert_fusion.1), channel_id=1, source_target_pairs={{0,16},{2,18},{4,20},{6,22},{8,24},{10,26},{12,28},{14,30},{16,0},... | collective-permute-start | bytes 884744 | tf_op jit(solution)/shard_map/ppermute | solution.py:885
  82.3 4.4 %shard_map.364 = (bf16[272,384]{1,0:T(8,128)(2,1)S(1)}, bf16[272,384]{1,0:T(8,128)(2,1)S(1)}, bf16[272,384]{1,0:T(8,128)(2,1)S(1)}, bf16[272,384]{1,0:T(8,128)(2,1)S(1)}) custom-call(bf16[512,384]{1,0:T(8,128)(2,1)} %bitcast.15, bf16[512,384]{1,0:T(8,128)(2,1)} %refs_1_.2, bf16[3,2,512,64]{3,2,1,0:T(8,128)(2,1)} %get-tuple-element.138.refs_10_.refs_2_, ...), custom_call_target="tpu_custom_call" | custom-call | flops 1 | bytes 1 | tf_op jit(solution)/shard_map/pallas_call | solution.py:209
  86.7 1.4 %collective-permute-start.9 = (bf16[272,384]{1,0:T(8,128)(2,1)S(1)}, bf16[272,384]{1,0:T(8,128)(2,1)S(1)}, u32[]{:S(2)}, u32[]{:S(2)}) collective-permute-start(bf16[272,384]{1,0:T(8,128)(2,1)S(1)} %get-tuple-element.156), channel_id=1, source_target_pairs={{0,2},{2,0},{4,6},{6,4},{8,10},{10,8},{12,14},{14,12},{16,18},{18,... | collective-permute-start | bytes 626696 | tf_op jit(solution)/shard_map/ppermute | solution.py:755
  88.1 1.5 %collective-permute-start.10 = (bf16[272,384]{1,0:T(8,128)(2,1)S(1)}, bf16[272,384]{1,0:T(8,128)(2,1)S(1)}, u32[]{:S(2)}, u32[]{:S(2)}) collective-permute-start(bf16[272,384]{1,0:T(8,128)(2,1)S(1)} %get-tuple-element.157), channel_id=1, source_target_pairs={{0,4},{2,6},{4,0},{6,2},{8,12},{10,14},{12,8},{14,10},{16,20},{18,... | collective-permute-start | bytes 626696 | tf_op jit(solution)/shard_map/ppermute | solution.py:755
  89.6 0.7 collective-permute-start.11
  90.3 11.7 %shard_map.365 = (bf16[512,384]{1,0:T(8,128)(2,1)}, bf16[512,384]{1,0:T(8,128)(2,1)S(1)}) custom-call(s32[16]{0:T(128)S(1)} %copy-done.3, s32[16]{0:T(128)S(1)} %copy-done.4, bf16[16,32,384]{2,1,0:T(8,128)(2,1)} %copy-done, bf16[16,32,384]{2,1,0:T(8,128)(2,1)} %copy-done.1, bf16[2,3,64,1024]{3,2,1,0:T(8,128)(2,1)} %get-tuple-element.112.refs_4_.refs_12_.refs_8_, ...), custom_call_target="tpu_custom_call" | custom-call | flops 1 | bytes 1 | tf_op jit(solution)/shard_map/pallas_call | solution.py:209
  102.0 0.1 add_convert_fusion.refs_0_
  102.1 0.1 add_convert_fusion.5
  102.2 0.1 collective-permute-start.13
  102.3 0.6 collective-permute-start.14
  102.9 2.2 %collective-permute-start.18 = (bf16[384,384]{1,0:T(8,128)(2,1)S(1)}, bf16[384,384]{1,0:T(8,128)(2,1)S(1)}, u32[]{:S(2)}, u32[]{:S(2)}) collective-permute-start(bf16[384,384]{1,0:T(8,128)(2,1)S(1)} %add_convert_fusion.refs_0_), channel_id=1, source_target_pairs={{0,6},{2,4},{4,2},{6,0},{8,14},{10,12},{12,10},{14,8},{16,22},{18,... | collective-permute-start | bytes 884744 | tf_op jit(solution)/shard_map/ppermute | solution.py:755
  105.2 0.5 collective-permute-start.17
  105.7 0.7 collective-permute-start.16
  106.4 2.8 %shard_map.366 = (f32[512,384]{1,0:T(8,128)}, bf16[512,384]{1,0:T(8,128)(2,1)S(1)}) custom-call(bf16[512,384]{1,0:T(8,128)(2,1)} %get-tuple-element.165.refs_0_, bf16[512,384]{1,0:T(8,128)(2,1)S(1)} %get-tuple-element.167.refs_1_, bf16[512,384]{1,0:T(8,128)(2,1)S(1)} %collective-permute-done.13.refs_2_, bf16[384]{0:T(512)(128)(2,1)} %refs_3_.4, ...), custom_call_target="tpu_custom_call" | custom-call | flops 1 | bytes 1 | tf_op jit(solution)/shard_map/pallas_call | solution.py:209
  109.3 0.6 collective-permute-done.14
  109.9 0.1 add_convert_fusion.4
  109.9 2.2 %collective-permute-start.19 = (bf16[272,384]{1,0:T(8,128)(2,1)S(1)}, bf16[272,384]{1,0:T(8,128)(2,1)S(1)}, u32[]{:S(2)}, u32[]{:S(2)}) collective-permute-start(bf16[272,384]{1,0:T(8,128)(2,1)S(1)} %add_convert_fusion.4), channel_id=1, source_target_pairs={{0,16},{2,18},{4,20},{6,22},{8,24},{10,26},{12,28},{14,30},{16,0},... | collective-permute-start | bytes 626696 | tf_op jit(solution)/shard_map/ppermute | solution.py:885
  112.1 2.2 %shard_map.367 = bf16[512,384]{1,0:T(8,128)(2,1)} custom-call(f32[512,384]{1,0:T(8,128)} %get-tuple-element.172.refs_0_, bf16[768,384]{1,0:T(8,128)(2,1)} %get-tuple-element.152.refs_1_, bf16[768,384]{1,0:T(8,128)(2,1)} %copy-done.2), custom_call_target="tpu_custom_call" | custom-call | flops 6000000000 | bytes 1 | tf_op jit(solution)/shard_map/pallas_call | solution.py:209
  114.4 2.6 %shard_map.368 = bf16[512,384]{1,0:T(8,128)(2,1)} custom-call(bf16[512,384]{1,0:T(8,128)(2,1)S(1)} %get-tuple-element.171.refs_0_, bf16[512,384]{1,0:T(8,128)(2,1)S(1)} %collective-permute-done.15.refs_1_, bf16[384]{0:T(512)(128)(2,1)} %refs_2_.2, f32[512,384]{1,0:T(8,128)} %get-tuple-element.169.refs_3_, bf16[384]{0:T(512)(128)(2,1)} %refs_4_.5, ...), custom_call_target="tpu_custom_call" | custom-call | flops 6000000000 | bytes 1 | tf_op jit(solution)/shard_map/pallas_call | solution.py:209
  117.0 2.2 %collective-permute-done.17.refs_2_ = bf16[384,384]{1,0:T(8,128)(2,1)S(1)} collective-permute-done((bf16[384,384]{1,0:T(8,128)(2,1)S(1)}, bf16[384,384]{1,0:T(8,128)(2,1)S(1)}, u32[]{:S(2)}, u32[]{:S(2)}) %collective-permute-start.17) | collective-permute-done | bytes 294944 | tf_op jit(solution)/shard_map/ppermute | solution.py:755
  119.2 0.1 collective-permute-done.16.refs_1_
  119.3 1.8 %shard_map.369 = (f32[384,768]{1,0:T(8,128)}, f32[768,384]{1,0:T(8,128)}) custom-call(bf16[384,384]{1,0:T(8,128)(2,1)S(1)} %add_convert_fusion.refs_0_, bf16[384,384]{1,0:T(8,128)(2,1)S(1)} %collective-permute-done.16.refs_1_, bf16[384,384]{1,0:T(8,128)(2,1)S(1)} %collective-permute-done.17.refs_2_, bf16[384,384]{1,0:T(8,128)(2,1)S(1)} %collective-permute-done.18.refs_3_), custom_call_target="tpu_custom_call" | custom-call | flops 6000000000 | bytes 1 | tf_op jit(solution)/shard_map/pallas_call | solution.py:209
  121.0 1.0 collective-permute-done.19
  122.0 0.1 add_convert_fusion.3.refs_0_
  122.1 2.3 %collective-permute-start.22 = (bf16[272,384]{1,0:T(8,128)(2,1)S(1)}, bf16[272,384]{1,0:T(8,128)(2,1)S(1)}, u32[]{:S(2)}, u32[]{:S(2)}) collective-permute-start(bf16[272,384]{1,0:T(8,128)(2,1)S(1)} %add_convert_fusion.3.refs_0_), channel_id=1, source_target_pairs={{0,6},{2,4},{4,2},{6,0},{8,14},{10,12},{12,10},{14,8},{16,22},{18,... | collective-permute-start | bytes 626696 | tf_op jit(solution)/shard_map/ppermute | solution.py:755
  124.4 0.6 collective-permute-start.21
  124.9 0.7 collective-permute-start.20
  125.6 5.5 %collective-permute-done.22.refs_3_ = bf16[272,384]{1,0:T(8,128)(2,1)S(1)} collective-permute-done((bf16[272,384]{1,0:T(8,128)(2,1)S(1)}, bf16[272,384]{1,0:T(8,128)(2,1)S(1)}, u32[]{:S(2)}, u32[]{:S(2)}) %collective-permute-start.22) | collective-permute-done | bytes 208928 | tf_op jit(solution)/shard_map/ppermute | solution.py:755
  131.1 3.4 %collective-permute-done.21.refs_2_ = bf16[272,384]{1,0:T(8,128)(2,1)S(1)} collective-permute-done((bf16[272,384]{1,0:T(8,128)(2,1)S(1)}, bf16[272,384]{1,0:T(8,128)(2,1)S(1)}, u32[]{:S(2)}, u32[]{:S(2)}) %collective-permute-start.21) | collective-permute-done | bytes 208928 | tf_op jit(solution)/shard_map/ppermute | solution.py:755
  134.5 0.0 collective-permute-done.20.refs_1_
  134.6 1.1 shard_map.370.refs_0_
  135.7 0.1 collective-permute-start.23
  135.8 2.4 %shard_map.371 = (f32[192,384]{1,0:T(8,128)}, f32[192,384]{1,0:T(8,128)}, f32[192,384]{1,0:T(8,128)}, f32[192,384]{1,0:T(8,128)}, f32[768]{0:T(1024)}, /*index=5...) custom-call(bf16[272,384]{1,0:T(8,128)(2,1)S(1)} %add_convert_fusion, ...), custom_call_target="tpu_custom_call" | custom-call | flops 1 | bytes 1 | tf_op jit(solution)/shard_map/pallas_call | solution.py:209
  138.2 1.0 shard_map.372
  (25 shorter events, 0.1 us)
Async XLA Ops:
  0.7 10.4 %copy-start.5 = (s32[1023]{0:T(1024)S(1)}, s32[1023]{0:T(1024)}, u32[]{:S(2)}) copy-start(s32[1023]{0:T(1024)} %param.25) | copy-start | bytes 12280
  0.7 11.0 %copy-start.3 = (s32[16]{0:T(128)S(1)}, s32[16]{0:T(128)}, u32[]{:S(2)}) copy-start(s32[16]{0:T(128)} %refs_0_.10) | copy-start | bytes 196
  2.5 21.1 %copy-start.4 = (s32[16]{0:T(128)S(1)}, s32[16]{0:T(128)}, u32[]{:S(2)}) copy-start(s32[16]{0:T(128)} %refs_1_.3) | copy-start | bytes 196
  2.5 21.1 %all-to-all-start = ((bf16[16,32,384]{2,1,0:T(8,128)(2,1)}), bf16[16,32,384]{2,1,0:T(8,128)(2,1)S(1)}, u32[]{:S(2)}, u32[]{:S(2)}) async-start(bf16[16,32,384]{2,1,0:T(8,128)(2,1)} %pad_maximum_fusion), calls=%async_computation | async-start | bytes 786432 | tf_op jit(solution)/shard_map/all_to_all | solution.py:748
  25.0 18.1 %all-to-all-start.1 = ((bf16[16,32,384]{2,1,0:T(8,128)(2,1)}), bf16[16,32,384]{2,1,0:T(8,128)(2,1)S(1)}, u32[]{:S(2)}, u32[]{:S(2)}) async-start(bf16[16,32,384]{2,1,0:T(8,128)(2,1)} %shard_map.358), calls=%async_computation.1 | async-start | bytes 786432 | tf_op jit(solution)/shard_map/all_to_all | solution.py:748
  36.2 1.8 %collective-permute-start = (bf16[512,384]{1,0:T(8,128)(2,1)S(1)}, bf16[512,384]{1,0:T(8,128)(2,1)S(1)}, u32[]{:S(2)}, u32[]{:S(2)}) collective-permute-start(bf16[512,384]{1,0:T(8,128)(2,1)S(1)} %get-tuple-element.116.refs_1_), channel_id=1, source_target_pairs={{0,1},{1,0},{2,3},{3,2},{4,5},{5,4},{6,7},{7,6},{8,9},{9,8},{10,11... | collective-permute-start | bytes 1179656 | tf_op jit(solution)/shard_map/ppermute | solution.py:744
  41.8 1.8 %collective-permute-start.1 = (bf16[512,384]{1,0:T(8,128)(2,1)S(1)}, bf16[512,384]{1,0:T(8,128)(2,1)S(1)}, u32[]{:S(2)}, u32[]{:S(2)}) collective-permute-start(bf16[512,384]{1,0:T(8,128)(2,1)S(1)} %get-tuple-element.117.refs_1_), channel_id=1, source_target_pairs={{0,1},{1,0},{2,3},{3,2},{4,5},{5,4},{6,7},{7,6},{8,9},{9,8},{10,11... | collective-permute-start | bytes 1179656 | tf_op jit(solution)/shard_map/ppermute | solution.py:744
  43.1 7.8 %copy-start = (bf16[16,32,384]{2,1,0:T(8,128)(2,1)}, bf16[16,32,384]{2,1,0:T(8,128)(2,1)S(1)}, u32[]{:S(2)}) copy-start(bf16[16,32,384]{2,1,0:T(8,128)(2,1)S(1)} %all-to-all-done.1.refs_8_.refs_2_) | copy-start | bytes 1179652
  43.1 1.7 %collective-permute-start.2 = (bf16[16,32,384]{2,1,0:T(8,128)(2,1)S(1)}, bf16[16,32,384]{2,1,0:T(8,128)(2,1)S(1)}, u32[]{:S(2)}, u32[]{:S(2)}) collective-permute-start(bf16[16,32,384]{2,1,0:T(8,128)(2,1)S(1)} %all-to-all-done.1.refs_8_.refs_2_), channel_id=1, source_target_pairs={{0,1},{1,0},{2,3},{3,2},{4,5},{5,4},{6,7},{7,6},{8,9},{9,8},{10,11... | collective-permute-start | bytes 1179656 | tf_op jit(solution)/shard_map/ppermute | solution.py:744
  44.8 6.1 %copy-start.1 = (bf16[16,32,384]{2,1,0:T(8,128)(2,1)}, bf16[16,32,384]{2,1,0:T(8,128)(2,1)S(1)}, u32[]{:S(2)}) copy-start(bf16[16,32,384]{2,1,0:T(8,128)(2,1)S(1)} %collective-permute-done.2.refs_9_.refs_3_) | copy-start | bytes 1179652
  50.9 3.7 %collective-permute-start.3 = (bf16[512,384]{1,0:T(8,128)(2,1)S(1)}, bf16[512,384]{1,0:T(8,128)(2,1)S(1)}, u32[]{:S(2)}, u32[]{:S(2)}) collective-permute-start(bf16[512,384]{1,0:T(8,128)(2,1)S(1)} %get-tuple-element.124.refs_1_), channel_id=1, source_target_pairs={{0,1},{1,0},{2,3},{3,2},{4,5},{5,4},{6,7},{7,6},{8,9},{9,8},{10,11... | collective-permute-start | bytes 1179656 | tf_op jit(solution)/shard_map/ppermute | solution.py:744
  51.1 16.6 %collective-permute-start.4 = (bf16[384,384]{1,0:T(8,128)(2,1)S(1)}, bf16[384,384]{1,0:T(8,128)(2,1)S(1)}, u32[]{:S(2)}, u32[]{:S(2)}) collective-permute-start(bf16[384,384]{1,0:T(8,128)(2,1)S(1)} %get-tuple-element.132), channel_id=1, source_target_pairs={{0,2},{2,0},{4,6},{6,4},{8,10},{10,8},{12,14},{14,12},{16,18},{18,... | collective-permute-start | bytes 884744 | tf_op jit(solution)/shard_map/ppermute | solution.py:755
  52.3 15.5 %collective-permute-start.5 = (bf16[384,384]{1,0:T(8,128)(2,1)S(1)}, bf16[384,384]{1,0:T(8,128)(2,1)S(1)}, u32[]{:S(2)}, u32[]{:S(2)}) collective-permute-start(bf16[384,384]{1,0:T(8,128)(2,1)S(1)} %get-tuple-element.133), channel_id=1, source_target_pairs={{0,4},{2,6},{4,0},{6,2},{8,12},{10,14},{12,8},{14,10},{16,20},{18,... | collective-permute-start | bytes 884744 | tf_op jit(solution)/shard_map/ppermute | solution.py:755
  53.8 14.0 %collective-permute-start.6 = (bf16[384,384]{1,0:T(8,128)(2,1)S(1)}, bf16[384,384]{1,0:T(8,128)(2,1)S(1)}, u32[]{:S(2)}, u32[]{:S(2)}) collective-permute-start(bf16[384,384]{1,0:T(8,128)(2,1)S(1)} %get-tuple-element.134), channel_id=1, source_target_pairs={{0,6},{2,4},{4,2},{6,0},{8,14},{10,12},{12,10},{14,8},{16,22},{18,... | collective-permute-start | bytes 884744 | tf_op jit(solution)/shard_map/ppermute | solution.py:755
  68.0 11.7 %collective-permute-start.7 = (bf16[384,384]{1,0:T(8,128)(2,1)S(1)}, bf16[384,384]{1,0:T(8,128)(2,1)S(1)}, u32[]{:S(2)}, u32[]{:S(2)}) collective-permute-start(bf16[384,384]{1,0:T(8,128)(2,1)S(1)} %add_convert_fusion.2), channel_id=1, source_target_pairs={{0,8},{2,10},{4,12},{6,14},{8,0},{10,2},{12,4},{14,6},{16,24},{18,... | collective-permute-start | bytes 884744 | tf_op jit(solution)/shard_map/ppermute | solution.py:885
  79.8 2.5 %collective-permute-start.8 = (bf16[768,384]{1,0:T(8,128)(2,1)}, bf16[768,384]{1,0:T(8,128)(2,1)S(1)}, u32[]{:S(2)}, u32[]{:S(2)}) collective-permute-start(bf16[768,384]{1,0:T(8,128)(2,1)} %get-tuple-element.152.refs_1_), channel_id=1, source_target_pairs={{0,1},{1,0},{2,3},{3,2},{4,5},{5,4},{6,7},{7,6},{8,9},{9,8},{10,11... | collective-permute-start | bytes 1769480 | tf_op jit(solution)/shard_map/ppermute | solution.py:744
  79.9 22.2 %collective-permute-start.12 = (bf16[384,384]{1,0:T(8,128)(2,1)S(1)}, bf16[384,384]{1,0:T(8,128)(2,1)S(1)}, u32[]{:S(2)}, u32[]{:S(2)}) collective-permute-start(bf16[384,384]{1,0:T(8,128)(2,1)S(1)} %add_convert_fusion.1), channel_id=1, source_target_pairs={{0,16},{2,18},{4,20},{6,22},{8,24},{10,26},{12,28},{14,30},{16,0},... | collective-permute-start | bytes 884744 | tf_op jit(solution)/shard_map/ppermute | solution.py:885
  82.3 4.4 %copy-start.2 = (bf16[768,384]{1,0:T(8,128)(2,1)}, bf16[768,384]{1,0:T(8,128)(2,1)S(1)}, u32[]{:S(2)}) copy-start(bf16[768,384]{1,0:T(8,128)(2,1)S(1)} %collective-permute-done.8.refs_11_.refs_2_) | copy-start | bytes 1769476
  86.7 15.3 %collective-permute-start.9 = (bf16[272,384]{1,0:T(8,128)(2,1)S(1)}, bf16[272,384]{1,0:T(8,128)(2,1)S(1)}, u32[]{:S(2)}, u32[]{:S(2)}) collective-permute-start(bf16[272,384]{1,0:T(8,128)(2,1)S(1)} %get-tuple-element.156), channel_id=1, source_target_pairs={{0,2},{2,0},{4,6},{6,4},{8,10},{10,8},{12,14},{14,12},{16,18},{18,... | collective-permute-start | bytes 626696 | tf_op jit(solution)/shard_map/ppermute | solution.py:755
  88.1 13.9 %collective-permute-start.10 = (bf16[272,384]{1,0:T(8,128)(2,1)S(1)}, bf16[272,384]{1,0:T(8,128)(2,1)S(1)}, u32[]{:S(2)}, u32[]{:S(2)}) collective-permute-start(bf16[272,384]{1,0:T(8,128)(2,1)S(1)} %get-tuple-element.157), channel_id=1, source_target_pairs={{0,4},{2,6},{4,0},{6,2},{8,12},{10,14},{12,8},{14,10},{16,20},{18,... | collective-permute-start | bytes 626696 | tf_op jit(solution)/shard_map/ppermute | solution.py:755
  89.6 12.4 %collective-permute-start.11 = (bf16[272,384]{1,0:T(8,128)(2,1)S(1)}, bf16[272,384]{1,0:T(8,128)(2,1)S(1)}, u32[]{:S(2)}, u32[]{:S(2)}) collective-permute-start(bf16[272,384]{1,0:T(8,128)(2,1)S(1)} %get-tuple-element.158), channel_id=1, source_target_pairs={{0,6},{2,4},{4,2},{6,0},{8,14},{10,12},{12,10},{14,8},{16,22},{18,... | collective-permute-start | bytes 626696 | tf_op jit(solution)/shard_map/ppermute | solution.py:755
  102.2 4.2 %collective-permute-start.13 = (bf16[512,384]{1,0:T(8,128)(2,1)S(1)}, bf16[512,384]{1,0:T(8,128)(2,1)S(1)}, u32[]{:S(2)}, u32[]{:S(2)}) collective-permute-start(bf16[512,384]{1,0:T(8,128)(2,1)S(1)} %get-tuple-element.167.refs_1_), channel_id=1, source_target_pairs={{0,1},{1,0},{2,3},{3,2},{4,5},{5,4},{6,7},{7,6},{8,9},{9,8},{10,11... | collective-permute-start | bytes 1179656 | tf_op jit(solution)/shard_map/ppermute | solution.py:744
  102.3 7.6 %collective-permute-start.14 = (bf16[272,384]{1,0:T(8,128)(2,1)S(1)}, bf16[272,384]{1,0:T(8,128)(2,1)S(1)}, u32[]{:S(2)}, u32[]{:S(2)}) collective-permute-start(bf16[272,384]{1,0:T(8,128)(2,1)S(1)} %add_convert_fusion.5), channel_id=1, source_target_pairs={{0,8},{2,10},{4,12},{6,14},{8,0},{10,2},{12,4},{14,6},{16,24},{18,... | collective-permute-start | bytes 626696 | tf_op jit(solution)/shard_map/ppermute | solution.py:885
  102.9 14.0 %collective-permute-start.18 = (bf16[384,384]{1,0:T(8,128)(2,1)S(1)}, bf16[384,384]{1,0:T(8,128)(2,1)S(1)}, u32[]{:S(2)}, u32[]{:S(2)}) collective-permute-start(bf16[384,384]{1,0:T(8,128)(2,1)S(1)} %add_convert_fusion.refs_0_), channel_id=1, source_target_pairs={{0,6},{2,4},{4,2},{6,0},{8,14},{10,12},{12,10},{14,8},{16,22},{18,... | collective-permute-start | bytes 884744 | tf_op jit(solution)/shard_map/ppermute | solution.py:755
  105.2 14.1 %collective-permute-start.17 = (bf16[384,384]{1,0:T(8,128)(2,1)S(1)}, bf16[384,384]{1,0:T(8,128)(2,1)S(1)}, u32[]{:S(2)}, u32[]{:S(2)}) collective-permute-start(bf16[384,384]{1,0:T(8,128)(2,1)S(1)} %add_convert_fusion.refs_0_), channel_id=1, source_target_pairs={{0,4},{2,6},{4,0},{6,2},{8,12},{10,14},{12,8},{14,10},{16,20},{18,... | collective-permute-start | bytes 884744 | tf_op jit(solution)/shard_map/ppermute | solution.py:755
  105.7 13.6 %collective-permute-start.16 = (bf16[384,384]{1,0:T(8,128)(2,1)S(1)}, bf16[384,384]{1,0:T(8,128)(2,1)S(1)}, u32[]{:S(2)}, u32[]{:S(2)}) collective-permute-start(bf16[384,384]{1,0:T(8,128)(2,1)S(1)} %add_convert_fusion.refs_0_), channel_id=1, source_target_pairs={{0,2},{2,0},{4,6},{6,4},{8,10},{10,8},{12,14},{14,12},{16,18},{18,... | collective-permute-start | bytes 884744 | tf_op jit(solution)/shard_map/ppermute | solution.py:755
  109.9 12.1 %collective-permute-start.19 = (bf16[272,384]{1,0:T(8,128)(2,1)S(1)}, bf16[272,384]{1,0:T(8,128)(2,1)S(1)}, u32[]{:S(2)}, u32[]{:S(2)}) collective-permute-start(bf16[272,384]{1,0:T(8,128)(2,1)S(1)} %add_convert_fusion.4), channel_id=1, source_target_pairs={{0,16},{2,18},{4,20},{6,22},{8,24},{10,26},{12,28},{14,30},{16,0},... | collective-permute-start | bytes 626696 | tf_op jit(solution)/shard_map/ppermute | solution.py:885
  112.1 2.3 %collective-permute-start.15 = (bf16[512,384]{1,0:T(8,128)(2,1)S(1)}, bf16[512,384]{1,0:T(8,128)(2,1)S(1)}, u32[]{:S(2)}, u32[]{:S(2)}) collective-permute-start(bf16[512,384]{1,0:T(8,128)(2,1)S(1)} %get-tuple-element.171.refs_0_), channel_id=1, source_target_pairs={{0,1},{1,0},{2,3},{3,2},{4,5},{5,4},{6,7},{7,6},{8,9},{9,8},{10,11... | collective-permute-start | bytes 1179656 | tf_op jit(solution)/shard_map/ppermute | solution.py:744
  122.1 9.0 %collective-permute-start.22 = (bf16[272,384]{1,0:T(8,128)(2,1)S(1)}, bf16[272,384]{1,0:T(8,128)(2,1)S(1)}, u32[]{:S(2)}, u32[]{:S(2)}) collective-permute-start(bf16[272,384]{1,0:T(8,128)(2,1)S(1)} %add_convert_fusion.3.refs_0_), channel_id=1, source_target_pairs={{0,6},{2,4},{4,2},{6,0},{8,14},{10,12},{12,10},{14,8},{16,22},{18,... | collective-permute-start | bytes 626696 | tf_op jit(solution)/shard_map/ppermute | solution.py:755
  124.4 10.2 %collective-permute-start.21 = (bf16[272,384]{1,0:T(8,128)(2,1)S(1)}, bf16[272,384]{1,0:T(8,128)(2,1)S(1)}, u32[]{:S(2)}, u32[]{:S(2)}) collective-permute-start(bf16[272,384]{1,0:T(8,128)(2,1)S(1)} %add_convert_fusion.3.refs_0_), channel_id=1, source_target_pairs={{0,4},{2,6},{4,0},{6,2},{8,12},{10,14},{12,8},{14,10},{16,20},{18,... | collective-permute-start | bytes 626696 | tf_op jit(solution)/shard_map/ppermute | solution.py:755
  124.9 9.7 %collective-permute-start.20 = (bf16[272,384]{1,0:T(8,128)(2,1)S(1)}, bf16[272,384]{1,0:T(8,128)(2,1)S(1)}, u32[]{:S(2)}, u32[]{:S(2)}) collective-permute-start(bf16[272,384]{1,0:T(8,128)(2,1)S(1)} %add_convert_fusion.3.refs_0_), channel_id=1, source_target_pairs={{0,2},{2,0},{4,6},{6,4},{8,10},{10,8},{12,14},{14,12},{16,18},{18,... | collective-permute-start | bytes 626696 | tf_op jit(solution)/shard_map/ppermute | solution.py:755
  135.7 2.5 %collective-permute-start.23 = (bf16[256,384]{1,0:T(8,128)(2,1)S(1)}, bf16[256,384]{1,0:T(8,128)(2,1)S(1)}, u32[]{:S(2)}, u32[]{:S(2)}) collective-permute-start(bf16[256,384]{1,0:T(8,128)(2,1)S(1)} %shard_map.370.refs_0_), channel_id=1, source_target_pairs={{0,1},{1,0},{2,3},{3,2},{4,5},{5,4},{6,7},{7,6},{8,9},{9,8},{10,11... | collective-permute-start | bytes 589832 | tf_op jit(solution)/shard_map/ppermute | solution.py:744
